TPU v7x, 32 devices: a whole 2x2x4 slice. The times are simulated.
32 devices in a mesh: gx: 4 (over z), gy: 8 (over y, x, core).
Axes of the slice: x: 2, y: 2, z: 4, core: 2. Of those that a mesh axis runs over, the one named last changes fastest.
Arguments:
- gauss_params: float32 [55, 65536], P(None, ('gx', 'gy')), may hold values from -16 to 2064, as said below
- first_moment: float32 [55, 65536], P(None, ('gx', 'gy')), may hold values from -0.3 to 0.3
- second_moment: float32 [55, 65536], P(None, ('gx', 'gy')), may hold values from 0.001 to 0.1
- splat_lists: int32 [2, 512, 512], P(None, ('gx', 'gy')), may hold values from 0 to 65535, as said below
- tile_ids: int32 [2, 512], P(None, ('gx', 'gy')), may hold values from 0 to 2047, as said below
- targets: float32 [2, 512, 3, 256], P(None, ('gx', 'gy')), may hold values from 0 to 1
- camera: float32 [2, 2], replicated, may hold values from -3 to 3
Outputs:
- updated_params: float32 [55, 65536], P(None, ('gx', 'gy'))
- updated_first: float32 [55, 65536], P(None, ('gx', 'gy'))
- updated_second: float32 [55, 65536], P(None, ('gx', 'gy'))
- rendered: float32 [2, 512, 3, 256], P(None, ('gx', 'gy'))
- loss: float32 [2], replicated
Inputs may be any that keep to these rules, and one draw needn't show every extreme that they name: `gauss_params`: rows of each column: x and y (positions scaled by depth), depth z in [1, 2], two log scales, an angle, an opacity logit, then 16 harmonic coefficients for red, green and blue in turn. `splat_lists`: gaussian ids; the Gaussians with ids k * 2048 to (k + 1) * 2048 - 1 belong to device k along gx+gy. In each step, the entries of one device's 16 tile slots name Gaussians of one owner at most 512 times, and some owner is named exactly 512 times by every device. `tile_ids`: image tiles numbered row by row over 64 columns; within a step, slots show distinct tiles while 512 <= 2048.
All inputs are finite; a program needn't handle non-finite values.
Results may differ from a plain program's by a relative error of at most 0.0014.
Values sent between devices are 32-bit elements; how exact they have to be, the bound alone decides.
No kernel may reach another device: no remote copies, remote signals or barrier semaphores. Data moves between devices by JAX's collectives and lax.ppermute only.
A program may use at most 64 MiB of HBM per device.

v0:
```python
import jax
import jax.numpy as jnp
from jax import lax
from jax.sharding import PartitionSpec as P

SIDE = 16
NCOEF = 16
STEPS = 2
IMG_TX = 64
IMG_TY = 32


beta_one = 0.9
beta_two = 0.999
adam_eps = 1e-08
learn_rate = 0.01
adam_start = 1000
splat_fields = 9
band_zero = 0.28209479177387814
band_one = 0.4886025119029199
band_two = (
    1.0925484305920792,
    -1.0925484305920792,
    0.31539156525252005,
    -1.0925484305920792,
    0.5462742152960396,
)
band_three = (
    -0.5900435899266435,
    2.890611442640554,
    -0.4570457994644658,
    0.3731763325901154,
    -0.4570457994644658,
    1.445305721320277,
    -0.5900435899266435,
)


def harmonics(ray_x, ray_y, ray_z):
    sq_x = ray_x * ray_x
    sq_y = ray_y * ray_y
    sq_z = ray_z * ray_z
    return jnp.stack(
        [
            band_zero * jnp.ones_like(ray_x),
            -band_one * ray_y,
            band_one * ray_z,
            -band_one * ray_x,
            band_two[0] * ray_x * ray_y,
            band_two[1] * ray_y * ray_z,
            band_two[2] * (2.0 * sq_z - sq_x - sq_y),
            band_two[3] * ray_x * ray_z,
            band_two[4] * (sq_x - sq_y),
            band_three[0] * ray_y * (3.0 * sq_x - sq_y),
            band_three[1] * ray_x * ray_y * ray_z,
            band_three[2] * ray_y * (4.0 * sq_z - sq_x - sq_y),
            band_three[3] * ray_z * (2.0 * sq_z - 3.0 * sq_x - 3.0 * sq_y),
            band_three[4] * ray_x * (4.0 * sq_z - sq_x - sq_y),
            band_three[5] * ray_z * (sq_x - sq_y),
            band_three[6] * ray_x * (sq_x - 3.0 * sq_y),
        ]
    )


def project(gauss_rows, camera_row):
    image_width = 1.0 * SIDE * IMG_TX
    image_height = 1.0 * SIDE * IMG_TY
    depth_z = gauss_rows[2]
    screen_u = (gauss_rows[0] - camera_row[0]) / depth_z
    screen_v = (gauss_rows[1] - camera_row[1]) / depth_z
    inv_one = depth_z * depth_z * jnp.exp(-2.0 * gauss_rows[3])
    inv_two = depth_z * depth_z * jnp.exp(-2.0 * gauss_rows[4])
    cosine = jnp.cos(gauss_rows[5])
    sine_angle = jnp.sin(gauss_rows[5])
    conic_a = cosine * cosine * inv_one + sine_angle * sine_angle * inv_two
    conic_b = cosine * sine_angle * (inv_one - inv_two)
    conic_c = sine_angle * sine_angle * inv_one + cosine * cosine * inv_two
    opacity = 0.99 * jax.nn.sigmoid(gauss_rows[6])
    ray_x = (screen_u - 0.5 * image_width) / image_width
    ray_y = (screen_v - 0.5 * image_height) / image_width
    factor = lax.rsqrt(ray_x * ray_x + ray_y * ray_y + 1.0)
    harmonic_basis = harmonics(ray_x * factor, ray_y * factor, factor)
    coeffs = gauss_rows[7:].reshape(3, NCOEF, gauss_rows.shape[1])
    colour = 0.5 + jnp.sum(coeffs * harmonic_basis[None], axis=1)
    geometry = jnp.stack([screen_u, screen_v, conic_a, conic_b, conic_c, opacity])
    return jnp.concatenate([geometry, colour], 0)


def pixel_grid(tile_row):
    cell_index = jnp.arange(SIDE * SIDE, dtype=jnp.int32)
    column = (tile_row % IMG_TX)[:, None] * SIDE + cell_index % SIDE
    row_pix = (tile_row // IMG_TX)[:, None] * SIDE + cell_index // SIDE
    return jnp.stack([column, row_pix], 1).astype(jnp.float32) + 0.5


def lower_mask(dtype):
    return (
        lax.broadcasted_iota(jnp.int32, (128, 128), 0)
        > lax.broadcasted_iota(jnp.int32, (128, 128), 1)
    ).astype(dtype)


def prefix_sum(log_keep):
    block_count = log_keep.shape[0] // 128
    blocks = log_keep.reshape(block_count, 128, log_keep.shape[1])
    within = jnp.einsum(
        "ij,bjp->bip", lower_mask(jnp.float32), blocks, precision=lax.Precision.HIGHEST
    )
    totals = jnp.sum(blocks, axis=1)
    carry_in = jnp.cumsum(totals, axis=0) - totals
    return (within + carry_in[:, None, :]).reshape(log_keep.shape)


def render(splat_rows, centres):
    delta_x = centres[0][None, :] - splat_rows[0][:, None]
    delta_y = centres[1][None, :] - splat_rows[1][:, None]
    exponent = -0.5 * (
        splat_rows[2][:, None] * delta_x * delta_x
        + 2.0 * splat_rows[3][:, None] * delta_x * delta_y
        + splat_rows[4][:, None] * delta_y * delta_y
    )
    opaque = splat_rows[5][:, None] * jnp.exp(exponent)
    log_keep = jnp.log1p(-opaque)
    weight = jnp.exp(prefix_sum(log_keep)) * opaque
    return jnp.dot(
        splat_rows[6:9], weight, precision=lax.Precision.HIGHEST, preferred_element_type=jnp.float32
    )


def tile_terms(splat_rows, centres, target):
    picture, pullback = jax.vjp(lambda values: render(values, centres), splat_rows)
    residual = picture - target
    return (picture, pullback(residual)[0], 0.5 * jnp.sum(residual * residual))


def bucket_positions(owner_of, owners, capacity):
    slot_count = owner_of.shape[0]
    block_count = slot_count // 128
    member = (owner_of[:, None] == jnp.arange(owners, dtype=jnp.int32)[None, :]).reshape(
        block_count, 128, owners
    )
    blocks = member.astype(jnp.bfloat16)
    within = jnp.einsum(
        "ij,bjo->bio", lower_mask(jnp.bfloat16), blocks, preferred_element_type=jnp.float32
    )
    totals = within[:, 127, :] + blocks[:, 127, :].astype(jnp.float32)
    carry_in = jnp.cumsum(totals, axis=0) - totals
    ahead_of = within + carry_in[:, None, :]
    rank_in = jnp.sum(jnp.where(member, ahead_of, 0.0), axis=2).reshape(slot_count)
    return owner_of * capacity + rank_in.astype(jnp.int32)


def route_ids(request):
    return lax.all_to_all(request, ("gx", "gy"), split_axis=0, concat_axis=0, tiled=True)


def route_rows(outgoing):
    return lax.all_to_all(outgoing, ("gx", "gy"), split_axis=1, concat_axis=1, tiled=True)


def adam_update(params, moment_one, second, gradient, step_index):
    step_count = adam_start + step_index + 1
    moment_one = beta_one * moment_one + (1.0 - beta_one) * gradient
    second = beta_two * second + (1.0 - beta_two) * gradient * gradient
    scaled_first = moment_one / (1.0 - beta_one**step_count)
    scaled_second = second / (1.0 - beta_two**step_count)
    params = params - learn_rate * scaled_first / (jnp.sqrt(scaled_second) + adam_eps)
    return (params, moment_one, second)


def per_device(gauss_params, first_moment, second_moment, splat_lists, tile_ids, targets, camera):
    owners = lax.axis_size(("gx", "gy"))
    local_count = gauss_params.shape[1]
    tile_count = splat_lists.shape[1]
    list_length = splat_lists.shape[2]
    capacity = 2 * tile_count * list_length // owners
    params, moment_one, moment_two = (gauss_params, first_moment, second_moment)
    pictures = []
    local_losses = []
    for step_index in range(STEPS):
        camera_row = camera[step_index]
        listed = splat_lists[step_index].reshape(-1)
        owner_of = listed // local_count
        local_id = listed % local_count
        slot_pos = bucket_positions(owner_of, owners, capacity)
        request = jnp.zeros((owners * capacity,), jnp.int32).at[slot_pos].set(local_id)
        wanted = route_ids(request)
        centres = pixel_grid(tile_ids[step_index])
        projected, pullback = jax.vjp(lambda values: project(values, camera_row), params)
        reply = route_rows(projected[:, wanted])
        gathered = jnp.moveaxis(
            reply[:, slot_pos].reshape(splat_fields, tile_count, list_length), 1, 0
        )
        picture, slot_grads, halves = lax.map(
            lambda tile_parts: tile_terms(tile_parts[0], tile_parts[1], tile_parts[2]),
            (gathered, centres, targets[step_index]),
        )
        field_count = slot_grads.shape[1]
        flat_grads = jnp.moveaxis(slot_grads, 0, 1).reshape(field_count, tile_count * list_length)
        outgoing = (
            jnp.zeros((field_count, owners * capacity), jnp.float32).at[:, slot_pos].set(flat_grads)
        )
        incoming = route_rows(outgoing)
        summed = jnp.zeros((field_count, local_count), jnp.float32).at[:, wanted].add(incoming)
        gradient = pullback(summed)[0]
        params, moment_one, moment_two = adam_update(
            params, moment_one, moment_two, gradient, step_index
        )
        pictures.append(picture)
        local_losses.append(jnp.sum(halves))
    totals = lax.psum(jnp.stack(local_losses), ("gx", "gy"))
    loss_values = totals / (3.0 * SIDE * SIDE * tile_count * owners)
    return (params, moment_one, moment_two, jnp.stack(pictures), loss_values)


def solution(mesh):
    in_specs = (
        P(None, ("gx", "gy")),
        P(None, ("gx", "gy")),
        P(None, ("gx", "gy")),
        P(None, ("gx", "gy"), None),
        P(None, ("gx", "gy")),
        P(None, ("gx", "gy"), None, None),
        P(),
    )
    out_specs = (
        P(None, ("gx", "gy")),
        P(None, ("gx", "gy")),
        P(None, ("gx", "gy")),
        P(None, ("gx", "gy"), None, None),
        P(),
    )
    return jax.shard_map(
        per_device, mesh=mesh, in_specs=in_specs, out_specs=out_specs, check_vma=False
    )
```

profile of v0, /device:TPU:0, one launch (start us, length us, event | category | flops | bytes accessed | tf_op | source)
XLA Modules:
  0.0 1099.1 jit_solution(10450591155480129241)
XLA Ops:
  8.0 31.0 %scatter_custom_fusion = s32[16384]{0:T(1024)} fusion(s32[8192]{0:T(1024)S(1)} %bitcast.584, s32[8192]{0:T(1024)S(1)} %add_select_fusion.3, s32[]{:T(128)} %constant.221.clone.1), kind=kCustom, calls=%fused_computation.239 | custom fusion | bytes 65540 | tf_op jit(solution)/shard_map/scatter | solution.py:186
  39.0 7.8 all-to-all-start
  50.0 3.2 broadcast_multiply_fusion.13
  65.1 54.4 %gather_fusion = f32[16384,9]{1,0:T(8,128)} fusion(f32[9,2048]{0,1:T(8,128)S(1)} %copy.916, s32[16384]{0:T(1024)S(1)} %broadcast_clamp_fusion.1), kind=kCustom, calls=%fused_computation | custom fusion | bytes 1245184 | tf_op jit(solution)/shard_map/gather | solution.py:190
  119.5 6.1 copy.917
  125.6 5.9 all-to-all-start.1
  131.6 31.0 %scatter_custom_fusion.3 = s32[16384]{0:T(1024)} fusion(s32[8192]{0:T(1024)S(1)} %bitcast.581, s32[8192]{0:T(1024)S(1)} %add_select_fusion.2, s32[]{:T(128)} %constant.221.clone.1), kind=kCustom, calls=%fused_computation.237 | custom fusion | bytes 65540 | tf_op jit(solution)/shard_map/scatter | solution.py:186
  164.1 6.0 all-to-all-start.3
  170.1 4.7 copy.918
  174.8 31.1 %gather_fusion.1 = f32[8192,9]{1,0:T(8,128)} fusion(f32[9,16384]{0,1:T(8,128)} %bitcast.446, s32[8192]{0:T(1024)S(1)} %broadcast_clamp_fusion.3), kind=kCustom, calls=%fused_computation.1 | custom fusion | bytes 622592 | tf_op jit(solution)/shard_map/gather | solution.py:192
  208.8 127.7 %while.28 = (s32[]{:T(128)}, f32[16,3,256]{2,0,1:T(8,128)S(1)}, f32[16,9,512]{2,1,0:T(8,128)S(1)}, f32[16]{0:T(128)S(1)}, f32[16,9,512]{2,1,0:T(8,128)S(1)}, /*i...) while((s32[]{:T(128)}, f32[16,3,256]{2,0,1:T(8,128)S(1)}, ...), condition=%wide.region_16.17_spmd, body=%wide.region_4.16_spmd.sunk | while | flops 431557888 | bytes 10248509 | solution.py:194
  339.7 24.5 %scatter_custom_fusion.1 = f32[9,16384]{0,1:T(8,128)} fusion(s32[8192]{0:T(1024)S(1)} %bitcast.586, f32[8192,9]{1,0:T(8,128)} %copy.922, f32[]{:T(128)} %constant.220.clone.1), kind=kCustom, calls=%fused_computation.164 | custom fusion | bytes 590336 | tf_op jit(solution)/shard_map/scatter | solution.py:201
  364.3 6.1 copy.923
  370.4 6.2 all-to-all-start.2
  377.9 24.9 %all-to-all-done.2 = f32[9,32,512]{2,0,1:T(8,128)S(1)} async-done(((f32[9,32,512]{2,0,1:T(8,128)}), f32[9,32,512]{2,0,1:T(8,128)S(1)}, u32[]{:S(2)}, u32[]{:S(2)}) %all-to-all-start.2) | async-done | bytes 589856 | tf_op jit(solution)/shard_map/all_to_all | solution.py:158
  403.8 4.7 copy.925
  408.5 101.2 %scatter_custom_fusion.2 = f32[9,2048]{0,1:T(8,128)S(1)} fusion(s32[16384]{0:T(1024)S(1)} %bitcast.534, f32[16384,9]{1,0:T(8,128)} %copy.925, f32[]{:T(128)} %constant.220.clone.1), kind=kCustom, calls=%fused_computation.174 | custom fusion | flops 147456 | bytes 74240 | tf_op jit(solution)/shard_map/scatter-add | solution.py:204
  509.7 3.4 fusion.178
  539.1 54.4 %gather_fusion.2 = f32[16384,9]{1,0:T(8,128)} fusion(f32[9,2048]{0,1:T(8,128)S(1)} %copy.942, s32[16384]{0:T(1024)S(1)} %copy-done.8), kind=kCustom, calls=%fused_computation.2 | custom fusion | bytes 1245184 | tf_op jit(solution)/shard_map/gather | solution.py:190
  593.5 6.1 copy.943
  599.6 4.0 all-to-all-start.4
  605.0 24.8 %all-to-all-done.4 = f32[9,32,512]{2,0,1:T(8,128)S(1)} async-done(((f32[9,32,512]{2,0,1:T(8,128)}), f32[9,32,512]{2,0,1:T(8,128)S(1)}, u32[]{:S(2)}, u32[]{:S(2)}) %all-to-all-start.4) | async-done | bytes 589856 | tf_op jit(solution)/shard_map/all_to_all | solution.py:158
  629.8 4.7 copy.944
  634.5 31.1 %gather_fusion.3 = f32[8192,9]{1,0:T(8,128)} fusion(f32[9,16384]{0,1:T(8,128)} %bitcast.447, s32[8192]{0:T(1024)S(1)} %broadcast_clamp_fusion.2), kind=kCustom, calls=%fused_computation.3 | custom fusion | bytes 622592 | tf_op jit(solution)/shard_map/gather | solution.py:192
  670.5 210.4 %while.29 = (s32[]{:T(128)}, f32[16,3,256]{2,0,1:T(8,128)}, f32[16,9,512]{2,1,0:T(8,128)}, f32[16]{0:T(128)}, f32[16,9,512]{2,1,0:T(8,128)S(1)}, /*index=5*/f32[...) while((s32[]{:T(128)}, f32[16,3,256]{2,0,1:T(8,128)}, ...), condition=%wide.region_36.37_spmd, body=%wide.region_24.36_spmd.sunk | while | flops 431557888 | bytes 12605805 | solution.py:194
  885.1 24.5 %scatter_custom_fusion.4 = f32[9,16384]{0,1:T(8,128)} fusion(s32[8192]{0:T(1024)} %bitcast.582, f32[8192,9]{1,0:T(8,128)} %copy.948, f32[]{:T(128)} %constant.220.clone.1), kind=kCustom, calls=%fused_computation.162 | custom fusion | bytes 590336 | tf_op jit(solution)/shard_map/scatter | solution.py:201
  909.6 6.1 copy.949
  915.7 3.6 all-to-all-start.5
  922.0 43.9 %psum.7 = f32[2]{0:T(128)S(1)} all-reduce(f32[2]{0:T(128)S(1)} %pad_maximum_fusion.1), channel_id=1, replica_groups=mesh['gx'=4,'gy'=8] {'gx','gy'}, use_global_device_ids=true, to_apply=%region_42.43 | all-reduce | flops 2 | bytes 16 | tf_op jit(solution)/shard_map/psum | solution.py:211
  968.1 4.7 copy.951
  972.8 100.6 %scatter_custom_fusion.5 = f32[9,2048]{0,1:T(8,128)S(1)} fusion(s32[16384]{0:T(1024)} %bitcast.532, f32[16384,9]{1,0:T(8,128)} %copy.951, f32[]{:T(128)} %constant.220.clone.1), kind=kCustom, calls=%fused_computation.172 | custom fusion | flops 147456 | bytes 74240 | tf_op jit(solution)/shard_map/scatter-add | solution.py:204
  1073.4 3.7 fusion.177
  (995 shorter events, 410.5 us)
Async XLA Ops:
  3.8 45.5 %copy-start.44 = (f32[2,2]{1,0:T(2,128)S(1)}, f32[2,2]{1,0:T(2,128)}, u32[]{:S(2)}) copy-start(f32[2,2]{1,0:T(2,128)} %param.17) | copy-start | bytes 52
  6.0 49.7 %copy-start.16 = (f32[2,16,3,256]{3,1,2,0:T(8,128)S(1)}, f32[2,16,3,256]{3,1,2,0:T(8,128)}, u32[]{:S(2)}) copy-start(f32[2,16,3,256]{3,1,2,0:T(8,128)} %param.16) | copy-start | bytes 294916
  39.0 25.9 %all-to-all-start = ((s32[32,512,1]{1,2,0:T(1,128)}), s32[32,512,1]{1,2,0:T(1,128)S(1)}, u32[]{:S(2)}, u32[]{:S(2)}) async-start(s32[32,512,1]{1,2,0:T(1,128)} %bitcast.75), calls=%async_computation | async-start | bytes 131072 | tf_op jit(solution)/shard_map/all_to_all | solution.py:154
  56.7 8.2 copy-start.43
  64.9 66.7 %copy-start.14 = (s32[8192,1]{0,1:T(1,128)}, s32[8192,1]{0,1:T(1,128)S(1)}, u32[]{:S(2)}) copy-start(s32[8192,1]{0,1:T(1,128)S(1)} %compare_select_fusion.2) | copy-start | bytes 98308
  125.6 38.5 %all-to-all-start.1 = ((f32[9,32,512]{2,0,1:T(8,128)}), f32[9,32,512]{2,0,1:T(8,128)S(1)}, u32[]{:S(2)}, u32[]{:S(2)}) async-start(f32[9,32,512]{2,0,1:T(8,128)} %copy.917), calls=%async_computation.1 | async-start | bytes 2097152 | tf_op jit(solution)/shard_map/all_to_all | solution.py:158
  164.1 206.3 %all-to-all-start.3 = ((s32[32,512,1]{1,2,0:T(1,128)}), s32[32,512,1]{1,2,0:T(1,128)S(1)}, u32[]{:S(2)}, u32[]{:S(2)}) async-start(s32[32,512,1]{1,2,0:T(1,128)} %bitcast.100), calls=%async_computation.3 | async-start | bytes 131072 | tf_op jit(solution)/shard_map/all_to_all | solution.py:154
  336.5 27.8 %copy-start.11 = (f32[16,3,256]{2,0,1:T(8,128)}, f32[16,3,256]{2,0,1:T(8,128)S(1)}, u32[]{:S(2)}) copy-start(f32[16,3,256]{2,0,1:T(8,128)S(1)} %get-tuple-element.85) | copy-start | bytes 147460
  336.5 27.8 %copy-start.45 = (f32[16]{0:T(128)}, f32[16]{0:T(128)S(1)}, u32[]{:S(2)}) copy-start(f32[16]{0:T(128)S(1)} %get-tuple-element.87) | copy-start | bytes 196
  370.4 32.3 %all-to-all-start.2 = ((f32[9,32,512]{2,0,1:T(8,128)}), f32[9,32,512]{2,0,1:T(8,128)S(1)}, u32[]{:S(2)}, u32[]{:S(2)}) async-start(f32[9,32,512]{2,0,1:T(8,128)} %copy.923), calls=%async_computation.2 | async-start | bytes 2097152 | tf_op jit(solution)/shard_map/all_to_all | solution.py:158
  514.4 10.5 copy-start.1
  525.9 12.3 %copy-start.34 = (f32[1,2048]{1,0:T(1,128)S(1)}, f32[1,2048]{1,0:T(1,128)}, u32[]{:S(2)}) copy-start(f32[1,2048]{1,0:T(1,128)} %copy-done.33) | copy-start | bytes 24580
  526.2 12.9 %copy-start.8 = (s32[16384]{0:T(1024)S(1)}, s32[16384]{0:T(1024)}, u32[]{:S(2)}) copy-start(s32[16384]{0:T(1024)} %broadcast_clamp_fusion) | copy-start | bytes 196612
  528.4 6.5 copy-start.28
  537.5 56.0 %copy-start.40 = (f32[1,2048]{1,0:T(1,128)}, f32[1,2048]{1,0:T(1,128)S(1)}, u32[]{:S(2)}) copy-start(f32[1,2048]{1,0:T(1,128)S(1)} %get-tuple-element.278) | copy-start | bytes 24580
  593.5 10.1 copy-start.10
  593.5 10.8 copy-start.41
  593.5 10.8 copy-start.42
  593.5 11.5 %copy-start.15 = (s32[8192,1]{0,1:T(1,128)S(1)}, s32[8192,1]{0,1:T(1,128)}, u32[]{:S(2)}) copy-start(s32[8192,1]{0,1:T(1,128)} %copy-done.14) | copy-start | bytes 98308
  599.6 30.2 %all-to-all-start.4 = ((f32[9,32,512]{2,0,1:T(8,128)}), f32[9,32,512]{2,0,1:T(8,128)S(1)}, u32[]{:S(2)}, u32[]{:S(2)}) async-start(f32[9,32,512]{2,0,1:T(8,128)} %copy.943), calls=%async_computation.4 | async-start | bytes 2097152 | tf_op jit(solution)/shard_map/all_to_all | solution.py:158
  743.0 6.4 copy-start.7
  861.3 6.4 copy-start.7
  909.6 9.8 copy-start.46
  909.6 10.4 copy-start.47
  909.6 56.2 %copy-start.12 = (f32[16,3,256]{2,0,1:T(8,128)S(1)}, f32[16,3,256]{2,0,1:T(8,128)}, u32[]{:S(2)}) copy-start(f32[16,3,256]{2,0,1:T(8,128)} %copy-done.11) | copy-start | bytes 147460
  909.6 56.2 %copy-start.13 = (f32[16,3,256]{2,0,1:T(8,128)S(1)}, f32[16,3,256]{2,0,1:T(8,128)}, u32[]{:S(2)}) copy-start(f32[16,3,256]{2,0,1:T(8,128)} %get-tuple-element.86) | copy-start | bytes 147460
  915.7 51.3 %all-to-all-start.5 = ((f32[9,32,512]{2,0,1:T(8,128)}), f32[9,32,512]{2,0,1:T(8,128)S(1)}, u32[]{:S(2)}, u32[]{:S(2)}) async-start(f32[9,32,512]{2,0,1:T(8,128)} %copy.949), calls=%async_computation.5 | async-start | bytes 2097152 | tf_op jit(solution)/shard_map/all_to_all | solution.py:158
  1078.4 11.8 %copy-start = (f32[1,2048]{0,1:T(8,128)S(1)}, f32[1,2048]{0,1:T(8,128)}, u32[]{:S(2)}) copy-start(f32[1,2048]{0,1:T(8,128)} %get-tuple-element.246) | copy-start | bytes 24580
  1080.6 15.3 %copy-start.18 = (f32[1,2048]{1,0:T(1,128)S(1)}, f32[1,2048]{1,0:T(1,128)}, u32[]{:S(2)}) copy-start(f32[1,2048]{1,0:T(1,128)} %copy-done.17) | copy-start | bytes 24580
  1080.6 15.3 %copy-start.20 = (f32[1,2048]{1,0:T(1,128)S(1)}, f32[1,2048]{1,0:T(1,128)}, u32[]{:S(2)}) copy-start(f32[1,2048]{1,0:T(1,128)} %copy-done.19) | copy-start | bytes 24580
  1080.6 15.3 %copy-start.22 = (f32[1,2048]{1,0:T(1,128)S(1)}, f32[1,2048]{1,0:T(1,128)}, u32[]{:S(2)}) copy-start(f32[1,2048]{1,0:T(1,128)} %copy-done.21) | copy-start | bytes 24580
  1080.6 15.3 %copy-start.24 = (f32[1,2048]{1,0:T(1,128)S(1)}, f32[1,2048]{1,0:T(1,128)}, u32[]{:S(2)}) copy-start(f32[1,2048]{1,0:T(1,128)} %copy-done.23) | copy-start | bytes 24580
  (52 other events, 229.0 us)
where the time goes:
time: 1110 us; the launch traced here: 1100 us
  local copies, waits for them, and re-layouts  455 us (41%)
  other arithmetic  321 us (29%)
  matrix products  172 us (15%)
  waiting for transfers between devices  49.7 us (4%)
  blocking collectives  43.9 us (4%)
  starting transfers between devices  33.6 us (3%)
  loops' own time  22.3 us (2%)
    scatter-add x2, other arithmetic, per_device(): jnp.zeros((field_count, local_count), jnp.float32).at[:, wanted]  202 us
    gather x2, local copies, waits for them, and re-layouts, per_device(): reply = route_rows(projected[:, wanted])  109 us
    dot_general x96, matrix products, render(): jnp.dot(splat_rows[6:9], weight, precision=lax.Precision.HIGHEST, preferr...  99.2 us
    dot_general x64, matrix products, prefix_sum(): jnp.einsum('ij,bjp->bip', lower_mask(jnp.float32), blocks, precision=lax....  70.7 us
    gather x2, local copies, waits for them, and re-layouts, per_device(): reply[:, slot_pos].reshape(splat_fields, tile_count, list_length)  62.2 us
    scatter x2, local copies, waits for them, and re-layouts, per_device(): jnp.zeros((owners * capacity,), jnp.int32).at[slot_pos].set(local_id)  62.1 us
    all_to_all x4, waiting for transfers between devices, route_rows(): lax.all_to_all(outgoing, ('gx', 'gy'), split_axis=1, concat_axis=1, tiled...  49.7 us
    scatter x2, local copies, waits for them, and re-layouts, per_device(): jnp.zeros((field_count, owners * capacity), jnp.float32).at[:, slot_pos]  49 us
  transfers between devices with their start and end apart: 6, of which 2 were waited for; matrix products, arithmetic and copies ran while one was open for 22% of the time, Pallas kernels for 0%

commit v1 on v0

v1 whole, which is shorter than its diff:
```python
import functools

import jax
import jax.numpy as jnp
from jax import lax
from jax.experimental import pallas as pl
from jax.experimental.pallas import tpu as pltpu
from jax.sharding import PartitionSpec as P

SIDE = 16
NCOEF = 16
STEPS = 2
IMG_TX = 64
IMG_TY = 32

FIELDS = 9
LANES = 128
ROWSUB = 8
AXES = ("gx", "gy")

beta_one = 0.9
beta_two = 0.999
adam_eps = 1e-08
learn_rate = 0.01
adam_start = 1000
band_zero = 0.28209479177387814
band_one = 0.4886025119029199
band_two = (
    1.0925484305920792,
    -1.0925484305920792,
    0.31539156525252005,
    -1.0925484305920792,
    0.5462742152960396,
)
band_three = (
    -0.5900435899266435,
    2.890611442640554,
    -0.4570457994644658,
    0.3731763325901154,
    -0.4570457994644658,
    1.445305721320277,
    -0.5900435899266435,
)
LOG2E = 1.4426950408889634
LOG_CAP = -0.01005033585350145


def harmonic_rows(ray_x, ray_y, ray_z):
    sq_x = ray_x * ray_x
    sq_y = ray_y * ray_y
    sq_z = ray_z * ray_z
    return [
        band_zero * jnp.ones_like(ray_x),
        -band_one * ray_y,
        band_one * ray_z,
        -band_one * ray_x,
        band_two[0] * ray_x * ray_y,
        band_two[1] * ray_y * ray_z,
        band_two[2] * (2.0 * sq_z - sq_x - sq_y),
        band_two[3] * ray_x * ray_z,
        band_two[4] * (sq_x - sq_y),
        band_three[0] * ray_y * (3.0 * sq_x - sq_y),
        band_three[1] * ray_x * ray_y * ray_z,
        band_three[2] * ray_y * (4.0 * sq_z - sq_x - sq_y),
        band_three[3] * ray_z * (2.0 * sq_z - 3.0 * sq_x - 3.0 * sq_y),
        band_three[4] * ray_x * (4.0 * sq_z - sq_x - sq_y),
        band_three[5] * ray_z * (sq_x - sq_y),
        band_three[6] * ray_x * (sq_x - 3.0 * sq_y),
    ]


def geometry_rows(p0, p1, p2, p3, p4, p5, p6, cam_x, cam_y):
    screen_u = (p0 - cam_x) / p2
    screen_v = (p1 - cam_y) / p2
    inv_one = p2 * p2 * jnp.exp(-2.0 * p3)
    inv_two = p2 * p2 * jnp.exp(-2.0 * p4)
    cosine = jnp.cos(p5)
    sine = jnp.sin(p5)
    conic_a = cosine * cosine * inv_one + sine * sine * inv_two
    conic_b = cosine * sine * (inv_one - inv_two)
    conic_c = sine * sine * inv_one + cosine * cosine * inv_two
    tail = jnp.log(1.0 + jnp.exp(-jnp.abs(p6)))
    log_opacity = LOG_CAP - (jnp.maximum(-p6, 0.0) + tail)
    return screen_u, screen_v, conic_a, conic_b, conic_c, log_opacity


def ray_rows(screen_u, screen_v):
    image_width = 1.0 * SIDE * IMG_TX
    image_height = 1.0 * SIDE * IMG_TY
    ray_x = (screen_u - 0.5 * image_width) / image_width
    ray_y = (screen_v - 0.5 * image_height) / image_width
    factor = lax.rsqrt(ray_x * ray_x + ray_y * ray_y + 1.0)
    return ray_x, ray_y, factor


def project_to(param_ref, cam_x, cam_y, out_ref):
    rows = [param_ref[i : i + 1, :] for i in range(7)]
    geo = geometry_rows(*rows, cam_x, cam_y)
    ray_x, ray_y, factor = ray_rows(geo[0], geo[1])
    basis = jnp.concatenate(harmonic_rows(ray_x * factor, ray_y * factor, factor), 0)
    colours = []
    for ch in range(3):
        coef = param_ref[7 + NCOEF * ch : 7 + NCOEF * (ch + 1), :]
        colours.append(0.5 + jnp.sum(coef * basis, axis=0, keepdims=True))
    fields = jnp.concatenate(list(geo) + colours, 0)
    per_field = fields.shape[1] // LANES
    for k in range(per_field):
        out_ref[pl.ds(k, FIELDS, stride=per_field), :] = fields[:, k * LANES : (k + 1) * LANES]


def project_kernel(cam_ref, param_ref, out_ref, *, step):
    project_to(param_ref, cam_ref[step, 0], cam_ref[step, 1], out_ref)


def gradient_to(param_ref, cam_x, cam_y, grad_ref, full_ref):
    count = param_ref.shape[1]
    per_field = count // LANES
    pieces = [grad_ref[pl.ds(k, FIELDS, stride=per_field), :] for k in range(per_field)]
    grads = jnp.concatenate(pieces, 1)
    g = [grads[i : i + 1, :] for i in range(FIELDS)]
    p0, p1, p2, p3, p4, p5, p6 = [param_ref[i : i + 1, :] for i in range(7)]
    inv_z = 1.0 / p2
    screen_u = (p0 - cam_x) / p2
    screen_v = (p1 - cam_y) / p2
    inv_one = p2 * p2 * jnp.exp(-2.0 * p3)
    inv_two = p2 * p2 * jnp.exp(-2.0 * p4)
    cosine = jnp.cos(p5)
    sine = jnp.sin(p5)
    cc = cosine * cosine
    ss = sine * sine
    cs = cosine * sine
    ray_x, ray_y, factor = ray_rows(screen_u, screen_v)
    nx, ny, nz = ray_x * factor, ray_y * factor, factor
    basis_rows, basis_vjp = jax.vjp(lambda a, b, c: tuple(harmonic_rows(a, b, c)), nx, ny, nz)
    basis = jnp.concatenate(basis_rows, 0)
    d_basis = jnp.zeros_like(basis)
    for ch in range(3):
        coef = param_ref[7 + NCOEF * ch : 7 + NCOEF * (ch + 1), :]
        full_ref[7 + NCOEF * ch : 7 + NCOEF * (ch + 1), :] = g[6 + ch] * basis
        d_basis = d_basis + g[6 + ch] * coef
    d_nx, d_ny, d_nz = basis_vjp(tuple(d_basis[i : i + 1, :] for i in range(NCOEF)))
    dot = d_nx * nx + d_ny * ny + d_nz * nz
    image_width = 1.0 * SIDE * IMG_TX
    d_u = g[0] + factor * (d_nx - nx * dot) / image_width
    d_v = g[1] + factor * (d_ny - ny * dot) / image_width
    d_one = g[2] * cc + g[3] * cs + g[4] * ss
    d_two = g[2] * ss - g[3] * cs + g[4] * cc
    diff = inv_one - inv_two
    d_angle = diff * (2.0 * cs * (g[4] - g[2]) + (cc - ss) * g[3])
    d_x = d_u * inv_z
    d_y = d_v * inv_z
    d_z = 2.0 * (d_one * inv_one + d_two * inv_two) * inv_z - d_x * screen_u - d_y * screen_v
    full_ref[0:1, :] = d_x
    full_ref[1:2, :] = d_y
    full_ref[2:3, :] = d_z
    full_ref[3:4, :] = -2.0 * inv_one * d_one
    full_ref[4:5, :] = -2.0 * inv_two * d_two
    full_ref[5:6, :] = d_angle
    full_ref[6:7, :] = g[5] / (1.0 + jnp.exp(p6))


def update_kernel(
    cam_ref, param_ref, first_ref, second_ref, grad_ref, *refs, step, project_next
):
    if project_next:
        new_param, new_first, new_second, field_ref, full_ref = refs
    else:
        new_param, new_first, new_second, full_ref = refs
    gradient_to(param_ref, cam_ref[step, 0], cam_ref[step, 1], grad_ref, full_ref)
    step_count = adam_start + step + 1
    gradient = full_ref[...]
    first = beta_one * first_ref[...] + (1.0 - beta_one) * gradient
    second = beta_two * second_ref[...] + (1.0 - beta_two) * gradient * gradient
    scaled_first = first / (1.0 - beta_one**step_count)
    scaled_second = second / (1.0 - beta_two**step_count)
    new_first[...] = first
    new_second[...] = second
    new_param[...] = param_ref[...] - learn_rate * scaled_first / (
        jnp.sqrt(scaled_second) + adam_eps
    )
    if project_next:
        project_to(new_param, cam_ref[step + 1, 0], cam_ref[step + 1, 1], field_ref)


def split_two(values):
    high = values.astype(jnp.bfloat16)
    rest = (values - high.astype(jnp.float32)).astype(jnp.bfloat16)
    return high, rest


def pixel_basis(rows):
    pix = lax.broadcasted_iota(jnp.int32, (rows, SIDE * SIDE), 1)
    which = lax.broadcasted_iota(jnp.int32, (rows, SIDE * SIDE), 0)
    x = (pix % SIDE).astype(jnp.float32) + (0.5 - 0.5 * SIDE)
    y = (pix // SIDE).astype(jnp.float32) + (0.5 - 0.5 * SIDE)
    which = which % 8
    out = jnp.where(which == 0, 1.0, 0.0)
    for index, value in enumerate((x, y, x * x, x * y, y * y)):
        out = jnp.where(which == index + 1, value, out)
    return out


def dot_nn(a, b):
    return jnp.dot(a, b, preferred_element_type=jnp.float32)


def dot_nt(a, b):
    return lax.dot_general(
        a, b, (((1,), (1,)), ((), ())), preferred_element_type=jnp.float32
    )


def render_kernel(
    rows_ref,
    group_ref,
    middle_ref,
    target_ref,
    table_in,
    picture_ref,
    grad_out,
    planes,
    entries,
    fields,
    picture_sum,
    residual,
    in_sem,
    out_sem,
    *tables,
    devices,
    per_owner,
    groups,
    depth,
):
    planes_in = FIELDS * per_owner
    planes_out = planes_in + ROWSUB
    halves = per_owner // ROWSUB
    total = groups * ROWSUB * depth
    table = tables[0]
    blocks = depth * ROWSUB // LANES
    per_block = LANES // ROWSUB
    pixels = SIDE * SIDE
    wide = pixels // LANES

    load = pltpu.make_async_copy(table_in, planes.at[pl.ds(0, devices * planes_in)], in_sem)
    load.start()
    load.wait()

    pad = jnp.zeros((LANES - FIELDS * ROWSUB, LANES), jnp.float32)

    def build(owner, carry):
        start = pl.multiple_of(owner * planes_in, 8)
        for half in range(halves):
            parts = [
                planes[pl.ds(start + f * per_owner + half * ROWSUB, ROWSUB), :]
                for f in range(FIELDS)
            ]
            block = jnp.concatenate(parts + [pad], 0)
            at = pl.multiple_of((owner * halves + half) * LANES, LANES)
            table[pl.ds(at, LANES), :] = block.T
        return carry

    lax.fori_loop(0, devices, build, 0)

    unroll = 32

    def gather(index, carry):
        base = pl.multiple_of(index * unroll, unroll)
        for q in range(unroll):
            row = rows_ref[base + q]
            entries[pl.ds(base + q, 1), :] = table[pl.ds(row, 1), :]
        return carry

    lax.fori_loop(0, total // unroll, gather, 0)

    sub = lax.broadcasted_iota(jnp.int32, (ROWSUB, LANES), 0)
    lane = lax.broadcasted_iota(jnp.int32, (ROWSUB, LANES), 1)
    own_tile = sub == lane % ROWSUB
    basis = pixel_basis(32)
    basis_three = jnp.where(
        lax.broadcasted_iota(jnp.int32, (32, pixels), 0) < 24, basis, 0.0
    ).astype(jnp.bfloat16)
    basis_rows = jnp.where(
        lax.broadcasted_iota(jnp.int32, (16, pixels), 0) < 8, pixel_basis(16), 0.0
    ).astype(jnp.bfloat16)

    def field_mask(block):
        return sub == group_ref[pl.ds(block, 1), :]

    def colour_rows(block):
        parts = []
        for ch in range(3):
            row = fields[pl.ds(block * 16 + 6 + ch, 1), :]
            parts.append(jnp.where(own_tile, row, 0.0))
        full = jnp.concatenate(parts, 0)
        high = full.astype(jnp.bfloat16).astype(jnp.float32)
        return high, full - high

    for group in range(groups):
        picture_sum[group] = jnp.zeros((48, pixels), jnp.float32)

    w_base = [h * total for h in range(wide)]
    a_base = [(wide + h) * total for h in range(wide)]

    def forward(step, carry):
        out = []
        for group in range(groups):
            block = group * blocks + step
            at = pl.multiple_of(block * LANES, LANES)
            mask = field_mask(block)
            turned = entries[pl.ds(at, LANES), :].T
            rows = []
            for f in range(FIELDS):
                part = jnp.where(mask, turned[f * ROWSUB : (f + 1) * ROWSUB, :], 0.0)
                rows.append(jnp.sum(part, axis=0, keepdims=True))
            u = rows[0] - middle_ref[2 * group : 2 * group + 1, :]
            v = rows[1] - middle_ref[2 * group + 1 : 2 * group + 2, :]
            rows[0], rows[1] = u, v
            a, b, c = rows[2], rows[3], rows[4]
            for f in range(FIELDS):
                fields[pl.ds(block * 16 + f, 1), :] = rows[f]
            au = a * u + b * v
            bv = b * u + c * v
            coefs = (
                LOG2E * (rows[5] - 0.5 * (u * au + v * bv)),
                LOG2E * au,
                LOG2E * bv,
                (-0.5 * LOG2E) * a,
                -LOG2E * b,
                (-0.5 * LOG2E) * c,
            )
            coef = jnp.zeros((ROWSUB, LANES), jnp.float32)
            for i, row in enumerate(coefs):
                coef = jnp.where(sub == i, row, coef)
            high = coef.astype(jnp.bfloat16).astype(jnp.float32)
            rest = coef - high
            mid = rest.astype(jnp.bfloat16).astype(jnp.float32)
            low = rest - mid
            stacked = jnp.concatenate([high, mid, low, jnp.zeros_like(low)], 0)
            exponent = dot_nn(stacked.T.astype(jnp.bfloat16), basis_three)
            trans = list(carry[group])
            weights = [[] for _ in range(wide)]
            for s in range(per_block):
                for h in range(wide):
                    e = exponent[s * ROWSUB : (s + 1) * ROWSUB, h * LANES : (h + 1) * LANES]
                    alpha = jnp.exp2(jnp.minimum(e, LOG2E * LOG_CAP))
                    w = trans[h] * alpha
                    trans[h] = trans[h] - w
                    planes[pl.ds(a_base[h] + at + s * ROWSUB, ROWSUB), :] = alpha
                    planes[pl.ds(w_base[h] + at + s * ROWSUB, ROWSUB), :] = w
                    weights[h].append(w)
            weight = jnp.concatenate([jnp.concatenate(ws, 0) for ws in weights], 1)
            w_high, w_rest = split_two(weight)
            c_high, c_rest = colour_rows(block)
            both = jnp.concatenate([c_high, c_rest], 0).astype(jnp.bfloat16)
            picture_sum[group] += dot_nn(both, w_high) + dot_nn(both, w_rest)
            out.append(tuple(trans))
        return tuple(out)

    ones = jnp.ones((ROWSUB, LANES), jnp.float32)
    start = tuple(tuple(ones for _ in range(wide)) for _ in range(groups))
    lax.fori_loop(0, blocks, forward, start)

    loss = jnp.zeros((1, 1), jnp.float32)
    for group in range(groups):
        both = picture_sum[group]
        picture = both[:24] + both[24:]
        parts = []
        for ch in range(3):
            pair = []
            for h in range(wide):
                where = pl.ds((group * ROWSUB * 3 + ch) * wide + h, ROWSUB, stride=3 * wide)
                part = picture[ch * ROWSUB : (ch + 1) * ROWSUB, h * LANES : (h + 1) * LANES]
                picture_ref[where, :] = part
                pair.append(part - target_ref[where, :])
            parts.append(jnp.concatenate(pair, 1))
        left = jnp.concatenate(parts, 0)
        square = left * left
        loss = loss + 0.5 * jnp.sum(
            jnp.sum(square, axis=0, keepdims=True), axis=1, keepdims=True
        )
        high = left.astype(jnp.bfloat16).astype(jnp.float32)
        residual[group] = jnp.concatenate([high, left - high] * 2, 0).astype(jnp.bfloat16)

    def backward(index, carry):
        step = blocks - 1 - index
        out = []
        for group in range(groups):
            block = group * blocks + step
            at = pl.multiple_of(block * LANES, LANES)
            mask = field_mask(block)
            c_high, c_rest = colour_rows(block)
            four = jnp.concatenate([c_high, c_high, c_rest, c_rest], 0)
            q = dot_nn(four.T.astype(jnp.bfloat16), residual[group])
            behind = list(carry[group])
            slopes = [[None] * per_block for _ in range(wide)]
            weights = [[None] * per_block for _ in range(wide)]
            for s in reversed(range(per_block)):
                for h in range(wide):
                    w = planes[pl.ds(w_base[h] + at + s * ROWSUB, ROWSUB), :]
                    alpha = planes[pl.ds(a_base[h] + at + s * ROWSUB, ROWSUB), :]
                    d = q[s * ROWSUB : (s + 1) * ROWSUB, h * LANES : (h + 1) * LANES] - behind[h]
                    slopes[h][s] = w * d
                    weights[h][s] = w
                    behind[h] = behind[h] + alpha * d
            slope = jnp.concatenate([jnp.concatenate(ws, 0) for ws in slopes], 1)
            weight = jnp.concatenate([jnp.concatenate(ws, 0) for ws in weights], 1)
            g_high, g_rest = split_two(slope)
            w_high, w_rest = split_two(weight)
            moments = dot_nt(basis_rows, g_high) + dot_nt(basis_rows, g_rest)
            res = residual[group, 0:48, :]
            tone = dot_nt(res, w_high) + dot_nt(res, w_rest)
            tone = tone[:24] + tone[24:]
            m = [moments[i : i + 1, :] for i in range(6)]
            u, v, a, b, c = [fields[pl.ds(block * 16 + f, 1), :] for f in range(5)]
            m_x = m[1] - u * m[0]
            m_y = m[2] - v * m[0]
            rows = [
                a * m_x + b * m_y,
                b * m_x + c * m_y,
                -0.5 * (m[3] - u * (m[1] + m_x)),
                -(m[4] - u * m[2] - v * m_x),
                -0.5 * (m[5] - v * (m[2] + m_y)),
                m[0],
            ]
            for ch in range(3):
                part = jnp.where(own_tile, tone[ch * ROWSUB : (ch + 1) * ROWSUB, :], 0.0)
                rows.append(jnp.sum(part, axis=0, keepdims=True))
            placed = [jnp.where(mask, row, 0.0) for row in rows]
            entries[pl.ds(at, LANES), :] = jnp.concatenate(placed + [pad], 0).T
            out.append(tuple(behind))
        return tuple(out)

    zeros = jnp.zeros((ROWSUB, LANES), jnp.float32)
    start = tuple(tuple(zeros for _ in range(wide)) for _ in range(groups))
    lax.fori_loop(0, blocks, backward, start)

    tall = jnp.zeros((LANES, LANES), jnp.float32)

    def clear(index, carry):
        at = pl.multiple_of(index * LANES, LANES)
        for one in tables:
            one[pl.ds(at, LANES), :] = tall
        return carry

    lax.fori_loop(0, devices * halves, clear, 0)

    def scatter(index, carry):
        base = pl.multiple_of(index * unroll, unroll)
        for q in range(unroll):
            one = tables[q % len(tables)]
            row = rows_ref[base + q]
            one[pl.ds(row, 1), :] = one[pl.ds(row, 1), :] + entries[pl.ds(base + q, 1), :]
        return carry

    lax.fori_loop(0, total // unroll, scatter, 0)

    loss_rows = jnp.broadcast_to(loss, (ROWSUB, LANES))

    def collect(owner, carry):
        start = pl.multiple_of(owner * planes_out, 8)
        for half in range(halves):
            at = pl.multiple_of((owner * halves + half) * LANES, LANES)
            block = tables[0][pl.ds(at, LANES), :]
            for one in tables[1:]:
                block = block + one[pl.ds(at, LANES), :]
            turned = block.T
            for f in range(FIELDS):
                planes[pl.ds(start + f * per_owner + half * ROWSUB, ROWSUB), :] = turned[
                    f * ROWSUB : (f + 1) * ROWSUB, :
                ]
        planes[pl.ds(start + planes_in, ROWSUB), :] = loss_rows
        return carry

    lax.fori_loop(0, devices, collect, 0)

    store = pltpu.make_async_copy(planes.at[pl.ds(0, devices * planes_out)], grad_out, out_sem)
    store.start()
    store.wait()


def exchange_order(gx_size, gy_size):
    gx_bits = gx_size.bit_length() - 1
    gy_bits = gy_size.bit_length() - 1
    order = [("gx", gx_size, 1 << b, gy_bits + b) for b in range(gx_bits)]
    order += [("gy", gy_size, 1 << b, b) for b in reversed(range(gy_bits))]
    return order


def swap(values, phase):
    axis, size, flip, _ = phase
    return lax.ppermute(values, axis, [(i, i ^ flip) for i in range(size)])


def spread(values, order):
    for phase in order:
        values = jnp.concatenate([values, swap(values, phase)], 0)
    return values


def fold(values, order):
    for phase in reversed(order):
        half = values.shape[0] // 2
        values = values[:half] + swap(values[half:], phase)
    return values


def per_device(gauss_params, first_moment, second_moment, splat_lists, tile_ids, targets, camera):
    gx_size = lax.axis_size("gx")
    gy_size = lax.axis_size("gy")
    devices = gx_size * gy_size
    order = exchange_order(gx_size, gy_size)
    params_rows, count = gauss_params.shape
    tiles, depth = splat_lists.shape[1:]
    per_owner = count // LANES
    groups = tiles // ROWSUB
    planes_in = FIELDS * per_owner
    planes_out = planes_in + ROWSUB
    total = tiles * depth
    pixels = SIDE * SIDE

    me = lax.axis_index("gx") * gy_size + lax.axis_index("gy")
    apart = (splat_lists // count) ^ me
    local = splat_lists % count
    place = jnp.zeros_like(apart)
    for bit, phase in enumerate(order):
        place = place + (((apart >> phase[3]) & 1) << bit)
    rows = place * (count // ROWSUB) + (local // (ROWSUB * LANES)) * LANES + local % LANES
    which = (local // LANES) % ROWSUB

    def interleave(values):
        return (
            values.reshape(STEPS, groups, ROWSUB, depth)
            .transpose(0, 1, 3, 2)
            .reshape(STEPS, total)
        )

    rows = interleave(rows)
    which = interleave(which).reshape(STEPS, total // LANES, LANES)
    middle_x = (tile_ids % IMG_TX * SIDE + SIDE // 2).astype(jnp.float32)
    middle_y = (tile_ids // IMG_TX * SIDE + SIDE // 2).astype(jnp.float32)
    middle = jnp.stack([middle_x, middle_y], 1).reshape(STEPS, 2, groups, ROWSUB)
    middle = middle.transpose(0, 2, 1, 3).reshape(STEPS, 2 * groups, ROWSUB)
    middle = jnp.tile(middle, (1, 1, LANES // ROWSUB))
    target_rows = targets.reshape(STEPS, tiles * 3 * pixels // LANES, LANES)

    vmem = pl.BlockSpec(memory_space=pltpu.VMEM)
    smem = pl.BlockSpec(memory_space=pltpu.SMEM)
    hbm = pl.BlockSpec(memory_space=pl.ANY)
    f32 = jnp.float32
    state = jax.ShapeDtypeStruct((params_rows, count), f32)
    field_shape = jax.ShapeDtypeStruct((planes_in, LANES), f32)

    table_bytes = devices * count // ROWSUB * LANES * 4
    copies = max(1, min(4, (24 << 20) // table_bytes))
    render = pl.pallas_call(
        functools.partial(
            render_kernel, devices=devices, per_owner=per_owner, groups=groups, depth=depth
        ),
        out_shape=(
            jax.ShapeDtypeStruct((tiles * 3 * pixels // LANES, LANES), f32),
            jax.ShapeDtypeStruct((devices * planes_out, LANES), f32),
        ),
        in_specs=[smem, vmem, vmem, vmem, hbm],
        out_specs=(vmem, hbm),
        scratch_shapes=[
            pltpu.VMEM((max(2 * pixels // LANES * total, devices * planes_out), LANES), f32),
            pltpu.VMEM((total, LANES), f32),
            pltpu.VMEM((total // LANES * 16, LANES), f32),
            pltpu.VMEM((groups, 48, pixels), f32),
            pltpu.VMEM((groups, 96, pixels), jnp.bfloat16),
            pltpu.SemaphoreType.DMA(()),
            pltpu.SemaphoreType.DMA(()),
        ]
        + [pltpu.VMEM((devices * count // ROWSUB, LANES), f32)] * copies,
        compiler_params=pltpu.CompilerParams(vmem_limit_bytes=60 << 20),
        name="render",
    )

    params, first, second = gauss_params, first_moment, second_moment
    fields = pl.pallas_call(
        functools.partial(project_kernel, step=0),
        out_shape=field_shape,
        in_specs=[smem, vmem],
        out_specs=vmem,
        name="project",
    )(camera, params)
    pictures = []
    losses = []
    for step in range(STEPS):
        table = spread(fields, order)
        picture, grads = render(
            rows[step], which[step], middle[step], target_rows[step], table
        )
        pictures.append(picture)
        summed = fold(grads, order)
        losses.append(summed[planes_in, 0])
        more = step + 1 < STEPS
        result = pl.pallas_call(
            functools.partial(update_kernel, step=step, project_next=more),
            out_shape=(state, state, state) + ((field_shape,) if more else ()),
            in_specs=[smem, vmem, vmem, vmem, vmem],
            out_specs=(vmem,) * (4 if more else 3),
            scratch_shapes=[pltpu.VMEM((params_rows, count), f32)],
            name="update",
        )(camera, params, first, second, summed)
        params, first, second = result[:3]
        if more:
            fields = result[3]
    rendered = jnp.stack(pictures).reshape(STEPS, tiles, 3, pixels)
    loss = jnp.stack(losses) / (3.0 * pixels * tiles * devices)
    return params, first, second, rendered, loss


def solution(mesh):
    along = P(None, AXES)
    lists = P(None, AXES, None)
    frames = P(None, AXES, None, None)
    return jax.shard_map(
        per_device,
        mesh=mesh,
        in_specs=(along, along, along, lists, along, frames, P()),
        out_specs=(along, along, along, frames, P()),
        check_vma=False,
    )
```

time: 1110 us -> 340 us (0.31)
  local copies, waits for them, and re-layouts: 455 us -> 33.2 us
  other arithmetic: 321 us -> 10.3 us
  matrix products: 172 us -> 0 us
  Pallas kernels: 0 us -> 158 us
  waiting for transfers between devices: 49.7 us -> 117 us
  blocking collectives: 43.9 us -> 0 us
  loops' own time: 22.3 us -> 0 us
  starting transfers between devices: 33.6 us -> 19.6 us
    scatter-add x2 -> x0, other arithmetic: 202 us -> none  [per_device(): jnp.zeros((field_count, local_count), jnp.float32).at[:, wanted]]
    dot_general x162 -> x0, matrix products: 172 us -> none  [the longest x96 99.2 us: render(): jnp.dot(splat_rows[6:9], weight, precision=lax.Precision.HIGHEST, preferr...]
    gather x4 -> x0, local copies, waits for them, and re-layouts: 171 us -> none  [the longest x2 109 us: per_device(): reply = route_rows(projected[:, wanted])]
    pallas_call x0 -> x5, Pallas kernels: none -> 158 us  [the longest x2 149 us: per_device(): render(rows[step], which[step], middle[step], target_rows[step], table)]
    ppermute x0 -> x20, waiting for transfers between devices: none -> 117 us  [swap(): return lax.ppermute(values, axis, [(i, i ^ flip) for i in range(size)])]
    scatter x4 -> x0, local copies, waits for them, and re-layouts: 111 us -> none  [the longest x2 62.1 us: per_device(): jnp.zeros((owners * capacity,), jnp.int32).at[slot_pos].set(local_id)]
    reduce_sum x70 -> x0, other arithmetic: 53.4 us -> none  [the longest x32 34 us: render(): delta_y = centres[1][None, :] - splat_rows[1][:, None]]
    all_to_all x6 -> x0, waiting for transfers between devices: 49.7 us -> none  [the longest x4 49.7 us: route_rows(): lax.all_to_all(outgoing, ('gx', 'gy'), split_axis=1, concat_axis=1, tiled...]
  transfers between devices with their start and end apart: 6 -> 20, of which waited for: 2 -> 19; matrix products, arithmetic and copies ran while one was open for 22% -> 6% of each run, Pallas kernels for 0% -> 0%
where the time goes in v1:
time: 340 us; the launch traced here: 339 us
  Pallas kernels  158 us (46%)
  waiting for transfers between devices  117 us (34%)
  local copies, waits for them, and re-layouts  33.2 us (10%)
  starting transfers between devices  19.6 us (6%)
  other arithmetic  10.3 us (3%)
    pallas_call x2, Pallas kernels, per_device(): render(rows[step], which[step], middle[step], target_rows[step], table)  149 us
    ppermute x20, waiting for transfers between devices, swap(): return lax.ppermute(values, axis, [(i, i ^ flip) for i in range(size)])  117 us
    ppermute x20, starting transfers between devices, swap(): return lax.ppermute(values, axis, [(i, i ^ flip) for i in range(size)])  19.6 us
    unnamed x45, local copies, waits for them, and re-layouts  10.9 us
    pallas_call x2, Pallas kernels, per_device(): pl.pallas_call(functools.partial(update_kernel, step=step, project_next=m...  6.81 us
  transfers between devices with their start and end apart: 20, of which 19 were waited for; matrix products, arithmetic and copies ran while one was open for 6% of the time, Pallas kernels for 0%

profile of v1, /device:TPU:0, one launch (start us, length us, event | category | flops | bytes accessed | tf_op | source)
XLA Modules:
  0.0 338.9 jit_solution(1564959772840344512)
XLA Ops:
  0.6 2.0 project.1
  2.6 3.1 collective-permute-start
  5.7 2.5 collective-permute-done
  9.1 3.1 collective-permute-start.1
  12.2 5.9 %collective-permute-done.1 = f32[288,128]{1,0:T(8,128)S(1)} collective-permute-done((f32[288,128]{1,0:T(8,128)S(1)}, f32[288,128]{1,0:T(8,128)S(1)}, u32[]{:S(2)}, u32[]{:S(2)}) %collective-permute-start.1) | collective-permute-done | bytes 147488 | tf_op jit(solution)/shard_map/ppermute | solution.py:491
  20.7 6.3 %collective-permute-done.2 = f32[576,128]{1,0:T(8,128)S(1)} collective-permute-done((f32[576,128]{1,0:T(8,128)S(1)}, f32[576,128]{1,0:T(8,128)S(1)}, u32[]{:S(2)}, u32[]{:S(2)}) %collective-permute-start.2) | collective-permute-done | bytes 294944 | tf_op jit(solution)/shard_map/ppermute | solution.py:491
  27.0 1.8 pad_maximum_fusion
  34.4 1.7 constant_dynamic-update-slice_fusion.1
  36.1 6.3 %collective-permute-done.3 = f32[1152,128]{1,0:T(8,128)} collective-permute-done((f32[1152,128]{1,0:T(8,128)}, f32[1152,128]{1,0:T(8,128)}, u32[]{:S(2)}, u32[]{:S(2)}) %collective-permute-start.3) | collective-permute-done | bytes 589856 | tf_op jit(solution)/shard_map/ppermute | solution.py:491
  42.4 2.0 constant_dynamic-update-slice_fusion
  45.4 1.9 squeeze.20.rows_ref
  48.7 1.9 squeeze.21.group_ref
  55.6 74.4 %render.2 = (f32[96,128]{1,0:T(8,128)}, f32[4864,128]{1,0:T(8,128)}) custom-call(s32[8192]{0:T(1024)} %squeeze.20.rows_ref, s32[64,128]{1,0:T(8,128)} %squeeze.21.group_ref, f32[4,128]{1,0:T(4,128)} %tile.13.middle_ref, f32[96,128]{1,0:T(8,128)} %squeeze.22.target_ref, f32[4608,128]{1,0:T(8,128)} %copy-done), custom_call_target="tpu_custom_call" | custom-call | tf_op jit(solution)/shard_map/render/pallas_call | solution.py:591
  132.1 2.6 collective-permute-done.5
  136.5 14.7 %collective-permute-done.6 = f32[1216,128]{1,0:T(8,128)S(1)} collective-permute-done((f32[1216,128]{1,0:T(8,128)S(1)}, f32[1216,128]{1,0:T(8,128)S(1)}, u32[]{:S(2)}, u32[]{:S(2)}) %collective-permute-start.6) | collective-permute-done | bytes 622624 | tf_op jit(solution)/shard_map/ppermute | solution.py:491
  151.3 1.7 collective-permute-start.7
  153.1 7.1 %collective-permute-done.7 = f32[608,128]{1,0:T(8,128)S(1)} collective-permute-done((f32[608,128]{1,0:T(8,128)S(1)}, f32[608,128]{1,0:T(8,128)S(1)}, u32[]{:S(2)}, u32[]{:S(2)}) %collective-permute-start.7) | collective-permute-done | bytes 311328 | tf_op jit(solution)/shard_map/ppermute | solution.py:491
  160.3 8.9 %collective-permute-done.8 = f32[304,128]{1,0:T(8,128)S(1)} collective-permute-done((f32[304,128]{1,0:T(8,128)S(1)}, f32[304,128]{1,0:T(8,128)S(1)}, u32[]{:S(2)}, u32[]{:S(2)}) %collective-permute-start.8) | collective-permute-done | bytes 155680 | tf_op jit(solution)/shard_map/ppermute | solution.py:491
  169.3 4.4 %collective-permute-done.9 = f32[152,128]{1,0:T(8,128)S(1)} collective-permute-done((f32[152,128]{1,0:T(8,128)S(1)}, f32[152,128]{1,0:T(8,128)S(1)}, u32[]{:S(2)}, u32[]{:S(2)}) %collective-permute-start.9) | collective-permute-done | bytes 77856 | tf_op jit(solution)/shard_map/ppermute | solution.py:491
  174.4 3.5 %update.2 = (f32[55,2048]{1,0:T(8,128)}, f32[55,2048]{1,0:T(8,128)}, f32[55,2048]{1,0:T(8,128)}, f32[144,128]{1,0:T(8,128)}) custom-call(f32[2,2]{1,0:T(2,128)} %cam_ref.5, f32[55,2048]{1,0:T(8,128)} %param_ref.3, f32[55,2048]{1,0:T(8,128)} %first_ref.1, f32[55,2048]{1,0:T(8,128)} %second_ref.1, f32[152,128]{1,0:T(8,128)} %slice_add_fusion.9.grad_ref), custom_call_target="tpu_custom_call" | custom-call | tf_op jit(solution)/shard_map/update/pallas_call | solution.py:598
  177.9 5.0 %collective-permute-done.10 = f32[144,128]{1,0:T(8,128)S(1)} collective-permute-done((f32[144,128]{1,0:T(8,128)}, f32[144,128]{1,0:T(8,128)S(1)}, u32[]{:S(2)}, u32[]{:S(2)}) %collective-permute-start.10) | collective-permute-done | bytes 73760 | tf_op jit(solution)/shard_map/ppermute | solution.py:491
  183.9 7.0 %collective-permute-done.11 = f32[288,128]{1,0:T(8,128)S(1)} collective-permute-done((f32[288,128]{1,0:T(8,128)S(1)}, f32[288,128]{1,0:T(8,128)S(1)}, u32[]{:S(2)}, u32[]{:S(2)}) %collective-permute-start.11) | collective-permute-done | bytes 147488 | tf_op jit(solution)/shard_map/ppermute | solution.py:491
  193.2 5.4 %collective-permute-done.12 = f32[576,128]{1,0:T(8,128)S(1)} collective-permute-done((f32[576,128]{1,0:T(8,128)S(1)}, f32[576,128]{1,0:T(8,128)S(1)}, u32[]{:S(2)}, u32[]{:S(2)}) %collective-permute-start.12) | collective-permute-done | bytes 294944 | tf_op jit(solution)/shard_map/ppermute | solution.py:491
  203.5 5.9 %collective-permute-done.13 = f32[1152,128]{1,0:T(8,128)S(1)} collective-permute-done((f32[1152,128]{1,0:T(8,128)S(1)}, f32[1152,128]{1,0:T(8,128)S(1)}, u32[]{:S(2)}, u32[]{:S(2)}) %collective-permute-start.13) | collective-permute-done | bytes 589856 | tf_op jit(solution)/shard_map/ppermute | solution.py:491
  216.4 74.4 %render.3 = (f32[96,128]{1,0:T(8,128)}, f32[4864,128]{1,0:T(8,128)}) custom-call(s32[8192]{0:T(1024)} %squeeze.23.rows_ref, s32[64,128]{1,0:T(8,128)} %squeeze.24.group_ref, f32[4,128]{1,0:T(4,128)} %tile.15.middle_ref, f32[96,128]{1,0:T(8,128)} %squeeze.25.target_ref, f32[4608,128]{1,0:T(8,128)} %copy-done.1), custom_call_target="tpu_custom_call" | custom-call | tf_op jit(solution)/shard_map/render/pallas_call | solution.py:591
  292.7 2.6 collective-permute-done.15
  296.8 15.0 %collective-permute-done.16 = f32[1216,128]{1,0:T(8,128)S(1)} collective-permute-done((f32[1216,128]{1,0:T(8,128)S(1)}, f32[1216,128]{1,0:T(8,128)S(1)}, u32[]{:S(2)}, u32[]{:S(2)}) %collective-permute-start.16) | collective-permute-done | bytes 622624 | tf_op jit(solution)/shard_map/ppermute | solution.py:491
  313.4 7.5 %collective-permute-done.17 = f32[608,128]{1,0:T(8,128)S(1)} collective-permute-done((f32[608,128]{1,0:T(8,128)S(1)}, f32[608,128]{1,0:T(8,128)S(1)}, u32[]{:S(2)}, u32[]{:S(2)}) %collective-permute-start.17) | collective-permute-done | bytes 311328 | tf_op jit(solution)/shard_map/ppermute | solution.py:491
  322.3 6.4 %collective-permute-done.18 = f32[304,128]{1,0:T(8,128)S(1)} collective-permute-done((f32[304,128]{1,0:T(8,128)S(1)}, f32[304,128]{1,0:T(8,128)S(1)}, u32[]{:S(2)}, u32[]{:S(2)}) %collective-permute-start.18) | collective-permute-done | bytes 155680 | tf_op jit(solution)/shard_map/ppermute | solution.py:491
  329.5 3.7 %collective-permute-done.19 = f32[152,128]{1,0:T(8,128)S(1)} collective-permute-done((f32[152,128]{1,0:T(8,128)S(1)}, f32[152,128]{1,0:T(8,128)S(1)}, u32[]{:S(2)}, u32[]{:S(2)}) %collective-permute-start.19) | collective-permute-done | bytes 77856 | tf_op jit(solution)/shard_map/ppermute | solution.py:491
  333.7 1.9 maximum_multiply_fusion
  335.6 3.3 update.3
  (119 shorter events, 44.3 us)
Async XLA Ops:
  0.6 29.7 %copy-start.13 = (s32[2,16,512]{2,1,0:T(8,128)S(1)}, s32[2,16,512]{2,1,0:T(8,128)}, u32[]{:S(2)}) copy-start(s32[2,16,512]{2,1,0:T(8,128)} %param.10) | copy-start | bytes 196612
  2.6 5.6 %collective-permute-start = (f32[144,128]{1,0:T(8,128)}, f32[144,128]{1,0:T(8,128)S(1)}, u32[]{:S(2)}, u32[]{:S(2)}) collective-permute-start(f32[144,128]{1,0:T(8,128)} %project.1), channel_id=1, source_target_pairs={{0,8},{8,0},{16,24},{24,16},{1,9},{9,1},{17,25},{25,17},{2,10},{10... | collective-permute-start | bytes 221192 | tf_op jit(solution)/shard_map/ppermute | solution.py:491
  9.1 9.0 %collective-permute-start.1 = (f32[288,128]{1,0:T(8,128)S(1)}, f32[288,128]{1,0:T(8,128)S(1)}, u32[]{:S(2)}, u32[]{:S(2)}) collective-permute-start(f32[288,128]{1,0:T(8,128)S(1)} %pad_maximum_fusion.4), channel_id=1, source_target_pairs={{0,16},{8,24},{16,0},{24,8},{1,17},{9,25},{17,1},{25,9},{2,18},{10... | collective-permute-start | bytes 442376 | tf_op jit(solution)/shard_map/ppermute | solution.py:491
  18.1 13.1 %copy-start.7 = (f32[288,128]{1,0:T(8,128)}, f32[288,128]{1,0:T(8,128)S(1)}, u32[]{:S(2)}) copy-start(f32[288,128]{1,0:T(8,128)S(1)} %collective-permute-done.1) | copy-start | bytes 442372
  19.0 7.9 %collective-permute-start.2 = (f32[576,128]{1,0:T(8,128)S(1)}, f32[576,128]{1,0:T(8,128)S(1)}, u32[]{:S(2)}, u32[]{:S(2)}) collective-permute-start(f32[576,128]{1,0:T(8,128)S(1)} %pad_maximum_fusion.2), channel_id=1, source_target_pairs={{0,4},{1,5},{2,6},{3,7},{4,0},{5,1},{6,2},{7,3},{8,12},{9,13},{10,... | collective-permute-start | bytes 884744 | tf_op jit(solution)/shard_map/ppermute | solution.py:491
  20.7 10.9 %copy-start.6 = (f32[144,128]{1,0:T(8,128)S(1)}, f32[144,128]{1,0:T(8,128)}, u32[]{:S(2)}) copy-start(f32[144,128]{1,0:T(8,128)} %project.1) | copy-start | bytes 221188
  27.0 4.2 %copy-start.9 = (f32[576,128]{1,0:T(8,128)}, f32[576,128]{1,0:T(8,128)S(1)}, u32[]{:S(2)}) copy-start(f32[576,128]{1,0:T(8,128)S(1)} %collective-permute-done.2) | copy-start | bytes 884740
  28.7 13.6 %collective-permute-start.3 = (f32[1152,128]{1,0:T(8,128)}, f32[1152,128]{1,0:T(8,128)}, u32[]{:S(2)}, u32[]{:S(2)}) collective-permute-start(f32[1152,128]{1,0:T(8,128)} %pad_maximum_fusion), channel_id=1, source_target_pairs={{0,2},{1,3},{2,0},{3,1},{4,6},{5,7},{6,4},{7,5},{8,10},{9,11},{10,... | collective-permute-start | bytes 1769480 | tf_op jit(solution)/shard_map/ppermute | solution.py:491
  44.4 8.4 %collective-permute-start.4 = (f32[2304,128]{1,0:T(8,128)}, f32[2304,128]{1,0:T(8,128)}, u32[]{:S(2)}, u32[]{:S(2)}) collective-permute-start(f32[2304,128]{1,0:T(8,128)} %get-tuple-element.38), channel_id=1, source_target_pairs={{0,1},{1,0},{2,3},{3,2},{4,5},{5,4},{6,7},{7,6},{8,9},{9,8},{10,11... | collective-permute-start | bytes 3538952 | tf_op jit(solution)/shard_map/ppermute | solution.py:491
  47.7 4.4 %copy-start.12 = (f32[2,16,3,256]{3,1,2,0:T(8,128)S(1)}, f32[2,16,3,256]{3,1,2,0:T(8,128)}, u32[]{:S(2)}) copy-start(f32[2,16,3,256]{3,1,2,0:T(8,128)} %param.12) | copy-start | bytes 294916
  130.0 4.7 %copy-start.2 = (f32[4864,128]{1,0:T(8,128)S(1)}, f32[4864,128]{1,0:T(8,128)}, u32[]{:S(2)}) copy-start(f32[4864,128]{1,0:T(8,128)} %get-tuple-element.16) | copy-start | bytes 7471108
  131.5 3.1 collective-permute-start.5
  134.8 16.4 %collective-permute-start.6 = (f32[1216,128]{1,0:T(8,128)S(1)}, f32[1216,128]{1,0:T(8,128)S(1)}, u32[]{:S(2)}, u32[]{:S(2)}) collective-permute-start(f32[1216,128]{1,0:T(8,128)S(1)} %slice.142), channel_id=1, source_target_pairs={{0,2},{1,3},{2,0},{3,1},{4,6},{5,7},{6,4},{7,5},{8,10},{9,11},{10,... | collective-permute-start | bytes 1867784 | tf_op jit(solution)/shard_map/ppermute | solution.py:491
  151.3 8.8 %collective-permute-start.7 = (f32[608,128]{1,0:T(8,128)S(1)}, f32[608,128]{1,0:T(8,128)S(1)}, u32[]{:S(2)}, u32[]{:S(2)}) collective-permute-start(f32[608,128]{1,0:T(8,128)S(1)} %slice.144), channel_id=1, source_target_pairs={{0,4},{1,5},{2,6},{3,7},{4,0},{5,1},{6,2},{7,3},{8,12},{9,13},{10,... | collective-permute-start | bytes 933896 | tf_op jit(solution)/shard_map/ppermute | solution.py:491
  160.2 9.0 %collective-permute-start.8 = (f32[304,128]{1,0:T(8,128)S(1)}, f32[304,128]{1,0:T(8,128)S(1)}, u32[]{:S(2)}, u32[]{:S(2)}) collective-permute-start(f32[304,128]{1,0:T(8,128)S(1)} %slice.146), channel_id=1, source_target_pairs={{0,16},{8,24},{16,0},{24,8},{1,17},{9,25},{17,1},{25,9},{2,18},{10... | collective-permute-start | bytes 466952 | tf_op jit(solution)/shard_map/ppermute | solution.py:491
  169.3 4.5 %collective-permute-start.9 = (f32[152,128]{1,0:T(8,128)S(1)}, f32[152,128]{1,0:T(8,128)S(1)}, u32[]{:S(2)}, u32[]{:S(2)}) collective-permute-start(f32[152,128]{1,0:T(8,128)S(1)} %slice.148), channel_id=1, source_target_pairs={{0,8},{8,0},{16,24},{24,16},{1,9},{9,1},{17,25},{25,17},{2,10},{10... | collective-permute-start | bytes 233480 | tf_op jit(solution)/shard_map/ppermute | solution.py:491
  177.9 22.9 %copy-start.8 = (f32[144,128]{1,0:T(8,128)S(1)}, f32[144,128]{1,0:T(8,128)}, u32[]{:S(2)}) copy-start(f32[144,128]{1,0:T(8,128)} %get-tuple-element.20) | copy-start | bytes 221188
  177.9 5.0 %collective-permute-start.10 = (f32[144,128]{1,0:T(8,128)}, f32[144,128]{1,0:T(8,128)S(1)}, u32[]{:S(2)}, u32[]{:S(2)}) collective-permute-start(f32[144,128]{1,0:T(8,128)} %get-tuple-element.20), channel_id=1, source_target_pairs={{0,8},{8,0},{16,24},{24,16},{1,9},{9,1},{17,25},{25,17},{2,10},{10... | collective-permute-start | bytes 221192 | tf_op jit(solution)/shard_map/ppermute | solution.py:491
  183.8 7.1 %collective-permute-start.11 = (f32[288,128]{1,0:T(8,128)S(1)}, f32[288,128]{1,0:T(8,128)S(1)}, u32[]{:S(2)}, u32[]{:S(2)}) collective-permute-start(f32[288,128]{1,0:T(8,128)S(1)} %pad_maximum_fusion.5), channel_id=1, source_target_pairs={{0,16},{8,24},{16,0},{24,8},{1,17},{9,25},{17,1},{25,9},{2,18},{10... | collective-permute-start | bytes 442376 | tf_op jit(solution)/shard_map/ppermute | solution.py:491
  191.8 6.8 %collective-permute-start.12 = (f32[576,128]{1,0:T(8,128)S(1)}, f32[576,128]{1,0:T(8,128)S(1)}, u32[]{:S(2)}, u32[]{:S(2)}) collective-permute-start(f32[576,128]{1,0:T(8,128)S(1)} %pad_maximum_fusion.3), channel_id=1, source_target_pairs={{0,4},{1,5},{2,6},{3,7},{4,0},{5,1},{6,2},{7,3},{8,12},{9,13},{10,... | collective-permute-start | bytes 884744 | tf_op jit(solution)/shard_map/ppermute | solution.py:491
  199.5 9.9 %collective-permute-start.13 = (f32[1152,128]{1,0:T(8,128)S(1)}, f32[1152,128]{1,0:T(8,128)S(1)}, u32[]{:S(2)}, u32[]{:S(2)}) collective-permute-start(f32[1152,128]{1,0:T(8,128)S(1)} %pad_maximum_fusion.1), channel_id=1, source_target_pairs={{0,2},{1,3},{2,0},{3,1},{4,6},{5,7},{6,4},{7,5},{8,10},{9,11},{10,... | collective-permute-start | bytes 1769480 | tf_op jit(solution)/shard_map/ppermute | solution.py:491
  202.8 7.6 %copy-start.4 = (s32[1,2,512,8]{3,2,1,0:T(8,128)S(1)}, s32[1,2,512,8]{3,2,1,0:T(8,128)}, u32[]{:S(2)}) copy-start(s32[1,2,512,8]{3,2,1,0:T(8,128)} %get-tuple-element.34) | copy-start | bytes 98308
  203.5 7.7 %copy-start.5 = (s32[1,2,512,8]{3,2,1,0:T(8,128)S(1)}, s32[1,2,512,8]{3,2,1,0:T(8,128)}, u32[]{:S(2)}) copy-start(s32[1,2,512,8]{3,2,1,0:T(8,128)} %get-tuple-element.32) | copy-start | bytes 98308
  210.4 3.2 collective-permute-start.14
  290.7 4.6 %copy-start.3 = (f32[4864,128]{1,0:T(8,128)S(1)}, f32[4864,128]{1,0:T(8,128)}, u32[]{:S(2)}) copy-start(f32[4864,128]{1,0:T(8,128)} %get-tuple-element.21) | copy-start | bytes 7471108
  292.3 3.0 collective-permute-start.15
  295.5 16.4 %collective-permute-start.16 = (f32[1216,128]{1,0:T(8,128)S(1)}, f32[1216,128]{1,0:T(8,128)S(1)}, u32[]{:S(2)}, u32[]{:S(2)}) collective-permute-start(f32[1216,128]{1,0:T(8,128)S(1)} %slice.153), channel_id=1, source_target_pairs={{0,2},{1,3},{2,0},{3,1},{4,6},{5,7},{6,4},{7,5},{8,10},{9,11},{10,... | collective-permute-start | bytes 1867784 | tf_op jit(solution)/shard_map/ppermute | solution.py:491
  311.9 9.0 %copy-start.14 = (f32[96,128]{1,0:T(8,128)S(1)}, f32[96,128]{1,0:T(8,128)}, u32[]{:S(2)}) copy-start(f32[96,128]{1,0:T(8,128)} %get-tuple-element.25) | copy-start | bytes 147460
  312.0 10.3 %copy-start.15 = (f32[96,128]{1,0:T(8,128)S(1)}, f32[96,128]{1,0:T(8,128)}, u32[]{:S(2)}) copy-start(f32[96,128]{1,0:T(8,128)} %get-tuple-element.26) | copy-start | bytes 147460
  312.0 8.8 %collective-permute-start.17 = (f32[608,128]{1,0:T(8,128)S(1)}, f32[608,128]{1,0:T(8,128)S(1)}, u32[]{:S(2)}, u32[]{:S(2)}) collective-permute-start(f32[608,128]{1,0:T(8,128)S(1)} %slice.155), channel_id=1, source_target_pairs={{0,4},{1,5},{2,6},{3,7},{4,0},{5,1},{6,2},{7,3},{8,12},{9,13},{10,... | collective-permute-start | bytes 933896 | tf_op jit(solution)/shard_map/ppermute | solution.py:491
  320.9 7.8 %collective-permute-start.18 = (f32[304,128]{1,0:T(8,128)S(1)}, f32[304,128]{1,0:T(8,128)S(1)}, u32[]{:S(2)}, u32[]{:S(2)}) collective-permute-start(f32[304,128]{1,0:T(8,128)S(1)} %slice.157), channel_id=1, source_target_pairs={{0,16},{8,24},{16,0},{24,8},{1,17},{9,25},{17,1},{25,9},{2,18},{10... | collective-permute-start | bytes 466952 | tf_op jit(solution)/shard_map/ppermute | solution.py:491
  328.7 4.5 %collective-permute-start.19 = (f32[152,128]{1,0:T(8,128)S(1)}, f32[152,128]{1,0:T(8,128)S(1)}, u32[]{:S(2)}, u32[]{:S(2)}) collective-permute-start(f32[152,128]{1,0:T(8,128)S(1)} %slice.159), channel_id=1, source_target_pairs={{0,8},{8,0},{16,24},{24,16},{1,9},{9,1},{17,25},{25,17},{2,10},{10... | collective-permute-start | bytes 233480 | tf_op jit(solution)/shard_map/ppermute | solution.py:491
  (6 other events, 13.9 us)

commit v2 on v1

--- a/solution.py
+++ b/solution.py
@@ -204,6 +204,12 @@
     return jnp.dot(a, b, preferred_element_type=jnp.float32)
 
 
+def dot_tn(a, b):
+    return lax.dot_general(
+        a, b, (((0,), (0,)), ((), ())), preferred_element_type=jnp.float32
+    )
+
+
 def dot_nt(a, b):
     return lax.dot_general(
         a, b, (((1,), (1,)), ((), ())), preferred_element_type=jnp.float32
@@ -215,12 +221,15 @@
     group_ref,
     middle_ref,
     target_ref,
-    table_in,
+    table_own,
+    table_other,
     picture_ref,
-    grad_out,
+    grad_own,
+    grad_other,
     planes,
     entries,
     fields,
+    factors,
     picture_sum,
     residual,
     in_sem,
@@ -240,10 +249,18 @@
     per_block = LANES // ROWSUB
     pixels = SIDE * SIDE
     wide = pixels // LANES
-
-    load = pltpu.make_async_copy(table_in, planes.at[pl.ds(0, devices * planes_in)], in_sem)
-    load.start()
-    load.wait()
+    near = devices // 2
+
+    loads = [
+        pltpu.make_async_copy(
+            ref, planes.at[pl.ds(i * near * planes_in, near * planes_in)], in_sem.at[i]
+        )
+        for i, ref in enumerate((table_own, table_other))
+    ]
+    for load in loads:
+        load.start()
+    for load in loads:
+        load.wait()
 
     pad = jnp.zeros((LANES - FIELDS * ROWSUB, LANES), jnp.float32)
 
@@ -259,7 +276,7 @@
             table[pl.ds(at, LANES), :] = block.T
         return carry
 
-    lax.fori_loop(0, devices, build, 0)
+    lax.fori_loop(0, devices, build, 0, unroll=2)
 
     unroll = 32
 
@@ -275,70 +292,67 @@
     sub = lax.broadcasted_iota(jnp.int32, (ROWSUB, LANES), 0)
     lane = lax.broadcasted_iota(jnp.int32, (ROWSUB, LANES), 1)
     own_tile = sub == lane % ROWSUB
-    basis = pixel_basis(32)
     basis_three = jnp.where(
-        lax.broadcasted_iota(jnp.int32, (32, pixels), 0) < 24, basis, 0.0
+        lax.broadcasted_iota(jnp.int32, (LANES, pixels), 0) < 24, pixel_basis(LANES), 0.0
     ).astype(jnp.bfloat16)
     basis_rows = jnp.where(
         lax.broadcasted_iota(jnp.int32, (16, pixels), 0) < 8, pixel_basis(16), 0.0
     ).astype(jnp.bfloat16)
+    w_base = [h * total for h in range(wide)]
+    a_base = [(wide + h) * total for h in range(wide)]
 
     def field_mask(block):
         return sub == group_ref[pl.ds(block, 1), :]
 
-    def colour_rows(block):
-        parts = []
-        for ch in range(3):
-            row = fields[pl.ds(block * 16 + 6 + ch, 1), :]
-            parts.append(jnp.where(own_tile, row, 0.0))
-        full = jnp.concatenate(parts, 0)
-        high = full.astype(jnp.bfloat16).astype(jnp.float32)
-        return high, full - high
-
-    for group in range(groups):
-        picture_sum[group] = jnp.zeros((48, pixels), jnp.float32)
-
-    w_base = [h * total for h in range(wide)]
-    a_base = [(wide + h) * total for h in range(wide)]
+    def prepare(block, carry):
+        at = pl.multiple_of(block * LANES, LANES)
+        group = block // blocks
+        mask = field_mask(block)
+        turned = entries[pl.ds(at, LANES), :].T
+        rows = []
+        for f in range(FIELDS):
+            part = jnp.where(mask, turned[f * ROWSUB : (f + 1) * ROWSUB, :], 0.0)
+            rows.append(jnp.sum(part, axis=0, keepdims=True))
+        u = rows[0] - middle_ref[pl.ds(2 * group, 1), :]
+        v = rows[1] - middle_ref[pl.ds(2 * group + 1, 1), :]
+        rows[0], rows[1] = u, v
+        a, b, c = rows[2], rows[3], rows[4]
+        for f in range(5):
+            fields[pl.ds(block * ROWSUB + f, 1), :] = rows[f]
+        au = a * u + b * v
+        bv = b * u + c * v
+        coefs = (
+            LOG2E * (rows[5] - 0.5 * (u * au + v * bv)),
+            LOG2E * au,
+            LOG2E * bv,
+            (-0.5 * LOG2E) * a,
+            -LOG2E * b,
+            (-0.5 * LOG2E) * c,
+        )
+        coef = jnp.zeros((ROWSUB, LANES), jnp.float32)
+        for i, row in enumerate(coefs):
+            coef = jnp.where(sub == i, row, coef)
+        high = coef.astype(jnp.bfloat16).astype(jnp.float32)
+        rest = coef - high
+        mid = rest.astype(jnp.bfloat16).astype(jnp.float32)
+        low = rest - mid
+        full = [jnp.where(own_tile, rows[6 + ch], 0.0) for ch in range(3)]
+        c_high = [part.astype(jnp.bfloat16).astype(jnp.float32) for part in full]
+        c_rest = [part - top for part, top in zip(full, c_high)]
+        stacked = jnp.concatenate(
+            [high, mid, low, jnp.zeros_like(low)] + c_high + c_high + c_rest + c_rest, 0
+        )
+        factors[pl.ds(at, LANES), :] = stacked.T.astype(jnp.bfloat16)
+        return carry
+
+    lax.fori_loop(0, groups * blocks, prepare, 0, unroll=2)
 
     def forward(step, carry):
         out = []
         for group in range(groups):
-            block = group * blocks + step
-            at = pl.multiple_of(block * LANES, LANES)
-            mask = field_mask(block)
-            turned = entries[pl.ds(at, LANES), :].T
-            rows = []
-            for f in range(FIELDS):
-                part = jnp.where(mask, turned[f * ROWSUB : (f + 1) * ROWSUB, :], 0.0)
-                rows.append(jnp.sum(part, axis=0, keepdims=True))
-            u = rows[0] - middle_ref[2 * group : 2 * group + 1, :]
-            v = rows[1] - middle_ref[2 * group + 1 : 2 * group + 2, :]
-            rows[0], rows[1] = u, v
-            a, b, c = rows[2], rows[3], rows[4]
-            for f in range(FIELDS):
-                fields[pl.ds(block * 16 + f, 1), :] = rows[f]
-            au = a * u + b * v
-            bv = b * u + c * v
-            coefs = (
-                LOG2E * (rows[5] - 0.5 * (u * au + v * bv)),
-                LOG2E * au,
-                LOG2E * bv,
-                (-0.5 * LOG2E) * a,
-                -LOG2E * b,
-                (-0.5 * LOG2E) * c,
-            )
-            coef = jnp.zeros((ROWSUB, LANES), jnp.float32)
-            for i, row in enumerate(coefs):
-                coef = jnp.where(sub == i, row, coef)
-            high = coef.astype(jnp.bfloat16).astype(jnp.float32)
-            rest = coef - high
-            mid = rest.astype(jnp.bfloat16).astype(jnp.float32)
-            low = rest - mid
-            stacked = jnp.concatenate([high, mid, low, jnp.zeros_like(low)], 0)
-            exponent = dot_nn(stacked.T.astype(jnp.bfloat16), basis_three)
+            at = pl.multiple_of((group * blocks + step) * LANES, LANES)
+            exponent = dot_nn(factors[pl.ds(at, LANES), :], basis_three)
             trans = list(carry[group])
-            weights = [[] for _ in range(wide)]
             for s in range(per_block):
                 for h in range(wide):
                     e = exponent[s * ROWSUB : (s + 1) * ROWSUB, h * LANES : (h + 1) * LANES]
@@ -347,12 +361,6 @@
                     trans[h] = trans[h] - w
                     planes[pl.ds(a_base[h] + at + s * ROWSUB, ROWSUB), :] = alpha
                     planes[pl.ds(w_base[h] + at + s * ROWSUB, ROWSUB), :] = w
-                    weights[h].append(w)
-            weight = jnp.concatenate([jnp.concatenate(ws, 0) for ws in weights], 1)
-            w_high, w_rest = split_two(weight)
-            c_high, c_rest = colour_rows(block)
-            both = jnp.concatenate([c_high, c_rest], 0).astype(jnp.bfloat16)
-            picture_sum[group] += dot_nn(both, w_high) + dot_nn(both, w_rest)
             out.append(tuple(trans))
         return tuple(out)
 
@@ -360,10 +368,25 @@
     start = tuple(tuple(ones for _ in range(wide)) for _ in range(groups))
     lax.fori_loop(0, blocks, forward, start)
 
+    def wide_block(bases, at):
+        return jnp.concatenate([planes[pl.ds(base + at, LANES), :] for base in bases], 1)
+
+    for group in range(groups):
+        picture_sum[group] = jnp.zeros((LANES, pixels), jnp.float32)
+
+    def paint(step, carry):
+        for group in range(groups):
+            at = pl.multiple_of((group * blocks + step) * LANES, LANES)
+            w_high, w_rest = split_two(wide_block(w_base, at))
+            left = factors[pl.ds(at, LANES), :]
+            picture_sum[group] += dot_tn(left, w_high) + dot_tn(left, w_rest)
+        return carry
+
+    lax.fori_loop(0, blocks, paint, 0)
+
     loss = jnp.zeros((1, 1), jnp.float32)
     for group in range(groups):
-        both = picture_sum[group]
-        picture = both[:24] + both[24:]
+        picture = picture_sum[group, 32:56, :] + picture_sum[group, 80:104, :]
         parts = []
         for ch in range(3):
             pair = []
@@ -379,39 +402,44 @@
             jnp.sum(square, axis=0, keepdims=True), axis=1, keepdims=True
         )
         high = left.astype(jnp.bfloat16).astype(jnp.float32)
-        residual[group] = jnp.concatenate([high, left - high] * 2, 0).astype(jnp.bfloat16)
+        rest = left - high
+        none = jnp.zeros((32, pixels), jnp.float32)
+        residual[group] = jnp.concatenate([none, high, rest, high, rest], 0).astype(jnp.bfloat16)
 
     def backward(index, carry):
         step = blocks - 1 - index
         out = []
         for group in range(groups):
-            block = group * blocks + step
-            at = pl.multiple_of(block * LANES, LANES)
-            mask = field_mask(block)
-            c_high, c_rest = colour_rows(block)
-            four = jnp.concatenate([c_high, c_high, c_rest, c_rest], 0)
-            q = dot_nn(four.T.astype(jnp.bfloat16), residual[group])
+            at = pl.multiple_of((group * blocks + step) * LANES, LANES)
+            q = dot_nn(factors[pl.ds(at, LANES), :], residual[group])
             behind = list(carry[group])
-            slopes = [[None] * per_block for _ in range(wide)]
-            weights = [[None] * per_block for _ in range(wide)]
             for s in reversed(range(per_block)):
                 for h in range(wide):
                     w = planes[pl.ds(w_base[h] + at + s * ROWSUB, ROWSUB), :]
                     alpha = planes[pl.ds(a_base[h] + at + s * ROWSUB, ROWSUB), :]
                     d = q[s * ROWSUB : (s + 1) * ROWSUB, h * LANES : (h + 1) * LANES] - behind[h]
-                    slopes[h][s] = w * d
-                    weights[h][s] = w
+                    planes[pl.ds(a_base[h] + at + s * ROWSUB, ROWSUB), :] = w * d
                     behind[h] = behind[h] + alpha * d
-            slope = jnp.concatenate([jnp.concatenate(ws, 0) for ws in slopes], 1)
-            weight = jnp.concatenate([jnp.concatenate(ws, 0) for ws in weights], 1)
-            g_high, g_rest = split_two(slope)
-            w_high, w_rest = split_two(weight)
+            out.append(tuple(behind))
+        return tuple(out)
+
+    zeros = jnp.zeros((ROWSUB, LANES), jnp.float32)
+    start = tuple(tuple(zeros for _ in range(wide)) for _ in range(groups))
+    lax.fori_loop(0, blocks, backward, start)
+
+    def slopes(step, carry):
+        for group in range(groups):
+            block = group * blocks + step
+            at = pl.multiple_of(block * LANES, LANES)
+            mask = field_mask(block)
+            g_high, g_rest = split_two(wide_block(a_base, at))
+            w_high, w_rest = split_two(wide_block(w_base, at))
             moments = dot_nt(basis_rows, g_high) + dot_nt(basis_rows, g_rest)
-            res = residual[group, 0:48, :]
+            res = residual[group, 32:80, :]
             tone = dot_nt(res, w_high) + dot_nt(res, w_rest)
             tone = tone[:24] + tone[24:]
             m = [moments[i : i + 1, :] for i in range(6)]
-            u, v, a, b, c = [fields[pl.ds(block * 16 + f, 1), :] for f in range(5)]
+            u, v, a, b, c = [fields[pl.ds(block * ROWSUB + f, 1), :] for f in range(5)]
             m_x = m[1] - u * m[0]
             m_y = m[2] - v * m[0]
             rows = [
@@ -427,12 +455,9 @@
                 rows.append(jnp.sum(part, axis=0, keepdims=True))
             placed = [jnp.where(mask, row, 0.0) for row in rows]
             entries[pl.ds(at, LANES), :] = jnp.concatenate(placed + [pad], 0).T
-            out.append(tuple(behind))
-        return tuple(out)
-
-    zeros = jnp.zeros((ROWSUB, LANES), jnp.float32)
-    start = tuple(tuple(zeros for _ in range(wide)) for _ in range(groups))
-    lax.fori_loop(0, blocks, backward, start)
+        return carry
+
+    lax.fori_loop(0, blocks, slopes, 0)
 
     tall = jnp.zeros((LANES, LANES), jnp.float32)
 
@@ -471,36 +496,46 @@
         planes[pl.ds(start + planes_in, ROWSUB), :] = loss_rows
         return carry
 
-    lax.fori_loop(0, devices, collect, 0)
-
-    store = pltpu.make_async_copy(planes.at[pl.ds(0, devices * planes_out)], grad_out, out_sem)
-    store.start()
-    store.wait()
-
-
-def exchange_order(gx_size, gy_size):
-    gx_bits = gx_size.bit_length() - 1
-    gy_bits = gy_size.bit_length() - 1
-    order = [("gx", gx_size, 1 << b, gy_bits + b) for b in range(gx_bits)]
-    order += [("gy", gy_size, 1 << b, b) for b in reversed(range(gy_bits))]
-    return order
-
-
-def swap(values, phase):
-    axis, size, flip, _ = phase
-    return lax.ppermute(values, axis, [(i, i ^ flip) for i in range(size)])
-
-
-def spread(values, order):
-    for phase in order:
-        values = jnp.concatenate([values, swap(values, phase)], 0)
-    return values
-
-
-def fold(values, order):
-    for phase in reversed(order):
+    stores = [
+        pltpu.make_async_copy(
+            planes.at[pl.ds(i * near * planes_out, near * planes_out)], ref, out_sem.at[i]
+        )
+        for i, ref in enumerate((grad_own, grad_other))
+    ]
+    lax.fori_loop(near, devices, collect, 0, unroll=2)
+    stores[1].start()
+    lax.fori_loop(0, near, collect, 0, unroll=2)
+    stores[0].start()
+    for store in stores:
+        store.wait()
+
+
+def exchange_orders(gx_size, gy_size):
+    gx_bits = [gy_size.bit_length() - 1 + b for b in range(gx_size.bit_length() - 1)]
+    gy_bits = list(range(1, gy_size.bit_length() - 1))
+    cut = (len(gy_bits) + 1) // 2
+    low, high = gy_bits[:cut], gy_bits[cut:]
+    return gx_bits[::-1] + low + high, gx_bits + high + low
+
+
+def swap(values, devices, flips):
+    pairs = [(i, i ^ flips[i & 1]) for i in range(devices)]
+    return lax.ppermute(values, AXES, pairs)
+
+
+def spread(values, devices, orders):
+    for bits in zip(*orders):
+        flips = [1 << bit for bit in bits]
+        values = jnp.concatenate([values, swap(values, devices, flips)], 0)
+    return values, swap(values, devices, (1, 1))
+
+
+def fold(own, other, devices, orders):
+    values = own + swap(other, devices, (1, 1))
+    for bits in reversed(list(zip(*orders))):
+        flips = [1 << bit for bit in bits]
         half = values.shape[0] // 2
-        values = values[:half] + swap(values[half:], phase)
+        values = values[:half] + swap(values[half:], devices, flips)
     return values
 
 
@@ -508,7 +543,7 @@
     gx_size = lax.axis_size("gx")
     gy_size = lax.axis_size("gy")
     devices = gx_size * gy_size
-    order = exchange_order(gx_size, gy_size)
+    orders = exchange_orders(gx_size, gy_size)
     params_rows, count = gauss_params.shape
     tiles, depth = splat_lists.shape[1:]
     per_owner = count // LANES
@@ -519,11 +554,13 @@
     pixels = SIDE * SIDE
 
     me = lax.axis_index("gx") * gy_size + lax.axis_index("gy")
-    apart = (splat_lists // count) ^ me
+    owner = splat_lists // count
+    apart = owner ^ me
     local = splat_lists % count
-    place = jnp.zeros_like(apart)
-    for bit, phase in enumerate(order):
-        place = place + (((apart >> phase[3]) & 1) << bit)
+    place = (apart & 1) << len(orders[0])
+    for bit, (even, odd) in enumerate(zip(*orders)):
+        taken = jnp.where(owner & 1 == 0, apart >> even, apart >> odd)
+        place = place + ((taken & 1) << bit)
     rows = place * (count // ROWSUB) + (local // (ROWSUB * LANES)) * LANES + local % LANES
     which = (local // LANES) % ROWSUB
 
@@ -558,18 +595,20 @@
         ),
         out_shape=(
             jax.ShapeDtypeStruct((tiles * 3 * pixels // LANES, LANES), f32),
-            jax.ShapeDtypeStruct((devices * planes_out, LANES), f32),
+            jax.ShapeDtypeStruct((devices // 2 * planes_out, LANES), f32),
+            jax.ShapeDtypeStruct((devices // 2 * planes_out, LANES), f32),
         ),
-        in_specs=[smem, vmem, vmem, vmem, hbm],
-        out_specs=(vmem, hbm),
+        in_specs=[smem, vmem, vmem, vmem, hbm, hbm],
+        out_specs=(vmem, hbm, hbm),
         scratch_shapes=[
             pltpu.VMEM((max(2 * pixels // LANES * total, devices * planes_out), LANES), f32),
             pltpu.VMEM((total, LANES), f32),
-            pltpu.VMEM((total // LANES * 16, LANES), f32),
-            pltpu.VMEM((groups, 48, pixels), f32),
-            pltpu.VMEM((groups, 96, pixels), jnp.bfloat16),
-            pltpu.SemaphoreType.DMA(()),
-            pltpu.SemaphoreType.DMA(()),
+            pltpu.VMEM((total // LANES * ROWSUB, LANES), f32),
+            pltpu.VMEM((total, LANES), jnp.bfloat16),
+            pltpu.VMEM((groups, LANES, pixels), f32),
+            pltpu.VMEM((groups, LANES, pixels), jnp.bfloat16),
+            pltpu.SemaphoreType.DMA((2,)),
+            pltpu.SemaphoreType.DMA((2,)),
         ]
         + [pltpu.VMEM((devices * count // ROWSUB, LANES), f32)] * copies,
         compiler_params=pltpu.CompilerParams(vmem_limit_bytes=60 << 20),
@@ -587,12 +626,12 @@
     pictures = []
     losses = []
     for step in range(STEPS):
-        table = spread(fields, order)
-        picture, grads = render(
-            rows[step], which[step], middle[step], target_rows[step], table
+        near, far = spread(fields, devices, orders)
+        picture, own, other = render(
+            rows[step], which[step], middle[step], target_rows[step], near, far
         )
         pictures.append(picture)
-        summed = fold(grads, order)
+        summed = fold(own, other, devices, orders)
         losses.append(summed[planes_in, 0])
         more = step + 1 < STEPS
         result = pl.pallas_call(

time: 340 us -> 298 us (0.88)
  waiting for transfers between devices: 117 us -> 82.6 us
  starting transfers between devices: 19.6 us -> 38.3 us
  local copies, waits for them, and re-layouts: 33.2 us -> 14.6 us
  Pallas kernels: 158 us -> 149 us
    ppermute x20, waiting for transfers between devices: 117 us -> 82.6 us  [swap(): return lax.ppermute(values, AXES, pairs)]
    ppermute x20, starting transfers between devices: 19.6 us -> 38.3 us  [swap(): return lax.ppermute(values, AXES, pairs)]
    pallas_call x2, Pallas kernels: 149 us -> 140 us  [per_device(): render(rows[step], which[step], middle[step], target_rows[step], near, far)]
    unnamed x45 -> x29, local copies, waits for them, and re-layouts: 10.9 us -> 4.42 us
    concatenate x4 -> x2, local copies, waits for them, and re-layouts: 5.55 us -> 0.9 us  [spread(): values = jnp.concatenate([values, swap(values, devices, flips)], 0)]
  transfers between devices with their start and end apart: 20 -> 20, of which waited for: 19 -> 18; matrix products, arithmetic and copies ran while one was open for 6% -> 4% of each run, Pallas kernels for 0% -> 0%
where the time goes in v2:
time: 298 us; the launch traced here: 297 us
  Pallas kernels  149 us (50%)
  waiting for transfers between devices  82.6 us (28%)
  starting transfers between devices  38.3 us (13%)
  local copies, waits for them, and re-layouts  14.6 us (5%)
  other arithmetic  11.4 us (4%)
    pallas_call x2, Pallas kernels, per_device(): render(rows[step], which[step], middle[step], target_rows[step], near, far)  140 us
    ppermute x20, waiting for transfers between devices, swap(): return lax.ppermute(values, AXES, pairs)  82.6 us
    ppermute x20, starting transfers between devices, swap(): return lax.ppermute(values, AXES, pairs)  38.3 us
    pallas_call x2, Pallas kernels, per_device(): pl.pallas_call(functools.partial(update_kernel, step=step, project_next=m...  6.81 us
  transfers between devices with their start and end apart: 20, of which 18 were waited for; matrix products, arithmetic and copies ran while one was open for 4% of the time, Pallas kernels for 0%

profile of v2, /device:TPU:0, one launch (start us, length us, event | category | flops | bytes accessed | tf_op | source)
XLA Modules:
  0.0 296.8 jit_solution(9398886277840826718)
XLA Ops:
  0.6 1.9 project.1
  2.6 4.1 %collective-permute-start = (f32[144,128]{1,0:T(8,128)}, f32[144,128]{1,0:T(8,128)S(1)}, u32[]{:S(2)}, u32[]{:S(2)}) collective-permute-start(f32[144,128]{1,0:T(8,128)} %project.1), channel_id=1, source_target_pairs={{0,16},{1,9},{2,18},{3,11},{4,20},{5,13},{6,22},{7,15},{8,24},{9,1... | collective-permute-start | bytes 221192 | tf_op jit(solution)/shard_map/ppermute | solution.py:523
  6.7 2.6 collective-permute-done
  10.2 1.9 collective-permute-start.1
  12.1 3.7 %collective-permute-done.1 = f32[288,128]{1,0:T(8,128)S(1)} collective-permute-done((f32[288,128]{1,0:T(8,128)S(1)}, f32[288,128]{1,0:T(8,128)S(1)}, u32[]{:S(2)}, u32[]{:S(2)}) %collective-permute-start.1) | collective-permute-done | bytes 147488 | tf_op jit(solution)/shard_map/ppermute | solution.py:523
  18.6 4.9 %collective-permute-done.2 = f32[576,128]{1,0:T(8,128)S(1)} collective-permute-done((f32[576,128]{1,0:T(8,128)S(1)}, f32[576,128]{1,0:T(8,128)S(1)}, u32[]{:S(2)}, u32[]{:S(2)}) %collective-permute-start.2) | collective-permute-done | bytes 294944 | tf_op jit(solution)/shard_map/ppermute | solution.py:523
  24.4 1.9 collective-permute-start.3
  29.2 5.2 %collective-permute-done.3 = f32[1152,128]{1,0:T(8,128)S(1)} collective-permute-done((f32[1152,128]{1,0:T(8,128)S(1)}, f32[1152,128]{1,0:T(8,128)S(1)}, u32[]{:S(2)}, u32[]{:S(2)}) %collective-permute-start.3) | collective-permute-done | bytes 589856 | tf_op jit(solution)/shard_map/ppermute | solution.py:523
  39.4 70.1 %render.2 = (f32[96,128]{1,0:T(8,128)}, f32[2432,128]{1,0:T(8,128)}, f32[2432,128]{1,0:T(8,128)}) custom-call(s32[8192]{0:T(1024)} %squeeze.20.rows_ref, s32[64,128]{1,0:T(8,128)} %squeeze.21.group_ref, f32[4,128]{1,0:T(4,128)} %tile.13.middle_ref, f32[96,128]{1,0:T(8,128)} %squeeze.22.target_ref, f32[2304,128]{1,0:T(8,128)} %constant_dynamic-update-slice_fusion.table_own, ...), custom_call_target="tpu_custom_call" | custom-call | tf_op jit(solution)/shard_map/render/pallas_call | solution.py:630
  110.1 2.8 collective-permute-done.5
  114.3 1.9 collective-permute-start.6
  116.2 8.4 %collective-permute-done.6 = f32[1216,128]{1,0:T(8,128)S(1)} collective-permute-done((f32[1216,128]{1,0:T(8,128)S(1)}, f32[1216,128]{1,0:T(8,128)S(1)}, u32[]{:S(2)}, u32[]{:S(2)}) %collective-permute-start.6) | collective-permute-done | bytes 622624 | tf_op jit(solution)/shard_map/ppermute | solution.py:523
  126.6 5.1 %collective-permute-done.7 = f32[608,128]{1,0:T(8,128)S(1)} collective-permute-done((f32[608,128]{1,0:T(8,128)S(1)}, f32[608,128]{1,0:T(8,128)S(1)}, u32[]{:S(2)}, u32[]{:S(2)}) %collective-permute-start.7) | collective-permute-done | bytes 311328 | tf_op jit(solution)/shard_map/ppermute | solution.py:523
  133.3 4.1 %collective-permute-done.8 = f32[304,128]{1,0:T(8,128)S(1)} collective-permute-done((f32[304,128]{1,0:T(8,128)S(1)}, f32[304,128]{1,0:T(8,128)S(1)}, u32[]{:S(2)}, u32[]{:S(2)}) %collective-permute-start.8) | collective-permute-done | bytes 155680 | tf_op jit(solution)/shard_map/ppermute | solution.py:523
  137.4 3.3 %collective-permute-start.9 = (f32[152,128]{1,0:T(8,128)S(1)}, f32[152,128]{1,0:T(8,128)S(1)}, u32[]{:S(2)}, u32[]{:S(2)}) collective-permute-start(f32[152,128]{1,0:T(8,128)S(1)} %slice.132), channel_id=1, source_target_pairs={{0,16},{1,9},{2,18},{3,11},{4,20},{5,13},{6,22},{7,15},{8,24},{9,1... | collective-permute-start | bytes 233480 | tf_op jit(solution)/shard_map/ppermute | solution.py:523
  140.6 2.4 collective-permute-done.9
  143.6 3.5 %update.2 = (f32[55,2048]{1,0:T(8,128)}, f32[55,2048]{1,0:T(8,128)}, f32[55,2048]{1,0:T(8,128)}, f32[144,128]{1,0:T(8,128)}) custom-call(f32[2,2]{1,0:T(2,128)} %cam_ref.5, f32[55,2048]{1,0:T(8,128)} %param_ref.3, f32[55,2048]{1,0:T(8,128)} %first_ref.1, f32[55,2048]{1,0:T(8,128)} %second_ref.1, f32[152,128]{1,0:T(8,128)} %slice_add_fusion.7.grad_ref), custom_call_target="tpu_custom_call" | custom-call | tf_op jit(solution)/shard_map/update/pallas_call | solution.py:637
  147.2 2.9 collective-permute-start.10
  150.1 2.6 collective-permute-done.10
  153.6 4.3 %collective-permute-start.11 = (f32[288,128]{1,0:T(8,128)S(1)}, f32[288,128]{1,0:T(8,128)S(1)}, u32[]{:S(2)}, u32[]{:S(2)}) collective-permute-start(f32[288,128]{1,0:T(8,128)S(1)} %pad_maximum_fusion.5), channel_id=1, source_target_pairs={{0,8},{1,17},{2,10},{3,19},{4,12},{5,21},{6,14},{7,23},{8,0},{9,25... | collective-permute-start | bytes 442376 | tf_op jit(solution)/shard_map/ppermute | solution.py:523
  157.9 3.1 %collective-permute-done.11 = f32[288,128]{1,0:T(8,128)S(1)} collective-permute-done((f32[288,128]{1,0:T(8,128)S(1)}, f32[288,128]{1,0:T(8,128)S(1)}, u32[]{:S(2)}, u32[]{:S(2)}) %collective-permute-start.11) | collective-permute-done | bytes 147488 | tf_op jit(solution)/shard_map/ppermute | solution.py:523
  163.5 7.3 %collective-permute-done.12 = f32[576,128]{1,0:T(8,128)S(1)} collective-permute-done((f32[576,128]{1,0:T(8,128)S(1)}, f32[576,128]{1,0:T(8,128)S(1)}, u32[]{:S(2)}, u32[]{:S(2)}) %collective-permute-start.12) | collective-permute-done | bytes 294944 | tf_op jit(solution)/shard_map/ppermute | solution.py:523
  173.2 8.5 %collective-permute-done.13 = f32[1152,128]{1,0:T(8,128)S(1)} collective-permute-done((f32[1152,128]{1,0:T(8,128)S(1)}, f32[1152,128]{1,0:T(8,128)S(1)}, u32[]{:S(2)}, u32[]{:S(2)}) %collective-permute-start.13) | collective-permute-done | bytes 589856 | tf_op jit(solution)/shard_map/ppermute | solution.py:523
  186.1 70.1 %render.3 = (f32[96,128]{1,0:T(8,128)}, f32[2432,128]{1,0:T(8,128)}, f32[2432,128]{1,0:T(8,128)}) custom-call(s32[8192]{0:T(1024)} %squeeze.23.rows_ref, s32[64,128]{1,0:T(8,128)} %squeeze.24.group_ref, f32[4,128]{1,0:T(4,128)} %tile.15.middle_ref, f32[96,128]{1,0:T(8,128)} %squeeze.25.target_ref, f32[2304,128]{1,0:T(8,128)} %copy-done.1, f32[2304,128]{1,0:T(8,128)} %copy-done.3), custom_call_target="tpu_custom_call" | custom-call | tf_op jit(solution)/shard_map/render/pallas_call | solution.py:630
  256.6 2.9 collective-permute-done.15
  262.3 8.9 %collective-permute-done.16 = f32[1216,128]{1,0:T(8,128)S(1)} collective-permute-done((f32[1216,128]{1,0:T(8,128)S(1)}, f32[1216,128]{1,0:T(8,128)S(1)}, u32[]{:S(2)}, u32[]{:S(2)}) %collective-permute-start.16) | collective-permute-done | bytes 622624 | tf_op jit(solution)/shard_map/ppermute | solution.py:523
  272.7 5.6 %collective-permute-done.17 = f32[608,128]{1,0:T(8,128)S(1)} collective-permute-done((f32[608,128]{1,0:T(8,128)S(1)}, f32[608,128]{1,0:T(8,128)S(1)}, u32[]{:S(2)}, u32[]{:S(2)}) %collective-permute-start.17) | collective-permute-done | bytes 311328 | tf_op jit(solution)/shard_map/ppermute | solution.py:523
  278.4 2.9 collective-permute-start.18
  282.5 2.8 collective-permute-done.18
  285.4 3.3 %collective-permute-start.19 = (f32[152,128]{1,0:T(8,128)S(1)}, f32[152,128]{1,0:T(8,128)S(1)}, u32[]{:S(2)}, u32[]{:S(2)}) collective-permute-start(f32[152,128]{1,0:T(8,128)S(1)} %slice.143), channel_id=1, source_target_pairs={{0,16},{1,9},{2,18},{3,11},{4,20},{5,13},{6,22},{7,15},{8,24},{9,1... | collective-permute-start | bytes 233480 | tf_op jit(solution)/shard_map/ppermute | solution.py:523
  291.6 1.9 maximum_multiply_fusion
  293.5 3.3 %update.3 = (f32[55,2048]{1,0:T(8,128)}, f32[55,2048]{1,0:T(8,128)}, f32[55,2048]{1,0:T(8,128)}) custom-call(f32[2,2]{1,0:T(2,128)} %cam_ref.5, f32[55,2048]{1,0:T(8,128)} %get-tuple-element.20.param_ref, f32[55,2048]{1,0:T(8,128)} %get-tuple-element.21.first_ref, f32[55,2048]{1,0:T(8,128)} %get-tuple-element.22.second_ref, f32[152,128]{1,0:T(8,128)} %copy-done.4), custom_call_target="tpu_custom_call" | custom-call | tf_op jit(solution)/shard_map/update/pallas_call | solution.py:637
  (99 shorter events, 37.7 us)
Async XLA Ops:
  0.6 25.7 %copy-start.9 = (s32[2,16]{1,0:T(2,128)S(1)}, s32[2,16]{1,0:T(2,128)}, u32[]{:S(2)}) copy-start(s32[2,16]{1,0:T(2,128)} %param.11) | copy-start | bytes 388
  2.6 23.9 %copy-start = (f32[144,128]{1,0:T(8,128)S(1)}, f32[144,128]{1,0:T(8,128)}, u32[]{:S(2)}) copy-start(f32[144,128]{1,0:T(8,128)} %project.1) | copy-start | bytes 221188
  2.6 6.7 %collective-permute-start = (f32[144,128]{1,0:T(8,128)}, f32[144,128]{1,0:T(8,128)S(1)}, u32[]{:S(2)}, u32[]{:S(2)}) collective-permute-start(f32[144,128]{1,0:T(8,128)} %project.1), channel_id=1, source_target_pairs={{0,16},{1,9},{2,18},{3,11},{4,20},{5,13},{6,22},{7,15},{8,24},{9,1... | collective-permute-start | bytes 221192 | tf_op jit(solution)/shard_map/ppermute | solution.py:523
  10.2 5.6 %collective-permute-start.1 = (f32[288,128]{1,0:T(8,128)S(1)}, f32[288,128]{1,0:T(8,128)S(1)}, u32[]{:S(2)}, u32[]{:S(2)}) collective-permute-start(f32[288,128]{1,0:T(8,128)S(1)} %pad_maximum_fusion.4), channel_id=1, source_target_pairs={{0,8},{1,17},{2,10},{3,19},{4,12},{5,21},{6,14},{7,23},{8,0},{9,25... | collective-permute-start | bytes 442376 | tf_op jit(solution)/shard_map/ppermute | solution.py:523
  16.7 6.8 %collective-permute-start.2 = (f32[576,128]{1,0:T(8,128)S(1)}, f32[576,128]{1,0:T(8,128)S(1)}, u32[]{:S(2)}, u32[]{:S(2)}) collective-permute-start(f32[576,128]{1,0:T(8,128)S(1)} %pad_maximum_fusion.2), channel_id=1, source_target_pairs={{0,2},{1,5},{2,0},{3,7},{4,6},{5,1},{6,4},{7,3},{8,10},{9,13},{10,... | collective-permute-start | bytes 884744 | tf_op jit(solution)/shard_map/ppermute | solution.py:523
  24.4 9.9 %collective-permute-start.3 = (f32[1152,128]{1,0:T(8,128)S(1)}, f32[1152,128]{1,0:T(8,128)S(1)}, u32[]{:S(2)}, u32[]{:S(2)}) collective-permute-start(f32[1152,128]{1,0:T(8,128)S(1)} %pad_maximum_fusion), channel_id=1, source_target_pairs={{0,4},{1,3},{2,6},{3,1},{4,0},{5,7},{6,2},{7,5},{8,12},{9,11},{10,... | collective-permute-start | bytes 1769480 | tf_op jit(solution)/shard_map/ppermute | solution.py:523
  27.1 8.8 %copy-start.5 = (f32[2,16,3,256]{3,1,2,0:T(8,128)S(1)}, f32[2,16,3,256]{3,1,2,0:T(8,128)}, u32[]{:S(2)}) copy-start(f32[2,16,3,256]{3,1,2,0:T(8,128)} %param.12) | copy-start | bytes 294916
  28.4 8.2 %copy-start.6 = (s32[2,16,512]{2,1,0:T(8,128)S(1)}, s32[2,16,512]{2,1,0:T(8,128)}, u32[]{:S(2)}) copy-start(s32[2,16,512]{2,1,0:T(8,128)} %param.10) | copy-start | bytes 196612
  35.2 4.2 %collective-permute-start.4 = (f32[2304,128]{1,0:T(8,128)}, f32[2304,128]{1,0:T(8,128)}, u32[]{:S(2)}, u32[]{:S(2)}) collective-permute-start(f32[2304,128]{1,0:T(8,128)} %constant_dynamic-update-slice_fusion.table_own), channel_id=1, source_target_pairs={{0,1},{1,0},{2,3},{3,2},{4,5},{5,4},{6,7},{7,6},{8,9},{9,8},{10,11... | collective-permute-start | bytes 3538952 | tf_op jit(solution)/shard_map/ppermute | solution.py:523
  109.5 3.4 %collective-permute-start.5 = (f32[2432,128]{1,0:T(8,128)}, f32[2432,128]{1,0:T(8,128)S(1)}, u32[]{:S(2)}, u32[]{:S(2)}) collective-permute-start(f32[2432,128]{1,0:T(8,128)} %get-tuple-element.19), channel_id=1, source_target_pairs={{0,1},{1,0},{2,3},{3,2},{4,5},{5,4},{6,7},{7,6},{8,9},{9,8},{10,11... | collective-permute-start | bytes 3735560 | tf_op jit(solution)/shard_map/ppermute | solution.py:523
  114.3 10.3 %collective-permute-start.6 = (f32[1216,128]{1,0:T(8,128)S(1)}, f32[1216,128]{1,0:T(8,128)S(1)}, u32[]{:S(2)}, u32[]{:S(2)}) collective-permute-start(f32[1216,128]{1,0:T(8,128)S(1)} %slice.126), channel_id=1, source_target_pairs={{0,4},{1,3},{2,6},{3,1},{4,0},{5,7},{6,2},{7,5},{8,12},{9,11},{10,... | collective-permute-start | bytes 1867784 | tf_op jit(solution)/shard_map/ppermute | solution.py:523
  124.7 7.0 %collective-permute-start.7 = (f32[608,128]{1,0:T(8,128)S(1)}, f32[608,128]{1,0:T(8,128)S(1)}, u32[]{:S(2)}, u32[]{:S(2)}) collective-permute-start(f32[608,128]{1,0:T(8,128)S(1)} %slice.128), channel_id=1, source_target_pairs={{0,2},{1,5},{2,0},{3,7},{4,6},{5,1},{6,4},{7,3},{8,10},{9,13},{10,... | collective-permute-start | bytes 933896 | tf_op jit(solution)/shard_map/ppermute | solution.py:523
  131.8 5.6 %collective-permute-start.8 = (f32[304,128]{1,0:T(8,128)S(1)}, f32[304,128]{1,0:T(8,128)S(1)}, u32[]{:S(2)}, u32[]{:S(2)}) collective-permute-start(f32[304,128]{1,0:T(8,128)S(1)} %slice.130), channel_id=1, source_target_pairs={{0,8},{1,17},{2,10},{3,19},{4,12},{5,21},{6,14},{7,23},{8,0},{9,25... | collective-permute-start | bytes 466952 | tf_op jit(solution)/shard_map/ppermute | solution.py:523
  137.4 5.6 %collective-permute-start.9 = (f32[152,128]{1,0:T(8,128)S(1)}, f32[152,128]{1,0:T(8,128)S(1)}, u32[]{:S(2)}, u32[]{:S(2)}) collective-permute-start(f32[152,128]{1,0:T(8,128)S(1)} %slice.132), channel_id=1, source_target_pairs={{0,16},{1,9},{2,18},{3,11},{4,20},{5,13},{6,22},{7,15},{8,24},{9,1... | collective-permute-start | bytes 233480 | tf_op jit(solution)/shard_map/ppermute | solution.py:523
  147.2 26.0 %copy-start.2 = (f32[144,128]{1,0:T(8,128)S(1)}, f32[144,128]{1,0:T(8,128)}, u32[]{:S(2)}) copy-start(f32[144,128]{1,0:T(8,128)} %get-tuple-element.23) | copy-start | bytes 221188
  147.2 5.5 %collective-permute-start.10 = (f32[144,128]{1,0:T(8,128)}, f32[144,128]{1,0:T(8,128)S(1)}, u32[]{:S(2)}, u32[]{:S(2)}) collective-permute-start(f32[144,128]{1,0:T(8,128)} %get-tuple-element.23), channel_id=1, source_target_pairs={{0,16},{1,9},{2,18},{3,11},{4,20},{5,13},{6,22},{7,15},{8,24},{9,1... | collective-permute-start | bytes 221192 | tf_op jit(solution)/shard_map/ppermute | solution.py:523
  153.6 7.4 %collective-permute-start.11 = (f32[288,128]{1,0:T(8,128)S(1)}, f32[288,128]{1,0:T(8,128)S(1)}, u32[]{:S(2)}, u32[]{:S(2)}) collective-permute-start(f32[288,128]{1,0:T(8,128)S(1)} %pad_maximum_fusion.5), channel_id=1, source_target_pairs={{0,8},{1,17},{2,10},{3,19},{4,12},{5,21},{6,14},{7,23},{8,0},{9,25... | collective-permute-start | bytes 442376 | tf_op jit(solution)/shard_map/ppermute | solution.py:523
  161.9 8.9 %collective-permute-start.12 = (f32[576,128]{1,0:T(8,128)S(1)}, f32[576,128]{1,0:T(8,128)S(1)}, u32[]{:S(2)}, u32[]{:S(2)}) collective-permute-start(f32[576,128]{1,0:T(8,128)S(1)} %pad_maximum_fusion.3), channel_id=1, source_target_pairs={{0,2},{1,5},{2,0},{3,7},{4,6},{5,1},{6,4},{7,3},{8,10},{9,13},{10,... | collective-permute-start | bytes 884744 | tf_op jit(solution)/shard_map/ppermute | solution.py:523
  171.7 9.9 %collective-permute-start.13 = (f32[1152,128]{1,0:T(8,128)S(1)}, f32[1152,128]{1,0:T(8,128)S(1)}, u32[]{:S(2)}, u32[]{:S(2)}) collective-permute-start(f32[1152,128]{1,0:T(8,128)S(1)} %pad_maximum_fusion.1), channel_id=1, source_target_pairs={{0,4},{1,3},{2,6},{3,1},{4,0},{5,7},{6,2},{7,5},{8,12},{9,11},{10,... | collective-permute-start | bytes 1769480 | tf_op jit(solution)/shard_map/ppermute | solution.py:523
  181.7 3.4 %copy-start.1 = (f32[2304,128]{1,0:T(8,128)}, f32[2304,128]{1,0:T(8,128)S(1)}, u32[]{:S(2)}) copy-start(f32[2304,128]{1,0:T(8,128)S(1)} %constant_dynamic-update-slice_fusion.5.table_own) | copy-start | bytes 3538948
  181.7 3.4 %collective-permute-start.14 = (f32[2304,128]{1,0:T(8,128)S(1)}, f32[2304,128]{1,0:T(8,128)S(1)}, u32[]{:S(2)}, u32[]{:S(2)}) collective-permute-start(f32[2304,128]{1,0:T(8,128)S(1)} %constant_dynamic-update-slice_fusion.5.table_own), channel_id=1, source_target_pairs={{0,1},{1,0},{2,3},{3,2},{4,5},{5,4},{6,7},{7,6},{8,9},{9,8},{10,11... | collective-permute-start | bytes 3538952 | tf_op jit(solution)/shard_map/ppermute | solution.py:523
  185.1 1.0 copy-start.3
  256.2 3.2 %collective-permute-start.15 = (f32[2432,128]{1,0:T(8,128)}, f32[2432,128]{1,0:T(8,128)S(1)}, u32[]{:S(2)}, u32[]{:S(2)}) collective-permute-start(f32[2432,128]{1,0:T(8,128)} %get-tuple-element.25), channel_id=1, source_target_pairs={{0,1},{1,0},{2,3},{3,2},{4,5},{5,4},{6,7},{7,6},{8,9},{9,8},{10,11... | collective-permute-start | bytes 3735560 | tf_op jit(solution)/shard_map/ppermute | solution.py:523
  260.9 10.3 %collective-permute-start.16 = (f32[1216,128]{1,0:T(8,128)S(1)}, f32[1216,128]{1,0:T(8,128)S(1)}, u32[]{:S(2)}, u32[]{:S(2)}) collective-permute-start(f32[1216,128]{1,0:T(8,128)S(1)} %slice.137), channel_id=1, source_target_pairs={{0,4},{1,3},{2,6},{3,1},{4,0},{5,7},{6,2},{7,5},{8,12},{9,11},{10,... | collective-permute-start | bytes 1867784 | tf_op jit(solution)/shard_map/ppermute | solution.py:523
  271.3 10.0 %copy-start.7 = (f32[96,128]{1,0:T(8,128)S(1)}, f32[96,128]{1,0:T(8,128)}, u32[]{:S(2)}) copy-start(f32[96,128]{1,0:T(8,128)} %get-tuple-element.29) | copy-start | bytes 147460
  271.3 11.2 %copy-start.8 = (f32[96,128]{1,0:T(8,128)S(1)}, f32[96,128]{1,0:T(8,128)}, u32[]{:S(2)}) copy-start(f32[96,128]{1,0:T(8,128)} %get-tuple-element.30) | copy-start | bytes 147460
  271.3 7.0 %collective-permute-start.17 = (f32[608,128]{1,0:T(8,128)S(1)}, f32[608,128]{1,0:T(8,128)S(1)}, u32[]{:S(2)}, u32[]{:S(2)}) collective-permute-start(f32[608,128]{1,0:T(8,128)S(1)} %slice.139), channel_id=1, source_target_pairs={{0,2},{1,5},{2,0},{3,7},{4,6},{5,1},{6,4},{7,3},{8,10},{9,13},{10,... | collective-permute-start | bytes 933896 | tf_op jit(solution)/shard_map/ppermute | solution.py:523
  278.4 7.0 %collective-permute-start.18 = (f32[304,128]{1,0:T(8,128)S(1)}, f32[304,128]{1,0:T(8,128)S(1)}, u32[]{:S(2)}, u32[]{:S(2)}) collective-permute-start(f32[304,128]{1,0:T(8,128)S(1)} %slice.141), channel_id=1, source_target_pairs={{0,8},{1,17},{2,10},{3,19},{4,12},{5,21},{6,14},{7,23},{8,0},{9,25... | collective-permute-start | bytes 466952 | tf_op jit(solution)/shard_map/ppermute | solution.py:523
  285.4 5.7 %collective-permute-start.19 = (f32[152,128]{1,0:T(8,128)S(1)}, f32[152,128]{1,0:T(8,128)S(1)}, u32[]{:S(2)}, u32[]{:S(2)}) collective-permute-start(f32[152,128]{1,0:T(8,128)S(1)} %slice.143), channel_id=1, source_target_pairs={{0,16},{1,9},{2,18},{3,11},{4,20},{5,13},{6,22},{7,15},{8,24},{9,1... | collective-permute-start | bytes 233480 | tf_op jit(solution)/shard_map/ppermute | solution.py:523
  291.1 2.4 copy-start.4

commit v3 on v2

--- a/solution.py
+++ b/solution.py
@@ -204,18 +204,6 @@
     return jnp.dot(a, b, preferred_element_type=jnp.float32)
 
 
-def dot_tn(a, b):
-    return lax.dot_general(
-        a, b, (((0,), (0,)), ((), ())), preferred_element_type=jnp.float32
-    )
-
-
-def dot_nt(a, b):
-    return lax.dot_general(
-        a, b, (((1,), (1,)), ((), ())), preferred_element_type=jnp.float32
-    )
-
-
 def render_kernel(
     rows_ref,
     group_ref,
@@ -226,65 +214,83 @@
     picture_ref,
     grad_own,
     grad_other,
-    planes,
     entries,
     fields,
     factors,
-    picture_sum,
     residual,
+    across,
+    w_high,
+    w_rest,
+    g_high,
+    g_rest,
     in_sem,
     out_sem,
-    *tables,
+    row_sem,
+    *scratch,
     devices,
     per_owner,
     groups,
     depth,
+    streams,
 ):
     planes_in = FIELDS * per_owner
     planes_out = planes_in + ROWSUB
     halves = per_owner // ROWSUB
     total = groups * ROWSUB * depth
-    table = tables[0]
+    row_lists, scratch = scratch[:streams], scratch[streams:]
+    table = scratch[0]
     blocks = depth * ROWSUB // LANES
     per_block = LANES // ROWSUB
     pixels = SIDE * SIDE
     wide = pixels // LANES
     near = devices // 2
+    w_planes = scratch[1 : 1 + wide]
+    a_planes = scratch[1 + wide : 1 + 2 * wide]
+    tables = [one for one in scratch if one.shape[0] >= devices * halves * LANES]
 
     loads = [
-        pltpu.make_async_copy(
-            ref, planes.at[pl.ds(i * near * planes_in, near * planes_in)], in_sem.at[i]
-        )
-        for i, ref in enumerate((table_own, table_other))
+        pltpu.make_async_copy(ref, stage.at[pl.ds(0, near * planes_in)], in_sem.at[i])
+        for i, (ref, stage) in enumerate(zip((table_own, table_other), w_planes))
     ]
-    for load in loads:
-        load.start()
-    for load in loads:
-        load.wait()
+    lists = [
+        pltpu.make_async_copy(rows_ref.at[i], one, row_sem.at[i])
+        for i, one in enumerate(row_lists)
+    ]
+    for copy in loads + lists:
+        copy.start()
 
     pad = jnp.zeros((LANES - FIELDS * ROWSUB, LANES), jnp.float32)
 
-    def build(owner, carry):
-        start = pl.multiple_of(owner * planes_in, 8)
-        for half in range(halves):
-            parts = [
-                planes[pl.ds(start + f * per_owner + half * ROWSUB, ROWSUB), :]
-                for f in range(FIELDS)
-            ]
-            block = jnp.concatenate(parts + [pad], 0)
-            at = pl.multiple_of((owner * halves + half) * LANES, LANES)
-            table[pl.ds(at, LANES), :] = block.T
-        return carry
-
-    lax.fori_loop(0, devices, build, 0, unroll=2)
-
-    unroll = 32
+    for side in range(2):
+        loads[side].wait()
+        stage = w_planes[side]
+
+        def build(owner, carry, stage=stage, side=side):
+            start = pl.multiple_of(owner * planes_in, 8)
+            for half in range(halves):
+                parts = [
+                    stage[pl.ds(start + f * per_owner + half * ROWSUB, ROWSUB), :]
+                    for f in range(FIELDS)
+                ]
+                block = jnp.concatenate(parts + [pad], 0)
+                at = pl.multiple_of(((side * near + owner) * halves + half) * LANES, LANES)
+                table[pl.ds(at, LANES), :] = block.T
+            return carry
+
+        lax.fori_loop(0, near, build, 0, unroll=2)
+    for copy in lists:
+        copy.wait()
+
+    turns = 2
+    unroll = turns * streams
 
     def gather(index, carry):
-        base = pl.multiple_of(index * unroll, unroll)
-        for q in range(unroll):
-            row = rows_ref[base + q]
-            entries[pl.ds(base + q, 1), :] = table[pl.ds(row, 1), :]
+        some = entries.at[pl.ds(pl.multiple_of(index * unroll, unroll), unroll)]
+        for turn in range(turns):
+            place = index * turns + turn
+            for q in range(streams):
+                at = turn * streams + q
+                some[at : at + 1, :] = table[pl.ds(row_lists[q][place], 1), :]
         return carry
 
     lax.fori_loop(0, total // unroll, gather, 0)
@@ -292,29 +298,28 @@
     sub = lax.broadcasted_iota(jnp.int32, (ROWSUB, LANES), 0)
     lane = lax.broadcasted_iota(jnp.int32, (ROWSUB, LANES), 1)
     own_tile = sub == lane % ROWSUB
-    basis_three = jnp.where(
+    basis_in = jnp.where(
         lax.broadcasted_iota(jnp.int32, (LANES, pixels), 0) < 24, pixel_basis(LANES), 0.0
     ).astype(jnp.bfloat16)
-    basis_rows = jnp.where(
-        lax.broadcasted_iota(jnp.int32, (16, pixels), 0) < 8, pixel_basis(16), 0.0
-    ).astype(jnp.bfloat16)
-    w_base = [h * total for h in range(wide)]
-    a_base = [(wide + h) * total for h in range(wide)]
+    lit = lax.broadcasted_iota(jnp.int32, (LANES, 3 * LANES), 0) - 32
+    lit = jnp.where(lit < 0, -1, lit % 48)
+    shown = lax.broadcasted_iota(jnp.int32, (LANES, 3 * LANES), 1) // LANES
+    colour_in = jnp.where((lit >= 0) & (lit < 24) & (lit // ROWSUB == shown), 1.0, 0.0)
+    colour_in = colour_in.astype(jnp.bfloat16)
 
     def field_mask(block):
         return sub == group_ref[pl.ds(block, 1), :]
 
-    def prepare(block, carry):
+    def prepare(block, group):
         at = pl.multiple_of(block * LANES, LANES)
-        group = block // blocks
         mask = field_mask(block)
-        turned = entries[pl.ds(at, LANES), :].T
+        raw = entries[pl.ds(at, LANES), :].T
         rows = []
         for f in range(FIELDS):
-            part = jnp.where(mask, turned[f * ROWSUB : (f + 1) * ROWSUB, :], 0.0)
+            part = jnp.where(mask, raw[f * ROWSUB : (f + 1) * ROWSUB, :], 0.0)
             rows.append(jnp.sum(part, axis=0, keepdims=True))
-        u = rows[0] - middle_ref[pl.ds(2 * group, 1), :]
-        v = rows[1] - middle_ref[pl.ds(2 * group + 1, 1), :]
+        u = rows[0] - middle_ref[2 * group : 2 * group + 1, :]
+        v = rows[1] - middle_ref[2 * group + 1 : 2 * group + 2, :]
         rows[0], rows[1] = u, v
         a, b, c = rows[2], rows[3], rows[4]
         for f in range(5):
@@ -343,56 +348,62 @@
             [high, mid, low, jnp.zeros_like(low)] + c_high + c_high + c_rest + c_rest, 0
         )
         factors[pl.ds(at, LANES), :] = stacked.T.astype(jnp.bfloat16)
-        return carry
-
-    lax.fori_loop(0, groups * blocks, prepare, 0, unroll=2)
+
+    def store_split(high_ref, rest_ref, at, values):
+        for h in range(wide):
+            high, rest = split_two(jnp.concatenate(values[h], 0))
+            span = pl.ds(at, high.shape[0])
+            high_ref[span, h * LANES : (h + 1) * LANES] = high
+            rest_ref[span, h * LANES : (h + 1) * LANES] = rest
+
+    for group in range(groups):
+        prepare(group * blocks, group)
 
     def forward(step, carry):
         out = []
         for group in range(groups):
             at = pl.multiple_of((group * blocks + step) * LANES, LANES)
-            exponent = dot_nn(factors[pl.ds(at, LANES), :], basis_three)
-            trans = list(carry[group])
+            left = factors[pl.ds(at, LANES), :]
+            exponent = dot_nn(left, basis_in)
+            tones = dot_nn(left, colour_in)
+            trans, sums = list(carry[group][0]), [list(x) for x in carry[group][1]]
+            kept = [[] for _ in range(wide)]
             for s in range(per_block):
+                span = pl.ds(at + s * ROWSUB, ROWSUB)
+                tone = tones[s * ROWSUB : (s + 1) * ROWSUB, :]
                 for h in range(wide):
                     e = exponent[s * ROWSUB : (s + 1) * ROWSUB, h * LANES : (h + 1) * LANES]
                     alpha = jnp.exp2(jnp.minimum(e, LOG2E * LOG_CAP))
                     w = trans[h] * alpha
                     trans[h] = trans[h] - w
-                    planes[pl.ds(a_base[h] + at + s * ROWSUB, ROWSUB), :] = alpha
-                    planes[pl.ds(w_base[h] + at + s * ROWSUB, ROWSUB), :] = w
-            out.append(tuple(trans))
+                    a_planes[h][span, :] = alpha
+                    w_planes[h][span, :] = w
+                    for ch in range(3):
+                        sums[ch][h] = sums[ch][h] + w * tone[:, ch * LANES : (ch + 1) * LANES]
+                    kept[h].append(w)
+                if s % 2:
+                    where = pl.multiple_of(at + (s - 1) * ROWSUB, 2 * ROWSUB)
+                    store_split(w_high, w_rest, where, kept)
+                    kept = [[] for _ in range(wide)]
+            out.append((tuple(trans), tuple(tuple(x) for x in sums)))
+        ahead = jnp.minimum(step + 1, blocks - 1)
+        for group in range(groups):
+            prepare(group * blocks + ahead, group)
         return tuple(out)
 
     ones = jnp.ones((ROWSUB, LANES), jnp.float32)
-    start = tuple(tuple(ones for _ in range(wide)) for _ in range(groups))
-    lax.fori_loop(0, blocks, forward, start)
-
-    def wide_block(bases, at):
-        return jnp.concatenate([planes[pl.ds(base + at, LANES), :] for base in bases], 1)
-
-    for group in range(groups):
-        picture_sum[group] = jnp.zeros((LANES, pixels), jnp.float32)
-
-    def paint(step, carry):
-        for group in range(groups):
-            at = pl.multiple_of((group * blocks + step) * LANES, LANES)
-            w_high, w_rest = split_two(wide_block(w_base, at))
-            left = factors[pl.ds(at, LANES), :]
-            picture_sum[group] += dot_tn(left, w_high) + dot_tn(left, w_rest)
-        return carry
-
-    lax.fori_loop(0, blocks, paint, 0)
+    zeros = jnp.zeros((ROWSUB, LANES), jnp.float32)
+    begin = (tuple(ones for _ in range(wide)), tuple((zeros,) * wide for _ in range(3)))
+    done = lax.fori_loop(0, blocks, forward, (begin,) * groups)
 
     loss = jnp.zeros((1, 1), jnp.float32)
     for group in range(groups):
-        picture = picture_sum[group, 32:56, :] + picture_sum[group, 80:104, :]
         parts = []
         for ch in range(3):
             pair = []
             for h in range(wide):
                 where = pl.ds((group * ROWSUB * 3 + ch) * wide + h, ROWSUB, stride=3 * wide)
-                part = picture[ch * ROWSUB : (ch + 1) * ROWSUB, h * LANES : (h + 1) * LANES]
+                part = done[group][1][ch][h]
                 picture_ref[where, :] = part
                 pair.append(part - target_ref[where, :])
             parts.append(jnp.concatenate(pair, 1))
@@ -404,40 +415,34 @@
         high = left.astype(jnp.bfloat16).astype(jnp.float32)
         rest = left - high
         none = jnp.zeros((32, pixels), jnp.float32)
-        residual[group] = jnp.concatenate([none, high, rest, high, rest], 0).astype(jnp.bfloat16)
-
-    def backward(index, carry):
-        step = blocks - 1 - index
-        out = []
-        for group in range(groups):
-            at = pl.multiple_of((group * blocks + step) * LANES, LANES)
-            q = dot_nn(factors[pl.ds(at, LANES), :], residual[group])
-            behind = list(carry[group])
-            for s in reversed(range(per_block)):
-                for h in range(wide):
-                    w = planes[pl.ds(w_base[h] + at + s * ROWSUB, ROWSUB), :]
-                    alpha = planes[pl.ds(a_base[h] + at + s * ROWSUB, ROWSUB), :]
-                    d = q[s * ROWSUB : (s + 1) * ROWSUB, h * LANES : (h + 1) * LANES] - behind[h]
-                    planes[pl.ds(a_base[h] + at + s * ROWSUB, ROWSUB), :] = w * d
-                    behind[h] = behind[h] + alpha * d
-            out.append(tuple(behind))
-        return tuple(out)
-
-    zeros = jnp.zeros((ROWSUB, LANES), jnp.float32)
-    start = tuple(tuple(zeros for _ in range(wide)) for _ in range(groups))
-    lax.fori_loop(0, blocks, backward, start)
-
-    def slopes(step, carry):
+        stacked = jnp.concatenate([none, high, rest, high, rest], 0)
+        residual[group] = stacked.astype(jnp.bfloat16)
+        stacked = jnp.concatenate([none, high, rest, jnp.zeros((48, pixels), jnp.float32)], 0)
+        across[group] = stacked.T.astype(jnp.bfloat16)
+    basis_out = jnp.where(
+        lax.broadcasted_iota(jnp.int32, (LANES, pixels), 0) < 8, pixel_basis(LANES), 0.0
+    )
+    across[groups] = basis_out.T.astype(jnp.bfloat16)
+
+    def slopes(step):
+        both = [g_high[group] for group in range(groups)]
+        both += [g_rest[group] for group in range(groups)]
+        shape_sums = dot_nn(jnp.concatenate(both, 0), across[groups])
         for group in range(groups):
             block = group * blocks + step
             at = pl.multiple_of(block * LANES, LANES)
+            span = pl.ds(at, LANES)
             mask = field_mask(block)
-            g_high, g_rest = split_two(wide_block(a_base, at))
-            w_high, w_rest = split_two(wide_block(w_base, at))
-            moments = dot_nt(basis_rows, g_high) + dot_nt(basis_rows, g_rest)
-            res = residual[group, 32:80, :]
-            tone = dot_nt(res, w_high) + dot_nt(res, w_rest)
-            tone = tone[:24] + tone[24:]
+            tone_sums = dot_nn(
+                jnp.concatenate([w_high[span, :], w_rest[span, :]], 0), across[group]
+            )
+            first, second = group * LANES, (groups + group) * LANES
+            moments = (
+                shape_sums[first : first + LANES]
+                + shape_sums[second : second + LANES]
+                + tone_sums[:LANES]
+                + tone_sums[LANES:]
+            ).T
             m = [moments[i : i + 1, :] for i in range(6)]
             u, v, a, b, c = [fields[pl.ds(block * ROWSUB + f, 1), :] for f in range(5)]
             m_x = m[1] - u * m[0]
@@ -451,13 +456,37 @@
                 m[0],
             ]
             for ch in range(3):
-                part = jnp.where(own_tile, tone[ch * ROWSUB : (ch + 1) * ROWSUB, :], 0.0)
-                rows.append(jnp.sum(part, axis=0, keepdims=True))
+                low = 32 + ch * ROWSUB
+                part = moments[low : low + ROWSUB, :] + moments[low + 24 : low + 24 + ROWSUB, :]
+                rows.append(jnp.sum(jnp.where(own_tile, part, 0.0), axis=0, keepdims=True))
             placed = [jnp.where(mask, row, 0.0) for row in rows]
-            entries[pl.ds(at, LANES), :] = jnp.concatenate(placed + [pad], 0).T
-        return carry
-
-    lax.fori_loop(0, blocks, slopes, 0)
+            entries[span, :] = jnp.concatenate(placed + [pad], 0).T
+
+    def backward(index, carry):
+        step = blocks - 1 - index
+        slopes(jnp.minimum(step + 1, blocks - 1))
+        out = []
+        for group in range(groups):
+            at = pl.multiple_of((group * blocks + step) * LANES, LANES)
+            q = dot_nn(factors[pl.ds(at, LANES), :], residual[group])
+            behind = list(carry[group])
+            kept = [[] for _ in range(wide)]
+            for s in reversed(range(per_block)):
+                span = pl.ds(at + s * ROWSUB, ROWSUB)
+                for h in range(wide):
+                    w = w_planes[h][span, :]
+                    alpha = a_planes[h][span, :]
+                    d = q[s * ROWSUB : (s + 1) * ROWSUB, h * LANES : (h + 1) * LANES] - behind[h]
+                    kept[h].insert(0, w * d)
+                    behind[h] = behind[h] + alpha * d
+                if s % 2 == 0:
+                    store_split(g_high.at[group], g_rest.at[group], s * ROWSUB, kept)
+                    kept = [[] for _ in range(wide)]
+            out.append(tuple(behind))
+        return tuple(out)
+
+    lax.fori_loop(0, blocks, backward, ((zeros,) * wide,) * groups)
+    slopes(0)
 
     tall = jnp.zeros((LANES, LANES), jnp.float32)
 
@@ -470,42 +499,45 @@
     lax.fori_loop(0, devices * halves, clear, 0)
 
     def scatter(index, carry):
-        base = pl.multiple_of(index * unroll, unroll)
-        for q in range(unroll):
-            one = tables[q % len(tables)]
-            row = rows_ref[base + q]
-            one[pl.ds(row, 1), :] = one[pl.ds(row, 1), :] + entries[pl.ds(base + q, 1), :]
+        some = entries.at[pl.ds(pl.multiple_of(index * unroll, unroll), unroll)]
+        for turn in range(turns):
+            place = index * turns + turn
+            for q in range(streams):
+                one = tables[q % len(tables)]
+                row = pl.ds(row_lists[q][place], 1)
+                at = turn * streams + q
+                one[row, :] = one[row, :] + some[at : at + 1, :]
         return carry
 
     lax.fori_loop(0, total // unroll, scatter, 0)
 
     loss_rows = jnp.broadcast_to(loss, (ROWSUB, LANES))
-
-    def collect(owner, carry):
-        start = pl.multiple_of(owner * planes_out, 8)
-        for half in range(halves):
-            at = pl.multiple_of((owner * halves + half) * LANES, LANES)
-            block = tables[0][pl.ds(at, LANES), :]
-            for one in tables[1:]:
-                block = block + one[pl.ds(at, LANES), :]
-            turned = block.T
-            for f in range(FIELDS):
-                planes[pl.ds(start + f * per_owner + half * ROWSUB, ROWSUB), :] = turned[
-                    f * ROWSUB : (f + 1) * ROWSUB, :
-                ]
-        planes[pl.ds(start + planes_in, ROWSUB), :] = loss_rows
-        return carry
-
-    stores = [
-        pltpu.make_async_copy(
-            planes.at[pl.ds(i * near * planes_out, near * planes_out)], ref, out_sem.at[i]
+    stores = []
+    for side, ref, stage in ((1, grad_other, entries), (0, grad_own, w_planes[0])):
+
+        def collect(owner, carry, side=side, stage=stage):
+            start = pl.multiple_of(owner * planes_out, 8)
+            turned = []
+            for half in range(halves):
+                at = pl.multiple_of(((side * near + owner) * halves + half) * LANES, LANES)
+                block = tables[0][pl.ds(at, LANES), :]
+                for one in tables[1:]:
+                    block = block + one[pl.ds(at, LANES), :]
+                turned.append(block.T)
+            for half in range(halves):
+                for f in range(FIELDS):
+                    stage[pl.ds(start + f * per_owner + half * ROWSUB, ROWSUB), :] = turned[
+                        half
+                    ][f * ROWSUB : (f + 1) * ROWSUB, :]
+            stage[pl.ds(start + planes_in, ROWSUB), :] = loss_rows
+            return carry
+
+        lax.fori_loop(0, near, collect, 0)
+        store = pltpu.make_async_copy(
+            stage.at[pl.ds(0, near * planes_out)], ref, out_sem.at[side]
         )
-        for i, ref in enumerate((grad_own, grad_other))
-    ]
-    lax.fori_loop(near, devices, collect, 0, unroll=2)
-    stores[1].start()
-    lax.fori_loop(0, near, collect, 0, unroll=2)
-    stores[0].start()
+        store.start()
+        stores.append(store)
     for store in stores:
         store.wait()
 
@@ -571,7 +603,7 @@
             .reshape(STEPS, total)
         )
 
-    rows = interleave(rows)
+    rows = interleave(rows).reshape(STEPS, total // 16, 16).transpose(0, 2, 1)
     which = interleave(which).reshape(STEPS, total // LANES, LANES)
     middle_x = (tile_ids % IMG_TX * SIDE + SIDE // 2).astype(jnp.float32)
     middle_y = (tile_ids // IMG_TX * SIDE + SIDE // 2).astype(jnp.float32)
@@ -583,34 +615,49 @@
     vmem = pl.BlockSpec(memory_space=pltpu.VMEM)
     smem = pl.BlockSpec(memory_space=pltpu.SMEM)
     hbm = pl.BlockSpec(memory_space=pl.ANY)
-    f32 = jnp.float32
+    f32, bf16 = jnp.float32, jnp.bfloat16
     state = jax.ShapeDtypeStruct((params_rows, count), f32)
     field_shape = jax.ShapeDtypeStruct((planes_in, LANES), f32)
 
-    table_bytes = devices * count // ROWSUB * LANES * 4
-    copies = max(1, min(4, (24 << 20) // table_bytes))
+    streams = 16
+    wide = pixels // LANES
+    table_rows = devices * count // ROWSUB
+    plane_rows = max(total, devices // 2 * planes_out)
+    extra = max(0, 7 - 2 * wide) if table_rows <= plane_rows else 0
     render = pl.pallas_call(
         functools.partial(
-            render_kernel, devices=devices, per_owner=per_owner, groups=groups, depth=depth
+            render_kernel,
+            devices=devices,
+            per_owner=per_owner,
+            groups=groups,
+            depth=depth,
+            streams=streams,
         ),
         out_shape=(
             jax.ShapeDtypeStruct((tiles * 3 * pixels // LANES, LANES), f32),
             jax.ShapeDtypeStruct((devices // 2 * planes_out, LANES), f32),
             jax.ShapeDtypeStruct((devices // 2 * planes_out, LANES), f32),
         ),
-        in_specs=[smem, vmem, vmem, vmem, hbm, hbm],
+        in_specs=[hbm, vmem, vmem, vmem, hbm, hbm],
         out_specs=(vmem, hbm, hbm),
         scratch_shapes=[
-            pltpu.VMEM((max(2 * pixels // LANES * total, devices * planes_out), LANES), f32),
-            pltpu.VMEM((total, LANES), f32),
+            pltpu.VMEM((plane_rows, LANES), f32),
             pltpu.VMEM((total // LANES * ROWSUB, LANES), f32),
-            pltpu.VMEM((total, LANES), jnp.bfloat16),
-            pltpu.VMEM((groups, LANES, pixels), f32),
-            pltpu.VMEM((groups, LANES, pixels), jnp.bfloat16),
+            pltpu.VMEM((total, LANES), bf16),
+            pltpu.VMEM((groups, LANES, pixels), bf16),
+            pltpu.VMEM((groups + 1, pixels, LANES), bf16),
+            pltpu.VMEM((total, pixels), bf16),
+            pltpu.VMEM((total, pixels), bf16),
+            pltpu.VMEM((groups, LANES, pixels), bf16),
+            pltpu.VMEM((groups, LANES, pixels), bf16),
             pltpu.SemaphoreType.DMA((2,)),
             pltpu.SemaphoreType.DMA((2,)),
+            pltpu.SemaphoreType.DMA((streams,)),
         ]
-        + [pltpu.VMEM((devices * count // ROWSUB, LANES), f32)] * copies,
+        + [pltpu.SMEM((total // streams,), jnp.int32)] * streams
+        + [pltpu.VMEM((table_rows, LANES), f32)]
+        + [pltpu.VMEM((plane_rows, LANES), f32)] * (2 * wide)
+        + [pltpu.VMEM((table_rows, LANES), f32)] * extra,
         compiler_params=pltpu.CompilerParams(vmem_limit_bytes=60 << 20),
         name="render",
     )

time: 298 us -> 258 us (0.87)
  Pallas kernels: 149 us -> 110 us
  local copies, waits for them, and re-layouts: 14.6 us -> 10.6 us
    pallas_call x2, Pallas kernels: 140 us -> 102 us  [per_device(): render(rows[step], which[step], middle[step], target_rows[step], near, far)]
  transfers between devices with their start and end apart: 20 -> 20, of which waited for: 18 -> 19; matrix products, arithmetic and copies ran while one was open for 4% -> 4% of each run, Pallas kernels for 0% -> 0%
where the time goes in v3:
time: 258 us; the launch traced here: 257 us
  Pallas kernels  110 us (43%)
  waiting for transfers between devices  85.2 us (33%)
  starting transfers between devices  38.6 us (15%)
  other arithmetic  11.4 us (4%)
  local copies, waits for them, and re-layouts  10.6 us (4%)
    pallas_call x2, Pallas kernels, per_device(): render(rows[step], which[step], middle[step], target_rows[step], near, far)  102 us
    ppermute x20, waiting for transfers between devices, swap(): return lax.ppermute(values, AXES, pairs)  85.2 us
    ppermute x20, starting transfers between devices, swap(): return lax.ppermute(values, AXES, pairs)  38.6 us
    pallas_call x2, Pallas kernels, per_device(): pl.pallas_call(functools.partial(update_kernel, step=step, project_next=m...  6.81 us
    concatenate x6, other arithmetic, spread(): values = jnp.concatenate([values, swap(values, devices, flips)], 0)  5.44 us
  transfers between devices with their start and end apart: 20, of which 19 were waited for; matrix products, arithmetic and copies ran while one was open for 4% of the time, Pallas kernels for 0%

profile of v3, /device:TPU:0, one launch (start us, length us, event | category | flops | bytes accessed | tf_op | source)
XLA Modules:
  0.0 257.2 jit_solution(2626146013974689148)
XLA Ops:
  0.6 1.9 project.1
  2.6 4.1 %collective-permute-start = (f32[144,128]{1,0:T(8,128)}, f32[144,128]{1,0:T(8,128)S(1)}, u32[]{:S(2)}, u32[]{:S(2)}) collective-permute-start(f32[144,128]{1,0:T(8,128)} %project.1), channel_id=1, source_target_pairs={{0,16},{1,9},{2,18},{3,11},{4,20},{5,13},{6,22},{7,15},{8,24},{9,1... | collective-permute-start | bytes 221192 | tf_op jit(solution)/shard_map/ppermute | solution.py:555
  6.7 2.6 %collective-permute-done = f32[144,128]{1,0:T(8,128)S(1)} collective-permute-done((f32[144,128]{1,0:T(8,128)}, f32[144,128]{1,0:T(8,128)S(1)}, u32[]{:S(2)}, u32[]{:S(2)}) %collective-permute-start) | collective-permute-done | bytes 73760 | tf_op jit(solution)/shard_map/ppermute | solution.py:555
  10.2 1.9 collective-permute-start.1
  12.1 3.7 %collective-permute-done.1 = f32[288,128]{1,0:T(8,128)S(1)} collective-permute-done((f32[288,128]{1,0:T(8,128)S(1)}, f32[288,128]{1,0:T(8,128)S(1)}, u32[]{:S(2)}, u32[]{:S(2)}) %collective-permute-start.1) | collective-permute-done | bytes 147488 | tf_op jit(solution)/shard_map/ppermute | solution.py:555
  18.6 4.9 %collective-permute-done.2 = f32[576,128]{1,0:T(8,128)S(1)} collective-permute-done((f32[576,128]{1,0:T(8,128)S(1)}, f32[576,128]{1,0:T(8,128)S(1)}, u32[]{:S(2)}, u32[]{:S(2)}) %collective-permute-start.2) | collective-permute-done | bytes 294944 | tf_op jit(solution)/shard_map/ppermute | solution.py:555
  24.4 1.9 collective-permute-start.3
  26.6 7.8 %collective-permute-done.3 = f32[1152,128]{1,0:T(8,128)S(1)} collective-permute-done((f32[1152,128]{1,0:T(8,128)S(1)}, f32[1152,128]{1,0:T(8,128)S(1)}, u32[]{:S(2)}, u32[]{:S(2)}) %collective-permute-start.3) | collective-permute-done | bytes 589856 | tf_op jit(solution)/shard_map/ppermute | solution.py:555
  39.0 50.8 %render.2 = (f32[96,128]{1,0:T(8,128)}, f32[2432,128]{1,0:T(8,128)}, f32[2432,128]{1,0:T(8,128)}) custom-call(s32[16,512]{1,0:T(8,128)} %get-tuple-element.41.rows_ref, s32[64,128]{1,0:T(8,128)} %squeeze.21.group_ref, f32[4,128]{1,0:T(4,128)} %tile.13.middle_ref, f32[96,128]{1,0:T(8,128)} %squeeze.22.target_ref, f32[2304,128]{1,0:T(8,128)} %copy-done.1, ...), custom_call_target="tpu_custom_call" | custom-call | tf_op jit(solution)/shard_map/render/pallas_call | solution.py:677
  90.1 2.8 %collective-permute-done.5 = f32[2432,128]{1,0:T(8,128)S(1)} collective-permute-done((f32[2432,128]{1,0:T(8,128)}, f32[2432,128]{1,0:T(8,128)S(1)}, u32[]{:S(2)}, u32[]{:S(2)}) %collective-permute-start.5) | collective-permute-done | bytes 1245216 | tf_op jit(solution)/shard_map/ppermute | solution.py:555
  94.4 1.9 collective-permute-start.6
  96.3 8.4 %collective-permute-done.6 = f32[1216,128]{1,0:T(8,128)S(1)} collective-permute-done((f32[1216,128]{1,0:T(8,128)S(1)}, f32[1216,128]{1,0:T(8,128)S(1)}, u32[]{:S(2)}, u32[]{:S(2)}) %collective-permute-start.6) | collective-permute-done | bytes 622624 | tf_op jit(solution)/shard_map/ppermute | solution.py:555
  106.7 5.1 %collective-permute-done.7 = f32[608,128]{1,0:T(8,128)S(1)} collective-permute-done((f32[608,128]{1,0:T(8,128)S(1)}, f32[608,128]{1,0:T(8,128)S(1)}, u32[]{:S(2)}, u32[]{:S(2)}) %collective-permute-start.7) | collective-permute-done | bytes 311328 | tf_op jit(solution)/shard_map/ppermute | solution.py:555
  113.4 4.0 %collective-permute-done.8 = f32[304,128]{1,0:T(8,128)S(1)} collective-permute-done((f32[304,128]{1,0:T(8,128)S(1)}, f32[304,128]{1,0:T(8,128)S(1)}, u32[]{:S(2)}, u32[]{:S(2)}) %collective-permute-start.8) | collective-permute-done | bytes 155680 | tf_op jit(solution)/shard_map/ppermute | solution.py:555
  117.4 3.3 %collective-permute-start.9 = (f32[152,128]{1,0:T(8,128)S(1)}, f32[152,128]{1,0:T(8,128)S(1)}, u32[]{:S(2)}, u32[]{:S(2)}) collective-permute-start(f32[152,128]{1,0:T(8,128)S(1)} %slice.130), channel_id=1, source_target_pairs={{0,16},{1,9},{2,18},{3,11},{4,20},{5,13},{6,22},{7,15},{8,24},{9,1... | collective-permute-start | bytes 233480 | tf_op jit(solution)/shard_map/ppermute | solution.py:555
  120.8 2.4 collective-permute-done.9
  123.8 3.5 %update.2 = (f32[55,2048]{1,0:T(8,128)}, f32[55,2048]{1,0:T(8,128)}, f32[55,2048]{1,0:T(8,128)}, f32[144,128]{1,0:T(8,128)}) custom-call(f32[2,2]{1,0:T(2,128)} %cam_ref.5, f32[55,2048]{1,0:T(8,128)} %param_ref.3, f32[55,2048]{1,0:T(8,128)} %first_ref.1, f32[55,2048]{1,0:T(8,128)} %second_ref.1, f32[152,128]{1,0:T(8,128)} %slice_add_fusion.7.grad_ref), custom_call_target="tpu_custom_call" | custom-call | tf_op jit(solution)/shard_map/update/pallas_call | solution.py:684
  127.3 2.9 %collective-permute-start.10 = (f32[144,128]{1,0:T(8,128)}, f32[144,128]{1,0:T(8,128)S(1)}, u32[]{:S(2)}, u32[]{:S(2)}) collective-permute-start(f32[144,128]{1,0:T(8,128)} %get-tuple-element.23), channel_id=1, source_target_pairs={{0,16},{1,9},{2,18},{3,11},{4,20},{5,13},{6,22},{7,15},{8,24},{9,1... | collective-permute-start | bytes 221192 | tf_op jit(solution)/shard_map/ppermute | solution.py:555
  130.2 2.6 %collective-permute-done.10 = f32[144,128]{1,0:T(8,128)S(1)} collective-permute-done((f32[144,128]{1,0:T(8,128)}, f32[144,128]{1,0:T(8,128)S(1)}, u32[]{:S(2)}, u32[]{:S(2)}) %collective-permute-start.10) | collective-permute-done | bytes 73760 | tf_op jit(solution)/shard_map/ppermute | solution.py:555
  133.8 4.3 %collective-permute-start.11 = (f32[288,128]{1,0:T(8,128)S(1)}, f32[288,128]{1,0:T(8,128)S(1)}, u32[]{:S(2)}, u32[]{:S(2)}) collective-permute-start(f32[288,128]{1,0:T(8,128)S(1)} %pad_maximum_fusion.5), channel_id=1, source_target_pairs={{0,8},{1,17},{2,10},{3,19},{4,12},{5,21},{6,14},{7,23},{8,0},{9,25... | collective-permute-start | bytes 442376 | tf_op jit(solution)/shard_map/ppermute | solution.py:555
  138.0 3.1 %collective-permute-done.11 = f32[288,128]{1,0:T(8,128)S(1)} collective-permute-done((f32[288,128]{1,0:T(8,128)S(1)}, f32[288,128]{1,0:T(8,128)S(1)}, u32[]{:S(2)}, u32[]{:S(2)}) %collective-permute-start.11) | collective-permute-done | bytes 147488 | tf_op jit(solution)/shard_map/ppermute | solution.py:555
  143.6 7.3 %collective-permute-done.12 = f32[576,128]{1,0:T(8,128)S(1)} collective-permute-done((f32[576,128]{1,0:T(8,128)S(1)}, f32[576,128]{1,0:T(8,128)S(1)}, u32[]{:S(2)}, u32[]{:S(2)}) %collective-permute-start.12) | collective-permute-done | bytes 294944 | tf_op jit(solution)/shard_map/ppermute | solution.py:555
  153.4 8.4 %collective-permute-done.13 = f32[1152,128]{1,0:T(8,128)S(1)} collective-permute-done((f32[1152,128]{1,0:T(8,128)S(1)}, f32[1152,128]{1,0:T(8,128)S(1)}, u32[]{:S(2)}, u32[]{:S(2)}) %collective-permute-start.13) | collective-permute-done | bytes 589856 | tf_op jit(solution)/shard_map/ppermute | solution.py:555
  165.8 50.8 %render.3 = (f32[96,128]{1,0:T(8,128)}, f32[2432,128]{1,0:T(8,128)}, f32[2432,128]{1,0:T(8,128)}) custom-call(s32[16,512]{1,0:T(8,128)} %get-tuple-element.40.rows_ref, s32[64,128]{1,0:T(8,128)} %squeeze.24.group_ref, f32[4,128]{1,0:T(4,128)} %tile.15.middle_ref, f32[96,128]{1,0:T(8,128)} %squeeze.25.target_ref, f32[2304,128]{1,0:T(8,128)} %copy-done.2, ...), custom_call_target="tpu_custom_call" | custom-call | tf_op jit(solution)/shard_map/render/pallas_call | solution.py:677
  216.8 3.0 %collective-permute-done.15 = f32[2432,128]{1,0:T(8,128)S(1)} collective-permute-done((f32[2432,128]{1,0:T(8,128)}, f32[2432,128]{1,0:T(8,128)S(1)}, u32[]{:S(2)}, u32[]{:S(2)}) %collective-permute-start.15) | collective-permute-done | bytes 1245216 | tf_op jit(solution)/shard_map/ppermute | solution.py:555
  222.7 8.8 %collective-permute-done.16 = f32[1216,128]{1,0:T(8,128)S(1)} collective-permute-done((f32[1216,128]{1,0:T(8,128)S(1)}, f32[1216,128]{1,0:T(8,128)S(1)}, u32[]{:S(2)}, u32[]{:S(2)}) %collective-permute-start.16) | collective-permute-done | bytes 622624 | tf_op jit(solution)/shard_map/ppermute | solution.py:555
  233.3 5.4 %collective-permute-done.17 = f32[608,128]{1,0:T(8,128)S(1)} collective-permute-done((f32[608,128]{1,0:T(8,128)S(1)}, f32[608,128]{1,0:T(8,128)S(1)}, u32[]{:S(2)}, u32[]{:S(2)}) %collective-permute-start.17) | collective-permute-done | bytes 311328 | tf_op jit(solution)/shard_map/ppermute | solution.py:555
  238.8 2.9 %collective-permute-start.18 = (f32[304,128]{1,0:T(8,128)S(1)}, f32[304,128]{1,0:T(8,128)S(1)}, u32[]{:S(2)}, u32[]{:S(2)}) collective-permute-start(f32[304,128]{1,0:T(8,128)S(1)} %slice.139), channel_id=1, source_target_pairs={{0,8},{1,17},{2,10},{3,19},{4,12},{5,21},{6,14},{7,23},{8,0},{9,25... | collective-permute-start | bytes 466952 | tf_op jit(solution)/shard_map/ppermute | solution.py:555
  242.9 2.7 %collective-permute-done.18 = f32[304,128]{1,0:T(8,128)S(1)} collective-permute-done((f32[304,128]{1,0:T(8,128)S(1)}, f32[304,128]{1,0:T(8,128)S(1)}, u32[]{:S(2)}, u32[]{:S(2)}) %collective-permute-start.18) | collective-permute-done | bytes 155680 | tf_op jit(solution)/shard_map/ppermute | solution.py:555
  245.7 3.4 %collective-permute-start.19 = (f32[152,128]{1,0:T(8,128)S(1)}, f32[152,128]{1,0:T(8,128)S(1)}, u32[]{:S(2)}, u32[]{:S(2)}) collective-permute-start(f32[152,128]{1,0:T(8,128)S(1)} %slice.141), channel_id=1, source_target_pairs={{0,16},{1,9},{2,18},{3,11},{4,20},{5,13},{6,22},{7,15},{8,24},{9,1... | collective-permute-start | bytes 233480 | tf_op jit(solution)/shard_map/ppermute | solution.py:555
  252.0 1.9 maximum_multiply_fusion
  253.9 3.3 %update.3 = (f32[55,2048]{1,0:T(8,128)}, f32[55,2048]{1,0:T(8,128)}, f32[55,2048]{1,0:T(8,128)}) custom-call(f32[2,2]{1,0:T(2,128)} %cam_ref.5, f32[55,2048]{1,0:T(8,128)} %get-tuple-element.20.param_ref, f32[55,2048]{1,0:T(8,128)} %get-tuple-element.21.first_ref, f32[55,2048]{1,0:T(8,128)} %get-tuple-element.22.second_ref, f32[152,128]{1,0:T(8,128)} %copy-done.5), custom_call_target="tpu_custom_call" | custom-call | tf_op jit(solution)/shard_map/update/pallas_call | solution.py:684
  (101 shorter events, 34.2 us)
Async XLA Ops:
  0.6 25.7 %copy-start.10 = (s32[2,16]{1,0:T(2,128)S(1)}, s32[2,16]{1,0:T(2,128)}, u32[]{:S(2)}) copy-start(s32[2,16]{1,0:T(2,128)} %param.11) | copy-start | bytes 388
  2.6 23.9 %copy-start = (f32[144,128]{1,0:T(8,128)S(1)}, f32[144,128]{1,0:T(8,128)}, u32[]{:S(2)}) copy-start(f32[144,128]{1,0:T(8,128)} %project.1) | copy-start | bytes 221188
  2.6 6.7 %collective-permute-start = (f32[144,128]{1,0:T(8,128)}, f32[144,128]{1,0:T(8,128)S(1)}, u32[]{:S(2)}, u32[]{:S(2)}) collective-permute-start(f32[144,128]{1,0:T(8,128)} %project.1), channel_id=1, source_target_pairs={{0,16},{1,9},{2,18},{3,11},{4,20},{5,13},{6,22},{7,15},{8,24},{9,1... | collective-permute-start | bytes 221192 | tf_op jit(solution)/shard_map/ppermute | solution.py:555
  10.2 5.6 %collective-permute-start.1 = (f32[288,128]{1,0:T(8,128)S(1)}, f32[288,128]{1,0:T(8,128)S(1)}, u32[]{:S(2)}, u32[]{:S(2)}) collective-permute-start(f32[288,128]{1,0:T(8,128)S(1)} %pad_maximum_fusion.4), channel_id=1, source_target_pairs={{0,8},{1,17},{2,10},{3,19},{4,12},{5,21},{6,14},{7,23},{8,0},{9,25... | collective-permute-start | bytes 442376 | tf_op jit(solution)/shard_map/ppermute | solution.py:555
  16.7 6.8 %collective-permute-start.2 = (f32[576,128]{1,0:T(8,128)S(1)}, f32[576,128]{1,0:T(8,128)S(1)}, u32[]{:S(2)}, u32[]{:S(2)}) collective-permute-start(f32[576,128]{1,0:T(8,128)S(1)} %pad_maximum_fusion.2), channel_id=1, source_target_pairs={{0,2},{1,5},{2,0},{3,7},{4,6},{5,1},{6,4},{7,3},{8,10},{9,13},{10,... | collective-permute-start | bytes 884744 | tf_op jit(solution)/shard_map/ppermute | solution.py:555
  24.4 9.9 %collective-permute-start.3 = (f32[1152,128]{1,0:T(8,128)S(1)}, f32[1152,128]{1,0:T(8,128)S(1)}, u32[]{:S(2)}, u32[]{:S(2)}) collective-permute-start(f32[1152,128]{1,0:T(8,128)S(1)} %pad_maximum_fusion), channel_id=1, source_target_pairs={{0,4},{1,3},{2,6},{3,1},{4,0},{5,7},{6,2},{7,5},{8,12},{9,11},{10,... | collective-permute-start | bytes 1769480 | tf_op jit(solution)/shard_map/ppermute | solution.py:555
  26.5 8.9 %copy-start.6 = (f32[2,16,3,256]{3,1,2,0:T(8,128)S(1)}, f32[2,16,3,256]{3,1,2,0:T(8,128)}, u32[]{:S(2)}) copy-start(f32[2,16,3,256]{3,1,2,0:T(8,128)} %param.12) | copy-start | bytes 294916
  26.5 9.6 %copy-start.7 = (s32[2,16,512]{2,1,0:T(8,128)S(1)}, s32[2,16,512]{2,1,0:T(8,128)}, u32[]{:S(2)}) copy-start(s32[2,16,512]{2,1,0:T(8,128)} %param.10) | copy-start | bytes 196612
  34.4 2.3 copy-start.1
  34.4 4.6 %collective-permute-start.4 = (f32[2304,128]{1,0:T(8,128)S(1)}, f32[2304,128]{1,0:T(8,128)}, u32[]{:S(2)}, u32[]{:S(2)}) collective-permute-start(f32[2304,128]{1,0:T(8,128)S(1)} %constant_dynamic-update-slice_fusion.table_own), channel_id=1, source_target_pairs={{0,1},{1,0},{2,3},{3,2},{4,5},{5,4},{6,7},{7,6},{8,9},{9,8},{10,11... | collective-permute-start | bytes 3538952 | tf_op jit(solution)/shard_map/ppermute | solution.py:555
  89.8 3.2 %collective-permute-start.5 = (f32[2432,128]{1,0:T(8,128)}, f32[2432,128]{1,0:T(8,128)S(1)}, u32[]{:S(2)}, u32[]{:S(2)}) collective-permute-start(f32[2432,128]{1,0:T(8,128)} %get-tuple-element.19), channel_id=1, source_target_pairs={{0,1},{1,0},{2,3},{3,2},{4,5},{5,4},{6,7},{7,6},{8,9},{9,8},{10,11... | collective-permute-start | bytes 3735560 | tf_op jit(solution)/shard_map/ppermute | solution.py:555
  94.4 10.3 %collective-permute-start.6 = (f32[1216,128]{1,0:T(8,128)S(1)}, f32[1216,128]{1,0:T(8,128)S(1)}, u32[]{:S(2)}, u32[]{:S(2)}) collective-permute-start(f32[1216,128]{1,0:T(8,128)S(1)} %slice.124), channel_id=1, source_target_pairs={{0,4},{1,3},{2,6},{3,1},{4,0},{5,7},{6,2},{7,5},{8,12},{9,11},{10,... | collective-permute-start | bytes 1867784 | tf_op jit(solution)/shard_map/ppermute | solution.py:555
  104.9 7.0 %collective-permute-start.7 = (f32[608,128]{1,0:T(8,128)S(1)}, f32[608,128]{1,0:T(8,128)S(1)}, u32[]{:S(2)}, u32[]{:S(2)}) collective-permute-start(f32[608,128]{1,0:T(8,128)S(1)} %slice.126), channel_id=1, source_target_pairs={{0,2},{1,5},{2,0},{3,7},{4,6},{5,1},{6,4},{7,3},{8,10},{9,13},{10,... | collective-permute-start | bytes 933896 | tf_op jit(solution)/shard_map/ppermute | solution.py:555
  111.9 5.5 %collective-permute-start.8 = (f32[304,128]{1,0:T(8,128)S(1)}, f32[304,128]{1,0:T(8,128)S(1)}, u32[]{:S(2)}, u32[]{:S(2)}) collective-permute-start(f32[304,128]{1,0:T(8,128)S(1)} %slice.128), channel_id=1, source_target_pairs={{0,8},{1,17},{2,10},{3,19},{4,12},{5,21},{6,14},{7,23},{8,0},{9,25... | collective-permute-start | bytes 466952 | tf_op jit(solution)/shard_map/ppermute | solution.py:555
  117.4 5.7 %collective-permute-start.9 = (f32[152,128]{1,0:T(8,128)S(1)}, f32[152,128]{1,0:T(8,128)S(1)}, u32[]{:S(2)}, u32[]{:S(2)}) collective-permute-start(f32[152,128]{1,0:T(8,128)S(1)} %slice.130), channel_id=1, source_target_pairs={{0,16},{1,9},{2,18},{3,11},{4,20},{5,13},{6,22},{7,15},{8,24},{9,1... | collective-permute-start | bytes 233480 | tf_op jit(solution)/shard_map/ppermute | solution.py:555
  127.3 26.0 %copy-start.3 = (f32[144,128]{1,0:T(8,128)S(1)}, f32[144,128]{1,0:T(8,128)}, u32[]{:S(2)}) copy-start(f32[144,128]{1,0:T(8,128)} %get-tuple-element.23) | copy-start | bytes 221188
  127.3 5.5 %collective-permute-start.10 = (f32[144,128]{1,0:T(8,128)}, f32[144,128]{1,0:T(8,128)S(1)}, u32[]{:S(2)}, u32[]{:S(2)}) collective-permute-start(f32[144,128]{1,0:T(8,128)} %get-tuple-element.23), channel_id=1, source_target_pairs={{0,16},{1,9},{2,18},{3,11},{4,20},{5,13},{6,22},{7,15},{8,24},{9,1... | collective-permute-start | bytes 221192 | tf_op jit(solution)/shard_map/ppermute | solution.py:555
  133.8 7.4 %collective-permute-start.11 = (f32[288,128]{1,0:T(8,128)S(1)}, f32[288,128]{1,0:T(8,128)S(1)}, u32[]{:S(2)}, u32[]{:S(2)}) collective-permute-start(f32[288,128]{1,0:T(8,128)S(1)} %pad_maximum_fusion.5), channel_id=1, source_target_pairs={{0,8},{1,17},{2,10},{3,19},{4,12},{5,21},{6,14},{7,23},{8,0},{9,25... | collective-permute-start | bytes 442376 | tf_op jit(solution)/shard_map/ppermute | solution.py:555
  142.1 8.9 %collective-permute-start.12 = (f32[576,128]{1,0:T(8,128)S(1)}, f32[576,128]{1,0:T(8,128)S(1)}, u32[]{:S(2)}, u32[]{:S(2)}) collective-permute-start(f32[576,128]{1,0:T(8,128)S(1)} %pad_maximum_fusion.3), channel_id=1, source_target_pairs={{0,2},{1,5},{2,0},{3,7},{4,6},{5,1},{6,4},{7,3},{8,10},{9,13},{10,... | collective-permute-start | bytes 884744 | tf_op jit(solution)/shard_map/ppermute | solution.py:555
  151.9 9.9 %collective-permute-start.13 = (f32[1152,128]{1,0:T(8,128)S(1)}, f32[1152,128]{1,0:T(8,128)S(1)}, u32[]{:S(2)}, u32[]{:S(2)}) collective-permute-start(f32[1152,128]{1,0:T(8,128)S(1)} %pad_maximum_fusion.1), channel_id=1, source_target_pairs={{0,4},{1,3},{2,6},{3,1},{4,0},{5,7},{6,2},{7,5},{8,12},{9,11},{10,... | collective-permute-start | bytes 1769480 | tf_op jit(solution)/shard_map/ppermute | solution.py:555
  161.9 2.9 %copy-start.2 = (f32[2304,128]{1,0:T(8,128)}, f32[2304,128]{1,0:T(8,128)S(1)}, u32[]{:S(2)}) copy-start(f32[2304,128]{1,0:T(8,128)S(1)} %constant_dynamic-update-slice_fusion.5.table_own) | copy-start | bytes 3538948
  161.9 2.9 %collective-permute-start.14 = (f32[2304,128]{1,0:T(8,128)S(1)}, f32[2304,128]{1,0:T(8,128)S(1)}, u32[]{:S(2)}, u32[]{:S(2)}) collective-permute-start(f32[2304,128]{1,0:T(8,128)S(1)} %constant_dynamic-update-slice_fusion.5.table_own), channel_id=1, source_target_pairs={{0,1},{1,0},{2,3},{3,2},{4,5},{5,4},{6,7},{7,6},{8,9},{9,8},{10,11... | collective-permute-start | bytes 3538952 | tf_op jit(solution)/shard_map/ppermute | solution.py:555
  164.8 1.0 copy-start.4
  216.6 3.2 %collective-permute-start.15 = (f32[2432,128]{1,0:T(8,128)}, f32[2432,128]{1,0:T(8,128)S(1)}, u32[]{:S(2)}, u32[]{:S(2)}) collective-permute-start(f32[2432,128]{1,0:T(8,128)} %get-tuple-element.25), channel_id=1, source_target_pairs={{0,1},{1,0},{2,3},{3,2},{4,5},{5,4},{6,7},{7,6},{8,9},{9,8},{10,11... | collective-permute-start | bytes 3735560 | tf_op jit(solution)/shard_map/ppermute | solution.py:555
  221.3 10.3 %collective-permute-start.16 = (f32[1216,128]{1,0:T(8,128)S(1)}, f32[1216,128]{1,0:T(8,128)S(1)}, u32[]{:S(2)}, u32[]{:S(2)}) collective-permute-start(f32[1216,128]{1,0:T(8,128)S(1)} %slice.135), channel_id=1, source_target_pairs={{0,4},{1,3},{2,6},{3,1},{4,0},{5,7},{6,2},{7,5},{8,12},{9,11},{10,... | collective-permute-start | bytes 1867784 | tf_op jit(solution)/shard_map/ppermute | solution.py:555
  231.7 10.0 %copy-start.8 = (f32[96,128]{1,0:T(8,128)S(1)}, f32[96,128]{1,0:T(8,128)}, u32[]{:S(2)}) copy-start(f32[96,128]{1,0:T(8,128)} %get-tuple-element.29) | copy-start | bytes 147460
  231.7 11.2 %copy-start.9 = (f32[96,128]{1,0:T(8,128)S(1)}, f32[96,128]{1,0:T(8,128)}, u32[]{:S(2)}) copy-start(f32[96,128]{1,0:T(8,128)} %get-tuple-element.30) | copy-start | bytes 147460
  231.7 7.0 %collective-permute-start.17 = (f32[608,128]{1,0:T(8,128)S(1)}, f32[608,128]{1,0:T(8,128)S(1)}, u32[]{:S(2)}, u32[]{:S(2)}) collective-permute-start(f32[608,128]{1,0:T(8,128)S(1)} %slice.137), channel_id=1, source_target_pairs={{0,2},{1,5},{2,0},{3,7},{4,6},{5,1},{6,4},{7,3},{8,10},{9,13},{10,... | collective-permute-start | bytes 933896 | tf_op jit(solution)/shard_map/ppermute | solution.py:555
  238.8 6.9 %collective-permute-start.18 = (f32[304,128]{1,0:T(8,128)S(1)}, f32[304,128]{1,0:T(8,128)S(1)}, u32[]{:S(2)}, u32[]{:S(2)}) collective-permute-start(f32[304,128]{1,0:T(8,128)S(1)} %slice.139), channel_id=1, source_target_pairs={{0,8},{1,17},{2,10},{3,19},{4,12},{5,21},{6,14},{7,23},{8,0},{9,25... | collective-permute-start | bytes 466952 | tf_op jit(solution)/shard_map/ppermute | solution.py:555
  245.7 5.8 %collective-permute-start.19 = (f32[152,128]{1,0:T(8,128)S(1)}, f32[152,128]{1,0:T(8,128)S(1)}, u32[]{:S(2)}, u32[]{:S(2)}) collective-permute-start(f32[152,128]{1,0:T(8,128)S(1)} %slice.141), channel_id=1, source_target_pairs={{0,16},{1,9},{2,18},{3,11},{4,20},{5,13},{6,22},{7,15},{8,24},{9,1... | collective-permute-start | bytes 233480 | tf_op jit(solution)/shard_map/ppermute | solution.py:555
  251.5 2.4 copy-start.5

commit v4 on v3

--- a/solution.py
+++ b/solution.py
@@ -16,6 +16,7 @@
 FIELDS = 9
 LANES = 128
 ROWSUB = 8
+PARTS = 8
 AXES = ("gx", "gy")
 
 beta_one = 0.9
@@ -160,12 +161,15 @@
 
 
 def update_kernel(
-    cam_ref, param_ref, first_ref, second_ref, grad_ref, *refs, step, project_next
+    cam_ref, param_ref, first_ref, second_ref, grad_ref, *refs, step, project_next, pixel_count
 ):
     if project_next:
         new_param, new_first, new_second, field_ref, full_ref = refs
     else:
-        new_param, new_first, new_second, full_ref = refs
+        before, (new_param, new_first, new_second, loss_ref, full_ref) = refs[:step], refs[step:]
+        tail = grad_ref.shape[0] - ROWSUB
+        for i, one in enumerate(before + (grad_ref,)):
+            loss_ref[i] = jnp.max(one[tail : tail + 1, :]) / pixel_count
     gradient_to(param_ref, cam_ref[step, 0], cam_ref[step, 1], grad_ref, full_ref)
     step_count = adam_start + step + 1
     gradient = full_ref[...]
@@ -209,30 +213,33 @@
     group_ref,
     middle_ref,
     target_ref,
-    table_own,
-    table_other,
-    picture_ref,
-    grad_own,
-    grad_other,
-    entries,
-    fields,
-    factors,
-    residual,
-    across,
-    w_high,
-    w_rest,
-    g_high,
-    g_rest,
-    in_sem,
-    out_sem,
-    row_sem,
-    *scratch,
+    *refs,
     devices,
     per_owner,
     groups,
     depth,
     streams,
+    step_index,
 ):
+    table_parts, refs = refs[:PARTS], refs[PARTS:]
+    picture_ref, refs = refs[0], refs[1:]
+    grad_parts, refs = refs[:PARTS], refs[PARTS:]
+    (
+        entries,
+        fields,
+        factors,
+        residual,
+        across,
+        w_high,
+        w_rest,
+        g_high,
+        g_rest,
+        sums,
+        in_sem,
+        out_sem,
+        row_sem,
+        *scratch,
+    ) = refs
     planes_in = FIELDS * per_owner
     planes_out = planes_in + ROWSUB
     halves = per_owner // ROWSUB
@@ -244,16 +251,22 @@
     pixels = SIDE * SIDE
     wide = pixels // LANES
     near = devices // 2
+    quarter = PARTS // 2
+    part = near // quarter
     w_planes = scratch[1 : 1 + wide]
     a_planes = scratch[1 + wide : 1 + 2 * wide]
     tables = [one for one in scratch if one.shape[0] >= devices * halves * LANES]
 
     loads = [
-        pltpu.make_async_copy(ref, stage.at[pl.ds(0, near * planes_in)], in_sem.at[i])
-        for i, (ref, stage) in enumerate(zip((table_own, table_other), w_planes))
+        pltpu.make_async_copy(
+            ref,
+            w_planes[i // quarter].at[pl.ds(i % quarter * part * planes_in, part * planes_in)],
+            in_sem.at[i],
+        )
+        for i, ref in enumerate(table_parts)
     ]
     lists = [
-        pltpu.make_async_copy(rows_ref.at[i], one, row_sem.at[i])
+        pltpu.make_async_copy(rows_ref.at[step_index, i], one, row_sem.at[i])
         for i, one in enumerate(row_lists)
     ]
     for copy in loads + lists:
@@ -262,7 +275,8 @@
     pad = jnp.zeros((LANES - FIELDS * ROWSUB, LANES), jnp.float32)
 
     for side in range(2):
-        loads[side].wait()
+        for load in loads[side * quarter : (side + 1) * quarter]:
+            load.wait()
         stage = w_planes[side]
 
         def build(owner, carry, stage=stage, side=side):
@@ -308,7 +322,7 @@
     colour_in = colour_in.astype(jnp.bfloat16)
 
     def field_mask(block):
-        return sub == group_ref[pl.ds(block, 1), :]
+        return sub == group_ref[step_index, pl.ds(block, 1), :]
 
     def prepare(block, group):
         at = pl.multiple_of(block * LANES, LANES)
@@ -318,8 +332,8 @@
         for f in range(FIELDS):
             part = jnp.where(mask, raw[f * ROWSUB : (f + 1) * ROWSUB, :], 0.0)
             rows.append(jnp.sum(part, axis=0, keepdims=True))
-        u = rows[0] - middle_ref[2 * group : 2 * group + 1, :]
-        v = rows[1] - middle_ref[2 * group + 1 : 2 * group + 2, :]
+        u = rows[0] - middle_ref[step_index, 2 * group : 2 * group + 1, :]
+        v = rows[1] - middle_ref[step_index, 2 * group + 1 : 2 * group + 2, :]
         rows[0], rows[1] = u, v
         a, b, c = rows[2], rows[3], rows[4]
         for f in range(5):
@@ -403,9 +417,9 @@
             pair = []
             for h in range(wide):
                 where = pl.ds((group * ROWSUB * 3 + ch) * wide + h, ROWSUB, stride=3 * wide)
-                part = done[group][1][ch][h]
-                picture_ref[where, :] = part
-                pair.append(part - target_ref[where, :])
+                shade = done[group][1][ch][h]
+                picture_ref[where, :] = shade
+                pair.append(shade - target_ref[step_index, where, :])
             parts.append(jnp.concatenate(pair, 1))
         left = jnp.concatenate(parts, 0)
         square = left * left
@@ -424,26 +438,29 @@
     )
     across[groups] = basis_out.T.astype(jnp.bfloat16)
 
-    def slopes(step):
+    def sum_slopes(step):
         both = [g_high[group] for group in range(groups)]
         both += [g_rest[group] for group in range(groups)]
         shape_sums = dot_nn(jnp.concatenate(both, 0), across[groups])
         for group in range(groups):
-            block = group * blocks + step
-            at = pl.multiple_of(block * LANES, LANES)
-            span = pl.ds(at, LANES)
-            mask = field_mask(block)
+            span = pl.ds(pl.multiple_of((group * blocks + step) * LANES, LANES), LANES)
             tone_sums = dot_nn(
                 jnp.concatenate([w_high[span, :], w_rest[span, :]], 0), across[group]
             )
             first, second = group * LANES, (groups + group) * LANES
-            moments = (
+            sums[group] = (
                 shape_sums[first : first + LANES]
                 + shape_sums[second : second + LANES]
                 + tone_sums[:LANES]
                 + tone_sums[LANES:]
             ).T
-            m = [moments[i : i + 1, :] for i in range(6)]
+
+    def place_slopes(step):
+        for group in range(groups):
+            block = group * blocks + step
+            span = pl.ds(pl.multiple_of(block * LANES, LANES), LANES)
+            mask = field_mask(block)
+            m = [sums[group, i : i + 1, :] for i in range(6)]
             u, v, a, b, c = [fields[pl.ds(block * ROWSUB + f, 1), :] for f in range(5)]
             m_x = m[1] - u * m[0]
             m_y = m[2] - v * m[0]
@@ -457,14 +474,18 @@
             ]
             for ch in range(3):
                 low = 32 + ch * ROWSUB
-                part = moments[low : low + ROWSUB, :] + moments[low + 24 : low + 24 + ROWSUB, :]
-                rows.append(jnp.sum(jnp.where(own_tile, part, 0.0), axis=0, keepdims=True))
+                tint = (
+                    sums[group, low : low + ROWSUB, :]
+                    + sums[group, low + 24 : low + 24 + ROWSUB, :]
+                )
+                rows.append(jnp.sum(jnp.where(own_tile, tint, 0.0), axis=0, keepdims=True))
             placed = [jnp.where(mask, row, 0.0) for row in rows]
             entries[span, :] = jnp.concatenate(placed + [pad], 0).T
 
     def backward(index, carry):
         step = blocks - 1 - index
-        slopes(jnp.minimum(step + 1, blocks - 1))
+        place_slopes(jnp.minimum(step + 2, blocks - 1))
+        sum_slopes(jnp.minimum(step + 1, blocks - 1))
         out = []
         for group in range(groups):
             at = pl.multiple_of((group * blocks + step) * LANES, LANES)
@@ -486,7 +507,9 @@
         return tuple(out)
 
     lax.fori_loop(0, blocks, backward, ((zeros,) * wide,) * groups)
-    slopes(0)
+    place_slopes(min(1, blocks - 1))
+    sum_slopes(0)
+    place_slopes(0)
 
     tall = jnp.zeros((LANES, LANES), jnp.float32)
 
@@ -513,7 +536,8 @@
 
     loss_rows = jnp.broadcast_to(loss, (ROWSUB, LANES))
     stores = []
-    for side, ref, stage in ((1, grad_other, entries), (0, grad_own, w_planes[0])):
+    for side, skip in ((1, 0), (1, near // 2), (0, 0), (0, near // 2)):
+        stage = entries if side else w_planes[0]
 
         def collect(owner, carry, side=side, stage=stage):
             start = pl.multiple_of(owner * planes_out, 8)
@@ -532,50 +556,78 @@
             stage[pl.ds(start + planes_in, ROWSUB), :] = loss_rows
             return carry
 
-        lax.fori_loop(0, near, collect, 0)
-        store = pltpu.make_async_copy(
-            stage.at[pl.ds(0, near * planes_out)], ref, out_sem.at[side]
-        )
-        store.start()
-        stores.append(store)
+        lax.fori_loop(skip, skip + near // 2, collect, 0)
+        for first in range(skip, skip + near // 2, part):
+            index = side * quarter + first // part
+            store = pltpu.make_async_copy(
+                stage.at[pl.ds(first * planes_out, part * planes_out)],
+                grad_parts[index],
+                out_sem.at[index],
+            )
+            store.start()
+            stores.append(store)
     for store in stores:
         store.wait()
 
 
-def exchange_orders(gx_size, gy_size):
-    gx_bits = [gy_size.bit_length() - 1 + b for b in range(gx_size.bit_length() - 1)]
-    gy_bits = list(range(1, gy_size.bit_length() - 1))
-    cut = (len(gy_bits) + 1) // 2
-    low, high = gy_bits[:cut], gy_bits[cut:]
-    return gx_bits[::-1] + low + high, gx_bits + high + low
-
-
-def swap(values, devices, flips):
+def exchange_flips(gy_size):
+    bits = list(range(1, gy_size.bit_length() - 1))
+    cut = (len(bits) + 1) // 2
+    low, high = bits[:cut], bits[cut:]
+    return list(zip(low + high, high + low))
+
+
+def swap(values, devices, even, odd=None):
+    flips = (even, even if odd is None else odd)
     pairs = [(i, i ^ flips[i & 1]) for i in range(devices)]
     return lax.ppermute(values, AXES, pairs)
 
 
-def spread(values, devices, orders):
-    for bits in zip(*orders):
-        flips = [1 << bit for bit in bits]
-        values = jnp.concatenate([values, swap(values, devices, flips)], 0)
-    return values, swap(values, devices, (1, 1))
-
-
-def fold(own, other, devices, orders):
-    values = own + swap(other, devices, (1, 1))
-    for bits in reversed(list(zip(*orders))):
-        flips = [1 << bit for bit in bits]
-        half = values.shape[0] // 2
-        values = values[:half] + swap(values[half:], devices, flips)
-    return values
+def spread(values, gx_size, gy_size, hold):
+    devices = gx_size * gy_size
+    order = exchange_flips(gy_size)
+    blocks = [values] + [swap(values, devices, z * gy_size) for z in range(1, gx_size)]
+    own, other = [], []
+    for chunk in range(2):
+        values = jnp.concatenate(blocks[chunk * gx_size // 2 : (chunk + 1) * gx_size // 2], 0)
+        if chunk == 0:
+            values, hold = lax.optimization_barrier((values, hold))
+        for even, odd in order[:-1]:
+            values = jnp.concatenate([values, swap(values, devices, 1 << even, 1 << odd)], 0)
+        even, odd = order[-1]
+        last = swap(values, devices, 1 << even, 1 << odd)
+        own += [values, last]
+        other += [swap(values, devices, 1), swap(last, devices, 1)]
+    return own + other, hold
+
+
+def fold(parts, gx_size, gy_size):
+    devices = gx_size * gy_size
+    order = exchange_flips(gy_size)
+    own, other = parts[: PARTS // 2], parts[PARTS // 2 :]
+    chunks = [None, None]
+    for chunk in (1, 0):
+        high = own[2 * chunk + 1] + swap(other[2 * chunk + 1], devices, 1)
+        low = own[2 * chunk] + swap(other[2 * chunk], devices, 1)
+        even, odd = order[-1]
+        values = low + swap(high, devices, 1 << even, 1 << odd)
+        for even, odd in reversed(order[:-1]):
+            half = values.shape[0] // 2
+            values = values[:half] + swap(values[half:], devices, 1 << even, 1 << odd)
+        chunks[chunk] = values
+    size = 2 * chunks[0].shape[0] // gx_size
+    total = chunks[0][:size]
+    for z in range(1, gx_size):
+        at = z % (gx_size // 2) * size
+        block = chunks[z // (gx_size // 2)][at : at + size]
+        total = total + swap(block, devices, z * gy_size)
+    return total
 
 
 def per_device(gauss_params, first_moment, second_moment, splat_lists, tile_ids, targets, camera):
     gx_size = lax.axis_size("gx")
     gy_size = lax.axis_size("gy")
     devices = gx_size * gy_size
-    orders = exchange_orders(gx_size, gy_size)
     params_rows, count = gauss_params.shape
     tiles, depth = splat_lists.shape[1:]
     per_owner = count // LANES
@@ -589,10 +641,12 @@
     owner = splat_lists // count
     apart = owner ^ me
     local = splat_lists % count
-    place = (apart & 1) << len(orders[0])
-    for bit, (even, odd) in enumerate(zip(*orders)):
+    lows = gx_size // 2
+    apart_gx = apart // gy_size
+    place = (apart & 1) * (devices // 2) + apart_gx // lows * (devices // 4) + apart_gx % lows
+    for bit, (even, odd) in enumerate(exchange_flips(gy_size)):
         taken = jnp.where(owner & 1 == 0, apart >> even, apart >> odd)
-        place = place + ((taken & 1) << bit)
+        place = place + (taken & 1) * (lows << bit)
     rows = place * (count // ROWSUB) + (local // (ROWSUB * LANES)) * LANES + local % LANES
     which = (local // LANES) % ROWSUB
 
@@ -624,22 +678,12 @@
     table_rows = devices * count // ROWSUB
     plane_rows = max(total, devices // 2 * planes_out)
     extra = max(0, 7 - 2 * wide) if table_rows <= plane_rows else 0
-    render = pl.pallas_call(
-        functools.partial(
-            render_kernel,
-            devices=devices,
-            per_owner=per_owner,
-            groups=groups,
-            depth=depth,
-            streams=streams,
-        ),
-        out_shape=(
-            jax.ShapeDtypeStruct((tiles * 3 * pixels // LANES, LANES), f32),
-            jax.ShapeDtypeStruct((devices // 2 * planes_out, LANES), f32),
-            jax.ShapeDtypeStruct((devices // 2 * planes_out, LANES), f32),
-        ),
-        in_specs=[hbm, vmem, vmem, vmem, hbm, hbm],
-        out_specs=(vmem, hbm, hbm),
+    render = functools.partial(
+        pl.pallas_call,
+        out_shape=(jax.ShapeDtypeStruct((tiles * 3 * pixels // LANES, LANES), f32),)
+        + (jax.ShapeDtypeStruct((devices // PARTS * planes_out, LANES), f32),) * PARTS,
+        in_specs=[hbm, vmem, vmem, vmem] + [hbm] * PARTS,
+        out_specs=(vmem,) + (hbm,) * PARTS,
         scratch_shapes=[
             pltpu.VMEM((plane_rows, LANES), f32),
             pltpu.VMEM((total // LANES * ROWSUB, LANES), f32),
@@ -650,8 +694,9 @@
             pltpu.VMEM((total, pixels), bf16),
             pltpu.VMEM((groups, LANES, pixels), bf16),
             pltpu.VMEM((groups, LANES, pixels), bf16),
-            pltpu.SemaphoreType.DMA((2,)),
-            pltpu.SemaphoreType.DMA((2,)),
+            pltpu.VMEM((groups, LANES, LANES), f32),
+            pltpu.SemaphoreType.DMA((PARTS,)),
+            pltpu.SemaphoreType.DMA((PARTS,)),
             pltpu.SemaphoreType.DMA((streams,)),
         ]
         + [pltpu.SMEM((total // streams,), jnp.int32)] * streams
@@ -670,31 +715,43 @@
         out_specs=vmem,
         name="project",
     )(camera, params)
+    settings = (rows, which, middle, target_rows)
     pictures = []
-    losses = []
+    sums = []
     for step in range(STEPS):
-        near, far = spread(fields, devices, orders)
-        picture, own, other = render(
-            rows[step], which[step], middle[step], target_rows[step], near, far
+        kernel = functools.partial(
+            render_kernel,
+            devices=devices,
+            per_owner=per_owner,
+            groups=groups,
+            depth=depth,
+            streams=streams,
+            step_index=step,
         )
+        table, settings = spread(fields, gx_size, gy_size, settings)
+        picture, *grads = render(kernel)(*settings, *table)
         pictures.append(picture)
-        summed = fold(own, other, devices, orders)
-        losses.append(summed[planes_in, 0])
+        summed = fold(grads, gx_size, gy_size)
+        sums.append(summed)
         more = step + 1 < STEPS
+        before = [] if more else sums[:-1]
         result = pl.pallas_call(
-            functools.partial(update_kernel, step=step, project_next=more),
-            out_shape=(state, state, state) + ((field_shape,) if more else ()),
-            in_specs=[smem, vmem, vmem, vmem, vmem],
-            out_specs=(vmem,) * (4 if more else 3),
+            functools.partial(
+                update_kernel,
+                step=step,
+                project_next=more,
+                pixel_count=3.0 * pixels * tiles * devices,
+            ),
+            out_shape=(state, state, state)
+            + (field_shape if more else jax.ShapeDtypeStruct((STEPS,), f32),),
+            in_specs=[smem] + [vmem] * (4 + len(before)),
+            out_specs=(vmem,) * 3 + (vmem if more else smem,),
             scratch_shapes=[pltpu.VMEM((params_rows, count), f32)],
             name="update",
-        )(camera, params, first, second, summed)
-        params, first, second = result[:3]
-        if more:
-            fields = result[3]
+        )(camera, params, first, second, summed, *before)
+        params, first, second, fields = result
     rendered = jnp.stack(pictures).reshape(STEPS, tiles, 3, pixels)
-    loss = jnp.stack(losses) / (3.0 * pixels * tiles * devices)
-    return params, first, second, rendered, loss
+    return params, first, second, rendered, fields
 
 
 def solution(mesh):

time: 258 us -> 214 us (0.83)
  waiting for transfers between devices: 85.2 us -> 51.9 us
  other arithmetic: 11.4 us -> 5.06 us
  Pallas kernels: 110 us -> 105 us
  starting transfers between devices: 38.6 us -> 41.8 us
  local copies, waits for them, and re-layouts: 10.6 us -> 7.74 us
    ppermute x20 -> x44, waiting for transfers between devices: 85.2 us -> 51.9 us  [swap(): return lax.ppermute(values, AXES, pairs)]
    pallas_call x2, Pallas kernels: 102 us -> 96.6 us  [per_device(): picture, *grads = render(kernel)(*settings, *table)]
    concatenate x6 -> x4, other arithmetic: 5.44 us -> 0.93 us  [spread(): jnp.concatenate(blocks[chunk * gx_size // 2:(chunk + 1) * gx_size // 2], 0)]
    squeeze x5 -> x0, local copies, waits for them, and re-layouts: 3.63 us -> none  [the longest x2 1.69 us: per_device(): which[step]]
    ppermute x20 -> x44, starting transfers between devices: 38.6 us -> 41.8 us  [swap(): return lax.ppermute(values, AXES, pairs)]
  transfers between devices with their start and end apart: 20 -> 44, of which waited for: 19 -> 25; matrix products, arithmetic and copies ran while one was open for 4% -> 4% of each run, Pallas kernels for 0% -> 0%
where the time goes in v4:
time: 214 us; the launch traced here: 213 us
  Pallas kernels  105 us (49%)
  waiting for transfers between devices  51.9 us (24%)
  starting transfers between devices  41.8 us (20%)
  local copies, waits for them, and re-layouts  7.74 us (4%)
  other arithmetic  5.06 us (2%)
    pallas_call x2, Pallas kernels, per_device(): picture, *grads = render(kernel)(*settings, *table)  96.6 us
    ppermute x44, waiting for transfers between devices, swap(): return lax.ppermute(values, AXES, pairs)  51.9 us
    ppermute x44, starting transfers between devices, swap(): return lax.ppermute(values, AXES, pairs)  41.8 us
    pallas_call x2, Pallas kernels, per_device(): pl.pallas_call(functools.partial(update_kernel, step=step, project_next=m...  6.88 us
  transfers between devices with their start and end apart: 44, of which 25 were waited for; matrix products, arithmetic and copies ran while one was open for 4% of the time, Pallas kernels for 0%

profile of v4, /device:TPU:0, one launch (start us, length us, event | category | flops | bytes accessed | tf_op | source)
XLA Modules:
  0.0 213.3 jit_solution(3467125592829752294)
XLA Ops:
  0.6 2.0 project.1
  2.6 3.1 %collective-permute-start = (f32[144,128]{1,0:T(8,128)}, f32[144,128]{1,0:T(8,128)S(1)}, u32[]{:S(2)}, u32[]{:S(2)}) collective-permute-start(f32[144,128]{1,0:T(8,128)} %project.1), channel_id=1, source_target_pairs={{0,8},{1,9},{2,10},{3,11},{4,12},{5,13},{6,14},{7,15},{8,0},{9,1},... | collective-permute-start | bytes 221192 | tf_op jit(solution)/shard_map/ppermute | solution.py:583
  5.7 2.6 %collective-permute-start.3 = (f32[144,128]{1,0:T(8,128)}, f32[144,128]{1,0:T(8,128)S(1)}, u32[]{:S(2)}, u32[]{:S(2)}) collective-permute-start(f32[144,128]{1,0:T(8,128)} %project.1), channel_id=1, source_target_pairs={{0,16},{1,17},{2,18},{3,19},{4,20},{5,21},{6,22},{7,23},{8,24},{9,... | collective-permute-start | bytes 221192 | tf_op jit(solution)/shard_map/ppermute | solution.py:583
  13.2 1.8 collective-permute-start.1
  16.3 2.1 collective-permute-done.1
  18.4 1.8 collective-permute-start.2
  21.3 1.6 collective-permute-start.6
  23.4 1.8 collective-permute-done.2.refs_1_
  25.2 3.2 %collective-permute-done.6.refs_3_ = f32[576,128]{1,0:T(8,128)S(1)} collective-permute-done((f32[576,128]{1,0:T(8,128)S(1)}, f32[576,128]{1,0:T(8,128)S(1)}, u32[]{:S(2)}, u32[]{:S(2)}) %collective-permute-start.6) | collective-permute-done | bytes 294944 | tf_op jit(solution)/shard_map/ppermute | solution.py:583
  30.7 48.3 %render.2 = (f32[96,128]{1,0:T(8,128)}, f32[608,128]{1,0:T(8,128)}, f32[608,128]{1,0:T(8,128)}, f32[608,128]{1,0:T(8,128)}, f32[608,128]{1,0:T(8,128)}, /*index=...) custom-call(s32[2,16,512]{2,1,0:T(8,128)} %bitcast.18, ...), custom_call_target="tpu_custom_call" | custom-call | tf_op jit(solution)/shard_map/render/pallas_call | solution.py:732
  82.0 1.8 collective-permute-start.18
  85.3 3.7 %collective-permute-done.18 = f32[608,128]{1,0:T(8,128)S(1)} collective-permute-done((f32[608,128]{1,0:T(8,128)S(1)}, f32[608,128]{1,0:T(8,128)S(1)}, u32[]{:S(2)}, u32[]{:S(2)}) %collective-permute-start.18) | collective-permute-done | bytes 311328 | tf_op jit(solution)/shard_map/ppermute | solution.py:583
  89.1 1.7 collective-permute-start.19
  90.8 2.8 %collective-permute-done.13 = f32[608,128]{1,0:T(8,128)S(1)} collective-permute-done((f32[608,128]{1,0:T(8,128)S(1)}, f32[608,128]{1,0:T(8,128)S(1)}, u32[]{:S(2)}, u32[]{:S(2)}) %collective-permute-start.13) | collective-permute-done | bytes 311328 | tf_op jit(solution)/shard_map/ppermute | solution.py:583
  93.7 1.7 collective-permute-start.14
  95.5 3.7 %collective-permute-start.21 = (f32[152,128]{1,0:T(8,128)S(1)}, f32[152,128]{1,0:T(8,128)S(1)}, u32[]{:S(2)}, u32[]{:S(2)}) collective-permute-start(f32[152,128]{1,0:T(8,128)S(1)} %get-tuple-element.85), channel_id=1, source_target_pairs={{0,24},{1,25},{2,26},{3,27},{4,28},{5,29},{6,30},{7,31},{8,16},{9,... | collective-permute-start | bytes 233480 | tf_op jit(solution)/shard_map/ppermute | solution.py:583
  100.0 1.8 collective-permute-done.21
  101.8 3.0 %collective-permute-done.20 = f32[152,128]{1,0:T(8,128)S(1)} collective-permute-done((f32[152,128]{1,0:T(8,128)S(1)}, f32[152,128]{1,0:T(8,128)S(1)}, u32[]{:S(2)}, u32[]{:S(2)}) %collective-permute-start.20) | collective-permute-done | bytes 77856 | tf_op jit(solution)/shard_map/ppermute | solution.py:583
  105.8 3.5 %update.2 = (f32[55,2048]{1,0:T(8,128)}, f32[55,2048]{1,0:T(8,128)}, f32[55,2048]{1,0:T(8,128)}, f32[144,128]{1,0:T(8,128)}) custom-call(f32[2,2]{1,0:T(2,128)} %cam_ref.5, f32[55,2048]{1,0:T(8,128)} %param_ref.3, f32[55,2048]{1,0:T(8,128)} %first_ref.1, f32[55,2048]{1,0:T(8,128)} %second_ref.1, f32[152,128]{1,0:T(8,128)} %fusion.3.grad_ref.refs_0_), custom_call_target="tpu_custom_call" | custom-call | tf_op jit(solution)/shard_map/update/pallas_call | solution.py:738
  109.9 3.0 %collective-permute-start.25 = (f32[144,128]{1,0:T(8,128)}, f32[144,128]{1,0:T(8,128)S(1)}, u32[]{:S(2)}, u32[]{:S(2)}) collective-permute-start(f32[144,128]{1,0:T(8,128)} %get-tuple-element.57), channel_id=1, source_target_pairs={{0,16},{1,17},{2,18},{3,19},{4,20},{5,21},{6,22},{7,23},{8,24},{9,... | collective-permute-start | bytes 221192 | tf_op jit(solution)/shard_map/ppermute | solution.py:583
  117.0 2.3 %collective-permute-done.26 = f32[144,128]{1,0:T(8,128)S(1)} collective-permute-done((f32[144,128]{1,0:T(8,128)}, f32[144,128]{1,0:T(8,128)S(1)}, u32[]{:S(2)}, u32[]{:S(2)}) %collective-permute-start.26) | collective-permute-done | bytes 73760 | tf_op jit(solution)/shard_map/ppermute | solution.py:583
  120.3 1.8 collective-permute-start.24
  122.1 4.0 %collective-permute-done.27 = f32[288,128]{1,0:T(8,128)S(1)} collective-permute-done((f32[288,128]{1,0:T(8,128)S(1)}, f32[288,128]{1,0:T(8,128)S(1)}, u32[]{:S(2)}, u32[]{:S(2)}) %collective-permute-start.27) | collective-permute-done | bytes 147488 | tf_op jit(solution)/shard_map/ppermute | solution.py:583
  128.1 4.7 %collective-permute-done.28.refs_3_ = f32[576,128]{1,0:T(8,128)S(1)} collective-permute-done((f32[576,128]{1,0:T(8,128)S(1)}, f32[576,128]{1,0:T(8,128)S(1)}, u32[]{:S(2)}, u32[]{:S(2)}) %collective-permute-start.28) | collective-permute-done | bytes 294944 | tf_op jit(solution)/shard_map/ppermute | solution.py:583
  135.2 48.3 %render.3 = (f32[96,128]{1,0:T(8,128)}, f32[608,128]{1,0:T(8,128)}, f32[608,128]{1,0:T(8,128)}, f32[608,128]{1,0:T(8,128)}, f32[608,128]{1,0:T(8,128)}, /*index=...) custom-call(s32[2,16,512]{2,1,0:T(8,128)} %bitcast.19, ...), custom_call_target="tpu_custom_call" | custom-call | tf_op jit(solution)/shard_map/render/pallas_call | solution.py:732
  189.7 3.8 %collective-permute-done.40 = f32[608,128]{1,0:T(8,128)S(1)} collective-permute-done((f32[608,128]{1,0:T(8,128)S(1)}, f32[608,128]{1,0:T(8,128)S(1)}, u32[]{:S(2)}, u32[]{:S(2)}) %collective-permute-start.40) | collective-permute-done | bytes 311328 | tf_op jit(solution)/shard_map/ppermute | solution.py:583
  194.4 3.7 %collective-permute-done.35 = f32[608,128]{1,0:T(8,128)S(1)} collective-permute-done((f32[608,128]{1,0:T(8,128)S(1)}, f32[608,128]{1,0:T(8,128)S(1)}, u32[]{:S(2)}, u32[]{:S(2)}) %collective-permute-start.35) | collective-permute-done | bytes 311328 | tf_op jit(solution)/shard_map/ppermute | solution.py:583
  199.0 1.6 collective-permute-start.43
  201.2 2.3 %collective-permute-done.36 = f32[304,128]{1,0:T(8,128)S(1)} collective-permute-done((f32[304,128]{1,0:T(8,128)S(1)}, f32[304,128]{1,0:T(8,128)S(1)}, u32[]{:S(2)}, u32[]{:S(2)}) %collective-permute-start.36) | collective-permute-done | bytes 155680 | tf_op jit(solution)/shard_map/ppermute | solution.py:583
  204.3 1.8 collective-permute-done.43
  206.1 2.5 %collective-permute-done.42 = f32[152,128]{1,0:T(8,128)S(1)} collective-permute-done((f32[152,128]{1,0:T(8,128)S(1)}, f32[152,128]{1,0:T(8,128)S(1)}, u32[]{:S(2)}, u32[]{:S(2)}) %collective-permute-start.42) | collective-permute-done | bytes 77856 | tf_op jit(solution)/shard_map/ppermute | solution.py:583
  209.8 3.3 %update.3 = (f32[55,2048]{1,0:T(8,128)}, f32[55,2048]{1,0:T(8,128)}, f32[55,2048]{1,0:T(8,128)}, f32[2]{0:T(128)}) custom-call(f32[2,2]{1,0:T(2,128)} %cam_ref.5, f32[55,2048]{1,0:T(8,128)} %get-tuple-element.54.param_ref, f32[55,2048]{1,0:T(8,128)} %get-tuple-element.55.first_ref, f32[55,2048]{1,0:T(8,128)} %get-tuple-element.56.second_ref, ...), custom_call_target="tpu_custom_call" | custom-call | tf_op jit(solution)/shard_map/update/pallas_call | solution.py:738
  (176 shorter events, 36.9 us)
Async XLA Ops:
  2.6 10.4 %collective-permute-start = (f32[144,128]{1,0:T(8,128)}, f32[144,128]{1,0:T(8,128)S(1)}, u32[]{:S(2)}, u32[]{:S(2)}) collective-permute-start(f32[144,128]{1,0:T(8,128)} %project.1), channel_id=1, source_target_pairs={{0,8},{1,9},{2,10},{3,11},{4,12},{5,13},{6,14},{7,15},{8,0},{9,1},... | collective-permute-start | bytes 221192 | tf_op jit(solution)/shard_map/ppermute | solution.py:583
  5.7 9.3 %collective-permute-start.3 = (f32[144,128]{1,0:T(8,128)}, f32[144,128]{1,0:T(8,128)S(1)}, u32[]{:S(2)}, u32[]{:S(2)}) collective-permute-start(f32[144,128]{1,0:T(8,128)} %project.1), channel_id=1, source_target_pairs={{0,16},{1,17},{2,18},{3,19},{4,20},{5,21},{6,22},{7,23},{8,24},{9,... | collective-permute-start | bytes 221192 | tf_op jit(solution)/shard_map/ppermute | solution.py:583
  8.3 6.8 %collective-permute-start.4 = (f32[144,128]{1,0:T(8,128)}, f32[144,128]{1,0:T(8,128)S(1)}, u32[]{:S(2)}, u32[]{:S(2)}) collective-permute-start(f32[144,128]{1,0:T(8,128)} %project.1), channel_id=1, source_target_pairs={{0,24},{1,25},{2,26},{3,27},{4,28},{5,29},{6,30},{7,31},{8,16},{9,... | collective-permute-start | bytes 221192 | tf_op jit(solution)/shard_map/ppermute | solution.py:583
  15.0 6.2 %collective-permute-start.5 = (f32[288,128]{1,0:T(8,128)S(1)}, f32[288,128]{1,0:T(8,128)S(1)}, u32[]{:S(2)}, u32[]{:S(2)}) collective-permute-start(f32[288,128]{1,0:T(8,128)S(1)} %pad_maximum_fusion.1), channel_id=1, source_target_pairs={{0,2},{1,5},{2,0},{3,7},{4,6},{5,1},{6,4},{7,3},{8,10},{9,13},{10,... | collective-permute-start | bytes 442376 | tf_op jit(solution)/shard_map/ppermute | solution.py:583
  18.4 6.8 %collective-permute-start.2 = (f32[576,128]{1,0:T(8,128)S(1)}, f32[576,128]{1,0:T(8,128)S(1)}, u32[]{:S(2)}, u32[]{:S(2)}) collective-permute-start(f32[576,128]{1,0:T(8,128)S(1)} %constant_dynamic-update-slice_fusion.refs_0_), channel_id=1, source_target_pairs={{0,4},{1,3},{2,6},{3,1},{4,0},{5,7},{6,2},{7,5},{8,12},{9,11},{10,... | collective-permute-start | bytes 884744 | tf_op jit(solution)/shard_map/ppermute | solution.py:583
  21.3 7.1 %collective-permute-start.6 = (f32[576,128]{1,0:T(8,128)S(1)}, f32[576,128]{1,0:T(8,128)S(1)}, u32[]{:S(2)}, u32[]{:S(2)}) collective-permute-start(f32[576,128]{1,0:T(8,128)S(1)} %constant_dynamic-update-slice_fusion.2.refs_2_), channel_id=1, source_target_pairs={{0,4},{1,3},{2,6},{3,1},{4,0},{5,7},{6,2},{7,5},{8,12},{9,11},{10,... | collective-permute-start | bytes 884744 | tf_op jit(solution)/shard_map/ppermute | solution.py:583
  22.9 5.5 %collective-permute-start.7 = (f32[576,128]{1,0:T(8,128)S(1)}, f32[576,128]{1,0:T(8,128)S(1)}, u32[]{:S(2)}, u32[]{:S(2)}) collective-permute-start(f32[576,128]{1,0:T(8,128)S(1)} %constant_dynamic-update-slice_fusion.refs_0_), channel_id=1, source_target_pairs={{0,1},{1,0},{2,3},{3,2},{4,5},{5,4},{6,7},{7,6},{8,9},{9,8},{10,11... | collective-permute-start | bytes 884744 | tf_op jit(solution)/shard_map/ppermute | solution.py:583
  22.9 5.5 %collective-permute-start.9 = (f32[576,128]{1,0:T(8,128)S(1)}, f32[576,128]{1,0:T(8,128)S(1)}, u32[]{:S(2)}, u32[]{:S(2)}) collective-permute-start(f32[576,128]{1,0:T(8,128)S(1)} %constant_dynamic-update-slice_fusion.2.refs_2_), channel_id=1, source_target_pairs={{0,1},{1,0},{2,3},{3,2},{4,5},{5,4},{6,7},{7,6},{8,9},{9,8},{10,11... | collective-permute-start | bytes 884744 | tf_op jit(solution)/shard_map/ppermute | solution.py:583
  79.7 5.7 %collective-permute-start.16 = (f32[608,128]{1,0:T(8,128)}, f32[608,128]{1,0:T(8,128)S(1)}, u32[]{:S(2)}, u32[]{:S(2)}) collective-permute-start(f32[608,128]{1,0:T(8,128)} %get-tuple-element.51), channel_id=1, source_target_pairs={{0,1},{1,0},{2,3},{3,2},{4,5},{5,4},{6,7},{7,6},{8,9},{9,8},{10,11... | collective-permute-start | bytes 933896 | tf_op jit(solution)/shard_map/ppermute | solution.py:583
  82.0 7.0 %collective-permute-start.18 = (f32[608,128]{1,0:T(8,128)S(1)}, f32[608,128]{1,0:T(8,128)S(1)}, u32[]{:S(2)}, u32[]{:S(2)}) collective-permute-start(f32[608,128]{1,0:T(8,128)S(1)} %add.143), channel_id=1, source_target_pairs={{0,4},{1,3},{2,6},{3,1},{4,0},{5,7},{6,2},{7,5},{8,12},{9,11},{10,... | collective-permute-start | bytes 933896 | tf_op jit(solution)/shard_map/ppermute | solution.py:583
  83.9 7.0 %collective-permute-start.11 = (f32[608,128]{1,0:T(8,128)S(1)}, f32[608,128]{1,0:T(8,128)S(1)}, u32[]{:S(2)}, u32[]{:S(2)}) collective-permute-start(f32[608,128]{1,0:T(8,128)S(1)} %copy-done.29), channel_id=1, source_target_pairs={{0,1},{1,0},{2,3},{3,2},{4,5},{5,4},{6,7},{7,6},{8,9},{9,8},{10,11... | collective-permute-start | bytes 933896 | tf_op jit(solution)/shard_map/ppermute | solution.py:583
  83.9 9.7 %collective-permute-start.13 = (f32[608,128]{1,0:T(8,128)S(1)}, f32[608,128]{1,0:T(8,128)S(1)}, u32[]{:S(2)}, u32[]{:S(2)}) collective-permute-start(f32[608,128]{1,0:T(8,128)S(1)} %add.138), channel_id=1, source_target_pairs={{0,4},{1,3},{2,6},{3,1},{4,0},{5,7},{6,2},{7,5},{8,12},{9,11},{10,... | collective-permute-start | bytes 933896 | tf_op jit(solution)/shard_map/ppermute | solution.py:583
  89.1 6.3 %collective-permute-start.19 = (f32[304,128]{1,0:T(8,128)S(1)}, f32[304,128]{1,0:T(8,128)S(1)}, u32[]{:S(2)}, u32[]{:S(2)}) collective-permute-start(f32[304,128]{1,0:T(8,128)S(1)} %slice.69), channel_id=1, source_target_pairs={{0,2},{1,5},{2,0},{3,7},{4,6},{5,1},{6,4},{7,3},{8,10},{9,13},{10,... | collective-permute-start | bytes 466952 | tf_op jit(solution)/shard_map/ppermute | solution.py:583
  93.7 5.4 %collective-permute-start.14 = (f32[304,128]{1,0:T(8,128)S(1)}, f32[304,128]{1,0:T(8,128)S(1)}, u32[]{:S(2)}, u32[]{:S(2)}) collective-permute-start(f32[304,128]{1,0:T(8,128)S(1)} %slice.65), channel_id=1, source_target_pairs={{0,2},{1,5},{2,0},{3,7},{4,6},{5,1},{6,4},{7,3},{8,10},{9,13},{10,... | collective-permute-start | bytes 466952 | tf_op jit(solution)/shard_map/ppermute | solution.py:583
  95.5 6.4 %collective-permute-start.21 = (f32[152,128]{1,0:T(8,128)S(1)}, f32[152,128]{1,0:T(8,128)S(1)}, u32[]{:S(2)}, u32[]{:S(2)}) collective-permute-start(f32[152,128]{1,0:T(8,128)S(1)} %get-tuple-element.85), channel_id=1, source_target_pairs={{0,24},{1,25},{2,26},{3,27},{4,28},{5,29},{6,30},{7,31},{8,16},{9,... | collective-permute-start | bytes 233480 | tf_op jit(solution)/shard_map/ppermute | solution.py:583
  99.1 5.7 %collective-permute-start.20 = (f32[152,128]{1,0:T(8,128)S(1)}, f32[152,128]{1,0:T(8,128)S(1)}, u32[]{:S(2)}, u32[]{:S(2)}) collective-permute-start(f32[152,128]{1,0:T(8,128)S(1)} %get-tuple-element.84), channel_id=1, source_target_pairs={{0,16},{1,17},{2,18},{3,19},{4,20},{5,21},{6,22},{7,23},{8,24},{9,... | collective-permute-start | bytes 233480 | tf_op jit(solution)/shard_map/ppermute | solution.py:583
  99.2 6.0 %collective-permute-start.15 = (f32[152,128]{1,0:T(8,128)S(1)}, f32[152,128]{1,0:T(8,128)S(1)}, u32[]{:S(2)}, u32[]{:S(2)}) collective-permute-start(f32[152,128]{1,0:T(8,128)S(1)} %slice.67), channel_id=1, source_target_pairs={{0,8},{1,9},{2,10},{3,11},{4,12},{5,13},{6,14},{7,15},{8,0},{9,1},... | collective-permute-start | bytes 233480 | tf_op jit(solution)/shard_map/ppermute | solution.py:583
  109.9 7.1 %collective-permute-start.25 = (f32[144,128]{1,0:T(8,128)}, f32[144,128]{1,0:T(8,128)S(1)}, u32[]{:S(2)}, u32[]{:S(2)}) collective-permute-start(f32[144,128]{1,0:T(8,128)} %get-tuple-element.57), channel_id=1, source_target_pairs={{0,16},{1,17},{2,18},{3,19},{4,20},{5,21},{6,22},{7,23},{8,24},{9,... | collective-permute-start | bytes 221192 | tf_op jit(solution)/shard_map/ppermute | solution.py:583
  112.9 6.4 %collective-permute-start.26 = (f32[144,128]{1,0:T(8,128)}, f32[144,128]{1,0:T(8,128)S(1)}, u32[]{:S(2)}, u32[]{:S(2)}) collective-permute-start(f32[144,128]{1,0:T(8,128)} %get-tuple-element.57), channel_id=1, source_target_pairs={{0,24},{1,25},{2,26},{3,27},{4,28},{5,29},{6,30},{7,31},{8,16},{9,... | collective-permute-start | bytes 221192 | tf_op jit(solution)/shard_map/ppermute | solution.py:583
  114.8 5.5 %collective-permute-start.23 = (f32[288,128]{1,0:T(8,128)S(1)}, f32[288,128]{1,0:T(8,128)S(1)}, u32[]{:S(2)}, u32[]{:S(2)}) collective-permute-start(f32[288,128]{1,0:T(8,128)S(1)} %pad_maximum_fusion.2), channel_id=1, source_target_pairs={{0,2},{1,5},{2,0},{3,7},{4,6},{5,1},{6,4},{7,3},{8,10},{9,13},{10,... | collective-permute-start | bytes 442376 | tf_op jit(solution)/shard_map/ppermute | solution.py:583
  119.3 6.8 %collective-permute-start.27 = (f32[288,128]{1,0:T(8,128)S(1)}, f32[288,128]{1,0:T(8,128)S(1)}, u32[]{:S(2)}, u32[]{:S(2)}) collective-permute-start(f32[288,128]{1,0:T(8,128)S(1)} %pad_maximum_fusion.3), channel_id=1, source_target_pairs={{0,2},{1,5},{2,0},{3,7},{4,6},{5,1},{6,4},{7,3},{8,10},{9,13},{10,... | collective-permute-start | bytes 442376 | tf_op jit(solution)/shard_map/ppermute | solution.py:583
  120.3 7.7 %collective-permute-start.24 = (f32[576,128]{1,0:T(8,128)S(1)}, f32[576,128]{1,0:T(8,128)S(1)}, u32[]{:S(2)}, u32[]{:S(2)}) collective-permute-start(f32[576,128]{1,0:T(8,128)S(1)} %constant_dynamic-update-slice_fusion.5.refs_0_), channel_id=1, source_target_pairs={{0,4},{1,3},{2,6},{3,1},{4,0},{5,7},{6,2},{7,5},{8,12},{9,11},{10,... | collective-permute-start | bytes 884744 | tf_op jit(solution)/shard_map/ppermute | solution.py:583
  126.1 6.8 %collective-permute-start.28 = (f32[576,128]{1,0:T(8,128)S(1)}, f32[576,128]{1,0:T(8,128)S(1)}, u32[]{:S(2)}, u32[]{:S(2)}) collective-permute-start(f32[576,128]{1,0:T(8,128)S(1)} %constant_dynamic-update-slice_fusion.7.refs_2_), channel_id=1, source_target_pairs={{0,4},{1,3},{2,6},{3,1},{4,0},{5,7},{6,2},{7,5},{8,12},{9,11},{10,... | collective-permute-start | bytes 884744 | tf_op jit(solution)/shard_map/ppermute | solution.py:583
  127.5 5.3 %collective-permute-start.31 = (f32[576,128]{1,0:T(8,128)S(1)}, f32[576,128]{1,0:T(8,128)S(1)}, u32[]{:S(2)}, u32[]{:S(2)}) collective-permute-start(f32[576,128]{1,0:T(8,128)S(1)} %constant_dynamic-update-slice_fusion.7.refs_2_), channel_id=1, source_target_pairs={{0,1},{1,0},{2,3},{3,2},{4,5},{5,4},{6,7},{7,6},{8,9},{9,8},{10,11... | collective-permute-start | bytes 884744 | tf_op jit(solution)/shard_map/ppermute | solution.py:583
  184.1 5.5 %collective-permute-start.38 = (f32[608,128]{1,0:T(8,128)}, f32[608,128]{1,0:T(8,128)S(1)}, u32[]{:S(2)}, u32[]{:S(2)}) collective-permute-start(f32[608,128]{1,0:T(8,128)} %get-tuple-element.68), channel_id=1, source_target_pairs={{0,1},{1,0},{2,3},{3,2},{4,5},{5,4},{6,7},{7,6},{8,9},{9,8},{10,11... | collective-permute-start | bytes 933896 | tf_op jit(solution)/shard_map/ppermute | solution.py:583
  186.5 7.0 %collective-permute-start.40 = (f32[608,128]{1,0:T(8,128)S(1)}, f32[608,128]{1,0:T(8,128)S(1)}, u32[]{:S(2)}, u32[]{:S(2)}) collective-permute-start(f32[608,128]{1,0:T(8,128)S(1)} %add.154), channel_id=1, source_target_pairs={{0,4},{1,3},{2,6},{3,1},{4,0},{5,7},{6,2},{7,5},{8,12},{9,11},{10,... | collective-permute-start | bytes 933896 | tf_op jit(solution)/shard_map/ppermute | solution.py:583
  188.0 6.4 %collective-permute-start.33 = (f32[608,128]{1,0:T(8,128)S(1)}, f32[608,128]{1,0:T(8,128)S(1)}, u32[]{:S(2)}, u32[]{:S(2)}) collective-permute-start(f32[608,128]{1,0:T(8,128)S(1)} %copy-done.28), channel_id=1, source_target_pairs={{0,1},{1,0},{2,3},{3,2},{4,5},{5,4},{6,7},{7,6},{8,9},{9,8},{10,11... | collective-permute-start | bytes 933896 | tf_op jit(solution)/shard_map/ppermute | solution.py:583
  188.1 10.0 %collective-permute-start.35 = (f32[608,128]{1,0:T(8,128)S(1)}, f32[608,128]{1,0:T(8,128)S(1)}, u32[]{:S(2)}, u32[]{:S(2)}) collective-permute-start(f32[608,128]{1,0:T(8,128)S(1)} %add.149), channel_id=1, source_target_pairs={{0,4},{1,3},{2,6},{3,1},{4,0},{5,7},{6,2},{7,5},{8,12},{9,11},{10,... | collective-permute-start | bytes 933896 | tf_op jit(solution)/shard_map/ppermute | solution.py:583
  193.5 5.5 %collective-permute-start.41 = (f32[304,128]{1,0:T(8,128)S(1)}, f32[304,128]{1,0:T(8,128)S(1)}, u32[]{:S(2)}, u32[]{:S(2)}) collective-permute-start(f32[304,128]{1,0:T(8,128)S(1)} %slice.77), channel_id=1, source_target_pairs={{0,2},{1,5},{2,0},{3,7},{4,6},{5,1},{6,4},{7,3},{8,10},{9,13},{10,... | collective-permute-start | bytes 466952 | tf_op jit(solution)/shard_map/ppermute | solution.py:583
  199.0 7.1 %collective-permute-start.43 = (f32[152,128]{1,0:T(8,128)S(1)}, f32[152,128]{1,0:T(8,128)S(1)}, u32[]{:S(2)}, u32[]{:S(2)}) collective-permute-start(f32[152,128]{1,0:T(8,128)S(1)} %get-tuple-element.83), channel_id=1, source_target_pairs={{0,24},{1,25},{2,26},{3,27},{4,28},{5,29},{6,30},{7,31},{8,16},{9,... | collective-permute-start | bytes 233480 | tf_op jit(solution)/shard_map/ppermute | solution.py:583
  200.6 8.0 %collective-permute-start.42 = (f32[152,128]{1,0:T(8,128)S(1)}, f32[152,128]{1,0:T(8,128)S(1)}, u32[]{:S(2)}, u32[]{:S(2)}) collective-permute-start(f32[152,128]{1,0:T(8,128)S(1)} %get-tuple-element.82), channel_id=1, source_target_pairs={{0,16},{1,17},{2,18},{3,19},{4,20},{5,21},{6,22},{7,23},{8,24},{9,... | collective-permute-start | bytes 233480 | tf_op jit(solution)/shard_map/ppermute | solution.py:583
  203.5 5.7 %collective-permute-start.37 = (f32[152,128]{1,0:T(8,128)S(1)}, f32[152,128]{1,0:T(8,128)S(1)}, u32[]{:S(2)}, u32[]{:S(2)}) collective-permute-start(f32[152,128]{1,0:T(8,128)S(1)} %slice.75), channel_id=1, source_target_pairs={{0,8},{1,9},{2,10},{3,11},{4,12},{5,13},{6,14},{7,15},{8,0},{9,1},... | collective-permute-start | bytes 233480 | tf_op jit(solution)/shard_map/ppermute | solution.py:583
  (42 other events, 155.0 us)

commit v5 on v4

--- a/solution.py
+++ b/solution.py
@@ -225,7 +225,8 @@
     picture_ref, refs = refs[0], refs[1:]
     grad_parts, refs = refs[:PARTS], refs[PARTS:]
     (
-        entries,
+        fresh,
+        placed,
         fields,
         factors,
         residual,
@@ -245,7 +246,6 @@
     halves = per_owner // ROWSUB
     total = groups * ROWSUB * depth
     row_lists, scratch = scratch[:streams], scratch[streams:]
-    table = scratch[0]
     blocks = depth * ROWSUB // LANES
     per_block = LANES // ROWSUB
     pixels = SIDE * SIDE
@@ -253,9 +253,8 @@
     near = devices // 2
     quarter = PARTS // 2
     part = near // quarter
-    w_planes = scratch[1 : 1 + wide]
-    a_planes = scratch[1 + wide : 1 + 2 * wide]
-    tables = [one for one in scratch if one.shape[0] >= devices * halves * LANES]
+    w_planes, a_planes, tables = scratch[:wide], scratch[wide : 2 * wide], scratch[2 * wide :]
+    table = tables[0]
 
     loads = [
         pltpu.make_async_copy(
@@ -295,19 +294,25 @@
     for copy in lists:
         copy.wait()
 
-    turns = 2
-    unroll = turns * streams
-
-    def gather(index, carry):
-        some = entries.at[pl.ds(pl.multiple_of(index * unroll, unroll), unroll)]
-        for turn in range(turns):
-            place = index * turns + turn
-            for q in range(streams):
-                at = turn * streams + q
-                some[at : at + 1, :] = table[pl.ds(row_lists[q][place], 1), :]
-        return carry
-
-    lax.fori_loop(0, total // unroll, gather, 0)
+    turns = LANES // streams
+
+    def gather(step):
+        for group in range(groups):
+            for turn in range(turns):
+                place = (group * blocks + step) * turns + turn
+                for q in range(streams):
+                    at = group * LANES + turn * streams + q
+                    fresh[at : at + 1, :] = table[pl.ds(row_lists[q][place], 1), :]
+
+    def scatter(step):
+        for group in range(groups):
+            for turn in range(turns):
+                place = (group * blocks + step) * turns + turn
+                for q in range(streams):
+                    at = group * LANES + turn * streams + q
+                    one = tables[at % len(tables)]
+                    row = pl.ds(row_lists[q][place], 1)
+                    one[row, :] = one[row, :] + placed[at : at + 1, :]
 
     sub = lax.broadcasted_iota(jnp.int32, (ROWSUB, LANES), 0)
     lane = lax.broadcasted_iota(jnp.int32, (ROWSUB, LANES), 1)
@@ -327,7 +332,7 @@
     def prepare(block, group):
         at = pl.multiple_of(block * LANES, LANES)
         mask = field_mask(block)
-        raw = entries[pl.ds(at, LANES), :].T
+        raw = fresh[group * LANES : (group + 1) * LANES, :].T
         rows = []
         for f in range(FIELDS):
             part = jnp.where(mask, raw[f * ROWSUB : (f + 1) * ROWSUB, :], 0.0)
@@ -370,8 +375,10 @@
             high_ref[span, h * LANES : (h + 1) * LANES] = high
             rest_ref[span, h * LANES : (h + 1) * LANES] = rest
 
+    gather(0)
     for group in range(groups):
         prepare(group * blocks, group)
+    gather(min(1, blocks - 1))
 
     def forward(step, carry):
         out = []
@@ -403,6 +410,7 @@
         ahead = jnp.minimum(step + 1, blocks - 1)
         for group in range(groups):
             prepare(group * blocks + ahead, group)
+        gather(jnp.minimum(step + 2, blocks - 1))
         return tuple(out)
 
     ones = jnp.ones((ROWSUB, LANES), jnp.float32)
@@ -455,11 +463,10 @@
                 + tone_sums[LANES:]
             ).T
 
-    def place_slopes(step):
+    def place_slopes(step, skip):
         for group in range(groups):
             block = group * blocks + step
-            span = pl.ds(pl.multiple_of(block * LANES, LANES), LANES)
-            mask = field_mask(block)
+            mask = sub == group_ref[step_index, pl.ds(block, 1), :] + skip
             m = [sums[group, i : i + 1, :] for i in range(6)]
             u, v, a, b, c = [fields[pl.ds(block * ROWSUB + f, 1), :] for f in range(5)]
             m_x = m[1] - u * m[0]
@@ -479,13 +486,28 @@
                     + sums[group, low + 24 : low + 24 + ROWSUB, :]
                 )
                 rows.append(jnp.sum(jnp.where(own_tile, tint, 0.0), axis=0, keepdims=True))
-            placed = [jnp.where(mask, row, 0.0) for row in rows]
-            entries[span, :] = jnp.concatenate(placed + [pad], 0).T
+            rows = [jnp.where(mask, row, 0.0) for row in rows] + [pad]
+            placed[group * LANES : (group + 1) * LANES, :] = jnp.concatenate(rows, 0).T
+
+    tall = jnp.zeros((LANES, LANES), jnp.float32)
+    for group in range(groups):
+        placed[group * LANES : (group + 1) * LANES, :] = tall
+
+    def clear(index, carry):
+        at = pl.multiple_of(index * LANES, LANES)
+        for one in tables:
+            one[pl.ds(at, LANES), :] = tall
+        return carry
+
+    lax.fori_loop(0, devices * halves, clear, 0)
 
     def backward(index, carry):
-        step = blocks - 1 - index
-        place_slopes(jnp.minimum(step + 2, blocks - 1))
-        sum_slopes(jnp.minimum(step + 1, blocks - 1))
+        newest = blocks - 1 - index
+        later = [jnp.clip(newest + i, 0, blocks - 1) for i in range(4)]
+        step = later[0]
+        scatter(later[3])
+        place_slopes(later[2], jnp.where(newest + 2 < blocks, 0, ROWSUB))
+        sum_slopes(later[1])
         out = []
         for group in range(groups):
             at = pl.multiple_of((group * blocks + step) * LANES, LANES)
@@ -506,38 +528,12 @@
             out.append(tuple(behind))
         return tuple(out)
 
-    lax.fori_loop(0, blocks, backward, ((zeros,) * wide,) * groups)
-    place_slopes(min(1, blocks - 1))
-    sum_slopes(0)
-    place_slopes(0)
-
-    tall = jnp.zeros((LANES, LANES), jnp.float32)
-
-    def clear(index, carry):
-        at = pl.multiple_of(index * LANES, LANES)
-        for one in tables:
-            one[pl.ds(at, LANES), :] = tall
-        return carry
-
-    lax.fori_loop(0, devices * halves, clear, 0)
-
-    def scatter(index, carry):
-        some = entries.at[pl.ds(pl.multiple_of(index * unroll, unroll), unroll)]
-        for turn in range(turns):
-            place = index * turns + turn
-            for q in range(streams):
-                one = tables[q % len(tables)]
-                row = pl.ds(row_lists[q][place], 1)
-                at = turn * streams + q
-                one[row, :] = one[row, :] + some[at : at + 1, :]
-        return carry
-
-    lax.fori_loop(0, total // unroll, scatter, 0)
+    lax.fori_loop(0, blocks + 3, backward, ((zeros,) * wide,) * groups)
 
     loss_rows = jnp.broadcast_to(loss, (ROWSUB, LANES))
     stores = []
     for side, skip in ((1, 0), (1, near // 2), (0, 0), (0, near // 2)):
-        stage = entries if side else w_planes[0]
+        stage = w_planes[side]
 
         def collect(owner, carry, side=side, stage=stage):
             start = pl.multiple_of(owner * planes_out, 8)
@@ -677,7 +673,7 @@
     wide = pixels // LANES
     table_rows = devices * count // ROWSUB
     plane_rows = max(total, devices // 2 * planes_out)
-    extra = max(0, 7 - 2 * wide) if table_rows <= plane_rows else 0
+    copies = max(1, min(6, (26 << 20) // (table_rows * LANES * 4)))
     render = functools.partial(
         pl.pallas_call,
         out_shape=(jax.ShapeDtypeStruct((tiles * 3 * pixels // LANES, LANES), f32),)
@@ -685,7 +681,8 @@
         in_specs=[hbm, vmem, vmem, vmem] + [hbm] * PARTS,
         out_specs=(vmem,) + (hbm,) * PARTS,
         scratch_shapes=[
-            pltpu.VMEM((plane_rows, LANES), f32),
+            pltpu.VMEM((groups * LANES, LANES), f32),
+            pltpu.VMEM((groups * LANES, LANES), f32),
             pltpu.VMEM((total // LANES * ROWSUB, LANES), f32),
             pltpu.VMEM((total, LANES), bf16),
             pltpu.VMEM((groups, LANES, pixels), bf16),
@@ -700,9 +697,8 @@
             pltpu.SemaphoreType.DMA((streams,)),
         ]
         + [pltpu.SMEM((total // streams,), jnp.int32)] * streams
-        + [pltpu.VMEM((table_rows, LANES), f32)]
         + [pltpu.VMEM((plane_rows, LANES), f32)] * (2 * wide)
-        + [pltpu.VMEM((table_rows, LANES), f32)] * extra,
+        + [pltpu.VMEM((table_rows, LANES), f32)] * copies,
         compiler_params=pltpu.CompilerParams(vmem_limit_bytes=60 << 20),
         name="render",
     )

time: 214 us -> 194 us (0.907)
  Pallas kernels: 105 us -> 85.9 us
    pallas_call x2, Pallas kernels: 96.6 us -> 77.1 us  [per_device(): picture, *grads = render(kernel)(*settings, *table)]
  transfers between devices with their start and end apart: 44 -> 44, of which waited for: 25 -> 25; matrix products, arithmetic and copies ran while one was open for 4% -> 5% of each run, Pallas kernels for 0% -> 0%
where the time goes in v5:
time: 194 us; the launch traced here: 193 us
  Pallas kernels  85.9 us (44%)
  waiting for transfers between devices  50.7 us (26%)
  starting transfers between devices  42.5 us (22%)
  local copies, waits for them, and re-layouts  7.83 us (4%)
  other arithmetic  5.06 us (3%)
    pallas_call x2, Pallas kernels, per_device(): picture, *grads = render(kernel)(*settings, *table)  77.1 us
    ppermute x44, waiting for transfers between devices, swap(): return lax.ppermute(values, AXES, pairs)  50.7 us
    ppermute x44, starting transfers between devices, swap(): return lax.ppermute(values, AXES, pairs)  42.5 us
    pallas_call x2, Pallas kernels, per_device(): pl.pallas_call(functools.partial(update_kernel, step=step, project_next=m...  6.88 us
  transfers between devices with their start and end apart: 44, of which 25 were waited for; matrix products, arithmetic and copies ran while one was open for 5% of the time, Pallas kernels for 0%

profile of v5, /device:TPU:0, one launch (start us, length us, event | category | flops | bytes accessed | tf_op | source)
XLA Modules:
  0.0 193.4 jit_solution(13285663720030122414)
XLA Ops:
  0.6 2.0 %project.1 = f32[144,128]{1,0:T(8,128)} custom-call(f32[2,2]{1,0:T(2,128)} %cam_ref.5, f32[55,2048]{1,0:T(8,128)} %param_ref.3), custom_call_target="tpu_custom_call" | custom-call | tf_op jit(solution)/shard_map/project/pallas_call | solution.py:707
  2.6 3.1 %collective-permute-start = (f32[144,128]{1,0:T(8,128)}, f32[144,128]{1,0:T(8,128)S(1)}, u32[]{:S(2)}, u32[]{:S(2)}) collective-permute-start(f32[144,128]{1,0:T(8,128)} %project.1), channel_id=1, source_target_pairs={{0,8},{1,9},{2,10},{3,11},{4,12},{5,13},{6,14},{7,15},{8,0},{9,1},... | collective-permute-start | bytes 221192 | tf_op jit(solution)/shard_map/ppermute | solution.py:579
  5.7 2.6 %collective-permute-start.3 = (f32[144,128]{1,0:T(8,128)}, f32[144,128]{1,0:T(8,128)S(1)}, u32[]{:S(2)}, u32[]{:S(2)}) collective-permute-start(f32[144,128]{1,0:T(8,128)} %project.1), channel_id=1, source_target_pairs={{0,16},{1,17},{2,18},{3,19},{4,20},{5,21},{6,22},{7,23},{8,24},{9,... | collective-permute-start | bytes 221192 | tf_op jit(solution)/shard_map/ppermute | solution.py:579
  13.2 1.8 collective-permute-start.1
  16.3 2.1 %collective-permute-done.1 = f32[288,128]{1,0:T(8,128)S(1)} collective-permute-done((f32[288,128]{1,0:T(8,128)S(1)}, f32[288,128]{1,0:T(8,128)S(1)}, u32[]{:S(2)}, u32[]{:S(2)}) %collective-permute-start.1) | collective-permute-done | bytes 147488 | tf_op jit(solution)/shard_map/ppermute | solution.py:579
  18.4 1.8 collective-permute-start.2
  21.3 1.6 collective-permute-start.6
  23.4 1.8 collective-permute-done.2.refs_1_
  25.2 3.2 %collective-permute-done.6.refs_3_ = f32[576,128]{1,0:T(8,128)S(1)} collective-permute-done((f32[576,128]{1,0:T(8,128)S(1)}, f32[576,128]{1,0:T(8,128)S(1)}, u32[]{:S(2)}, u32[]{:S(2)}) %collective-permute-start.6) | collective-permute-done | bytes 294944 | tf_op jit(solution)/shard_map/ppermute | solution.py:579
  30.7 38.5 %render.2 = (f32[96,128]{1,0:T(8,128)}, f32[608,128]{1,0:T(8,128)}, f32[608,128]{1,0:T(8,128)}, f32[608,128]{1,0:T(8,128)}, f32[608,128]{1,0:T(8,128)}, /*index=...) custom-call(s32[2,16,512]{2,1,0:T(8,128)} %bitcast.18, ...), custom_call_target="tpu_custom_call" | custom-call | tf_op jit(solution)/shard_map/render/pallas_call | solution.py:728
  72.2 1.9 collective-permute-start.18
  75.5 3.7 %collective-permute-done.18 = f32[608,128]{1,0:T(8,128)S(1)} collective-permute-done((f32[608,128]{1,0:T(8,128)S(1)}, f32[608,128]{1,0:T(8,128)S(1)}, u32[]{:S(2)}, u32[]{:S(2)}) %collective-permute-start.18) | collective-permute-done | bytes 311328 | tf_op jit(solution)/shard_map/ppermute | solution.py:579
  79.3 1.8 collective-permute-start.19
  81.1 2.5 %collective-permute-done.13 = f32[608,128]{1,0:T(8,128)S(1)} collective-permute-done((f32[608,128]{1,0:T(8,128)S(1)}, f32[608,128]{1,0:T(8,128)S(1)}, u32[]{:S(2)}, u32[]{:S(2)}) %collective-permute-start.13) | collective-permute-done | bytes 311328 | tf_op jit(solution)/shard_map/ppermute | solution.py:579
  83.7 2.0 %collective-permute-start.14 = (f32[304,128]{1,0:T(8,128)S(1)}, f32[304,128]{1,0:T(8,128)S(1)}, u32[]{:S(2)}, u32[]{:S(2)}) collective-permute-start(f32[304,128]{1,0:T(8,128)S(1)} %slice.65), channel_id=1, source_target_pairs={{0,2},{1,5},{2,0},{3,7},{4,6},{5,1},{6,4},{7,3},{8,10},{9,13},{10,... | collective-permute-start | bytes 466952 | tf_op jit(solution)/shard_map/ppermute | solution.py:579
  85.8 3.5 %collective-permute-start.21 = (f32[152,128]{1,0:T(8,128)S(1)}, f32[152,128]{1,0:T(8,128)S(1)}, u32[]{:S(2)}, u32[]{:S(2)}) collective-permute-start(f32[152,128]{1,0:T(8,128)S(1)} %get-tuple-element.85), channel_id=1, source_target_pairs={{0,24},{1,25},{2,26},{3,27},{4,28},{5,29},{6,30},{7,31},{8,16},{9,... | collective-permute-start | bytes 233480 | tf_op jit(solution)/shard_map/ppermute | solution.py:579
  90.4 1.8 collective-permute-done.21
  92.1 2.9 %collective-permute-done.20 = f32[152,128]{1,0:T(8,128)S(1)} collective-permute-done((f32[152,128]{1,0:T(8,128)S(1)}, f32[152,128]{1,0:T(8,128)S(1)}, u32[]{:S(2)}, u32[]{:S(2)}) %collective-permute-start.20) | collective-permute-done | bytes 77856 | tf_op jit(solution)/shard_map/ppermute | solution.py:579
  96.0 3.5 %update.2 = (f32[55,2048]{1,0:T(8,128)}, f32[55,2048]{1,0:T(8,128)}, f32[55,2048]{1,0:T(8,128)}, f32[144,128]{1,0:T(8,128)}) custom-call(f32[2,2]{1,0:T(2,128)} %cam_ref.5, f32[55,2048]{1,0:T(8,128)} %param_ref.3, f32[55,2048]{1,0:T(8,128)} %first_ref.1, f32[55,2048]{1,0:T(8,128)} %second_ref.1, f32[152,128]{1,0:T(8,128)} %fusion.3.grad_ref.refs_0_), custom_call_target="tpu_custom_call" | custom-call | tf_op jit(solution)/shard_map/update/pallas_call | solution.py:734
  100.0 3.0 %collective-permute-start.25 = (f32[144,128]{1,0:T(8,128)}, f32[144,128]{1,0:T(8,128)S(1)}, u32[]{:S(2)}, u32[]{:S(2)}) collective-permute-start(f32[144,128]{1,0:T(8,128)} %get-tuple-element.57), channel_id=1, source_target_pairs={{0,16},{1,17},{2,18},{3,19},{4,20},{5,21},{6,22},{7,23},{8,24},{9,... | collective-permute-start | bytes 221192 | tf_op jit(solution)/shard_map/ppermute | solution.py:579
  107.1 2.3 %collective-permute-done.26 = f32[144,128]{1,0:T(8,128)S(1)} collective-permute-done((f32[144,128]{1,0:T(8,128)}, f32[144,128]{1,0:T(8,128)S(1)}, u32[]{:S(2)}, u32[]{:S(2)}) %collective-permute-start.26) | collective-permute-done | bytes 73760 | tf_op jit(solution)/shard_map/ppermute | solution.py:579
  110.6 1.8 collective-permute-start.24
  112.4 3.8 %collective-permute-done.27 = f32[288,128]{1,0:T(8,128)S(1)} collective-permute-done((f32[288,128]{1,0:T(8,128)S(1)}, f32[288,128]{1,0:T(8,128)S(1)}, u32[]{:S(2)}, u32[]{:S(2)}) %collective-permute-start.27) | collective-permute-done | bytes 147488 | tf_op jit(solution)/shard_map/ppermute | solution.py:579
  116.2 1.7 collective-permute-start.28
  118.5 4.5 %collective-permute-done.28.refs_3_ = f32[576,128]{1,0:T(8,128)S(1)} collective-permute-done((f32[576,128]{1,0:T(8,128)S(1)}, f32[576,128]{1,0:T(8,128)S(1)}, u32[]{:S(2)}, u32[]{:S(2)}) %collective-permute-start.28) | collective-permute-done | bytes 294944 | tf_op jit(solution)/shard_map/ppermute | solution.py:579
  125.4 38.6 %render.3 = (f32[96,128]{1,0:T(8,128)}, f32[608,128]{1,0:T(8,128)}, f32[608,128]{1,0:T(8,128)}, f32[608,128]{1,0:T(8,128)}, f32[608,128]{1,0:T(8,128)}, /*index=...) custom-call(s32[2,16,512]{2,1,0:T(8,128)} %bitcast.19, ...), custom_call_target="tpu_custom_call" | custom-call | tf_op jit(solution)/shard_map/render/pallas_call | solution.py:728
  170.1 3.7 %collective-permute-done.40 = f32[608,128]{1,0:T(8,128)S(1)} collective-permute-done((f32[608,128]{1,0:T(8,128)S(1)}, f32[608,128]{1,0:T(8,128)S(1)}, u32[]{:S(2)}, u32[]{:S(2)}) %collective-permute-start.40) | collective-permute-done | bytes 311328 | tf_op jit(solution)/shard_map/ppermute | solution.py:579
  174.9 3.6 %collective-permute-done.35 = f32[608,128]{1,0:T(8,128)S(1)} collective-permute-done((f32[608,128]{1,0:T(8,128)S(1)}, f32[608,128]{1,0:T(8,128)S(1)}, u32[]{:S(2)}, u32[]{:S(2)}) %collective-permute-start.35) | collective-permute-done | bytes 311328 | tf_op jit(solution)/shard_map/ppermute | solution.py:579
  181.1 2.7 %collective-permute-done.36 = f32[304,128]{1,0:T(8,128)S(1)} collective-permute-done((f32[304,128]{1,0:T(8,128)S(1)}, f32[304,128]{1,0:T(8,128)S(1)}, u32[]{:S(2)}, u32[]{:S(2)}) %collective-permute-start.36) | collective-permute-done | bytes 155680 | tf_op jit(solution)/shard_map/ppermute | solution.py:579
  184.9 1.8 collective-permute-done.43
  186.7 1.9 collective-permute-done.42
  189.9 3.3 %update.3 = (f32[55,2048]{1,0:T(8,128)}, f32[55,2048]{1,0:T(8,128)}, f32[55,2048]{1,0:T(8,128)}, f32[2]{0:T(128)}) custom-call(f32[2,2]{1,0:T(2,128)} %cam_ref.5, f32[55,2048]{1,0:T(8,128)} %get-tuple-element.54.param_ref, f32[55,2048]{1,0:T(8,128)} %get-tuple-element.55.first_ref, f32[55,2048]{1,0:T(8,128)} %get-tuple-element.56.second_ref, ...), custom_call_target="tpu_custom_call" | custom-call | tf_op jit(solution)/shard_map/update/pallas_call | solution.py:734
  (176 shorter events, 37.2 us)
Async XLA Ops:
  2.6 10.4 %collective-permute-start = (f32[144,128]{1,0:T(8,128)}, f32[144,128]{1,0:T(8,128)S(1)}, u32[]{:S(2)}, u32[]{:S(2)}) collective-permute-start(f32[144,128]{1,0:T(8,128)} %project.1), channel_id=1, source_target_pairs={{0,8},{1,9},{2,10},{3,11},{4,12},{5,13},{6,14},{7,15},{8,0},{9,1},... | collective-permute-start | bytes 221192 | tf_op jit(solution)/shard_map/ppermute | solution.py:579
  5.7 9.3 %collective-permute-start.3 = (f32[144,128]{1,0:T(8,128)}, f32[144,128]{1,0:T(8,128)S(1)}, u32[]{:S(2)}, u32[]{:S(2)}) collective-permute-start(f32[144,128]{1,0:T(8,128)} %project.1), channel_id=1, source_target_pairs={{0,16},{1,17},{2,18},{3,19},{4,20},{5,21},{6,22},{7,23},{8,24},{9,... | collective-permute-start | bytes 221192 | tf_op jit(solution)/shard_map/ppermute | solution.py:579
  8.3 6.8 %collective-permute-start.4 = (f32[144,128]{1,0:T(8,128)}, f32[144,128]{1,0:T(8,128)S(1)}, u32[]{:S(2)}, u32[]{:S(2)}) collective-permute-start(f32[144,128]{1,0:T(8,128)} %project.1), channel_id=1, source_target_pairs={{0,24},{1,25},{2,26},{3,27},{4,28},{5,29},{6,30},{7,31},{8,16},{9,... | collective-permute-start | bytes 221192 | tf_op jit(solution)/shard_map/ppermute | solution.py:579
  15.0 6.2 %collective-permute-start.5 = (f32[288,128]{1,0:T(8,128)S(1)}, f32[288,128]{1,0:T(8,128)S(1)}, u32[]{:S(2)}, u32[]{:S(2)}) collective-permute-start(f32[288,128]{1,0:T(8,128)S(1)} %pad_maximum_fusion.1), channel_id=1, source_target_pairs={{0,2},{1,5},{2,0},{3,7},{4,6},{5,1},{6,4},{7,3},{8,10},{9,13},{10,... | collective-permute-start | bytes 442376 | tf_op jit(solution)/shard_map/ppermute | solution.py:579
  18.4 6.8 %collective-permute-start.2 = (f32[576,128]{1,0:T(8,128)S(1)}, f32[576,128]{1,0:T(8,128)S(1)}, u32[]{:S(2)}, u32[]{:S(2)}) collective-permute-start(f32[576,128]{1,0:T(8,128)S(1)} %constant_dynamic-update-slice_fusion.refs_0_), channel_id=1, source_target_pairs={{0,4},{1,3},{2,6},{3,1},{4,0},{5,7},{6,2},{7,5},{8,12},{9,11},{10,... | collective-permute-start | bytes 884744 | tf_op jit(solution)/shard_map/ppermute | solution.py:579
  21.3 7.1 %collective-permute-start.6 = (f32[576,128]{1,0:T(8,128)S(1)}, f32[576,128]{1,0:T(8,128)S(1)}, u32[]{:S(2)}, u32[]{:S(2)}) collective-permute-start(f32[576,128]{1,0:T(8,128)S(1)} %constant_dynamic-update-slice_fusion.2.refs_2_), channel_id=1, source_target_pairs={{0,4},{1,3},{2,6},{3,1},{4,0},{5,7},{6,2},{7,5},{8,12},{9,11},{10,... | collective-permute-start | bytes 884744 | tf_op jit(solution)/shard_map/ppermute | solution.py:579
  22.9 5.5 %collective-permute-start.7 = (f32[576,128]{1,0:T(8,128)S(1)}, f32[576,128]{1,0:T(8,128)S(1)}, u32[]{:S(2)}, u32[]{:S(2)}) collective-permute-start(f32[576,128]{1,0:T(8,128)S(1)} %constant_dynamic-update-slice_fusion.refs_0_), channel_id=1, source_target_pairs={{0,1},{1,0},{2,3},{3,2},{4,5},{5,4},{6,7},{7,6},{8,9},{9,8},{10,11... | collective-permute-start | bytes 884744 | tf_op jit(solution)/shard_map/ppermute | solution.py:579
  22.9 5.5 %collective-permute-start.9 = (f32[576,128]{1,0:T(8,128)S(1)}, f32[576,128]{1,0:T(8,128)S(1)}, u32[]{:S(2)}, u32[]{:S(2)}) collective-permute-start(f32[576,128]{1,0:T(8,128)S(1)} %constant_dynamic-update-slice_fusion.2.refs_2_), channel_id=1, source_target_pairs={{0,1},{1,0},{2,3},{3,2},{4,5},{5,4},{6,7},{7,6},{8,9},{9,8},{10,11... | collective-permute-start | bytes 884744 | tf_op jit(solution)/shard_map/ppermute | solution.py:579
  69.8 5.7 %collective-permute-start.16 = (f32[608,128]{1,0:T(8,128)}, f32[608,128]{1,0:T(8,128)S(1)}, u32[]{:S(2)}, u32[]{:S(2)}) collective-permute-start(f32[608,128]{1,0:T(8,128)} %get-tuple-element.51), channel_id=1, source_target_pairs={{0,1},{1,0},{2,3},{3,2},{4,5},{5,4},{6,7},{7,6},{8,9},{9,8},{10,11... | collective-permute-start | bytes 933896 | tf_op jit(solution)/shard_map/ppermute | solution.py:579
  72.2 7.0 %collective-permute-start.18 = (f32[608,128]{1,0:T(8,128)S(1)}, f32[608,128]{1,0:T(8,128)S(1)}, u32[]{:S(2)}, u32[]{:S(2)}) collective-permute-start(f32[608,128]{1,0:T(8,128)S(1)} %add.143), channel_id=1, source_target_pairs={{0,4},{1,3},{2,6},{3,1},{4,0},{5,7},{6,2},{7,5},{8,12},{9,11},{10,... | collective-permute-start | bytes 933896 | tf_op jit(solution)/shard_map/ppermute | solution.py:579
  74.1 7.0 %collective-permute-start.11 = (f32[608,128]{1,0:T(8,128)S(1)}, f32[608,128]{1,0:T(8,128)S(1)}, u32[]{:S(2)}, u32[]{:S(2)}) collective-permute-start(f32[608,128]{1,0:T(8,128)S(1)} %copy-done.29), channel_id=1, source_target_pairs={{0,1},{1,0},{2,3},{3,2},{4,5},{5,4},{6,7},{7,6},{8,9},{9,8},{10,11... | collective-permute-start | bytes 933896 | tf_op jit(solution)/shard_map/ppermute | solution.py:579
  74.2 9.5 %collective-permute-start.13 = (f32[608,128]{1,0:T(8,128)S(1)}, f32[608,128]{1,0:T(8,128)S(1)}, u32[]{:S(2)}, u32[]{:S(2)}) collective-permute-start(f32[608,128]{1,0:T(8,128)S(1)} %add.138), channel_id=1, source_target_pairs={{0,4},{1,3},{2,6},{3,1},{4,0},{5,7},{6,2},{7,5},{8,12},{9,11},{10,... | collective-permute-start | bytes 933896 | tf_op jit(solution)/shard_map/ppermute | solution.py:579
  79.3 6.5 %collective-permute-start.19 = (f32[304,128]{1,0:T(8,128)S(1)}, f32[304,128]{1,0:T(8,128)S(1)}, u32[]{:S(2)}, u32[]{:S(2)}) collective-permute-start(f32[304,128]{1,0:T(8,128)S(1)} %slice.69), channel_id=1, source_target_pairs={{0,2},{1,5},{2,0},{3,7},{4,6},{5,1},{6,4},{7,3},{8,10},{9,13},{10,... | collective-permute-start | bytes 466952 | tf_op jit(solution)/shard_map/ppermute | solution.py:579
  83.7 5.6 %collective-permute-start.14 = (f32[304,128]{1,0:T(8,128)S(1)}, f32[304,128]{1,0:T(8,128)S(1)}, u32[]{:S(2)}, u32[]{:S(2)}) collective-permute-start(f32[304,128]{1,0:T(8,128)S(1)} %slice.65), channel_id=1, source_target_pairs={{0,2},{1,5},{2,0},{3,7},{4,6},{5,1},{6,4},{7,3},{8,10},{9,13},{10,... | collective-permute-start | bytes 466952 | tf_op jit(solution)/shard_map/ppermute | solution.py:579
  85.8 6.4 %collective-permute-start.21 = (f32[152,128]{1,0:T(8,128)S(1)}, f32[152,128]{1,0:T(8,128)S(1)}, u32[]{:S(2)}, u32[]{:S(2)}) collective-permute-start(f32[152,128]{1,0:T(8,128)S(1)} %get-tuple-element.85), channel_id=1, source_target_pairs={{0,24},{1,25},{2,26},{3,27},{4,28},{5,29},{6,30},{7,31},{8,16},{9,... | collective-permute-start | bytes 233480 | tf_op jit(solution)/shard_map/ppermute | solution.py:579
  89.3 5.7 %collective-permute-start.20 = (f32[152,128]{1,0:T(8,128)S(1)}, f32[152,128]{1,0:T(8,128)S(1)}, u32[]{:S(2)}, u32[]{:S(2)}) collective-permute-start(f32[152,128]{1,0:T(8,128)S(1)} %get-tuple-element.84), channel_id=1, source_target_pairs={{0,16},{1,17},{2,18},{3,19},{4,20},{5,21},{6,22},{7,23},{8,24},{9,... | collective-permute-start | bytes 233480 | tf_op jit(solution)/shard_map/ppermute | solution.py:579
  89.3 6.1 %collective-permute-start.15 = (f32[152,128]{1,0:T(8,128)S(1)}, f32[152,128]{1,0:T(8,128)S(1)}, u32[]{:S(2)}, u32[]{:S(2)}) collective-permute-start(f32[152,128]{1,0:T(8,128)S(1)} %slice.67), channel_id=1, source_target_pairs={{0,8},{1,9},{2,10},{3,11},{4,12},{5,13},{6,14},{7,15},{8,0},{9,1},... | collective-permute-start | bytes 233480 | tf_op jit(solution)/shard_map/ppermute | solution.py:579
  100.0 7.1 %collective-permute-start.25 = (f32[144,128]{1,0:T(8,128)}, f32[144,128]{1,0:T(8,128)S(1)}, u32[]{:S(2)}, u32[]{:S(2)}) collective-permute-start(f32[144,128]{1,0:T(8,128)} %get-tuple-element.57), channel_id=1, source_target_pairs={{0,16},{1,17},{2,18},{3,19},{4,20},{5,21},{6,22},{7,23},{8,24},{9,... | collective-permute-start | bytes 221192 | tf_op jit(solution)/shard_map/ppermute | solution.py:579
  103.0 6.4 %collective-permute-start.26 = (f32[144,128]{1,0:T(8,128)}, f32[144,128]{1,0:T(8,128)S(1)}, u32[]{:S(2)}, u32[]{:S(2)}) collective-permute-start(f32[144,128]{1,0:T(8,128)} %get-tuple-element.57), channel_id=1, source_target_pairs={{0,24},{1,25},{2,26},{3,27},{4,28},{5,29},{6,30},{7,31},{8,16},{9,... | collective-permute-start | bytes 221192 | tf_op jit(solution)/shard_map/ppermute | solution.py:579
  105.0 5.5 %collective-permute-start.23 = (f32[288,128]{1,0:T(8,128)S(1)}, f32[288,128]{1,0:T(8,128)S(1)}, u32[]{:S(2)}, u32[]{:S(2)}) collective-permute-start(f32[288,128]{1,0:T(8,128)S(1)} %pad_maximum_fusion.2), channel_id=1, source_target_pairs={{0,2},{1,5},{2,0},{3,7},{4,6},{5,1},{6,4},{7,3},{8,10},{9,13},{10,... | collective-permute-start | bytes 442376 | tf_op jit(solution)/shard_map/ppermute | solution.py:579
  109.4 6.8 %collective-permute-start.27 = (f32[288,128]{1,0:T(8,128)S(1)}, f32[288,128]{1,0:T(8,128)S(1)}, u32[]{:S(2)}, u32[]{:S(2)}) collective-permute-start(f32[288,128]{1,0:T(8,128)S(1)} %pad_maximum_fusion.3), channel_id=1, source_target_pairs={{0,2},{1,5},{2,0},{3,7},{4,6},{5,1},{6,4},{7,3},{8,10},{9,13},{10,... | collective-permute-start | bytes 442376 | tf_op jit(solution)/shard_map/ppermute | solution.py:579
  110.6 7.8 %collective-permute-start.24 = (f32[576,128]{1,0:T(8,128)S(1)}, f32[576,128]{1,0:T(8,128)S(1)}, u32[]{:S(2)}, u32[]{:S(2)}) collective-permute-start(f32[576,128]{1,0:T(8,128)S(1)} %constant_dynamic-update-slice_fusion.5.refs_0_), channel_id=1, source_target_pairs={{0,4},{1,3},{2,6},{3,1},{4,0},{5,7},{6,2},{7,5},{8,12},{9,11},{10,... | collective-permute-start | bytes 884744 | tf_op jit(solution)/shard_map/ppermute | solution.py:579
  116.2 6.8 %collective-permute-start.28 = (f32[576,128]{1,0:T(8,128)S(1)}, f32[576,128]{1,0:T(8,128)S(1)}, u32[]{:S(2)}, u32[]{:S(2)}) collective-permute-start(f32[576,128]{1,0:T(8,128)S(1)} %constant_dynamic-update-slice_fusion.7.refs_2_), channel_id=1, source_target_pairs={{0,4},{1,3},{2,6},{3,1},{4,0},{5,7},{6,2},{7,5},{8,12},{9,11},{10,... | collective-permute-start | bytes 884744 | tf_op jit(solution)/shard_map/ppermute | solution.py:579
  164.5 5.6 %collective-permute-start.38 = (f32[608,128]{1,0:T(8,128)}, f32[608,128]{1,0:T(8,128)S(1)}, u32[]{:S(2)}, u32[]{:S(2)}) collective-permute-start(f32[608,128]{1,0:T(8,128)} %get-tuple-element.68), channel_id=1, source_target_pairs={{0,1},{1,0},{2,3},{3,2},{4,5},{5,4},{6,7},{7,6},{8,9},{9,8},{10,11... | collective-permute-start | bytes 933896 | tf_op jit(solution)/shard_map/ppermute | solution.py:579
  166.9 7.0 %collective-permute-start.40 = (f32[608,128]{1,0:T(8,128)S(1)}, f32[608,128]{1,0:T(8,128)S(1)}, u32[]{:S(2)}, u32[]{:S(2)}) collective-permute-start(f32[608,128]{1,0:T(8,128)S(1)} %add.154), channel_id=1, source_target_pairs={{0,4},{1,3},{2,6},{3,1},{4,0},{5,7},{6,2},{7,5},{8,12},{9,11},{10,... | collective-permute-start | bytes 933896 | tf_op jit(solution)/shard_map/ppermute | solution.py:579
  168.5 6.5 %collective-permute-start.33 = (f32[608,128]{1,0:T(8,128)S(1)}, f32[608,128]{1,0:T(8,128)S(1)}, u32[]{:S(2)}, u32[]{:S(2)}) collective-permute-start(f32[608,128]{1,0:T(8,128)S(1)} %copy-done.28), channel_id=1, source_target_pairs={{0,1},{1,0},{2,3},{3,2},{4,5},{5,4},{6,7},{7,6},{8,9},{9,8},{10,11... | collective-permute-start | bytes 933896 | tf_op jit(solution)/shard_map/ppermute | solution.py:579
  168.6 10.0 %collective-permute-start.35 = (f32[608,128]{1,0:T(8,128)S(1)}, f32[608,128]{1,0:T(8,128)S(1)}, u32[]{:S(2)}, u32[]{:S(2)}) collective-permute-start(f32[608,128]{1,0:T(8,128)S(1)} %add.149), channel_id=1, source_target_pairs={{0,4},{1,3},{2,6},{3,1},{4,0},{5,7},{6,2},{7,5},{8,12},{9,11},{10,... | collective-permute-start | bytes 933896 | tf_op jit(solution)/shard_map/ppermute | solution.py:579
  174.0 5.6 %collective-permute-start.41 = (f32[304,128]{1,0:T(8,128)S(1)}, f32[304,128]{1,0:T(8,128)S(1)}, u32[]{:S(2)}, u32[]{:S(2)}) collective-permute-start(f32[304,128]{1,0:T(8,128)S(1)} %slice.77), channel_id=1, source_target_pairs={{0,2},{1,5},{2,0},{3,7},{4,6},{5,1},{6,4},{7,3},{8,10},{9,13},{10,... | collective-permute-start | bytes 466952 | tf_op jit(solution)/shard_map/ppermute | solution.py:579
  178.6 5.3 %collective-permute-start.36 = (f32[304,128]{1,0:T(8,128)S(1)}, f32[304,128]{1,0:T(8,128)S(1)}, u32[]{:S(2)}, u32[]{:S(2)}) collective-permute-start(f32[304,128]{1,0:T(8,128)S(1)} %slice.73), channel_id=1, source_target_pairs={{0,2},{1,5},{2,0},{3,7},{4,6},{5,1},{6,4},{7,3},{8,10},{9,13},{10,... | collective-permute-start | bytes 466952 | tf_op jit(solution)/shard_map/ppermute | solution.py:579
  179.6 7.1 %collective-permute-start.43 = (f32[152,128]{1,0:T(8,128)S(1)}, f32[152,128]{1,0:T(8,128)S(1)}, u32[]{:S(2)}, u32[]{:S(2)}) collective-permute-start(f32[152,128]{1,0:T(8,128)S(1)} %get-tuple-element.83), channel_id=1, source_target_pairs={{0,24},{1,25},{2,26},{3,27},{4,28},{5,29},{6,30},{7,31},{8,16},{9,... | collective-permute-start | bytes 233480 | tf_op jit(solution)/shard_map/ppermute | solution.py:579
  181.1 7.5 %collective-permute-start.42 = (f32[152,128]{1,0:T(8,128)S(1)}, f32[152,128]{1,0:T(8,128)S(1)}, u32[]{:S(2)}, u32[]{:S(2)}) collective-permute-start(f32[152,128]{1,0:T(8,128)S(1)} %get-tuple-element.82), channel_id=1, source_target_pairs={{0,16},{1,17},{2,18},{3,19},{4,20},{5,21},{6,22},{7,23},{8,24},{9,... | collective-permute-start | bytes 233480 | tf_op jit(solution)/shard_map/ppermute | solution.py:579
  183.9 5.3 %collective-permute-start.37 = (f32[152,128]{1,0:T(8,128)S(1)}, f32[152,128]{1,0:T(8,128)S(1)}, u32[]{:S(2)}, u32[]{:S(2)}) collective-permute-start(f32[152,128]{1,0:T(8,128)S(1)} %slice.75), channel_id=1, source_target_pairs={{0,8},{1,9},{2,10},{3,11},{4,12},{5,13},{6,14},{7,15},{8,0},{9,1},... | collective-permute-start | bytes 233480 | tf_op jit(solution)/shard_map/ppermute | solution.py:579
  (42 other events, 154.2 us)

commit v6 on v5

--- a/solution.py
+++ b/solution.py
@@ -271,6 +271,16 @@
     for copy in loads + lists:
         copy.start()
 
+    tall = jnp.zeros((LANES, LANES), jnp.float32)
+
+    def clear(some, index, carry):
+        at = pl.multiple_of(index * LANES, LANES)
+        for one in some:
+            one[pl.ds(at, LANES), :] = tall
+        return carry
+
+    lax.fori_loop(0, devices * halves, functools.partial(clear, tables[1:]), 0)
+
     pad = jnp.zeros((LANES - FIELDS * ROWSUB, LANES), jnp.float32)
 
     for side in range(2):
@@ -489,17 +499,10 @@
             rows = [jnp.where(mask, row, 0.0) for row in rows] + [pad]
             placed[group * LANES : (group + 1) * LANES, :] = jnp.concatenate(rows, 0).T
 
-    tall = jnp.zeros((LANES, LANES), jnp.float32)
     for group in range(groups):
         placed[group * LANES : (group + 1) * LANES, :] = tall
 
-    def clear(index, carry):
-        at = pl.multiple_of(index * LANES, LANES)
-        for one in tables:
-            one[pl.ds(at, LANES), :] = tall
-        return carry
-
-    lax.fori_loop(0, devices * halves, clear, 0)
+    lax.fori_loop(0, devices * halves, functools.partial(clear, tables[:1]), 0)
 
     def backward(index, carry):
         newest = blocks - 1 - index
@@ -673,7 +676,7 @@
     wide = pixels // LANES
     table_rows = devices * count // ROWSUB
     plane_rows = max(total, devices // 2 * planes_out)
-    copies = max(1, min(6, (26 << 20) // (table_rows * LANES * 4)))
+    copies = max(1, min(5, (26 << 20) // (table_rows * LANES * 4)))
     render = functools.partial(
         pl.pallas_call,
         out_shape=(jax.ShapeDtypeStruct((tiles * 3 * pixels // LANES, LANES), f32),)
@@ -699,7 +702,7 @@
         + [pltpu.SMEM((total // streams,), jnp.int32)] * streams
         + [pltpu.VMEM((plane_rows, LANES), f32)] * (2 * wide)
         + [pltpu.VMEM((table_rows, LANES), f32)] * copies,
-        compiler_params=pltpu.CompilerParams(vmem_limit_bytes=60 << 20),
+        compiler_params=pltpu.CompilerParams(vmem_limit_bytes=48 << 20),
         name="render",
     )
 

time: 194 us -> 186 us (0.959)
  local copies, waits for them, and re-layouts: 7.83 us -> 4.41 us
  Pallas kernels: 85.9 us -> 82.6 us
  starting transfers between devices: 42.5 us -> 45 us
  other arithmetic: 5.06 us -> 2.99 us
    pallas_call x2, Pallas kernels: 77.1 us -> 73.8 us  [per_device(): picture, *grads = render(kernel)(*settings, *table)]
    ppermute x44, starting transfers between devices: 42.5 us -> 45 us  [swap(): return lax.ppermute(values, AXES, pairs)]
    add x4, other arithmetic: 2.21 us -> 0.13 us  [fold(): high = own[2 * chunk + 1] + swap(other[2 * chunk + 1], devices, 1)]
  transfers between devices with their start and end apart: 44 -> 44, of which waited for: 25 -> 25; matrix products, arithmetic and copies ran while one was open for 5% -> 2% of each run, Pallas kernels for 0% -> 0%
where the time goes in v6:
time: 186 us; the launch traced here: 185 us
  Pallas kernels  82.6 us (44%)
  waiting for transfers between devices  49.2 us (26%)
  starting transfers between devices  45 us (24%)
  local copies, waits for them, and re-layouts  4.41 us (2%)
  other arithmetic  2.99 us (2%)
    pallas_call x2, Pallas kernels, per_device(): picture, *grads = render(kernel)(*settings, *table)  73.8 us
    ppermute x44, waiting for transfers between devices, swap(): return lax.ppermute(values, AXES, pairs)  49.2 us
    ppermute x44, starting transfers between devices, swap(): return lax.ppermute(values, AXES, pairs)  45 us
    pallas_call x2, Pallas kernels, per_device(): pl.pallas_call(functools.partial(update_kernel, step=step, project_next=m...  6.88 us
  transfers between devices with their start and end apart: 44, of which 25 were waited for; matrix products, arithmetic and copies ran while one was open for 2% of the time, Pallas kernels for 0%

profile of v6, /device:TPU:0, one launch (start us, length us, event | category | flops | bytes accessed | tf_op | source)
XLA Modules:
  0.0 185.4 jit_solution(12980536202518820269)
XLA Ops:
  0.6 2.0 %project.1 = f32[144,128]{1,0:T(8,128)} custom-call(f32[2,2]{1,0:T(2,128)} %cam_ref.5, f32[55,2048]{1,0:T(8,128)} %param_ref.3), custom_call_target="tpu_custom_call" | custom-call | tf_op jit(solution)/shard_map/project/pallas_call | solution.py:710
  2.6 3.1 %collective-permute-start = (f32[144,128]{1,0:T(8,128)}, f32[144,128]{1,0:T(8,128)S(1)}, u32[]{:S(2)}, u32[]{:S(2)}) collective-permute-start(f32[144,128]{1,0:T(8,128)} %project.1), channel_id=1, source_target_pairs={{0,8},{1,9},{2,10},{3,11},{4,12},{5,13},{6,14},{7,15},{8,0},{9,1},... | collective-permute-start | bytes 221192 | tf_op jit(solution)/shard_map/ppermute | solution.py:582
  5.7 2.6 %collective-permute-start.3 = (f32[144,128]{1,0:T(8,128)}, f32[144,128]{1,0:T(8,128)S(1)}, u32[]{:S(2)}, u32[]{:S(2)}) collective-permute-start(f32[144,128]{1,0:T(8,128)} %project.1), channel_id=1, source_target_pairs={{0,16},{1,17},{2,18},{3,19},{4,20},{5,21},{6,22},{7,23},{8,24},{9,... | collective-permute-start | bytes 221192 | tf_op jit(solution)/shard_map/ppermute | solution.py:582
  12.2 1.8 collective-permute-start.1
  17.4 1.8 collective-permute-start.2
  19.2 2.3 %collective-permute-done.5 = f32[288,128]{1,0:T(8,128)S(1)} collective-permute-done((f32[288,128]{1,0:T(8,128)S(1)}, f32[288,128]{1,0:T(8,128)S(1)}, u32[]{:S(2)}, u32[]{:S(2)}) %collective-permute-start.5) | collective-permute-done | bytes 147488 | tf_op jit(solution)/shard_map/ppermute | solution.py:582
  21.5 1.6 collective-permute-start.6
  24.2 4.1 %collective-permute-done.6.refs_3_ = f32[576,128]{1,0:T(8,128)S(1)} collective-permute-done((f32[576,128]{1,0:T(8,128)S(1)}, f32[576,128]{1,0:T(8,128)S(1)}, u32[]{:S(2)}, u32[]{:S(2)}) %collective-permute-start.6) | collective-permute-done | bytes 294944 | tf_op jit(solution)/shard_map/ppermute | solution.py:582
  29.9 36.8 %render.2 = (f32[96,128]{1,0:T(8,128)S(1)}, f32[608,128]{1,0:T(8,128)S(1)}, f32[608,128]{1,0:T(8,128)S(1)}, f32[608,128]{1,0:T(8,128)S(1)}, f32[608,128]{1,0:T(8...) custom-call(s32[2,16,512]{2,1,0:T(8,128)S(1)} %bitcast.16, ...), custom_call_target="tpu_custom_call" | custom-call | tf_op jit(solution)/shard_map/render/pallas_call | solution.py:731
  68.5 1.6 collective-permute-start.18
  71.5 3.9 %collective-permute-done.18 = f32[608,128]{1,0:T(8,128)S(1)} collective-permute-done((f32[608,128]{1,0:T(8,128)S(1)}, f32[608,128]{1,0:T(8,128)S(1)}, u32[]{:S(2)}, u32[]{:S(2)}) %collective-permute-start.18) | collective-permute-done | bytes 311328 | tf_op jit(solution)/shard_map/ppermute | solution.py:582
  77.0 3.0 %collective-permute-done.13 = f32[608,128]{1,0:T(8,128)S(1)} collective-permute-done((f32[608,128]{1,0:T(8,128)S(1)}, f32[608,128]{1,0:T(8,128)S(1)}, u32[]{:S(2)}, u32[]{:S(2)}) %collective-permute-start.13) | collective-permute-done | bytes 311328 | tf_op jit(solution)/shard_map/ppermute | solution.py:582
  80.1 1.6 collective-permute-start.14
  81.7 3.1 %collective-permute-start.21 = (f32[152,128]{1,0:T(8,128)S(1)}, f32[152,128]{1,0:T(8,128)S(1)}, u32[]{:S(2)}, u32[]{:S(2)}) collective-permute-start(f32[152,128]{1,0:T(8,128)S(1)} %get-tuple-element.85), channel_id=1, source_target_pairs={{0,24},{1,25},{2,26},{3,27},{4,28},{5,29},{6,30},{7,31},{8,16},{9,... | collective-permute-start | bytes 233480 | tf_op jit(solution)/shard_map/ppermute | solution.py:582
  88.0 3.0 %collective-permute-done.20 = f32[152,128]{1,0:T(8,128)S(1)} collective-permute-done((f32[152,128]{1,0:T(8,128)S(1)}, f32[152,128]{1,0:T(8,128)S(1)}, u32[]{:S(2)}, u32[]{:S(2)}) %collective-permute-start.20) | collective-permute-done | bytes 77856 | tf_op jit(solution)/shard_map/ppermute | solution.py:582
  91.6 3.5 %update.2 = (f32[55,2048]{1,0:T(8,128)}, f32[55,2048]{1,0:T(8,128)}, f32[55,2048]{1,0:T(8,128)}, f32[144,128]{1,0:T(8,128)}) custom-call(f32[2,2]{1,0:T(2,128)} %cam_ref.5, f32[55,2048]{1,0:T(8,128)} %param_ref.3, f32[55,2048]{1,0:T(8,128)} %first_ref.1, f32[55,2048]{1,0:T(8,128)} %second_ref.1, f32[152,128]{1,0:T(8,128)} %fusion.3.grad_ref.refs_0_), custom_call_target="tpu_custom_call" | custom-call | tf_op jit(solution)/shard_map/update/pallas_call | solution.py:737
  95.3 3.1 %collective-permute-start.25 = (f32[144,128]{1,0:T(8,128)}, f32[144,128]{1,0:T(8,128)S(1)}, u32[]{:S(2)}, u32[]{:S(2)}) collective-permute-start(f32[144,128]{1,0:T(8,128)} %get-tuple-element.57), channel_id=1, source_target_pairs={{0,16},{1,17},{2,18},{3,19},{4,20},{5,21},{6,22},{7,23},{8,24},{9,... | collective-permute-start | bytes 221192 | tf_op jit(solution)/shard_map/ppermute | solution.py:582
  100.6 1.9 %collective-permute-start.23 = (f32[288,128]{1,0:T(8,128)S(1)}, f32[288,128]{1,0:T(8,128)S(1)}, u32[]{:S(2)}, u32[]{:S(2)}) collective-permute-start(f32[288,128]{1,0:T(8,128)S(1)} %pad_maximum_fusion.2), channel_id=1, source_target_pairs={{0,2},{1,5},{2,0},{3,7},{4,6},{5,1},{6,4},{7,3},{8,10},{9,13},{10,... | collective-permute-start | bytes 442376 | tf_op jit(solution)/shard_map/ppermute | solution.py:582
  102.9 1.9 %collective-permute-done.26 = f32[144,128]{1,0:T(8,128)S(1)} collective-permute-done((f32[144,128]{1,0:T(8,128)}, f32[144,128]{1,0:T(8,128)S(1)}, u32[]{:S(2)}, u32[]{:S(2)}) %collective-permute-start.26) | collective-permute-done | bytes 73760 | tf_op jit(solution)/shard_map/ppermute | solution.py:582
  104.8 1.8 collective-permute-start.27
  108.2 3.4 %collective-permute-done.27 = f32[288,128]{1,0:T(8,128)S(1)} collective-permute-done((f32[288,128]{1,0:T(8,128)S(1)}, f32[288,128]{1,0:T(8,128)S(1)}, u32[]{:S(2)}, u32[]{:S(2)}) %collective-permute-start.27) | collective-permute-done | bytes 147488 | tf_op jit(solution)/shard_map/ppermute | solution.py:582
  111.6 1.7 collective-permute-start.28
  113.9 4.5 %collective-permute-done.28.refs_3_ = f32[576,128]{1,0:T(8,128)S(1)} collective-permute-done((f32[576,128]{1,0:T(8,128)S(1)}, f32[576,128]{1,0:T(8,128)S(1)}, u32[]{:S(2)}, u32[]{:S(2)}) %collective-permute-start.28) | collective-permute-done | bytes 294944 | tf_op jit(solution)/shard_map/ppermute | solution.py:582
  120.0 37.0 %render.3 = (f32[96,128]{1,0:T(8,128)S(1)}, f32[608,128]{1,0:T(8,128)S(1)}, f32[608,128]{1,0:T(8,128)S(1)}, f32[608,128]{1,0:T(8,128)S(1)}, f32[608,128]{1,0:T(8...) custom-call(s32[2,16,512]{2,1,0:T(8,128)S(1)} %bitcast.17, ...), custom_call_target="tpu_custom_call" | custom-call | tf_op jit(solution)/shard_map/render/pallas_call | solution.py:731
  158.7 1.6 collective-permute-start.40
  161.9 3.7 %collective-permute-done.40 = f32[608,128]{1,0:T(8,128)S(1)} collective-permute-done((f32[608,128]{1,0:T(8,128)S(1)}, f32[608,128]{1,0:T(8,128)S(1)}, u32[]{:S(2)}, u32[]{:S(2)}) %collective-permute-start.40) | collective-permute-done | bytes 311328 | tf_op jit(solution)/shard_map/ppermute | solution.py:582
  165.7 1.7 collective-permute-start.41
  167.4 2.8 %collective-permute-done.35 = f32[608,128]{1,0:T(8,128)S(1)} collective-permute-done((f32[608,128]{1,0:T(8,128)S(1)}, f32[608,128]{1,0:T(8,128)S(1)}, u32[]{:S(2)}, u32[]{:S(2)}) %collective-permute-start.35) | collective-permute-done | bytes 311328 | tf_op jit(solution)/shard_map/ppermute | solution.py:582
  170.3 1.6 collective-permute-start.36
  173.3 2.3 %collective-permute-done.36 = f32[304,128]{1,0:T(8,128)S(1)} collective-permute-done((f32[304,128]{1,0:T(8,128)S(1)}, f32[304,128]{1,0:T(8,128)S(1)}, u32[]{:S(2)}, u32[]{:S(2)}) %collective-permute-start.36) | collective-permute-done | bytes 155680 | tf_op jit(solution)/shard_map/ppermute | solution.py:582
  178.6 2.1 %collective-permute-done.42 = f32[152,128]{1,0:T(8,128)S(1)} collective-permute-done((f32[152,128]{1,0:T(8,128)S(1)}, f32[152,128]{1,0:T(8,128)S(1)}, u32[]{:S(2)}, u32[]{:S(2)}) %collective-permute-start.42) | collective-permute-done | bytes 77856 | tf_op jit(solution)/shard_map/ppermute | solution.py:582
  181.9 3.3 %update.3 = (f32[55,2048]{1,0:T(8,128)}, f32[55,2048]{1,0:T(8,128)}, f32[55,2048]{1,0:T(8,128)}, f32[2]{0:T(128)}) custom-call(f32[2,2]{1,0:T(2,128)} %cam_ref.5, f32[55,2048]{1,0:T(8,128)} %get-tuple-element.54.param_ref, f32[55,2048]{1,0:T(8,128)} %get-tuple-element.55.first_ref, f32[55,2048]{1,0:T(8,128)} %get-tuple-element.56.second_ref, ...), custom_call_target="tpu_custom_call" | custom-call | tf_op jit(solution)/shard_map/update/pallas_call | solution.py:737
  (124 shorter events, 33.8 us)
Async XLA Ops:
  2.6 8.7 %collective-permute-start = (f32[144,128]{1,0:T(8,128)}, f32[144,128]{1,0:T(8,128)S(1)}, u32[]{:S(2)}, u32[]{:S(2)}) collective-permute-start(f32[144,128]{1,0:T(8,128)} %project.1), channel_id=1, source_target_pairs={{0,8},{1,9},{2,10},{3,11},{4,12},{5,13},{6,14},{7,15},{8,0},{9,1},... | collective-permute-start | bytes 221192 | tf_op jit(solution)/shard_map/ppermute | solution.py:582
  5.7 8.3 %collective-permute-start.3 = (f32[144,128]{1,0:T(8,128)}, f32[144,128]{1,0:T(8,128)S(1)}, u32[]{:S(2)}, u32[]{:S(2)}) collective-permute-start(f32[144,128]{1,0:T(8,128)} %project.1), channel_id=1, source_target_pairs={{0,16},{1,17},{2,18},{3,19},{4,20},{5,21},{6,22},{7,23},{8,24},{9,... | collective-permute-start | bytes 221192 | tf_op jit(solution)/shard_map/ppermute | solution.py:582
  8.3 6.5 %collective-permute-start.4 = (f32[144,128]{1,0:T(8,128)}, f32[144,128]{1,0:T(8,128)S(1)}, u32[]{:S(2)}, u32[]{:S(2)}) collective-permute-start(f32[144,128]{1,0:T(8,128)} %project.1), channel_id=1, source_target_pairs={{0,24},{1,25},{2,26},{3,27},{4,28},{5,29},{6,30},{7,31},{8,16},{9,... | collective-permute-start | bytes 221192 | tf_op jit(solution)/shard_map/ppermute | solution.py:582
  12.2 5.2 %collective-permute-start.1 = (f32[288,128]{1,0:T(8,128)S(1)}, f32[288,128]{1,0:T(8,128)S(1)}, u32[]{:S(2)}, u32[]{:S(2)}) collective-permute-start(f32[288,128]{1,0:T(8,128)S(1)} %pad_maximum_fusion), channel_id=1, source_target_pairs={{0,2},{1,5},{2,0},{3,7},{4,6},{5,1},{6,4},{7,3},{8,10},{9,13},{10,... | collective-permute-start | bytes 442376 | tf_op jit(solution)/shard_map/ppermute | solution.py:582
  14.7 6.8 %collective-permute-start.5 = (f32[288,128]{1,0:T(8,128)S(1)}, f32[288,128]{1,0:T(8,128)S(1)}, u32[]{:S(2)}, u32[]{:S(2)}) collective-permute-start(f32[288,128]{1,0:T(8,128)S(1)} %pad_maximum_fusion.1), channel_id=1, source_target_pairs={{0,2},{1,5},{2,0},{3,7},{4,6},{5,1},{6,4},{7,3},{8,10},{9,13},{10,... | collective-permute-start | bytes 442376 | tf_op jit(solution)/shard_map/ppermute | solution.py:582
  17.4 6.8 %collective-permute-start.2 = (f32[576,128]{1,0:T(8,128)S(1)}, f32[576,128]{1,0:T(8,128)S(1)}, u32[]{:S(2)}, u32[]{:S(2)}) collective-permute-start(f32[576,128]{1,0:T(8,128)S(1)} %constant_dynamic-update-slice_fusion.refs_0_), channel_id=1, source_target_pairs={{0,4},{1,3},{2,6},{3,1},{4,0},{5,7},{6,2},{7,5},{8,12},{9,11},{10,... | collective-permute-start | bytes 884744 | tf_op jit(solution)/shard_map/ppermute | solution.py:582
  21.5 6.8 %collective-permute-start.6 = (f32[576,128]{1,0:T(8,128)S(1)}, f32[576,128]{1,0:T(8,128)S(1)}, u32[]{:S(2)}, u32[]{:S(2)}) collective-permute-start(f32[576,128]{1,0:T(8,128)S(1)} %constant_dynamic-update-slice_fusion.2.refs_2_), channel_id=1, source_target_pairs={{0,4},{1,3},{2,6},{3,1},{4,0},{5,7},{6,2},{7,5},{8,12},{9,11},{10,... | collective-permute-start | bytes 884744 | tf_op jit(solution)/shard_map/ppermute | solution.py:582
  23.1 5.2 %collective-permute-start.7 = (f32[576,128]{1,0:T(8,128)S(1)}, f32[576,128]{1,0:T(8,128)S(1)}, u32[]{:S(2)}, u32[]{:S(2)}) collective-permute-start(f32[576,128]{1,0:T(8,128)S(1)} %constant_dynamic-update-slice_fusion.refs_0_), channel_id=1, source_target_pairs={{0,1},{1,0},{2,3},{3,2},{4,5},{5,4},{6,7},{7,6},{8,9},{9,8},{10,11... | collective-permute-start | bytes 884744 | tf_op jit(solution)/shard_map/ppermute | solution.py:582
  23.1 5.2 %collective-permute-start.9 = (f32[576,128]{1,0:T(8,128)S(1)}, f32[576,128]{1,0:T(8,128)S(1)}, u32[]{:S(2)}, u32[]{:S(2)}) collective-permute-start(f32[576,128]{1,0:T(8,128)S(1)} %constant_dynamic-update-slice_fusion.2.refs_2_), channel_id=1, source_target_pairs={{0,1},{1,0},{2,3},{3,2},{4,5},{5,4},{6,7},{7,6},{8,9},{9,8},{10,11... | collective-permute-start | bytes 884744 | tf_op jit(solution)/shard_map/ppermute | solution.py:582
  68.5 7.0 %collective-permute-start.18 = (f32[608,128]{1,0:T(8,128)S(1)}, f32[608,128]{1,0:T(8,128)S(1)}, u32[]{:S(2)}, u32[]{:S(2)}) collective-permute-start(f32[608,128]{1,0:T(8,128)S(1)} %add.143), channel_id=1, source_target_pairs={{0,4},{1,3},{2,6},{3,1},{4,0},{5,7},{6,2},{7,5},{8,12},{9,11},{10,... | collective-permute-start | bytes 933896 | tf_op jit(solution)/shard_map/ppermute | solution.py:582
  70.1 6.9 %collective-permute-start.11 = (f32[608,128]{1,0:T(8,128)S(1)}, f32[608,128]{1,0:T(8,128)S(1)}, u32[]{:S(2)}, u32[]{:S(2)}) collective-permute-start(f32[608,128]{1,0:T(8,128)S(1)} %get-tuple-element.47), channel_id=1, source_target_pairs={{0,1},{1,0},{2,3},{3,2},{4,5},{5,4},{6,7},{7,6},{8,9},{9,8},{10,11... | collective-permute-start | bytes 933896 | tf_op jit(solution)/shard_map/ppermute | solution.py:582
  70.1 9.9 %collective-permute-start.13 = (f32[608,128]{1,0:T(8,128)S(1)}, f32[608,128]{1,0:T(8,128)S(1)}, u32[]{:S(2)}, u32[]{:S(2)}) collective-permute-start(f32[608,128]{1,0:T(8,128)S(1)} %add.138), channel_id=1, source_target_pairs={{0,4},{1,3},{2,6},{3,1},{4,0},{5,7},{6,2},{7,5},{8,12},{9,11},{10,... | collective-permute-start | bytes 933896 | tf_op jit(solution)/shard_map/ppermute | solution.py:582
  75.5 6.2 %collective-permute-start.19 = (f32[304,128]{1,0:T(8,128)S(1)}, f32[304,128]{1,0:T(8,128)S(1)}, u32[]{:S(2)}, u32[]{:S(2)}) collective-permute-start(f32[304,128]{1,0:T(8,128)S(1)} %slice.69), channel_id=1, source_target_pairs={{0,2},{1,5},{2,0},{3,7},{4,6},{5,1},{6,4},{7,3},{8,10},{9,13},{10,... | collective-permute-start | bytes 466952 | tf_op jit(solution)/shard_map/ppermute | solution.py:582
  80.1 5.3 %collective-permute-start.14 = (f32[304,128]{1,0:T(8,128)S(1)}, f32[304,128]{1,0:T(8,128)S(1)}, u32[]{:S(2)}, u32[]{:S(2)}) collective-permute-start(f32[304,128]{1,0:T(8,128)S(1)} %slice.65), channel_id=1, source_target_pairs={{0,2},{1,5},{2,0},{3,7},{4,6},{5,1},{6,4},{7,3},{8,10},{9,13},{10,... | collective-permute-start | bytes 466952 | tf_op jit(solution)/shard_map/ppermute | solution.py:582
  81.7 6.3 %collective-permute-start.21 = (f32[152,128]{1,0:T(8,128)S(1)}, f32[152,128]{1,0:T(8,128)S(1)}, u32[]{:S(2)}, u32[]{:S(2)}) collective-permute-start(f32[152,128]{1,0:T(8,128)S(1)} %get-tuple-element.85), channel_id=1, source_target_pairs={{0,24},{1,25},{2,26},{3,27},{4,28},{5,29},{6,30},{7,31},{8,16},{9,... | collective-permute-start | bytes 233480 | tf_op jit(solution)/shard_map/ppermute | solution.py:582
  84.8 6.2 %collective-permute-start.20 = (f32[152,128]{1,0:T(8,128)S(1)}, f32[152,128]{1,0:T(8,128)S(1)}, u32[]{:S(2)}, u32[]{:S(2)}) collective-permute-start(f32[152,128]{1,0:T(8,128)S(1)} %get-tuple-element.84), channel_id=1, source_target_pairs={{0,16},{1,17},{2,18},{3,19},{4,20},{5,21},{6,22},{7,23},{8,24},{9,... | collective-permute-start | bytes 233480 | tf_op jit(solution)/shard_map/ppermute | solution.py:582
  85.4 5.5 %collective-permute-start.15 = (f32[152,128]{1,0:T(8,128)S(1)}, f32[152,128]{1,0:T(8,128)S(1)}, u32[]{:S(2)}, u32[]{:S(2)}) collective-permute-start(f32[152,128]{1,0:T(8,128)S(1)} %slice.67), channel_id=1, source_target_pairs={{0,8},{1,9},{2,10},{3,11},{4,12},{5,13},{6,14},{7,15},{8,0},{9,1},... | collective-permute-start | bytes 233480 | tf_op jit(solution)/shard_map/ppermute | solution.py:582
  95.3 7.6 %collective-permute-start.25 = (f32[144,128]{1,0:T(8,128)}, f32[144,128]{1,0:T(8,128)S(1)}, u32[]{:S(2)}, u32[]{:S(2)}) collective-permute-start(f32[144,128]{1,0:T(8,128)} %get-tuple-element.57), channel_id=1, source_target_pairs={{0,16},{1,17},{2,18},{3,19},{4,20},{5,21},{6,22},{7,23},{8,24},{9,... | collective-permute-start | bytes 221192 | tf_op jit(solution)/shard_map/ppermute | solution.py:582
  98.4 6.4 %collective-permute-start.26 = (f32[144,128]{1,0:T(8,128)}, f32[144,128]{1,0:T(8,128)S(1)}, u32[]{:S(2)}, u32[]{:S(2)}) collective-permute-start(f32[144,128]{1,0:T(8,128)} %get-tuple-element.57), channel_id=1, source_target_pairs={{0,24},{1,25},{2,26},{3,27},{4,28},{5,29},{6,30},{7,31},{8,16},{9,... | collective-permute-start | bytes 221192 | tf_op jit(solution)/shard_map/ppermute | solution.py:582
  100.6 6.0 %collective-permute-start.23 = (f32[288,128]{1,0:T(8,128)S(1)}, f32[288,128]{1,0:T(8,128)S(1)}, u32[]{:S(2)}, u32[]{:S(2)}) collective-permute-start(f32[288,128]{1,0:T(8,128)S(1)} %pad_maximum_fusion.2), channel_id=1, source_target_pairs={{0,2},{1,5},{2,0},{3,7},{4,6},{5,1},{6,4},{7,3},{8,10},{9,13},{10,... | collective-permute-start | bytes 442376 | tf_op jit(solution)/shard_map/ppermute | solution.py:582
  104.8 6.8 %collective-permute-start.27 = (f32[288,128]{1,0:T(8,128)S(1)}, f32[288,128]{1,0:T(8,128)S(1)}, u32[]{:S(2)}, u32[]{:S(2)}) collective-permute-start(f32[288,128]{1,0:T(8,128)S(1)} %pad_maximum_fusion.3), channel_id=1, source_target_pairs={{0,2},{1,5},{2,0},{3,7},{4,6},{5,1},{6,4},{7,3},{8,10},{9,13},{10,... | collective-permute-start | bytes 442376 | tf_op jit(solution)/shard_map/ppermute | solution.py:582
  106.7 7.2 %collective-permute-start.24 = (f32[576,128]{1,0:T(8,128)S(1)}, f32[576,128]{1,0:T(8,128)S(1)}, u32[]{:S(2)}, u32[]{:S(2)}) collective-permute-start(f32[576,128]{1,0:T(8,128)S(1)} %constant_dynamic-update-slice_fusion.5.refs_0_), channel_id=1, source_target_pairs={{0,4},{1,3},{2,6},{3,1},{4,0},{5,7},{6,2},{7,5},{8,12},{9,11},{10,... | collective-permute-start | bytes 884744 | tf_op jit(solution)/shard_map/ppermute | solution.py:582
  111.6 6.8 %collective-permute-start.28 = (f32[576,128]{1,0:T(8,128)S(1)}, f32[576,128]{1,0:T(8,128)S(1)}, u32[]{:S(2)}, u32[]{:S(2)}) collective-permute-start(f32[576,128]{1,0:T(8,128)S(1)} %constant_dynamic-update-slice_fusion.7.refs_2_), channel_id=1, source_target_pairs={{0,4},{1,3},{2,6},{3,1},{4,0},{5,7},{6,2},{7,5},{8,12},{9,11},{10,... | collective-permute-start | bytes 884744 | tf_op jit(solution)/shard_map/ppermute | solution.py:582
  113.3 5.1 %collective-permute-start.29 = (f32[576,128]{1,0:T(8,128)S(1)}, f32[576,128]{1,0:T(8,128)S(1)}, u32[]{:S(2)}, u32[]{:S(2)}) collective-permute-start(f32[576,128]{1,0:T(8,128)S(1)} %constant_dynamic-update-slice_fusion.5.refs_0_), channel_id=1, source_target_pairs={{0,1},{1,0},{2,3},{3,2},{4,5},{5,4},{6,7},{7,6},{8,9},{9,8},{10,11... | collective-permute-start | bytes 884744 | tf_op jit(solution)/shard_map/ppermute | solution.py:582
  158.7 7.0 %collective-permute-start.40 = (f32[608,128]{1,0:T(8,128)S(1)}, f32[608,128]{1,0:T(8,128)S(1)}, u32[]{:S(2)}, u32[]{:S(2)}) collective-permute-start(f32[608,128]{1,0:T(8,128)S(1)} %add.154), channel_id=1, source_target_pairs={{0,4},{1,3},{2,6},{3,1},{4,0},{5,7},{6,2},{7,5},{8,12},{9,11},{10,... | collective-permute-start | bytes 933896 | tf_op jit(solution)/shard_map/ppermute | solution.py:582
  160.3 7.1 %collective-permute-start.33 = (f32[608,128]{1,0:T(8,128)S(1)}, f32[608,128]{1,0:T(8,128)S(1)}, u32[]{:S(2)}, u32[]{:S(2)}) collective-permute-start(f32[608,128]{1,0:T(8,128)S(1)} %get-tuple-element.64), channel_id=1, source_target_pairs={{0,1},{1,0},{2,3},{3,2},{4,5},{5,4},{6,7},{7,6},{8,9},{9,8},{10,11... | collective-permute-start | bytes 933896 | tf_op jit(solution)/shard_map/ppermute | solution.py:582
  160.4 9.8 %collective-permute-start.35 = (f32[608,128]{1,0:T(8,128)S(1)}, f32[608,128]{1,0:T(8,128)S(1)}, u32[]{:S(2)}, u32[]{:S(2)}) collective-permute-start(f32[608,128]{1,0:T(8,128)S(1)} %add.149), channel_id=1, source_target_pairs={{0,4},{1,3},{2,6},{3,1},{4,0},{5,7},{6,2},{7,5},{8,12},{9,11},{10,... | collective-permute-start | bytes 933896 | tf_op jit(solution)/shard_map/ppermute | solution.py:582
  165.7 6.2 %collective-permute-start.41 = (f32[304,128]{1,0:T(8,128)S(1)}, f32[304,128]{1,0:T(8,128)S(1)}, u32[]{:S(2)}, u32[]{:S(2)}) collective-permute-start(f32[304,128]{1,0:T(8,128)S(1)} %slice.77), channel_id=1, source_target_pairs={{0,2},{1,5},{2,0},{3,7},{4,6},{5,1},{6,4},{7,3},{8,10},{9,13},{10,... | collective-permute-start | bytes 466952 | tf_op jit(solution)/shard_map/ppermute | solution.py:582
  170.3 5.3 %collective-permute-start.36 = (f32[304,128]{1,0:T(8,128)S(1)}, f32[304,128]{1,0:T(8,128)S(1)}, u32[]{:S(2)}, u32[]{:S(2)}) collective-permute-start(f32[304,128]{1,0:T(8,128)S(1)} %slice.73), channel_id=1, source_target_pairs={{0,2},{1,5},{2,0},{3,7},{4,6},{5,1},{6,4},{7,3},{8,10},{9,13},{10,... | collective-permute-start | bytes 466952 | tf_op jit(solution)/shard_map/ppermute | solution.py:582
  172.0 6.6 %collective-permute-start.43 = (f32[152,128]{1,0:T(8,128)S(1)}, f32[152,128]{1,0:T(8,128)S(1)}, u32[]{:S(2)}, u32[]{:S(2)}) collective-permute-start(f32[152,128]{1,0:T(8,128)S(1)} %get-tuple-element.83), channel_id=1, source_target_pairs={{0,24},{1,25},{2,26},{3,27},{4,28},{5,29},{6,30},{7,31},{8,16},{9,... | collective-permute-start | bytes 233480 | tf_op jit(solution)/shard_map/ppermute | solution.py:582
  173.1 7.6 %collective-permute-start.42 = (f32[152,128]{1,0:T(8,128)S(1)}, f32[152,128]{1,0:T(8,128)S(1)}, u32[]{:S(2)}, u32[]{:S(2)}) collective-permute-start(f32[152,128]{1,0:T(8,128)S(1)} %get-tuple-element.82), channel_id=1, source_target_pairs={{0,16},{1,17},{2,18},{3,19},{4,20},{5,21},{6,22},{7,23},{8,24},{9,... | collective-permute-start | bytes 233480 | tf_op jit(solution)/shard_map/ppermute | solution.py:582
  175.6 5.6 %collective-permute-start.37 = (f32[152,128]{1,0:T(8,128)S(1)}, f32[152,128]{1,0:T(8,128)S(1)}, u32[]{:S(2)}, u32[]{:S(2)}) collective-permute-start(f32[152,128]{1,0:T(8,128)S(1)} %slice.75), channel_id=1, source_target_pairs={{0,8},{1,9},{2,10},{3,11},{4,12},{5,13},{6,14},{7,15},{8,0},{9,1},... | collective-permute-start | bytes 233480 | tf_op jit(solution)/shard_map/ppermute | solution.py:582
  (16 other events, 49.9 us)

commit v7 on v6

--- a/solution.py
+++ b/solution.py
@@ -94,32 +94,41 @@
     return ray_x, ray_y, factor
 
 
-def project_to(param_ref, cam_x, cam_y, out_ref):
-    rows = [param_ref[i : i + 1, :] for i in range(7)]
-    geo = geometry_rows(*rows, cam_x, cam_y)
+def chunk(index):
+    return slice(index * LANES, (index + 1) * LANES)
+
+
+def tiles_of(param_ref, turn):
+    size = param_ref.shape[1] // LANES
+    for k in range(size):
+        turn[pl.ds(k, ROWSUB, stride=size), :] = param_ref[0:ROWSUB, chunk(k)]
+    return [turn[i * size : (i + 1) * size, :] for i in range(7)]
+
+
+def project_to(param_ref, cam_x, cam_y, out_ref, turn, basis_turn):
+    size = param_ref.shape[1] // LANES
+    geo = geometry_rows(*tiles_of(param_ref, turn), cam_x, cam_y)
+    for i, tile in enumerate(geo):
+        out_ref[i * size : (i + 1) * size, :] = tile
     ray_x, ray_y, factor = ray_rows(geo[0], geo[1])
-    basis = jnp.concatenate(harmonic_rows(ray_x * factor, ray_y * factor, factor), 0)
-    colours = []
-    for ch in range(3):
-        coef = param_ref[7 + NCOEF * ch : 7 + NCOEF * (ch + 1), :]
-        colours.append(0.5 + jnp.sum(coef * basis, axis=0, keepdims=True))
-    fields = jnp.concatenate(list(geo) + colours, 0)
-    per_field = fields.shape[1] // LANES
-    for k in range(per_field):
-        out_ref[pl.ds(k, FIELDS, stride=per_field), :] = fields[:, k * LANES : (k + 1) * LANES]
-
-
-def project_kernel(cam_ref, param_ref, out_ref, *, step):
-    project_to(param_ref, cam_ref[step, 0], cam_ref[step, 1], out_ref)
-
-
-def gradient_to(param_ref, cam_x, cam_y, grad_ref, full_ref):
-    count = param_ref.shape[1]
-    per_field = count // LANES
-    pieces = [grad_ref[pl.ds(k, FIELDS, stride=per_field), :] for k in range(per_field)]
-    grads = jnp.concatenate(pieces, 1)
-    g = [grads[i : i + 1, :] for i in range(FIELDS)]
-    p0, p1, p2, p3, p4, p5, p6 = [param_ref[i : i + 1, :] for i in range(7)]
+    for i, tile in enumerate(harmonic_rows(ray_x * factor, ray_y * factor, factor)):
+        basis_turn[i * size : (i + 1) * size, :] = tile
+    for k in range(size):
+        basis = basis_turn[pl.ds(k, NCOEF, stride=size), :]
+        for ch in range(3):
+            coef = param_ref[7 + NCOEF * ch : 7 + NCOEF * (ch + 1), chunk(k)]
+            at = (6 + ch) * size + k
+            out_ref[at : at + 1, :] = 0.5 + jnp.sum(coef * basis, axis=0, keepdims=True)
+
+
+def project_kernel(cam_ref, param_ref, out_ref, turn, basis_turn, *, step):
+    project_to(param_ref, cam_ref[step, 0], cam_ref[step, 1], out_ref, turn, basis_turn)
+
+
+def gradient_to(param_ref, cam_x, cam_y, grad_ref, full_ref, turn, basis_turn):
+    size = param_ref.shape[1] // LANES
+    g = [grad_ref[i * size : (i + 1) * size, :] for i in range(6)]
+    p0, p1, p2, p3, p4, p5, p6 = tiles_of(param_ref, turn)
     inv_z = 1.0 / p2
     screen_u = (p0 - cam_x) / p2
     screen_v = (p1 - cam_y) / p2
@@ -133,13 +142,22 @@
     ray_x, ray_y, factor = ray_rows(screen_u, screen_v)
     nx, ny, nz = ray_x * factor, ray_y * factor, factor
     basis_rows, basis_vjp = jax.vjp(lambda a, b, c: tuple(harmonic_rows(a, b, c)), nx, ny, nz)
-    basis = jnp.concatenate(basis_rows, 0)
-    d_basis = jnp.zeros_like(basis)
-    for ch in range(3):
-        coef = param_ref[7 + NCOEF * ch : 7 + NCOEF * (ch + 1), :]
-        full_ref[7 + NCOEF * ch : 7 + NCOEF * (ch + 1), :] = g[6 + ch] * basis
-        d_basis = d_basis + g[6 + ch] * coef
-    d_nx, d_ny, d_nz = basis_vjp(tuple(d_basis[i : i + 1, :] for i in range(NCOEF)))
+    for i, tile in enumerate(basis_rows):
+        basis_turn[i * size : (i + 1) * size, :] = tile
+    for k in range(size):
+        where = pl.ds(k, NCOEF, stride=size)
+        basis = basis_turn[where, :]
+        d_basis = jnp.zeros_like(basis)
+        for ch in range(3):
+            rows = slice(7 + NCOEF * ch, 7 + NCOEF * (ch + 1))
+            at = (6 + ch) * size + k
+            tone = grad_ref[at : at + 1, :]
+            full_ref[rows, chunk(k)] = tone * basis
+            d_basis = d_basis + tone * param_ref[rows, chunk(k)]
+        basis_turn[where, :] = d_basis
+    d_nx, d_ny, d_nz = basis_vjp(
+        tuple(basis_turn[i * size : (i + 1) * size, :] for i in range(NCOEF))
+    )
     dot = d_nx * nx + d_ny * ny + d_nz * nz
     image_width = 1.0 * SIDE * IMG_TX
     d_u = g[0] + factor * (d_nx - nx * dot) / image_width
@@ -147,30 +165,36 @@
     d_one = g[2] * cc + g[3] * cs + g[4] * ss
     d_two = g[2] * ss - g[3] * cs + g[4] * cc
     diff = inv_one - inv_two
-    d_angle = diff * (2.0 * cs * (g[4] - g[2]) + (cc - ss) * g[3])
     d_x = d_u * inv_z
     d_y = d_v * inv_z
-    d_z = 2.0 * (d_one * inv_one + d_two * inv_two) * inv_z - d_x * screen_u - d_y * screen_v
-    full_ref[0:1, :] = d_x
-    full_ref[1:2, :] = d_y
-    full_ref[2:3, :] = d_z
-    full_ref[3:4, :] = -2.0 * inv_one * d_one
-    full_ref[4:5, :] = -2.0 * inv_two * d_two
-    full_ref[5:6, :] = d_angle
-    full_ref[6:7, :] = g[5] / (1.0 + jnp.exp(p6))
+    slopes = (
+        d_x,
+        d_y,
+        2.0 * (d_one * inv_one + d_two * inv_two) * inv_z - d_x * screen_u - d_y * screen_v,
+        -2.0 * inv_one * d_one,
+        -2.0 * inv_two * d_two,
+        diff * (2.0 * cs * (g[4] - g[2]) + (cc - ss) * g[3]),
+        g[5] / (1.0 + jnp.exp(p6)),
+    )
+    for i, tile in enumerate(slopes):
+        turn[i * size : (i + 1) * size, :] = tile
+    for k in range(size):
+        full_ref[0:7, chunk(k)] = turn[pl.ds(k, 7, stride=size), :]
 
 
 def update_kernel(
     cam_ref, param_ref, first_ref, second_ref, grad_ref, *refs, step, project_next, pixel_count
 ):
+    refs, (full_ref, turn, basis_turn) = refs[:-3], refs[-3:]
     if project_next:
-        new_param, new_first, new_second, field_ref, full_ref = refs
+        new_param, new_first, new_second, field_ref = refs
     else:
-        before, (new_param, new_first, new_second, loss_ref, full_ref) = refs[:step], refs[step:]
+        before, (new_param, new_first, new_second, loss_ref) = refs[:step], refs[step:]
         tail = grad_ref.shape[0] - ROWSUB
         for i, one in enumerate(before + (grad_ref,)):
             loss_ref[i] = jnp.max(one[tail : tail + 1, :]) / pixel_count
-    gradient_to(param_ref, cam_ref[step, 0], cam_ref[step, 1], grad_ref, full_ref)
+    camera = cam_ref[step, 0], cam_ref[step, 1]
+    gradient_to(param_ref, *camera, grad_ref, full_ref, turn, basis_turn)
     step_count = adam_start + step + 1
     gradient = full_ref[...]
     first = beta_one * first_ref[...] + (1.0 - beta_one) * gradient
@@ -183,7 +207,8 @@
         jnp.sqrt(scaled_second) + adam_eps
     )
     if project_next:
-        project_to(new_param, cam_ref[step + 1, 0], cam_ref[step + 1, 1], field_ref)
+        camera = cam_ref[step + 1, 0], cam_ref[step + 1, 1]
+        project_to(new_param, *camera, field_ref, turn, basis_turn)
 
 
 def split_two(values):
@@ -706,12 +731,17 @@
         name="render",
     )
 
+    turns = [
+        pltpu.VMEM((ROWSUB * per_owner, LANES), f32),
+        pltpu.VMEM((NCOEF * per_owner, LANES), f32),
+    ]
     params, first, second = gauss_params, first_moment, second_moment
     fields = pl.pallas_call(
         functools.partial(project_kernel, step=0),
         out_shape=field_shape,
         in_specs=[smem, vmem],
         out_specs=vmem,
+        scratch_shapes=turns,
         name="project",
     )(camera, params)
     settings = (rows, which, middle, target_rows)
@@ -745,7 +775,7 @@
             + (field_shape if more else jax.ShapeDtypeStruct((STEPS,), f32),),
             in_specs=[smem] + [vmem] * (4 + len(before)),
             out_specs=(vmem,) * 3 + (vmem if more else smem,),
-            scratch_shapes=[pltpu.VMEM((params_rows, count), f32)],
+            scratch_shapes=[pltpu.VMEM((params_rows, count), f32)] + turns,
             name="update",
         )(camera, params, first, second, summed, *before)
         params, first, second, fields = result

time: 186 us -> 185 us (level)
  transfers between devices with their start and end apart: 44 -> 44, of which waited for: 25 -> 26; matrix products, arithmetic and copies ran while one was open for 2% -> 2% of each run, Pallas kernels for 0% -> 0%
where the time goes in v7:
time: 185 us
  Pallas kernels  81.7 us (44%)
  waiting for transfers between devices  50.4 us (27%)
  starting transfers between devices  43.9 us (24%)
  local copies, waits for them, and re-layouts  4.41 us (2%)
  other arithmetic  2.99 us (2%)
    pallas_call x2, Pallas kernels, per_device(): picture, *grads = render(kernel)(*settings, *table)  73.8 us
    ppermute x44, waiting for transfers between devices, swap(): return lax.ppermute(values, AXES, pairs)  50.4 us
    ppermute x44, starting transfers between devices, swap(): return lax.ppermute(values, AXES, pairs)  43.9 us
    pallas_call x2, Pallas kernels, per_device(): pl.pallas_call(functools.partial(update_kernel, step=step, project_next=m...  6.05 us
  transfers between devices with their start and end apart: 44, of which 26 were waited for; matrix products, arithmetic and copies ran while one was open for 2% of the time, Pallas kernels for 0%

profile of v7, /device:TPU:0, one launch (start us, length us, event | category | flops | bytes accessed | tf_op | source)
XLA Modules:
  0.0 184.6 jit_solution(16568077164731732445)
XLA Ops:
  0.6 1.9 %project.1 = f32[144,128]{1,0:T(8,128)} custom-call(f32[2,2]{1,0:T(2,128)} %cam_ref.5, f32[55,2048]{1,0:T(8,128)} %param_ref.3), custom_call_target="tpu_custom_call" | custom-call | tf_op jit(solution)/shard_map/project/pallas_call | solution.py:739
  2.5 3.1 %collective-permute-start = (f32[144,128]{1,0:T(8,128)}, f32[144,128]{1,0:T(8,128)S(1)}, u32[]{:S(2)}, u32[]{:S(2)}) collective-permute-start(f32[144,128]{1,0:T(8,128)} %project.1), channel_id=1, source_target_pairs={{0,8},{1,9},{2,10},{3,11},{4,12},{5,13},{6,14},{7,15},{8,0},{9,1},... | collective-permute-start | bytes 221192 | tf_op jit(solution)/shard_map/ppermute | solution.py:607
  5.6 2.6 %collective-permute-start.3 = (f32[144,128]{1,0:T(8,128)}, f32[144,128]{1,0:T(8,128)S(1)}, u32[]{:S(2)}, u32[]{:S(2)}) collective-permute-start(f32[144,128]{1,0:T(8,128)} %project.1), channel_id=1, source_target_pairs={{0,16},{1,17},{2,18},{3,19},{4,20},{5,21},{6,22},{7,23},{8,24},{9,... | collective-permute-start | bytes 221192 | tf_op jit(solution)/shard_map/ppermute | solution.py:607
  12.1 1.8 collective-permute-start.1
  17.3 1.8 collective-permute-start.2
  19.1 2.3 %collective-permute-done.5 = f32[288,128]{1,0:T(8,128)S(1)} collective-permute-done((f32[288,128]{1,0:T(8,128)S(1)}, f32[288,128]{1,0:T(8,128)S(1)}, u32[]{:S(2)}, u32[]{:S(2)}) %collective-permute-start.5) | collective-permute-done | bytes 147488 | tf_op jit(solution)/shard_map/ppermute | solution.py:607
  21.5 1.6 collective-permute-start.6
  24.1 4.1 %collective-permute-done.6.refs_3_ = f32[576,128]{1,0:T(8,128)S(1)} collective-permute-done((f32[576,128]{1,0:T(8,128)S(1)}, f32[576,128]{1,0:T(8,128)S(1)}, u32[]{:S(2)}, u32[]{:S(2)}) %collective-permute-start.6) | collective-permute-done | bytes 294944 | tf_op jit(solution)/shard_map/ppermute | solution.py:607
  28.3 1.6 collective-permute-done.10.refs_7_
  29.8 36.9 %render.2 = (f32[96,128]{1,0:T(8,128)S(1)}, f32[608,128]{1,0:T(8,128)S(1)}, f32[608,128]{1,0:T(8,128)S(1)}, f32[608,128]{1,0:T(8,128)S(1)}, f32[608,128]{1,0:T(8...) custom-call(s32[2,16,512]{2,1,0:T(8,128)S(1)} %bitcast.16, ...), custom_call_target="tpu_custom_call" | custom-call | tf_op jit(solution)/shard_map/render/pallas_call | solution.py:761
  68.4 1.6 collective-permute-start.18
  71.4 4.0 %collective-permute-done.18 = f32[608,128]{1,0:T(8,128)S(1)} collective-permute-done((f32[608,128]{1,0:T(8,128)S(1)}, f32[608,128]{1,0:T(8,128)S(1)}, u32[]{:S(2)}, u32[]{:S(2)}) %collective-permute-start.18) | collective-permute-done | bytes 311328 | tf_op jit(solution)/shard_map/ppermute | solution.py:607
  77.0 3.1 %collective-permute-done.13 = f32[608,128]{1,0:T(8,128)S(1)} collective-permute-done((f32[608,128]{1,0:T(8,128)S(1)}, f32[608,128]{1,0:T(8,128)S(1)}, u32[]{:S(2)}, u32[]{:S(2)}) %collective-permute-start.13) | collective-permute-done | bytes 311328 | tf_op jit(solution)/shard_map/ppermute | solution.py:607
  81.6 3.0 %collective-permute-start.21 = (f32[152,128]{1,0:T(8,128)S(1)}, f32[152,128]{1,0:T(8,128)S(1)}, u32[]{:S(2)}, u32[]{:S(2)}) collective-permute-start(f32[152,128]{1,0:T(8,128)S(1)} %get-tuple-element.85), channel_id=1, source_target_pairs={{0,24},{1,25},{2,26},{3,27},{4,28},{5,29},{6,30},{7,31},{8,16},{9,... | collective-permute-start | bytes 233480 | tf_op jit(solution)/shard_map/ppermute | solution.py:607
  87.9 3.1 %collective-permute-done.20 = f32[152,128]{1,0:T(8,128)S(1)} collective-permute-done((f32[152,128]{1,0:T(8,128)S(1)}, f32[152,128]{1,0:T(8,128)S(1)}, u32[]{:S(2)}, u32[]{:S(2)}) %collective-permute-start.20) | collective-permute-done | bytes 77856 | tf_op jit(solution)/shard_map/ppermute | solution.py:607
  91.7 3.0 %update.2 = (f32[55,2048]{1,0:T(8,128)}, f32[55,2048]{1,0:T(8,128)}, f32[55,2048]{1,0:T(8,128)}, f32[144,128]{1,0:T(8,128)}) custom-call(f32[2,2]{1,0:T(2,128)} %cam_ref.5, f32[55,2048]{1,0:T(8,128)} %param_ref.3, f32[55,2048]{1,0:T(8,128)} %first_ref.1, f32[55,2048]{1,0:T(8,128)} %second_ref.1, f32[152,128]{1,0:T(8,128)} %fusion.3.grad_ref.refs_0_), custom_call_target="tpu_custom_call" | custom-call | tf_op jit(solution)/shard_map/update/pallas_call | solution.py:767
  94.9 3.1 %collective-permute-start.25 = (f32[144,128]{1,0:T(8,128)}, f32[144,128]{1,0:T(8,128)S(1)}, u32[]{:S(2)}, u32[]{:S(2)}) collective-permute-start(f32[144,128]{1,0:T(8,128)} %get-tuple-element.57), channel_id=1, source_target_pairs={{0,16},{1,17},{2,18},{3,19},{4,20},{5,21},{6,22},{7,23},{8,24},{9,... | collective-permute-start | bytes 221192 | tf_op jit(solution)/shard_map/ppermute | solution.py:607
  100.2 1.8 collective-permute-start.23
  102.4 1.9 %collective-permute-done.26 = f32[144,128]{1,0:T(8,128)S(1)} collective-permute-done((f32[144,128]{1,0:T(8,128)}, f32[144,128]{1,0:T(8,128)S(1)}, u32[]{:S(2)}, u32[]{:S(2)}) %collective-permute-start.26) | collective-permute-done | bytes 73760 | tf_op jit(solution)/shard_map/ppermute | solution.py:607
  104.4 1.7 collective-permute-start.27
  106.1 1.6 collective-permute-start.24
  107.7 3.5 %collective-permute-done.27 = f32[288,128]{1,0:T(8,128)S(1)} collective-permute-done((f32[288,128]{1,0:T(8,128)S(1)}, f32[288,128]{1,0:T(8,128)S(1)}, u32[]{:S(2)}, u32[]{:S(2)}) %collective-permute-start.27) | collective-permute-done | bytes 147488 | tf_op jit(solution)/shard_map/ppermute | solution.py:607
  113.2 4.7 %collective-permute-done.28.refs_3_ = f32[576,128]{1,0:T(8,128)S(1)} collective-permute-done((f32[576,128]{1,0:T(8,128)S(1)}, f32[576,128]{1,0:T(8,128)S(1)}, u32[]{:S(2)}, u32[]{:S(2)}) %collective-permute-start.28) | collective-permute-done | bytes 294944 | tf_op jit(solution)/shard_map/ppermute | solution.py:607
  118.0 1.6 collective-permute-done.32.refs_7_
  119.6 36.9 %render.3 = (f32[96,128]{1,0:T(8,128)S(1)}, f32[608,128]{1,0:T(8,128)S(1)}, f32[608,128]{1,0:T(8,128)S(1)}, f32[608,128]{1,0:T(8,128)S(1)}, f32[608,128]{1,0:T(8...) custom-call(s32[2,16,512]{2,1,0:T(8,128)S(1)} %bitcast.17, ...), custom_call_target="tpu_custom_call" | custom-call | tf_op jit(solution)/shard_map/render/pallas_call | solution.py:761
  159.7 1.6 collective-permute-start.35
  161.4 3.7 %collective-permute-done.40 = f32[608,128]{1,0:T(8,128)S(1)} collective-permute-done((f32[608,128]{1,0:T(8,128)S(1)}, f32[608,128]{1,0:T(8,128)S(1)}, u32[]{:S(2)}, u32[]{:S(2)}) %collective-permute-start.40) | collective-permute-done | bytes 311328 | tf_op jit(solution)/shard_map/ppermute | solution.py:607
  165.2 1.6 collective-permute-start.41
  166.7 3.0 %collective-permute-done.35 = f32[608,128]{1,0:T(8,128)S(1)} collective-permute-done((f32[608,128]{1,0:T(8,128)S(1)}, f32[608,128]{1,0:T(8,128)S(1)}, u32[]{:S(2)}, u32[]{:S(2)}) %collective-permute-start.35) | collective-permute-done | bytes 311328 | tf_op jit(solution)/shard_map/ppermute | solution.py:607
  172.7 2.4 %collective-permute-done.36 = f32[304,128]{1,0:T(8,128)S(1)} collective-permute-done((f32[304,128]{1,0:T(8,128)S(1)}, f32[304,128]{1,0:T(8,128)S(1)}, u32[]{:S(2)}, u32[]{:S(2)}) %collective-permute-start.36) | collective-permute-done | bytes 155680 | tf_op jit(solution)/shard_map/ppermute | solution.py:607
  178.1 2.1 %collective-permute-done.42 = f32[152,128]{1,0:T(8,128)S(1)} collective-permute-done((f32[152,128]{1,0:T(8,128)S(1)}, f32[152,128]{1,0:T(8,128)S(1)}, u32[]{:S(2)}, u32[]{:S(2)}) %collective-permute-start.42) | collective-permute-done | bytes 77856 | tf_op jit(solution)/shard_map/ppermute | solution.py:607
  181.4 3.0 %update.3 = (f32[55,2048]{1,0:T(8,128)}, f32[55,2048]{1,0:T(8,128)}, f32[55,2048]{1,0:T(8,128)}, f32[2]{0:T(128)}) custom-call(f32[2,2]{1,0:T(2,128)} %cam_ref.5, f32[55,2048]{1,0:T(8,128)} %get-tuple-element.54.param_ref, f32[55,2048]{1,0:T(8,128)} %get-tuple-element.55.first_ref, f32[55,2048]{1,0:T(8,128)} %get-tuple-element.56.second_ref, ...), custom_call_target="tpu_custom_call" | custom-call | tf_op jit(solution)/shard_map/update/pallas_call | solution.py:767
  (124 shorter events, 33.9 us)
Async XLA Ops:
  2.5 8.7 %collective-permute-start = (f32[144,128]{1,0:T(8,128)}, f32[144,128]{1,0:T(8,128)S(1)}, u32[]{:S(2)}, u32[]{:S(2)}) collective-permute-start(f32[144,128]{1,0:T(8,128)} %project.1), channel_id=1, source_target_pairs={{0,8},{1,9},{2,10},{3,11},{4,12},{5,13},{6,14},{7,15},{8,0},{9,1},... | collective-permute-start | bytes 221192 | tf_op jit(solution)/shard_map/ppermute | solution.py:607
  5.6 8.3 %collective-permute-start.3 = (f32[144,128]{1,0:T(8,128)}, f32[144,128]{1,0:T(8,128)S(1)}, u32[]{:S(2)}, u32[]{:S(2)}) collective-permute-start(f32[144,128]{1,0:T(8,128)} %project.1), channel_id=1, source_target_pairs={{0,16},{1,17},{2,18},{3,19},{4,20},{5,21},{6,22},{7,23},{8,24},{9,... | collective-permute-start | bytes 221192 | tf_op jit(solution)/shard_map/ppermute | solution.py:607
  8.2 6.5 %collective-permute-start.4 = (f32[144,128]{1,0:T(8,128)}, f32[144,128]{1,0:T(8,128)S(1)}, u32[]{:S(2)}, u32[]{:S(2)}) collective-permute-start(f32[144,128]{1,0:T(8,128)} %project.1), channel_id=1, source_target_pairs={{0,24},{1,25},{2,26},{3,27},{4,28},{5,29},{6,30},{7,31},{8,16},{9,... | collective-permute-start | bytes 221192 | tf_op jit(solution)/shard_map/ppermute | solution.py:607
  14.7 6.8 %collective-permute-start.5 = (f32[288,128]{1,0:T(8,128)S(1)}, f32[288,128]{1,0:T(8,128)S(1)}, u32[]{:S(2)}, u32[]{:S(2)}) collective-permute-start(f32[288,128]{1,0:T(8,128)S(1)} %pad_maximum_fusion.1), channel_id=1, source_target_pairs={{0,2},{1,5},{2,0},{3,7},{4,6},{5,1},{6,4},{7,3},{8,10},{9,13},{10,... | collective-permute-start | bytes 442376 | tf_op jit(solution)/shard_map/ppermute | solution.py:607
  17.3 6.8 %collective-permute-start.2 = (f32[576,128]{1,0:T(8,128)S(1)}, f32[576,128]{1,0:T(8,128)S(1)}, u32[]{:S(2)}, u32[]{:S(2)}) collective-permute-start(f32[576,128]{1,0:T(8,128)S(1)} %constant_dynamic-update-slice_fusion.refs_0_), channel_id=1, source_target_pairs={{0,4},{1,3},{2,6},{3,1},{4,0},{5,7},{6,2},{7,5},{8,12},{9,11},{10,... | collective-permute-start | bytes 884744 | tf_op jit(solution)/shard_map/ppermute | solution.py:607
  21.5 6.8 %collective-permute-start.6 = (f32[576,128]{1,0:T(8,128)S(1)}, f32[576,128]{1,0:T(8,128)S(1)}, u32[]{:S(2)}, u32[]{:S(2)}) collective-permute-start(f32[576,128]{1,0:T(8,128)S(1)} %constant_dynamic-update-slice_fusion.2.refs_2_), channel_id=1, source_target_pairs={{0,4},{1,3},{2,6},{3,1},{4,0},{5,7},{6,2},{7,5},{8,12},{9,11},{10,... | collective-permute-start | bytes 884744 | tf_op jit(solution)/shard_map/ppermute | solution.py:607
  23.0 5.2 %collective-permute-start.7 = (f32[576,128]{1,0:T(8,128)S(1)}, f32[576,128]{1,0:T(8,128)S(1)}, u32[]{:S(2)}, u32[]{:S(2)}) collective-permute-start(f32[576,128]{1,0:T(8,128)S(1)} %constant_dynamic-update-slice_fusion.refs_0_), channel_id=1, source_target_pairs={{0,1},{1,0},{2,3},{3,2},{4,5},{5,4},{6,7},{7,6},{8,9},{9,8},{10,11... | collective-permute-start | bytes 884744 | tf_op jit(solution)/shard_map/ppermute | solution.py:607
  23.0 5.2 %collective-permute-start.9 = (f32[576,128]{1,0:T(8,128)S(1)}, f32[576,128]{1,0:T(8,128)S(1)}, u32[]{:S(2)}, u32[]{:S(2)}) collective-permute-start(f32[576,128]{1,0:T(8,128)S(1)} %constant_dynamic-update-slice_fusion.2.refs_2_), channel_id=1, source_target_pairs={{0,1},{1,0},{2,3},{3,2},{4,5},{5,4},{6,7},{7,6},{8,9},{9,8},{10,11... | collective-permute-start | bytes 884744 | tf_op jit(solution)/shard_map/ppermute | solution.py:607
  68.4 7.0 %collective-permute-start.18 = (f32[608,128]{1,0:T(8,128)S(1)}, f32[608,128]{1,0:T(8,128)S(1)}, u32[]{:S(2)}, u32[]{:S(2)}) collective-permute-start(f32[608,128]{1,0:T(8,128)S(1)} %add.143), channel_id=1, source_target_pairs={{0,4},{1,3},{2,6},{3,1},{4,0},{5,7},{6,2},{7,5},{8,12},{9,11},{10,... | collective-permute-start | bytes 933896 | tf_op jit(solution)/shard_map/ppermute | solution.py:607
  70.1 6.9 %collective-permute-start.11 = (f32[608,128]{1,0:T(8,128)S(1)}, f32[608,128]{1,0:T(8,128)S(1)}, u32[]{:S(2)}, u32[]{:S(2)}) collective-permute-start(f32[608,128]{1,0:T(8,128)S(1)} %get-tuple-element.47), channel_id=1, source_target_pairs={{0,1},{1,0},{2,3},{3,2},{4,5},{5,4},{6,7},{7,6},{8,9},{9,8},{10,11... | collective-permute-start | bytes 933896 | tf_op jit(solution)/shard_map/ppermute | solution.py:607
  70.1 9.9 %collective-permute-start.13 = (f32[608,128]{1,0:T(8,128)S(1)}, f32[608,128]{1,0:T(8,128)S(1)}, u32[]{:S(2)}, u32[]{:S(2)}) collective-permute-start(f32[608,128]{1,0:T(8,128)S(1)} %add.138), channel_id=1, source_target_pairs={{0,4},{1,3},{2,6},{3,1},{4,0},{5,7},{6,2},{7,5},{8,12},{9,11},{10,... | collective-permute-start | bytes 933896 | tf_op jit(solution)/shard_map/ppermute | solution.py:607
  75.5 6.1 %collective-permute-start.19 = (f32[304,128]{1,0:T(8,128)S(1)}, f32[304,128]{1,0:T(8,128)S(1)}, u32[]{:S(2)}, u32[]{:S(2)}) collective-permute-start(f32[304,128]{1,0:T(8,128)S(1)} %slice.69), channel_id=1, source_target_pairs={{0,2},{1,5},{2,0},{3,7},{4,6},{5,1},{6,4},{7,3},{8,10},{9,13},{10,... | collective-permute-start | bytes 466952 | tf_op jit(solution)/shard_map/ppermute | solution.py:607
  80.1 5.3 %collective-permute-start.14 = (f32[304,128]{1,0:T(8,128)S(1)}, f32[304,128]{1,0:T(8,128)S(1)}, u32[]{:S(2)}, u32[]{:S(2)}) collective-permute-start(f32[304,128]{1,0:T(8,128)S(1)} %slice.65), channel_id=1, source_target_pairs={{0,2},{1,5},{2,0},{3,7},{4,6},{5,1},{6,4},{7,3},{8,10},{9,13},{10,... | collective-permute-start | bytes 466952 | tf_op jit(solution)/shard_map/ppermute | solution.py:607
  81.6 6.3 %collective-permute-start.21 = (f32[152,128]{1,0:T(8,128)S(1)}, f32[152,128]{1,0:T(8,128)S(1)}, u32[]{:S(2)}, u32[]{:S(2)}) collective-permute-start(f32[152,128]{1,0:T(8,128)S(1)} %get-tuple-element.85), channel_id=1, source_target_pairs={{0,24},{1,25},{2,26},{3,27},{4,28},{5,29},{6,30},{7,31},{8,16},{9,... | collective-permute-start | bytes 233480 | tf_op jit(solution)/shard_map/ppermute | solution.py:607
  84.6 6.3 %collective-permute-start.20 = (f32[152,128]{1,0:T(8,128)S(1)}, f32[152,128]{1,0:T(8,128)S(1)}, u32[]{:S(2)}, u32[]{:S(2)}) collective-permute-start(f32[152,128]{1,0:T(8,128)S(1)} %get-tuple-element.84), channel_id=1, source_target_pairs={{0,16},{1,17},{2,18},{3,19},{4,20},{5,21},{6,22},{7,23},{8,24},{9,... | collective-permute-start | bytes 233480 | tf_op jit(solution)/shard_map/ppermute | solution.py:607
  85.5 5.6 %collective-permute-start.15 = (f32[152,128]{1,0:T(8,128)S(1)}, f32[152,128]{1,0:T(8,128)S(1)}, u32[]{:S(2)}, u32[]{:S(2)}) collective-permute-start(f32[152,128]{1,0:T(8,128)S(1)} %slice.67), channel_id=1, source_target_pairs={{0,8},{1,9},{2,10},{3,11},{4,12},{5,13},{6,14},{7,15},{8,0},{9,1},... | collective-permute-start | bytes 233480 | tf_op jit(solution)/shard_map/ppermute | solution.py:607
  94.9 7.5 %collective-permute-start.25 = (f32[144,128]{1,0:T(8,128)}, f32[144,128]{1,0:T(8,128)S(1)}, u32[]{:S(2)}, u32[]{:S(2)}) collective-permute-start(f32[144,128]{1,0:T(8,128)} %get-tuple-element.57), channel_id=1, source_target_pairs={{0,16},{1,17},{2,18},{3,19},{4,20},{5,21},{6,22},{7,23},{8,24},{9,... | collective-permute-start | bytes 221192 | tf_op jit(solution)/shard_map/ppermute | solution.py:607
  98.0 6.4 %collective-permute-start.26 = (f32[144,128]{1,0:T(8,128)}, f32[144,128]{1,0:T(8,128)S(1)}, u32[]{:S(2)}, u32[]{:S(2)}) collective-permute-start(f32[144,128]{1,0:T(8,128)} %get-tuple-element.57), channel_id=1, source_target_pairs={{0,24},{1,25},{2,26},{3,27},{4,28},{5,29},{6,30},{7,31},{8,16},{9,... | collective-permute-start | bytes 221192 | tf_op jit(solution)/shard_map/ppermute | solution.py:607
  100.2 5.9 %collective-permute-start.23 = (f32[288,128]{1,0:T(8,128)S(1)}, f32[288,128]{1,0:T(8,128)S(1)}, u32[]{:S(2)}, u32[]{:S(2)}) collective-permute-start(f32[288,128]{1,0:T(8,128)S(1)} %pad_maximum_fusion.2), channel_id=1, source_target_pairs={{0,2},{1,5},{2,0},{3,7},{4,6},{5,1},{6,4},{7,3},{8,10},{9,13},{10,... | collective-permute-start | bytes 442376 | tf_op jit(solution)/shard_map/ppermute | solution.py:607
  104.4 6.8 %collective-permute-start.27 = (f32[288,128]{1,0:T(8,128)S(1)}, f32[288,128]{1,0:T(8,128)S(1)}, u32[]{:S(2)}, u32[]{:S(2)}) collective-permute-start(f32[288,128]{1,0:T(8,128)S(1)} %pad_maximum_fusion.3), channel_id=1, source_target_pairs={{0,2},{1,5},{2,0},{3,7},{4,6},{5,1},{6,4},{7,3},{8,10},{9,13},{10,... | collective-permute-start | bytes 442376 | tf_op jit(solution)/shard_map/ppermute | solution.py:607
  106.1 7.1 %collective-permute-start.24 = (f32[576,128]{1,0:T(8,128)S(1)}, f32[576,128]{1,0:T(8,128)S(1)}, u32[]{:S(2)}, u32[]{:S(2)}) collective-permute-start(f32[576,128]{1,0:T(8,128)S(1)} %constant_dynamic-update-slice_fusion.5.refs_0_), channel_id=1, source_target_pairs={{0,4},{1,3},{2,6},{3,1},{4,0},{5,7},{6,2},{7,5},{8,12},{9,11},{10,... | collective-permute-start | bytes 884744 | tf_op jit(solution)/shard_map/ppermute | solution.py:607
  111.2 6.8 %collective-permute-start.28 = (f32[576,128]{1,0:T(8,128)S(1)}, f32[576,128]{1,0:T(8,128)S(1)}, u32[]{:S(2)}, u32[]{:S(2)}) collective-permute-start(f32[576,128]{1,0:T(8,128)S(1)} %constant_dynamic-update-slice_fusion.7.refs_2_), channel_id=1, source_target_pairs={{0,4},{1,3},{2,6},{3,1},{4,0},{5,7},{6,2},{7,5},{8,12},{9,11},{10,... | collective-permute-start | bytes 884744 | tf_op jit(solution)/shard_map/ppermute | solution.py:607
  112.7 5.2 %collective-permute-start.29 = (f32[576,128]{1,0:T(8,128)S(1)}, f32[576,128]{1,0:T(8,128)S(1)}, u32[]{:S(2)}, u32[]{:S(2)}) collective-permute-start(f32[576,128]{1,0:T(8,128)S(1)} %constant_dynamic-update-slice_fusion.5.refs_0_), channel_id=1, source_target_pairs={{0,1},{1,0},{2,3},{3,2},{4,5},{5,4},{6,7},{7,6},{8,9},{9,8},{10,11... | collective-permute-start | bytes 884744 | tf_op jit(solution)/shard_map/ppermute | solution.py:607
  112.7 5.2 %collective-permute-start.31 = (f32[576,128]{1,0:T(8,128)S(1)}, f32[576,128]{1,0:T(8,128)S(1)}, u32[]{:S(2)}, u32[]{:S(2)}) collective-permute-start(f32[576,128]{1,0:T(8,128)S(1)} %constant_dynamic-update-slice_fusion.7.refs_2_), channel_id=1, source_target_pairs={{0,1},{1,0},{2,3},{3,2},{4,5},{5,4},{6,7},{7,6},{8,9},{9,8},{10,11... | collective-permute-start | bytes 884744 | tf_op jit(solution)/shard_map/ppermute | solution.py:607
  158.1 7.0 %collective-permute-start.40 = (f32[608,128]{1,0:T(8,128)S(1)}, f32[608,128]{1,0:T(8,128)S(1)}, u32[]{:S(2)}, u32[]{:S(2)}) collective-permute-start(f32[608,128]{1,0:T(8,128)S(1)} %add.154), channel_id=1, source_target_pairs={{0,4},{1,3},{2,6},{3,1},{4,0},{5,7},{6,2},{7,5},{8,12},{9,11},{10,... | collective-permute-start | bytes 933896 | tf_op jit(solution)/shard_map/ppermute | solution.py:607
  159.5 7.2 %collective-permute-start.33 = (f32[608,128]{1,0:T(8,128)S(1)}, f32[608,128]{1,0:T(8,128)S(1)}, u32[]{:S(2)}, u32[]{:S(2)}) collective-permute-start(f32[608,128]{1,0:T(8,128)S(1)} %get-tuple-element.64), channel_id=1, source_target_pairs={{0,1},{1,0},{2,3},{3,2},{4,5},{5,4},{6,7},{7,6},{8,9},{9,8},{10,11... | collective-permute-start | bytes 933896 | tf_op jit(solution)/shard_map/ppermute | solution.py:607
  159.7 10.0 %collective-permute-start.35 = (f32[608,128]{1,0:T(8,128)S(1)}, f32[608,128]{1,0:T(8,128)S(1)}, u32[]{:S(2)}, u32[]{:S(2)}) collective-permute-start(f32[608,128]{1,0:T(8,128)S(1)} %add.149), channel_id=1, source_target_pairs={{0,4},{1,3},{2,6},{3,1},{4,0},{5,7},{6,2},{7,5},{8,12},{9,11},{10,... | collective-permute-start | bytes 933896 | tf_op jit(solution)/shard_map/ppermute | solution.py:607
  165.2 6.1 %collective-permute-start.41 = (f32[304,128]{1,0:T(8,128)S(1)}, f32[304,128]{1,0:T(8,128)S(1)}, u32[]{:S(2)}, u32[]{:S(2)}) collective-permute-start(f32[304,128]{1,0:T(8,128)S(1)} %slice.77), channel_id=1, source_target_pairs={{0,2},{1,5},{2,0},{3,7},{4,6},{5,1},{6,4},{7,3},{8,10},{9,13},{10,... | collective-permute-start | bytes 466952 | tf_op jit(solution)/shard_map/ppermute | solution.py:607
  169.8 5.3 %collective-permute-start.36 = (f32[304,128]{1,0:T(8,128)S(1)}, f32[304,128]{1,0:T(8,128)S(1)}, u32[]{:S(2)}, u32[]{:S(2)}) collective-permute-start(f32[304,128]{1,0:T(8,128)S(1)} %slice.73), channel_id=1, source_target_pairs={{0,2},{1,5},{2,0},{3,7},{4,6},{5,1},{6,4},{7,3},{8,10},{9,13},{10,... | collective-permute-start | bytes 466952 | tf_op jit(solution)/shard_map/ppermute | solution.py:607
  171.3 6.8 %collective-permute-start.43 = (f32[152,128]{1,0:T(8,128)S(1)}, f32[152,128]{1,0:T(8,128)S(1)}, u32[]{:S(2)}, u32[]{:S(2)}) collective-permute-start(f32[152,128]{1,0:T(8,128)S(1)} %get-tuple-element.83), channel_id=1, source_target_pairs={{0,24},{1,25},{2,26},{3,27},{4,28},{5,29},{6,30},{7,31},{8,16},{9,... | collective-permute-start | bytes 233480 | tf_op jit(solution)/shard_map/ppermute | solution.py:607
  172.7 7.5 %collective-permute-start.42 = (f32[152,128]{1,0:T(8,128)S(1)}, f32[152,128]{1,0:T(8,128)S(1)}, u32[]{:S(2)}, u32[]{:S(2)}) collective-permute-start(f32[152,128]{1,0:T(8,128)S(1)} %get-tuple-element.82), channel_id=1, source_target_pairs={{0,16},{1,17},{2,18},{3,19},{4,20},{5,21},{6,22},{7,23},{8,24},{9,... | collective-permute-start | bytes 233480 | tf_op jit(solution)/shard_map/ppermute | solution.py:607
  175.2 5.6 %collective-permute-start.37 = (f32[152,128]{1,0:T(8,128)S(1)}, f32[152,128]{1,0:T(8,128)S(1)}, u32[]{:S(2)}, u32[]{:S(2)}) collective-permute-start(f32[152,128]{1,0:T(8,128)S(1)} %slice.75), channel_id=1, source_target_pairs={{0,8},{1,9},{2,10},{3,11},{4,12},{5,13},{6,14},{7,15},{8,0},{9,1},... | collective-permute-start | bytes 233480 | tf_op jit(solution)/shard_map/ppermute | solution.py:607
  (16 other events, 49.9 us)

commit v8 on v7

--- a/solution.py
+++ b/solution.py
@@ -325,7 +325,7 @@
                 table[pl.ds(at, LANES), :] = block.T
             return carry
 
-        lax.fori_loop(0, near, build, 0, unroll=2)
+        lax.fori_loop(0, near, build, 0, unroll=4)
     for copy in lists:
         copy.wait()
 
@@ -580,7 +580,7 @@
             stage[pl.ds(start + planes_in, ROWSUB), :] = loss_rows
             return carry
 
-        lax.fori_loop(skip, skip + near // 2, collect, 0)
+        lax.fori_loop(skip, skip + near // 2, collect, 0, unroll=2)
         for first in range(skip, skip + near // 2, part):
             index = side * quarter + first // part
             store = pltpu.make_async_copy(

time: 185 us -> 182 us (0.984)
  Pallas kernels: 81.7 us -> 78.7 us
    pallas_call x2, Pallas kernels: 73.8 us -> 70.7 us  [per_device(): picture, *grads = render(kernel)(*settings, *table)]
  transfers between devices with their start and end apart: 44 -> 44, of which waited for: 26 -> 25; matrix products, arithmetic and copies ran while one was open for 2% -> 2% of each run, Pallas kernels for 0% -> 0%
where the time goes in v8:
time: 182 us; the launch traced here: 181 us
  Pallas kernels  78.7 us (43%)
  waiting for transfers between devices  48.8 us (27%)
  starting transfers between devices  45.2 us (25%)
  local copies, waits for them, and re-layouts  4.41 us (2%)
  other arithmetic  2.99 us (2%)
    pallas_call x2, Pallas kernels, per_device(): picture, *grads = render(kernel)(*settings, *table)  70.7 us
    ppermute x44, waiting for transfers between devices, swap(): return lax.ppermute(values, AXES, pairs)  48.8 us
    ppermute x44, starting transfers between devices, swap(): return lax.ppermute(values, AXES, pairs)  45.2 us
    pallas_call x2, Pallas kernels, per_device(): pl.pallas_call(functools.partial(update_kernel, step=step, project_next=m...  6.05 us
  transfers between devices with their start and end apart: 44, of which 25 were waited for; matrix products, arithmetic and copies ran while one was open for 2% of the time, Pallas kernels for 0%

profile of v8, /device:TPU:0, one launch (start us, length us, event | category | flops | bytes accessed | tf_op | source)
XLA Modules:
  0.0 181.3 jit_solution(10569048742015441168)
XLA Ops:
  0.6 1.9 %project.1 = f32[144,128]{1,0:T(8,128)} custom-call(f32[2,2]{1,0:T(2,128)} %cam_ref.5, f32[55,2048]{1,0:T(8,128)} %param_ref.3), custom_call_target="tpu_custom_call" | custom-call | tf_op jit(solution)/shard_map/project/pallas_call | solution.py:739
  2.5 3.1 %collective-permute-start = (f32[144,128]{1,0:T(8,128)}, f32[144,128]{1,0:T(8,128)S(1)}, u32[]{:S(2)}, u32[]{:S(2)}) collective-permute-start(f32[144,128]{1,0:T(8,128)} %project.1), channel_id=1, source_target_pairs={{0,8},{1,9},{2,10},{3,11},{4,12},{5,13},{6,14},{7,15},{8,0},{9,1},... | collective-permute-start | bytes 221192 | tf_op jit(solution)/shard_map/ppermute | solution.py:607
  5.6 2.6 %collective-permute-start.3 = (f32[144,128]{1,0:T(8,128)}, f32[144,128]{1,0:T(8,128)S(1)}, u32[]{:S(2)}, u32[]{:S(2)}) collective-permute-start(f32[144,128]{1,0:T(8,128)} %project.1), channel_id=1, source_target_pairs={{0,16},{1,17},{2,18},{3,19},{4,20},{5,21},{6,22},{7,23},{8,24},{9,... | collective-permute-start | bytes 221192 | tf_op jit(solution)/shard_map/ppermute | solution.py:607
  12.1 1.8 collective-permute-start.1
  17.3 1.8 collective-permute-start.2
  19.1 2.3 %collective-permute-done.5 = f32[288,128]{1,0:T(8,128)S(1)} collective-permute-done((f32[288,128]{1,0:T(8,128)S(1)}, f32[288,128]{1,0:T(8,128)S(1)}, u32[]{:S(2)}, u32[]{:S(2)}) %collective-permute-start.5) | collective-permute-done | bytes 147488 | tf_op jit(solution)/shard_map/ppermute | solution.py:607
  21.5 1.6 collective-permute-start.6
  24.1 4.1 %collective-permute-done.6.refs_3_ = f32[576,128]{1,0:T(8,128)S(1)} collective-permute-done((f32[576,128]{1,0:T(8,128)S(1)}, f32[576,128]{1,0:T(8,128)S(1)}, u32[]{:S(2)}, u32[]{:S(2)}) %collective-permute-start.6) | collective-permute-done | bytes 294944 | tf_op jit(solution)/shard_map/ppermute | solution.py:607
  29.8 35.4 %render.2 = (f32[96,128]{1,0:T(8,128)S(1)}, f32[608,128]{1,0:T(8,128)S(1)}, f32[608,128]{1,0:T(8,128)S(1)}, f32[608,128]{1,0:T(8,128)S(1)}, f32[608,128]{1,0:T(8...) custom-call(s32[2,16,512]{2,1,0:T(8,128)S(1)} %bitcast.16, ...), custom_call_target="tpu_custom_call" | custom-call | tf_op jit(solution)/shard_map/render/pallas_call | solution.py:761
  67.0 1.6 collective-permute-start.18
  70.1 3.9 %collective-permute-done.18 = f32[608,128]{1,0:T(8,128)S(1)} collective-permute-done((f32[608,128]{1,0:T(8,128)S(1)}, f32[608,128]{1,0:T(8,128)S(1)}, u32[]{:S(2)}, u32[]{:S(2)}) %collective-permute-start.18) | collective-permute-done | bytes 311328 | tf_op jit(solution)/shard_map/ppermute | solution.py:607
  75.4 3.1 %collective-permute-done.13 = f32[608,128]{1,0:T(8,128)S(1)} collective-permute-done((f32[608,128]{1,0:T(8,128)S(1)}, f32[608,128]{1,0:T(8,128)S(1)}, u32[]{:S(2)}, u32[]{:S(2)}) %collective-permute-start.13) | collective-permute-done | bytes 311328 | tf_op jit(solution)/shard_map/ppermute | solution.py:607
  80.1 2.9 %collective-permute-start.21 = (f32[152,128]{1,0:T(8,128)S(1)}, f32[152,128]{1,0:T(8,128)S(1)}, u32[]{:S(2)}, u32[]{:S(2)}) collective-permute-start(f32[152,128]{1,0:T(8,128)S(1)} %get-tuple-element.85), channel_id=1, source_target_pairs={{0,24},{1,25},{2,26},{3,27},{4,28},{5,29},{6,30},{7,31},{8,16},{9,... | collective-permute-start | bytes 233480 | tf_op jit(solution)/shard_map/ppermute | solution.py:607
  86.3 3.2 %collective-permute-done.20 = f32[152,128]{1,0:T(8,128)S(1)} collective-permute-done((f32[152,128]{1,0:T(8,128)S(1)}, f32[152,128]{1,0:T(8,128)S(1)}, u32[]{:S(2)}, u32[]{:S(2)}) %collective-permute-start.20) | collective-permute-done | bytes 77856 | tf_op jit(solution)/shard_map/ppermute | solution.py:607
  90.2 3.0 %update.2 = (f32[55,2048]{1,0:T(8,128)}, f32[55,2048]{1,0:T(8,128)}, f32[55,2048]{1,0:T(8,128)}, f32[144,128]{1,0:T(8,128)}) custom-call(f32[2,2]{1,0:T(2,128)} %cam_ref.5, f32[55,2048]{1,0:T(8,128)} %param_ref.3, f32[55,2048]{1,0:T(8,128)} %first_ref.1, f32[55,2048]{1,0:T(8,128)} %second_ref.1, f32[152,128]{1,0:T(8,128)} %fusion.3.grad_ref.refs_0_), custom_call_target="tpu_custom_call" | custom-call | tf_op jit(solution)/shard_map/update/pallas_call | solution.py:767
  93.5 3.1 %collective-permute-start.25 = (f32[144,128]{1,0:T(8,128)}, f32[144,128]{1,0:T(8,128)S(1)}, u32[]{:S(2)}, u32[]{:S(2)}) collective-permute-start(f32[144,128]{1,0:T(8,128)} %get-tuple-element.57), channel_id=1, source_target_pairs={{0,16},{1,17},{2,18},{3,19},{4,20},{5,21},{6,22},{7,23},{8,24},{9,... | collective-permute-start | bytes 221192 | tf_op jit(solution)/shard_map/ppermute | solution.py:607
  98.7 1.7 collective-permute-start.23
  101.0 1.9 %collective-permute-done.26 = f32[144,128]{1,0:T(8,128)S(1)} collective-permute-done((f32[144,128]{1,0:T(8,128)}, f32[144,128]{1,0:T(8,128)S(1)}, u32[]{:S(2)}, u32[]{:S(2)}) %collective-permute-start.26) | collective-permute-done | bytes 73760 | tf_op jit(solution)/shard_map/ppermute | solution.py:607
  104.4 1.7 collective-permute-start.24
  106.2 3.5 %collective-permute-done.27 = f32[288,128]{1,0:T(8,128)S(1)} collective-permute-done((f32[288,128]{1,0:T(8,128)S(1)}, f32[288,128]{1,0:T(8,128)S(1)}, u32[]{:S(2)}, u32[]{:S(2)}) %collective-permute-start.27) | collective-permute-done | bytes 147488 | tf_op jit(solution)/shard_map/ppermute | solution.py:607
  109.7 1.6 collective-permute-start.28
  111.9 4.6 %collective-permute-done.28.refs_3_ = f32[576,128]{1,0:T(8,128)S(1)} collective-permute-done((f32[576,128]{1,0:T(8,128)S(1)}, f32[576,128]{1,0:T(8,128)S(1)}, u32[]{:S(2)}, u32[]{:S(2)}) %collective-permute-start.28) | collective-permute-done | bytes 294944 | tf_op jit(solution)/shard_map/ppermute | solution.py:607
  118.1 35.3 %render.3 = (f32[96,128]{1,0:T(8,128)S(1)}, f32[608,128]{1,0:T(8,128)S(1)}, f32[608,128]{1,0:T(8,128)S(1)}, f32[608,128]{1,0:T(8,128)S(1)}, f32[608,128]{1,0:T(8...) custom-call(s32[2,16,512]{2,1,0:T(8,128)S(1)} %bitcast.17, ...), custom_call_target="tpu_custom_call" | custom-call | tf_op jit(solution)/shard_map/render/pallas_call | solution.py:761
  155.1 1.6 collective-permute-start.40
  156.8 1.7 collective-permute-start.35
  158.5 3.5 %collective-permute-done.40 = f32[608,128]{1,0:T(8,128)S(1)} collective-permute-done((f32[608,128]{1,0:T(8,128)S(1)}, f32[608,128]{1,0:T(8,128)S(1)}, u32[]{:S(2)}, u32[]{:S(2)}) %collective-permute-start.40) | collective-permute-done | bytes 311328 | tf_op jit(solution)/shard_map/ppermute | solution.py:607
  163.7 2.8 %collective-permute-done.35 = f32[608,128]{1,0:T(8,128)S(1)} collective-permute-done((f32[608,128]{1,0:T(8,128)S(1)}, f32[608,128]{1,0:T(8,128)S(1)}, u32[]{:S(2)}, u32[]{:S(2)}) %collective-permute-start.35) | collective-permute-done | bytes 311328 | tf_op jit(solution)/shard_map/ppermute | solution.py:607
  166.6 1.7 collective-permute-start.36
  168.3 1.7 collective-permute-start.43
  170.0 1.9 %collective-permute-done.36 = f32[304,128]{1,0:T(8,128)S(1)} collective-permute-done((f32[304,128]{1,0:T(8,128)S(1)}, f32[304,128]{1,0:T(8,128)S(1)}, u32[]{:S(2)}, u32[]{:S(2)}) %collective-permute-start.36) | collective-permute-done | bytes 155680 | tf_op jit(solution)/shard_map/ppermute | solution.py:607
  175.0 2.0 %collective-permute-done.42 = f32[152,128]{1,0:T(8,128)S(1)} collective-permute-done((f32[152,128]{1,0:T(8,128)S(1)}, f32[152,128]{1,0:T(8,128)S(1)}, u32[]{:S(2)}, u32[]{:S(2)}) %collective-permute-start.42) | collective-permute-done | bytes 77856 | tf_op jit(solution)/shard_map/ppermute | solution.py:607
  178.1 3.0 %update.3 = (f32[55,2048]{1,0:T(8,128)}, f32[55,2048]{1,0:T(8,128)}, f32[55,2048]{1,0:T(8,128)}, f32[2]{0:T(128)}) custom-call(f32[2,2]{1,0:T(2,128)} %cam_ref.5, f32[55,2048]{1,0:T(8,128)} %get-tuple-element.54.param_ref, f32[55,2048]{1,0:T(8,128)} %get-tuple-element.55.first_ref, f32[55,2048]{1,0:T(8,128)} %get-tuple-element.56.second_ref, ...), custom_call_target="tpu_custom_call" | custom-call | tf_op jit(solution)/shard_map/update/pallas_call | solution.py:767
  (124 shorter events, 34.5 us)
Async XLA Ops:
  2.5 8.7 %collective-permute-start = (f32[144,128]{1,0:T(8,128)}, f32[144,128]{1,0:T(8,128)S(1)}, u32[]{:S(2)}, u32[]{:S(2)}) collective-permute-start(f32[144,128]{1,0:T(8,128)} %project.1), channel_id=1, source_target_pairs={{0,8},{1,9},{2,10},{3,11},{4,12},{5,13},{6,14},{7,15},{8,0},{9,1},... | collective-permute-start | bytes 221192 | tf_op jit(solution)/shard_map/ppermute | solution.py:607
  5.6 8.3 %collective-permute-start.3 = (f32[144,128]{1,0:T(8,128)}, f32[144,128]{1,0:T(8,128)S(1)}, u32[]{:S(2)}, u32[]{:S(2)}) collective-permute-start(f32[144,128]{1,0:T(8,128)} %project.1), channel_id=1, source_target_pairs={{0,16},{1,17},{2,18},{3,19},{4,20},{5,21},{6,22},{7,23},{8,24},{9,... | collective-permute-start | bytes 221192 | tf_op jit(solution)/shard_map/ppermute | solution.py:607
  8.2 6.5 %collective-permute-start.4 = (f32[144,128]{1,0:T(8,128)}, f32[144,128]{1,0:T(8,128)S(1)}, u32[]{:S(2)}, u32[]{:S(2)}) collective-permute-start(f32[144,128]{1,0:T(8,128)} %project.1), channel_id=1, source_target_pairs={{0,24},{1,25},{2,26},{3,27},{4,28},{5,29},{6,30},{7,31},{8,16},{9,... | collective-permute-start | bytes 221192 | tf_op jit(solution)/shard_map/ppermute | solution.py:607
  12.1 5.2 %collective-permute-start.1 = (f32[288,128]{1,0:T(8,128)S(1)}, f32[288,128]{1,0:T(8,128)S(1)}, u32[]{:S(2)}, u32[]{:S(2)}) collective-permute-start(f32[288,128]{1,0:T(8,128)S(1)} %pad_maximum_fusion), channel_id=1, source_target_pairs={{0,2},{1,5},{2,0},{3,7},{4,6},{5,1},{6,4},{7,3},{8,10},{9,13},{10,... | collective-permute-start | bytes 442376 | tf_op jit(solution)/shard_map/ppermute | solution.py:607
  14.7 6.8 %collective-permute-start.5 = (f32[288,128]{1,0:T(8,128)S(1)}, f32[288,128]{1,0:T(8,128)S(1)}, u32[]{:S(2)}, u32[]{:S(2)}) collective-permute-start(f32[288,128]{1,0:T(8,128)S(1)} %pad_maximum_fusion.1), channel_id=1, source_target_pairs={{0,2},{1,5},{2,0},{3,7},{4,6},{5,1},{6,4},{7,3},{8,10},{9,13},{10,... | collective-permute-start | bytes 442376 | tf_op jit(solution)/shard_map/ppermute | solution.py:607
  17.3 6.8 %collective-permute-start.2 = (f32[576,128]{1,0:T(8,128)S(1)}, f32[576,128]{1,0:T(8,128)S(1)}, u32[]{:S(2)}, u32[]{:S(2)}) collective-permute-start(f32[576,128]{1,0:T(8,128)S(1)} %constant_dynamic-update-slice_fusion.refs_0_), channel_id=1, source_target_pairs={{0,4},{1,3},{2,6},{3,1},{4,0},{5,7},{6,2},{7,5},{8,12},{9,11},{10,... | collective-permute-start | bytes 884744 | tf_op jit(solution)/shard_map/ppermute | solution.py:607
  21.5 6.8 %collective-permute-start.6 = (f32[576,128]{1,0:T(8,128)S(1)}, f32[576,128]{1,0:T(8,128)S(1)}, u32[]{:S(2)}, u32[]{:S(2)}) collective-permute-start(f32[576,128]{1,0:T(8,128)S(1)} %constant_dynamic-update-slice_fusion.2.refs_2_), channel_id=1, source_target_pairs={{0,4},{1,3},{2,6},{3,1},{4,0},{5,7},{6,2},{7,5},{8,12},{9,11},{10,... | collective-permute-start | bytes 884744 | tf_op jit(solution)/shard_map/ppermute | solution.py:607
  23.0 5.2 %collective-permute-start.7 = (f32[576,128]{1,0:T(8,128)S(1)}, f32[576,128]{1,0:T(8,128)S(1)}, u32[]{:S(2)}, u32[]{:S(2)}) collective-permute-start(f32[576,128]{1,0:T(8,128)S(1)} %constant_dynamic-update-slice_fusion.refs_0_), channel_id=1, source_target_pairs={{0,1},{1,0},{2,3},{3,2},{4,5},{5,4},{6,7},{7,6},{8,9},{9,8},{10,11... | collective-permute-start | bytes 884744 | tf_op jit(solution)/shard_map/ppermute | solution.py:607
  23.0 5.2 %collective-permute-start.9 = (f32[576,128]{1,0:T(8,128)S(1)}, f32[576,128]{1,0:T(8,128)S(1)}, u32[]{:S(2)}, u32[]{:S(2)}) collective-permute-start(f32[576,128]{1,0:T(8,128)S(1)} %constant_dynamic-update-slice_fusion.2.refs_2_), channel_id=1, source_target_pairs={{0,1},{1,0},{2,3},{3,2},{4,5},{5,4},{6,7},{7,6},{8,9},{9,8},{10,11... | collective-permute-start | bytes 884744 | tf_op jit(solution)/shard_map/ppermute | solution.py:607
  67.0 7.0 %collective-permute-start.18 = (f32[608,128]{1,0:T(8,128)S(1)}, f32[608,128]{1,0:T(8,128)S(1)}, u32[]{:S(2)}, u32[]{:S(2)}) collective-permute-start(f32[608,128]{1,0:T(8,128)S(1)} %add.143), channel_id=1, source_target_pairs={{0,4},{1,3},{2,6},{3,1},{4,0},{5,7},{6,2},{7,5},{8,12},{9,11},{10,... | collective-permute-start | bytes 933896 | tf_op jit(solution)/shard_map/ppermute | solution.py:607
  68.6 6.8 %collective-permute-start.11 = (f32[608,128]{1,0:T(8,128)S(1)}, f32[608,128]{1,0:T(8,128)S(1)}, u32[]{:S(2)}, u32[]{:S(2)}) collective-permute-start(f32[608,128]{1,0:T(8,128)S(1)} %get-tuple-element.47), channel_id=1, source_target_pairs={{0,1},{1,0},{2,3},{3,2},{4,5},{5,4},{6,7},{7,6},{8,9},{9,8},{10,11... | collective-permute-start | bytes 933896 | tf_op jit(solution)/shard_map/ppermute | solution.py:607
  68.7 9.9 %collective-permute-start.13 = (f32[608,128]{1,0:T(8,128)S(1)}, f32[608,128]{1,0:T(8,128)S(1)}, u32[]{:S(2)}, u32[]{:S(2)}) collective-permute-start(f32[608,128]{1,0:T(8,128)S(1)} %add.138), channel_id=1, source_target_pairs={{0,4},{1,3},{2,6},{3,1},{4,0},{5,7},{6,2},{7,5},{8,12},{9,11},{10,... | collective-permute-start | bytes 933896 | tf_op jit(solution)/shard_map/ppermute | solution.py:607
  74.0 6.0 %collective-permute-start.19 = (f32[304,128]{1,0:T(8,128)S(1)}, f32[304,128]{1,0:T(8,128)S(1)}, u32[]{:S(2)}, u32[]{:S(2)}) collective-permute-start(f32[304,128]{1,0:T(8,128)S(1)} %slice.69), channel_id=1, source_target_pairs={{0,2},{1,5},{2,0},{3,7},{4,6},{5,1},{6,4},{7,3},{8,10},{9,13},{10,... | collective-permute-start | bytes 466952 | tf_op jit(solution)/shard_map/ppermute | solution.py:607
  78.6 5.3 %collective-permute-start.14 = (f32[304,128]{1,0:T(8,128)S(1)}, f32[304,128]{1,0:T(8,128)S(1)}, u32[]{:S(2)}, u32[]{:S(2)}) collective-permute-start(f32[304,128]{1,0:T(8,128)S(1)} %slice.65), channel_id=1, source_target_pairs={{0,2},{1,5},{2,0},{3,7},{4,6},{5,1},{6,4},{7,3},{8,10},{9,13},{10,... | collective-permute-start | bytes 466952 | tf_op jit(solution)/shard_map/ppermute | solution.py:607
  80.1 6.3 %collective-permute-start.21 = (f32[152,128]{1,0:T(8,128)S(1)}, f32[152,128]{1,0:T(8,128)S(1)}, u32[]{:S(2)}, u32[]{:S(2)}) collective-permute-start(f32[152,128]{1,0:T(8,128)S(1)} %get-tuple-element.85), channel_id=1, source_target_pairs={{0,24},{1,25},{2,26},{3,27},{4,28},{5,29},{6,30},{7,31},{8,16},{9,... | collective-permute-start | bytes 233480 | tf_op jit(solution)/shard_map/ppermute | solution.py:607
  83.0 6.5 %collective-permute-start.20 = (f32[152,128]{1,0:T(8,128)S(1)}, f32[152,128]{1,0:T(8,128)S(1)}, u32[]{:S(2)}, u32[]{:S(2)}) collective-permute-start(f32[152,128]{1,0:T(8,128)S(1)} %get-tuple-element.84), channel_id=1, source_target_pairs={{0,16},{1,17},{2,18},{3,19},{4,20},{5,21},{6,22},{7,23},{8,24},{9,... | collective-permute-start | bytes 233480 | tf_op jit(solution)/shard_map/ppermute | solution.py:607
  84.0 5.6 %collective-permute-start.15 = (f32[152,128]{1,0:T(8,128)S(1)}, f32[152,128]{1,0:T(8,128)S(1)}, u32[]{:S(2)}, u32[]{:S(2)}) collective-permute-start(f32[152,128]{1,0:T(8,128)S(1)} %slice.67), channel_id=1, source_target_pairs={{0,8},{1,9},{2,10},{3,11},{4,12},{5,13},{6,14},{7,15},{8,0},{9,1},... | collective-permute-start | bytes 233480 | tf_op jit(solution)/shard_map/ppermute | solution.py:607
  93.5 7.5 %collective-permute-start.25 = (f32[144,128]{1,0:T(8,128)}, f32[144,128]{1,0:T(8,128)S(1)}, u32[]{:S(2)}, u32[]{:S(2)}) collective-permute-start(f32[144,128]{1,0:T(8,128)} %get-tuple-element.57), channel_id=1, source_target_pairs={{0,16},{1,17},{2,18},{3,19},{4,20},{5,21},{6,22},{7,23},{8,24},{9,... | collective-permute-start | bytes 221192 | tf_op jit(solution)/shard_map/ppermute | solution.py:607
  96.5 6.4 %collective-permute-start.26 = (f32[144,128]{1,0:T(8,128)}, f32[144,128]{1,0:T(8,128)S(1)}, u32[]{:S(2)}, u32[]{:S(2)}) collective-permute-start(f32[144,128]{1,0:T(8,128)} %get-tuple-element.57), channel_id=1, source_target_pairs={{0,24},{1,25},{2,26},{3,27},{4,28},{5,29},{6,30},{7,31},{8,16},{9,... | collective-permute-start | bytes 221192 | tf_op jit(solution)/shard_map/ppermute | solution.py:607
  98.7 5.7 %collective-permute-start.23 = (f32[288,128]{1,0:T(8,128)S(1)}, f32[288,128]{1,0:T(8,128)S(1)}, u32[]{:S(2)}, u32[]{:S(2)}) collective-permute-start(f32[288,128]{1,0:T(8,128)S(1)} %pad_maximum_fusion.2), channel_id=1, source_target_pairs={{0,2},{1,5},{2,0},{3,7},{4,6},{5,1},{6,4},{7,3},{8,10},{9,13},{10,... | collective-permute-start | bytes 442376 | tf_op jit(solution)/shard_map/ppermute | solution.py:607
  102.9 6.8 %collective-permute-start.27 = (f32[288,128]{1,0:T(8,128)S(1)}, f32[288,128]{1,0:T(8,128)S(1)}, u32[]{:S(2)}, u32[]{:S(2)}) collective-permute-start(f32[288,128]{1,0:T(8,128)S(1)} %pad_maximum_fusion.3), channel_id=1, source_target_pairs={{0,2},{1,5},{2,0},{3,7},{4,6},{5,1},{6,4},{7,3},{8,10},{9,13},{10,... | collective-permute-start | bytes 442376 | tf_op jit(solution)/shard_map/ppermute | solution.py:607
  104.4 7.4 %collective-permute-start.24 = (f32[576,128]{1,0:T(8,128)S(1)}, f32[576,128]{1,0:T(8,128)S(1)}, u32[]{:S(2)}, u32[]{:S(2)}) collective-permute-start(f32[576,128]{1,0:T(8,128)S(1)} %constant_dynamic-update-slice_fusion.5.refs_0_), channel_id=1, source_target_pairs={{0,4},{1,3},{2,6},{3,1},{4,0},{5,7},{6,2},{7,5},{8,12},{9,11},{10,... | collective-permute-start | bytes 884744 | tf_op jit(solution)/shard_map/ppermute | solution.py:607
  109.7 6.8 %collective-permute-start.28 = (f32[576,128]{1,0:T(8,128)S(1)}, f32[576,128]{1,0:T(8,128)S(1)}, u32[]{:S(2)}, u32[]{:S(2)}) collective-permute-start(f32[576,128]{1,0:T(8,128)S(1)} %constant_dynamic-update-slice_fusion.7.refs_2_), channel_id=1, source_target_pairs={{0,4},{1,3},{2,6},{3,1},{4,0},{5,7},{6,2},{7,5},{8,12},{9,11},{10,... | collective-permute-start | bytes 884744 | tf_op jit(solution)/shard_map/ppermute | solution.py:607
  111.4 5.2 %collective-permute-start.29 = (f32[576,128]{1,0:T(8,128)S(1)}, f32[576,128]{1,0:T(8,128)S(1)}, u32[]{:S(2)}, u32[]{:S(2)}) collective-permute-start(f32[576,128]{1,0:T(8,128)S(1)} %constant_dynamic-update-slice_fusion.5.refs_0_), channel_id=1, source_target_pairs={{0,1},{1,0},{2,3},{3,2},{4,5},{5,4},{6,7},{7,6},{8,9},{9,8},{10,11... | collective-permute-start | bytes 884744 | tf_op jit(solution)/shard_map/ppermute | solution.py:607
  155.1 7.0 %collective-permute-start.40 = (f32[608,128]{1,0:T(8,128)S(1)}, f32[608,128]{1,0:T(8,128)S(1)}, u32[]{:S(2)}, u32[]{:S(2)}) collective-permute-start(f32[608,128]{1,0:T(8,128)S(1)} %add.154), channel_id=1, source_target_pairs={{0,4},{1,3},{2,6},{3,1},{4,0},{5,7},{6,2},{7,5},{8,12},{9,11},{10,... | collective-permute-start | bytes 933896 | tf_op jit(solution)/shard_map/ppermute | solution.py:607
  156.7 7.0 %collective-permute-start.33 = (f32[608,128]{1,0:T(8,128)S(1)}, f32[608,128]{1,0:T(8,128)S(1)}, u32[]{:S(2)}, u32[]{:S(2)}) collective-permute-start(f32[608,128]{1,0:T(8,128)S(1)} %get-tuple-element.64), channel_id=1, source_target_pairs={{0,1},{1,0},{2,3},{3,2},{4,5},{5,4},{6,7},{7,6},{8,9},{9,8},{10,11... | collective-permute-start | bytes 933896 | tf_op jit(solution)/shard_map/ppermute | solution.py:607
  156.8 9.8 %collective-permute-start.35 = (f32[608,128]{1,0:T(8,128)S(1)}, f32[608,128]{1,0:T(8,128)S(1)}, u32[]{:S(2)}, u32[]{:S(2)}) collective-permute-start(f32[608,128]{1,0:T(8,128)S(1)} %add.149), channel_id=1, source_target_pairs={{0,4},{1,3},{2,6},{3,1},{4,0},{5,7},{6,2},{7,5},{8,12},{9,11},{10,... | collective-permute-start | bytes 933896 | tf_op jit(solution)/shard_map/ppermute | solution.py:607
  162.1 6.2 %collective-permute-start.41 = (f32[304,128]{1,0:T(8,128)S(1)}, f32[304,128]{1,0:T(8,128)S(1)}, u32[]{:S(2)}, u32[]{:S(2)}) collective-permute-start(f32[304,128]{1,0:T(8,128)S(1)} %slice.77), channel_id=1, source_target_pairs={{0,2},{1,5},{2,0},{3,7},{4,6},{5,1},{6,4},{7,3},{8,10},{9,13},{10,... | collective-permute-start | bytes 466952 | tf_op jit(solution)/shard_map/ppermute | solution.py:607
  166.6 5.3 %collective-permute-start.36 = (f32[304,128]{1,0:T(8,128)S(1)}, f32[304,128]{1,0:T(8,128)S(1)}, u32[]{:S(2)}, u32[]{:S(2)}) collective-permute-start(f32[304,128]{1,0:T(8,128)S(1)} %slice.73), channel_id=1, source_target_pairs={{0,2},{1,5},{2,0},{3,7},{4,6},{5,1},{6,4},{7,3},{8,10},{9,13},{10,... | collective-permute-start | bytes 466952 | tf_op jit(solution)/shard_map/ppermute | solution.py:607
  168.3 6.7 %collective-permute-start.43 = (f32[152,128]{1,0:T(8,128)S(1)}, f32[152,128]{1,0:T(8,128)S(1)}, u32[]{:S(2)}, u32[]{:S(2)}) collective-permute-start(f32[152,128]{1,0:T(8,128)S(1)} %get-tuple-element.83), channel_id=1, source_target_pairs={{0,24},{1,25},{2,26},{3,27},{4,28},{5,29},{6,30},{7,31},{8,16},{9,... | collective-permute-start | bytes 233480 | tf_op jit(solution)/shard_map/ppermute | solution.py:607
  170.0 7.0 %collective-permute-start.42 = (f32[152,128]{1,0:T(8,128)S(1)}, f32[152,128]{1,0:T(8,128)S(1)}, u32[]{:S(2)}, u32[]{:S(2)}) collective-permute-start(f32[152,128]{1,0:T(8,128)S(1)} %get-tuple-element.82), channel_id=1, source_target_pairs={{0,16},{1,17},{2,18},{3,19},{4,20},{5,21},{6,22},{7,23},{8,24},{9,... | collective-permute-start | bytes 233480 | tf_op jit(solution)/shard_map/ppermute | solution.py:607
  171.9 5.5 %collective-permute-start.37 = (f32[152,128]{1,0:T(8,128)S(1)}, f32[152,128]{1,0:T(8,128)S(1)}, u32[]{:S(2)}, u32[]{:S(2)}) collective-permute-start(f32[152,128]{1,0:T(8,128)S(1)} %slice.75), channel_id=1, source_target_pairs={{0,8},{1,9},{2,10},{3,11},{4,12},{5,13},{6,14},{7,15},{8,0},{9,1},... | collective-permute-start | bytes 233480 | tf_op jit(solution)/shard_map/ppermute | solution.py:607
  (16 other events, 49.9 us)

commit v9 on v8

--- a/solution.py
+++ b/solution.py
@@ -527,7 +527,7 @@
     for group in range(groups):
         placed[group * LANES : (group + 1) * LANES, :] = tall
 
-    lax.fori_loop(0, devices * halves, functools.partial(clear, tables[:1]), 0)
+    lax.fori_loop(0, devices * halves, functools.partial(clear, tables[:1]), 0, unroll=4)
 
     def backward(index, carry):
         newest = blocks - 1 - index
@@ -580,7 +580,7 @@
             stage[pl.ds(start + planes_in, ROWSUB), :] = loss_rows
             return carry
 
-        lax.fori_loop(skip, skip + near // 2, collect, 0, unroll=2)
+        lax.fori_loop(skip, skip + near // 2, collect, 0, unroll=4)
         for first in range(skip, skip + near // 2, part):
             index = side * quarter + first // part
             store = pltpu.make_async_copy(

time: 182 us -> 181 us (level)
  transfers between devices with their start and end apart: 44 -> 44, of which waited for: 25 -> 26; matrix products, arithmetic and copies ran while one was open for 2% -> 3% of each run, Pallas kernels for 0% -> 0%
where the time goes in v9:
time: 181 us; the launch traced here: 180 us
  Pallas kernels  77.7 us (43%)
  waiting for transfers between devices  48.1 us (27%)
  starting transfers between devices  46 us (25%)
  local copies, waits for them, and re-layouts  4.41 us (2%)
  other arithmetic  2.99 us (2%)
    pallas_call x2, Pallas kernels, per_device(): picture, *grads = render(kernel)(*settings, *table)  69.8 us
    ppermute x44, waiting for transfers between devices, swap(): return lax.ppermute(values, AXES, pairs)  48.1 us
    ppermute x44, starting transfers between devices, swap(): return lax.ppermute(values, AXES, pairs)  46 us
    pallas_call x2, Pallas kernels, per_device(): pl.pallas_call(functools.partial(update_kernel, step=step, project_next=m...  6.05 us
  transfers between devices with their start and end apart: 44, of which 26 were waited for; matrix products, arithmetic and copies ran while one was open for 3% of the time, Pallas kernels for 0%

profile of v9, /device:TPU:0, one launch (start us, length us, event | category | flops | bytes accessed | tf_op | source)
XLA Modules:
  0.0 180.4 jit_solution(16339676439393490919)
XLA Ops:
  0.6 1.9 %project.1 = f32[144,128]{1,0:T(8,128)} custom-call(f32[2,2]{1,0:T(2,128)} %cam_ref.5, f32[55,2048]{1,0:T(8,128)} %param_ref.3), custom_call_target="tpu_custom_call" | custom-call | tf_op jit(solution)/shard_map/project/pallas_call | solution.py:739
  2.5 3.1 %collective-permute-start = (f32[144,128]{1,0:T(8,128)}, f32[144,128]{1,0:T(8,128)S(1)}, u32[]{:S(2)}, u32[]{:S(2)}) collective-permute-start(f32[144,128]{1,0:T(8,128)} %project.1), channel_id=1, source_target_pairs={{0,8},{1,9},{2,10},{3,11},{4,12},{5,13},{6,14},{7,15},{8,0},{9,1},... | collective-permute-start | bytes 221192 | tf_op jit(solution)/shard_map/ppermute | solution.py:607
  5.6 2.6 %collective-permute-start.3 = (f32[144,128]{1,0:T(8,128)}, f32[144,128]{1,0:T(8,128)S(1)}, u32[]{:S(2)}, u32[]{:S(2)}) collective-permute-start(f32[144,128]{1,0:T(8,128)} %project.1), channel_id=1, source_target_pairs={{0,16},{1,17},{2,18},{3,19},{4,20},{5,21},{6,22},{7,23},{8,24},{9,... | collective-permute-start | bytes 221192 | tf_op jit(solution)/shard_map/ppermute | solution.py:607
  12.1 1.8 collective-permute-start.1
  17.3 1.8 collective-permute-start.2
  19.1 2.3 %collective-permute-done.5 = f32[288,128]{1,0:T(8,128)S(1)} collective-permute-done((f32[288,128]{1,0:T(8,128)S(1)}, f32[288,128]{1,0:T(8,128)S(1)}, u32[]{:S(2)}, u32[]{:S(2)}) %collective-permute-start.5) | collective-permute-done | bytes 147488 | tf_op jit(solution)/shard_map/ppermute | solution.py:607
  21.5 1.6 collective-permute-start.6
  24.1 4.1 %collective-permute-done.6.refs_3_ = f32[576,128]{1,0:T(8,128)S(1)} collective-permute-done((f32[576,128]{1,0:T(8,128)S(1)}, f32[576,128]{1,0:T(8,128)S(1)}, u32[]{:S(2)}, u32[]{:S(2)}) %collective-permute-start.6) | collective-permute-done | bytes 294944 | tf_op jit(solution)/shard_map/ppermute | solution.py:607
  28.3 1.6 collective-permute-done.10.refs_7_
  29.8 34.9 %render.2 = (f32[96,128]{1,0:T(8,128)S(1)}, f32[608,128]{1,0:T(8,128)S(1)}, f32[608,128]{1,0:T(8,128)S(1)}, f32[608,128]{1,0:T(8,128)S(1)}, f32[608,128]{1,0:T(8...) custom-call(s32[2,16,512]{2,1,0:T(8,128)S(1)} %bitcast.16, ...), custom_call_target="tpu_custom_call" | custom-call | tf_op jit(solution)/shard_map/render/pallas_call | solution.py:761
  69.5 4.0 %collective-permute-done.18 = f32[608,128]{1,0:T(8,128)S(1)} collective-permute-done((f32[608,128]{1,0:T(8,128)S(1)}, f32[608,128]{1,0:T(8,128)S(1)}, u32[]{:S(2)}, u32[]{:S(2)}) %collective-permute-start.18) | collective-permute-done | bytes 311328 | tf_op jit(solution)/shard_map/ppermute | solution.py:607
  75.0 3.1 %collective-permute-done.13 = f32[608,128]{1,0:T(8,128)S(1)} collective-permute-done((f32[608,128]{1,0:T(8,128)S(1)}, f32[608,128]{1,0:T(8,128)S(1)}, u32[]{:S(2)}, u32[]{:S(2)}) %collective-permute-start.13) | collective-permute-done | bytes 311328 | tf_op jit(solution)/shard_map/ppermute | solution.py:607
  79.7 3.1 %collective-permute-start.21 = (f32[152,128]{1,0:T(8,128)S(1)}, f32[152,128]{1,0:T(8,128)S(1)}, u32[]{:S(2)}, u32[]{:S(2)}) collective-permute-start(f32[152,128]{1,0:T(8,128)S(1)} %get-tuple-element.85), channel_id=1, source_target_pairs={{0,24},{1,25},{2,26},{3,27},{4,28},{5,29},{6,30},{7,31},{8,16},{9,... | collective-permute-start | bytes 233480 | tf_op jit(solution)/shard_map/ppermute | solution.py:607
  86.0 2.9 %collective-permute-done.20 = f32[152,128]{1,0:T(8,128)S(1)} collective-permute-done((f32[152,128]{1,0:T(8,128)S(1)}, f32[152,128]{1,0:T(8,128)S(1)}, u32[]{:S(2)}, u32[]{:S(2)}) %collective-permute-start.20) | collective-permute-done | bytes 77856 | tf_op jit(solution)/shard_map/ppermute | solution.py:607
  89.7 3.0 %update.2 = (f32[55,2048]{1,0:T(8,128)}, f32[55,2048]{1,0:T(8,128)}, f32[55,2048]{1,0:T(8,128)}, f32[144,128]{1,0:T(8,128)}) custom-call(f32[2,2]{1,0:T(2,128)} %cam_ref.5, f32[55,2048]{1,0:T(8,128)} %param_ref.3, f32[55,2048]{1,0:T(8,128)} %first_ref.1, f32[55,2048]{1,0:T(8,128)} %second_ref.1, f32[152,128]{1,0:T(8,128)} %fusion.3.grad_ref.refs_0_), custom_call_target="tpu_custom_call" | custom-call | tf_op jit(solution)/shard_map/update/pallas_call | solution.py:767
  92.8 3.0 %collective-permute-start.25 = (f32[144,128]{1,0:T(8,128)}, f32[144,128]{1,0:T(8,128)S(1)}, u32[]{:S(2)}, u32[]{:S(2)}) collective-permute-start(f32[144,128]{1,0:T(8,128)} %get-tuple-element.57), channel_id=1, source_target_pairs={{0,16},{1,17},{2,18},{3,19},{4,20},{5,21},{6,22},{7,23},{8,24},{9,... | collective-permute-start | bytes 221192 | tf_op jit(solution)/shard_map/ppermute | solution.py:607
  98.2 1.7 collective-permute-start.23
  100.6 1.6 collective-permute-done.26
  102.2 1.9 %collective-permute-start.27 = (f32[288,128]{1,0:T(8,128)S(1)}, f32[288,128]{1,0:T(8,128)S(1)}, u32[]{:S(2)}, u32[]{:S(2)}) collective-permute-start(f32[288,128]{1,0:T(8,128)S(1)} %pad_maximum_fusion.3), channel_id=1, source_target_pairs={{0,2},{1,5},{2,0},{3,7},{4,6},{5,1},{6,4},{7,3},{8,10},{9,13},{10,... | collective-permute-start | bytes 442376 | tf_op jit(solution)/shard_map/ppermute | solution.py:607
  105.5 3.4 %collective-permute-done.27 = f32[288,128]{1,0:T(8,128)S(1)} collective-permute-done((f32[288,128]{1,0:T(8,128)S(1)}, f32[288,128]{1,0:T(8,128)S(1)}, u32[]{:S(2)}, u32[]{:S(2)}) %collective-permute-start.27) | collective-permute-done | bytes 147488 | tf_op jit(solution)/shard_map/ppermute | solution.py:607
  109.0 1.7 collective-permute-start.28
  111.2 4.5 %collective-permute-done.28.refs_3_ = f32[576,128]{1,0:T(8,128)S(1)} collective-permute-done((f32[576,128]{1,0:T(8,128)S(1)}, f32[576,128]{1,0:T(8,128)S(1)}, u32[]{:S(2)}, u32[]{:S(2)}) %collective-permute-start.28) | collective-permute-done | bytes 294944 | tf_op jit(solution)/shard_map/ppermute | solution.py:607
  115.8 1.6 collective-permute-done.32.refs_7_
  117.3 34.9 %render.3 = (f32[96,128]{1,0:T(8,128)S(1)}, f32[608,128]{1,0:T(8,128)S(1)}, f32[608,128]{1,0:T(8,128)S(1)}, f32[608,128]{1,0:T(8,128)S(1)}, f32[608,128]{1,0:T(8...) custom-call(s32[2,16,512]{2,1,0:T(8,128)S(1)} %bitcast.17, ...), custom_call_target="tpu_custom_call" | custom-call | tf_op jit(solution)/shard_map/render/pallas_call | solution.py:761
  153.9 1.7 collective-permute-start.40
  157.3 3.6 %collective-permute-done.40 = f32[608,128]{1,0:T(8,128)S(1)} collective-permute-done((f32[608,128]{1,0:T(8,128)S(1)}, f32[608,128]{1,0:T(8,128)S(1)}, u32[]{:S(2)}, u32[]{:S(2)}) %collective-permute-start.40) | collective-permute-done | bytes 311328 | tf_op jit(solution)/shard_map/ppermute | solution.py:607
  161.0 2.0 %collective-permute-start.41 = (f32[304,128]{1,0:T(8,128)S(1)}, f32[304,128]{1,0:T(8,128)S(1)}, u32[]{:S(2)}, u32[]{:S(2)}) collective-permute-start(f32[304,128]{1,0:T(8,128)S(1)} %slice.77), channel_id=1, source_target_pairs={{0,2},{1,5},{2,0},{3,7},{4,6},{5,1},{6,4},{7,3},{8,10},{9,13},{10,... | collective-permute-start | bytes 466952 | tf_op jit(solution)/shard_map/ppermute | solution.py:607
  163.0 2.3 %collective-permute-done.35 = f32[608,128]{1,0:T(8,128)S(1)} collective-permute-done((f32[608,128]{1,0:T(8,128)S(1)}, f32[608,128]{1,0:T(8,128)S(1)}, u32[]{:S(2)}, u32[]{:S(2)}) %collective-permute-start.35) | collective-permute-done | bytes 311328 | tf_op jit(solution)/shard_map/ppermute | solution.py:607
  165.4 2.3 %collective-permute-start.36 = (f32[304,128]{1,0:T(8,128)S(1)}, f32[304,128]{1,0:T(8,128)S(1)}, u32[]{:S(2)}, u32[]{:S(2)}) collective-permute-start(f32[304,128]{1,0:T(8,128)S(1)} %slice.73), channel_id=1, source_target_pairs={{0,2},{1,5},{2,0},{3,7},{4,6},{5,1},{6,4},{7,3},{8,10},{9,13},{10,... | collective-permute-start | bytes 466952 | tf_op jit(solution)/shard_map/ppermute | solution.py:607
  168.8 2.1 %collective-permute-done.36 = f32[304,128]{1,0:T(8,128)S(1)} collective-permute-done((f32[304,128]{1,0:T(8,128)S(1)}, f32[304,128]{1,0:T(8,128)S(1)}, u32[]{:S(2)}, u32[]{:S(2)}) %collective-permute-start.36) | collective-permute-done | bytes 155680 | tf_op jit(solution)/shard_map/ppermute | solution.py:607
  174.1 2.1 %collective-permute-done.42 = f32[152,128]{1,0:T(8,128)S(1)} collective-permute-done((f32[152,128]{1,0:T(8,128)S(1)}, f32[152,128]{1,0:T(8,128)S(1)}, u32[]{:S(2)}, u32[]{:S(2)}) %collective-permute-start.42) | collective-permute-done | bytes 77856 | tf_op jit(solution)/shard_map/ppermute | solution.py:607
  177.2 3.0 %update.3 = (f32[55,2048]{1,0:T(8,128)}, f32[55,2048]{1,0:T(8,128)}, f32[55,2048]{1,0:T(8,128)}, f32[2]{0:T(128)}) custom-call(f32[2,2]{1,0:T(2,128)} %cam_ref.5, f32[55,2048]{1,0:T(8,128)} %get-tuple-element.54.param_ref, f32[55,2048]{1,0:T(8,128)} %get-tuple-element.55.first_ref, f32[55,2048]{1,0:T(8,128)} %get-tuple-element.56.second_ref, ...), custom_call_target="tpu_custom_call" | custom-call | tf_op jit(solution)/shard_map/update/pallas_call | solution.py:767
  (124 shorter events, 34.0 us)
Async XLA Ops:
  2.5 8.7 %collective-permute-start = (f32[144,128]{1,0:T(8,128)}, f32[144,128]{1,0:T(8,128)S(1)}, u32[]{:S(2)}, u32[]{:S(2)}) collective-permute-start(f32[144,128]{1,0:T(8,128)} %project.1), channel_id=1, source_target_pairs={{0,8},{1,9},{2,10},{3,11},{4,12},{5,13},{6,14},{7,15},{8,0},{9,1},... | collective-permute-start | bytes 221192 | tf_op jit(solution)/shard_map/ppermute | solution.py:607
  5.6 8.3 %collective-permute-start.3 = (f32[144,128]{1,0:T(8,128)}, f32[144,128]{1,0:T(8,128)S(1)}, u32[]{:S(2)}, u32[]{:S(2)}) collective-permute-start(f32[144,128]{1,0:T(8,128)} %project.1), channel_id=1, source_target_pairs={{0,16},{1,17},{2,18},{3,19},{4,20},{5,21},{6,22},{7,23},{8,24},{9,... | collective-permute-start | bytes 221192 | tf_op jit(solution)/shard_map/ppermute | solution.py:607
  8.2 6.5 %collective-permute-start.4 = (f32[144,128]{1,0:T(8,128)}, f32[144,128]{1,0:T(8,128)S(1)}, u32[]{:S(2)}, u32[]{:S(2)}) collective-permute-start(f32[144,128]{1,0:T(8,128)} %project.1), channel_id=1, source_target_pairs={{0,24},{1,25},{2,26},{3,27},{4,28},{5,29},{6,30},{7,31},{8,16},{9,... | collective-permute-start | bytes 221192 | tf_op jit(solution)/shard_map/ppermute | solution.py:607
  12.1 5.2 %collective-permute-start.1 = (f32[288,128]{1,0:T(8,128)S(1)}, f32[288,128]{1,0:T(8,128)S(1)}, u32[]{:S(2)}, u32[]{:S(2)}) collective-permute-start(f32[288,128]{1,0:T(8,128)S(1)} %pad_maximum_fusion), channel_id=1, source_target_pairs={{0,2},{1,5},{2,0},{3,7},{4,6},{5,1},{6,4},{7,3},{8,10},{9,13},{10,... | collective-permute-start | bytes 442376 | tf_op jit(solution)/shard_map/ppermute | solution.py:607
  14.7 6.8 %collective-permute-start.5 = (f32[288,128]{1,0:T(8,128)S(1)}, f32[288,128]{1,0:T(8,128)S(1)}, u32[]{:S(2)}, u32[]{:S(2)}) collective-permute-start(f32[288,128]{1,0:T(8,128)S(1)} %pad_maximum_fusion.1), channel_id=1, source_target_pairs={{0,2},{1,5},{2,0},{3,7},{4,6},{5,1},{6,4},{7,3},{8,10},{9,13},{10,... | collective-permute-start | bytes 442376 | tf_op jit(solution)/shard_map/ppermute | solution.py:607
  17.3 6.8 %collective-permute-start.2 = (f32[576,128]{1,0:T(8,128)S(1)}, f32[576,128]{1,0:T(8,128)S(1)}, u32[]{:S(2)}, u32[]{:S(2)}) collective-permute-start(f32[576,128]{1,0:T(8,128)S(1)} %constant_dynamic-update-slice_fusion.refs_0_), channel_id=1, source_target_pairs={{0,4},{1,3},{2,6},{3,1},{4,0},{5,7},{6,2},{7,5},{8,12},{9,11},{10,... | collective-permute-start | bytes 884744 | tf_op jit(solution)/shard_map/ppermute | solution.py:607
  21.5 6.8 %collective-permute-start.6 = (f32[576,128]{1,0:T(8,128)S(1)}, f32[576,128]{1,0:T(8,128)S(1)}, u32[]{:S(2)}, u32[]{:S(2)}) collective-permute-start(f32[576,128]{1,0:T(8,128)S(1)} %constant_dynamic-update-slice_fusion.2.refs_2_), channel_id=1, source_target_pairs={{0,4},{1,3},{2,6},{3,1},{4,0},{5,7},{6,2},{7,5},{8,12},{9,11},{10,... | collective-permute-start | bytes 884744 | tf_op jit(solution)/shard_map/ppermute | solution.py:607
  23.0 5.2 %collective-permute-start.7 = (f32[576,128]{1,0:T(8,128)S(1)}, f32[576,128]{1,0:T(8,128)S(1)}, u32[]{:S(2)}, u32[]{:S(2)}) collective-permute-start(f32[576,128]{1,0:T(8,128)S(1)} %constant_dynamic-update-slice_fusion.refs_0_), channel_id=1, source_target_pairs={{0,1},{1,0},{2,3},{3,2},{4,5},{5,4},{6,7},{7,6},{8,9},{9,8},{10,11... | collective-permute-start | bytes 884744 | tf_op jit(solution)/shard_map/ppermute | solution.py:607
  23.0 5.2 %collective-permute-start.9 = (f32[576,128]{1,0:T(8,128)S(1)}, f32[576,128]{1,0:T(8,128)S(1)}, u32[]{:S(2)}, u32[]{:S(2)}) collective-permute-start(f32[576,128]{1,0:T(8,128)S(1)} %constant_dynamic-update-slice_fusion.2.refs_2_), channel_id=1, source_target_pairs={{0,1},{1,0},{2,3},{3,2},{4,5},{5,4},{6,7},{7,6},{8,9},{9,8},{10,11... | collective-permute-start | bytes 884744 | tf_op jit(solution)/shard_map/ppermute | solution.py:607
  66.5 7.0 %collective-permute-start.18 = (f32[608,128]{1,0:T(8,128)S(1)}, f32[608,128]{1,0:T(8,128)S(1)}, u32[]{:S(2)}, u32[]{:S(2)}) collective-permute-start(f32[608,128]{1,0:T(8,128)S(1)} %add.143), channel_id=1, source_target_pairs={{0,4},{1,3},{2,6},{3,1},{4,0},{5,7},{6,2},{7,5},{8,12},{9,11},{10,... | collective-permute-start | bytes 933896 | tf_op jit(solution)/shard_map/ppermute | solution.py:607
  68.0 7.0 %collective-permute-start.11 = (f32[608,128]{1,0:T(8,128)S(1)}, f32[608,128]{1,0:T(8,128)S(1)}, u32[]{:S(2)}, u32[]{:S(2)}) collective-permute-start(f32[608,128]{1,0:T(8,128)S(1)} %get-tuple-element.47), channel_id=1, source_target_pairs={{0,1},{1,0},{2,3},{3,2},{4,5},{5,4},{6,7},{7,6},{8,9},{9,8},{10,11... | collective-permute-start | bytes 933896 | tf_op jit(solution)/shard_map/ppermute | solution.py:607
  68.1 10.0 %collective-permute-start.13 = (f32[608,128]{1,0:T(8,128)S(1)}, f32[608,128]{1,0:T(8,128)S(1)}, u32[]{:S(2)}, u32[]{:S(2)}) collective-permute-start(f32[608,128]{1,0:T(8,128)S(1)} %add.138), channel_id=1, source_target_pairs={{0,4},{1,3},{2,6},{3,1},{4,0},{5,7},{6,2},{7,5},{8,12},{9,11},{10,... | collective-permute-start | bytes 933896 | tf_op jit(solution)/shard_map/ppermute | solution.py:607
  73.5 6.1 %collective-permute-start.19 = (f32[304,128]{1,0:T(8,128)S(1)}, f32[304,128]{1,0:T(8,128)S(1)}, u32[]{:S(2)}, u32[]{:S(2)}) collective-permute-start(f32[304,128]{1,0:T(8,128)S(1)} %slice.69), channel_id=1, source_target_pairs={{0,2},{1,5},{2,0},{3,7},{4,6},{5,1},{6,4},{7,3},{8,10},{9,13},{10,... | collective-permute-start | bytes 466952 | tf_op jit(solution)/shard_map/ppermute | solution.py:607
  78.1 5.3 %collective-permute-start.14 = (f32[304,128]{1,0:T(8,128)S(1)}, f32[304,128]{1,0:T(8,128)S(1)}, u32[]{:S(2)}, u32[]{:S(2)}) collective-permute-start(f32[304,128]{1,0:T(8,128)S(1)} %slice.65), channel_id=1, source_target_pairs={{0,2},{1,5},{2,0},{3,7},{4,6},{5,1},{6,4},{7,3},{8,10},{9,13},{10,... | collective-permute-start | bytes 466952 | tf_op jit(solution)/shard_map/ppermute | solution.py:607
  79.7 6.3 %collective-permute-start.21 = (f32[152,128]{1,0:T(8,128)S(1)}, f32[152,128]{1,0:T(8,128)S(1)}, u32[]{:S(2)}, u32[]{:S(2)}) collective-permute-start(f32[152,128]{1,0:T(8,128)S(1)} %get-tuple-element.85), channel_id=1, source_target_pairs={{0,24},{1,25},{2,26},{3,27},{4,28},{5,29},{6,30},{7,31},{8,16},{9,... | collective-permute-start | bytes 233480 | tf_op jit(solution)/shard_map/ppermute | solution.py:607
  82.8 6.2 %collective-permute-start.20 = (f32[152,128]{1,0:T(8,128)S(1)}, f32[152,128]{1,0:T(8,128)S(1)}, u32[]{:S(2)}, u32[]{:S(2)}) collective-permute-start(f32[152,128]{1,0:T(8,128)S(1)} %get-tuple-element.84), channel_id=1, source_target_pairs={{0,16},{1,17},{2,18},{3,19},{4,20},{5,21},{6,22},{7,23},{8,24},{9,... | collective-permute-start | bytes 233480 | tf_op jit(solution)/shard_map/ppermute | solution.py:607
  83.5 5.6 %collective-permute-start.15 = (f32[152,128]{1,0:T(8,128)S(1)}, f32[152,128]{1,0:T(8,128)S(1)}, u32[]{:S(2)}, u32[]{:S(2)}) collective-permute-start(f32[152,128]{1,0:T(8,128)S(1)} %slice.67), channel_id=1, source_target_pairs={{0,8},{1,9},{2,10},{3,11},{4,12},{5,13},{6,14},{7,15},{8,0},{9,1},... | collective-permute-start | bytes 233480 | tf_op jit(solution)/shard_map/ppermute | solution.py:607
  92.8 7.8 %collective-permute-start.25 = (f32[144,128]{1,0:T(8,128)}, f32[144,128]{1,0:T(8,128)S(1)}, u32[]{:S(2)}, u32[]{:S(2)}) collective-permute-start(f32[144,128]{1,0:T(8,128)} %get-tuple-element.57), channel_id=1, source_target_pairs={{0,16},{1,17},{2,18},{3,19},{4,20},{5,21},{6,22},{7,23},{8,24},{9,... | collective-permute-start | bytes 221192 | tf_op jit(solution)/shard_map/ppermute | solution.py:607
  95.8 6.4 %collective-permute-start.26 = (f32[144,128]{1,0:T(8,128)}, f32[144,128]{1,0:T(8,128)S(1)}, u32[]{:S(2)}, u32[]{:S(2)}) collective-permute-start(f32[144,128]{1,0:T(8,128)} %get-tuple-element.57), channel_id=1, source_target_pairs={{0,24},{1,25},{2,26},{3,27},{4,28},{5,29},{6,30},{7,31},{8,16},{9,... | collective-permute-start | bytes 221192 | tf_op jit(solution)/shard_map/ppermute | solution.py:607
  98.2 5.9 %collective-permute-start.23 = (f32[288,128]{1,0:T(8,128)S(1)}, f32[288,128]{1,0:T(8,128)S(1)}, u32[]{:S(2)}, u32[]{:S(2)}) collective-permute-start(f32[288,128]{1,0:T(8,128)S(1)} %pad_maximum_fusion.2), channel_id=1, source_target_pairs={{0,2},{1,5},{2,0},{3,7},{4,6},{5,1},{6,4},{7,3},{8,10},{9,13},{10,... | collective-permute-start | bytes 442376 | tf_op jit(solution)/shard_map/ppermute | solution.py:607
  102.2 6.8 %collective-permute-start.27 = (f32[288,128]{1,0:T(8,128)S(1)}, f32[288,128]{1,0:T(8,128)S(1)}, u32[]{:S(2)}, u32[]{:S(2)}) collective-permute-start(f32[288,128]{1,0:T(8,128)S(1)} %pad_maximum_fusion.3), channel_id=1, source_target_pairs={{0,2},{1,5},{2,0},{3,7},{4,6},{5,1},{6,4},{7,3},{8,10},{9,13},{10,... | collective-permute-start | bytes 442376 | tf_op jit(solution)/shard_map/ppermute | solution.py:607
  104.1 7.1 %collective-permute-start.24 = (f32[576,128]{1,0:T(8,128)S(1)}, f32[576,128]{1,0:T(8,128)S(1)}, u32[]{:S(2)}, u32[]{:S(2)}) collective-permute-start(f32[576,128]{1,0:T(8,128)S(1)} %constant_dynamic-update-slice_fusion.5.refs_0_), channel_id=1, source_target_pairs={{0,4},{1,3},{2,6},{3,1},{4,0},{5,7},{6,2},{7,5},{8,12},{9,11},{10,... | collective-permute-start | bytes 884744 | tf_op jit(solution)/shard_map/ppermute | solution.py:607
  109.0 6.8 %collective-permute-start.28 = (f32[576,128]{1,0:T(8,128)S(1)}, f32[576,128]{1,0:T(8,128)S(1)}, u32[]{:S(2)}, u32[]{:S(2)}) collective-permute-start(f32[576,128]{1,0:T(8,128)S(1)} %constant_dynamic-update-slice_fusion.7.refs_2_), channel_id=1, source_target_pairs={{0,4},{1,3},{2,6},{3,1},{4,0},{5,7},{6,2},{7,5},{8,12},{9,11},{10,... | collective-permute-start | bytes 884744 | tf_op jit(solution)/shard_map/ppermute | solution.py:607
  110.7 5.1 %collective-permute-start.29 = (f32[576,128]{1,0:T(8,128)S(1)}, f32[576,128]{1,0:T(8,128)S(1)}, u32[]{:S(2)}, u32[]{:S(2)}) collective-permute-start(f32[576,128]{1,0:T(8,128)S(1)} %constant_dynamic-update-slice_fusion.5.refs_0_), channel_id=1, source_target_pairs={{0,1},{1,0},{2,3},{3,2},{4,5},{5,4},{6,7},{7,6},{8,9},{9,8},{10,11... | collective-permute-start | bytes 884744 | tf_op jit(solution)/shard_map/ppermute | solution.py:607
  153.9 7.0 %collective-permute-start.40 = (f32[608,128]{1,0:T(8,128)S(1)}, f32[608,128]{1,0:T(8,128)S(1)}, u32[]{:S(2)}, u32[]{:S(2)}) collective-permute-start(f32[608,128]{1,0:T(8,128)S(1)} %add.154), channel_id=1, source_target_pairs={{0,4},{1,3},{2,6},{3,1},{4,0},{5,7},{6,2},{7,5},{8,12},{9,11},{10,... | collective-permute-start | bytes 933896 | tf_op jit(solution)/shard_map/ppermute | solution.py:607
  155.7 7.3 %collective-permute-start.33 = (f32[608,128]{1,0:T(8,128)S(1)}, f32[608,128]{1,0:T(8,128)S(1)}, u32[]{:S(2)}, u32[]{:S(2)}) collective-permute-start(f32[608,128]{1,0:T(8,128)S(1)} %get-tuple-element.64), channel_id=1, source_target_pairs={{0,1},{1,0},{2,3},{3,2},{4,5},{5,4},{6,7},{7,6},{8,9},{9,8},{10,11... | collective-permute-start | bytes 933896 | tf_op jit(solution)/shard_map/ppermute | solution.py:607
  155.9 9.4 %collective-permute-start.35 = (f32[608,128]{1,0:T(8,128)S(1)}, f32[608,128]{1,0:T(8,128)S(1)}, u32[]{:S(2)}, u32[]{:S(2)}) collective-permute-start(f32[608,128]{1,0:T(8,128)S(1)} %add.149), channel_id=1, source_target_pairs={{0,4},{1,3},{2,6},{3,1},{4,0},{5,7},{6,2},{7,5},{8,12},{9,11},{10,... | collective-permute-start | bytes 933896 | tf_op jit(solution)/shard_map/ppermute | solution.py:607
  161.0 6.7 %collective-permute-start.41 = (f32[304,128]{1,0:T(8,128)S(1)}, f32[304,128]{1,0:T(8,128)S(1)}, u32[]{:S(2)}, u32[]{:S(2)}) collective-permute-start(f32[304,128]{1,0:T(8,128)S(1)} %slice.77), channel_id=1, source_target_pairs={{0,2},{1,5},{2,0},{3,7},{4,6},{5,1},{6,4},{7,3},{8,10},{9,13},{10,... | collective-permute-start | bytes 466952 | tf_op jit(solution)/shard_map/ppermute | solution.py:607
  165.4 5.5 %collective-permute-start.36 = (f32[304,128]{1,0:T(8,128)S(1)}, f32[304,128]{1,0:T(8,128)S(1)}, u32[]{:S(2)}, u32[]{:S(2)}) collective-permute-start(f32[304,128]{1,0:T(8,128)S(1)} %slice.73), channel_id=1, source_target_pairs={{0,2},{1,5},{2,0},{3,7},{4,6},{5,1},{6,4},{7,3},{8,10},{9,13},{10,... | collective-permute-start | bytes 466952 | tf_op jit(solution)/shard_map/ppermute | solution.py:607
  167.7 6.4 %collective-permute-start.43 = (f32[152,128]{1,0:T(8,128)S(1)}, f32[152,128]{1,0:T(8,128)S(1)}, u32[]{:S(2)}, u32[]{:S(2)}) collective-permute-start(f32[152,128]{1,0:T(8,128)S(1)} %get-tuple-element.83), channel_id=1, source_target_pairs={{0,24},{1,25},{2,26},{3,27},{4,28},{5,29},{6,30},{7,31},{8,16},{9,... | collective-permute-start | bytes 233480 | tf_op jit(solution)/shard_map/ppermute | solution.py:607
  168.7 7.5 %collective-permute-start.42 = (f32[152,128]{1,0:T(8,128)S(1)}, f32[152,128]{1,0:T(8,128)S(1)}, u32[]{:S(2)}, u32[]{:S(2)}) collective-permute-start(f32[152,128]{1,0:T(8,128)S(1)} %get-tuple-element.82), channel_id=1, source_target_pairs={{0,16},{1,17},{2,18},{3,19},{4,20},{5,21},{6,22},{7,23},{8,24},{9,... | collective-permute-start | bytes 233480 | tf_op jit(solution)/shard_map/ppermute | solution.py:607
  170.9 5.6 %collective-permute-start.37 = (f32[152,128]{1,0:T(8,128)S(1)}, f32[152,128]{1,0:T(8,128)S(1)}, u32[]{:S(2)}, u32[]{:S(2)}) collective-permute-start(f32[152,128]{1,0:T(8,128)S(1)} %slice.75), channel_id=1, source_target_pairs={{0,8},{1,9},{2,10},{3,11},{4,12},{5,13},{6,14},{7,15},{8,0},{9,1},... | collective-permute-start | bytes 233480 | tf_op jit(solution)/shard_map/ppermute | solution.py:607
  (16 other events, 50.1 us)
